TPU v7x, 256 devices: a whole 4x4x8 slice. The times are simulated.
256 devices in a mesh: band: 32 (over x_hi, z, core), var: 8 (over y, x_lo).
Axes of the slice: x: 4 (x_hi: 2, x_lo: 2; x = x_hi * 2 + x_lo), y: 4, z: 8, core: 2. Of those that a mesh axis runs over, the one named last changes fastest.
Arguments:
- patches: bfloat16 [16, 32, 256, 64], P('var', 'band'), may hold values from -6 to 6
- w_embed: bfloat16 [16, 64, 2048], P('var'), may hold values from -0.75 to 0.75
- var_bias: float32 [16, 2048], P('var'), may hold values from -3 to 3
- agg_gain: float32 [2048], replicated, may hold values from 0.1 to 1.9
- wq: bfloat16 [2048, 2048], P(None, 'var'), may hold values from -4 to 4
- wk: bfloat16 [2048, 2048], P(None, 'var'), may hold values from -4 to 4
- wv: bfloat16 [2048, 2048], P(None, 'var'), may hold values from -0.125 to 0.125
- wo: bfloat16 [2048, 2048], P('var'), may hold values from -0.125 to 0.125
- w_up: bfloat16 [2048, 1024], replicated, may hold values from -0.125 to 0.125
- conv1: bfloat16 [9, 64, 64], replicated, may hold values from -0.25 to 0.25
- bias1: float32 [64], replicated, may hold values from -3 to 3
- conv2: bfloat16 [9, 64, 64], replicated, may hold values from -0.25 to 0.25
- cotangent: bfloat16 [128, 64, 1024], P('band', None, 'var'), may hold values from -6 to 6
Outputs:
- field_out: bfloat16 [128, 64, 1024], P('band', None, 'var')
- grad_fine: bfloat16 [128, 64, 1024], P('band', None, 'var')
- grad_conv1: float32 [9, 64, 64], replicated
- grad_conv2: float32 [9, 64, 64], replicated
- grad_bias: float32 [64], replicated
All inputs are finite; a program needn't handle non-finite values.
Results may differ from a plain program's by a relative error of at most 0.03.
Values may be sent and summed in bfloat16 or wider, within the bound.
No kernel may reach another device: no remote copies, remote signals or barrier semaphores. Data moves between devices by JAX's collectives and lax.ppermute only.
A program may use at most 128 MiB of HBM per device.

v0:
```python
import math

import jax
import jax.numpy as jnp
from jax import lax
from jax.sharding import PartitionSpec as P

D = 2048
HD = 128
C = 64
R = 4


def with_halo(cells, sides, width):
    for axis, dim in sides:
        count = lax.axis_size(axis)
        ends = count - 1
        head = lax.slice_in_dim(cells, 0, width, axis=dim)
        tail = lax.slice_in_dim(cells, cells.shape[dim] - width, cells.shape[dim], axis=dim)
        cells = jnp.concatenate(
            [
                lax.ppermute(tail, axis, [(i, (i + 1) % count) for i in range(ends)]),
                cells,
                lax.ppermute(head, axis, [((i + 1) % count, i) for i in range(ends)]),
            ],
            axis=dim,
        )
    return cells


def tap_stack(padded, height, width):
    pieces = [
        padded[row_tap : row_tap + height, :, col_tap : col_tap + width]
        for row_tap in range(3)
        for col_tap in range(3)
    ]
    return jnp.concatenate(pieces, axis=1)


def conv_padded(padded, weight, height, width):
    stacked = tap_stack(padded, height, width)
    return jnp.einsum(
        "ykx,ko->yox",
        stacked,
        weight.reshape(-1, weight.shape[2]),
        preferred_element_type=jnp.float32,
    )


def flipped(weight):
    return jnp.transpose(weight[::-1], (0, 2, 1))


def weight_grad(padded, grads):
    stacked = tap_stack(padded, grads.shape[0], grads.shape[2])
    summed = jnp.einsum("ykx,yox->ko", stacked, grads, preferred_element_type=jnp.float32)
    return summed.reshape(9, padded.shape[1], grads.shape[1])


def normalize(mixed, agg_gain):
    return (
        mixed * lax.rsqrt(jnp.mean(mixed * mixed, axis=-1, keepdims=True) + 1e-05) * agg_gain
    ).astype(jnp.bfloat16)


def gradient_rim(field):
    return with_halo(field, (("band", 0), ("var", 2)), 1)


def on_device(
    patches, w_embed, var_bias, agg_gain, wq, wk, wv, wo, w_up, conv1, bias1, conv2, cotangent
):
    var_count = lax.axis_size("var")
    band_count = lax.axis_size("band")
    var_local, lat_dev, lon_all, patch_len = patches.shape
    lon_dev = lon_all // var_count
    flattened = jnp.transpose(patches, (1, 2, 0, 3)).reshape(
        lat_dev * lon_all, var_local * patch_len
    )
    partial_mix = jnp.dot(
        flattened, w_embed.reshape(var_local * patch_len, D), preferred_element_type=jnp.float32
    )
    partial_mix = (partial_mix + jnp.sum(var_bias, axis=0)).reshape(lat_dev, lon_all, D)
    mixed = lax.psum(partial_mix.astype(jnp.bfloat16), "var").astype(jnp.float32)
    normed_band = normalize(mixed, agg_gain)
    normed_slab = lax.dynamic_slice_in_dim(normed_band, lax.axis_index("var") * lon_dev, lon_dev, 1)
    token_rows = jnp.transpose(
        normed_band.reshape(lat_dev, var_count, lon_dev, D), (1, 0, 2, 3)
    ).reshape(-1, D)
    heads_local = wq.shape[1] // HD
    query_rows = token_rows.shape[0]
    queries = jnp.dot(token_rows, wq, preferred_element_type=jnp.float32).astype(jnp.bfloat16)
    keys_local = jnp.dot(token_rows, wk, preferred_element_type=jnp.float32).astype(jnp.bfloat16)
    values_local = jnp.dot(token_rows, wv, preferred_element_type=jnp.float32).astype(jnp.bfloat16)
    query_heads = queries.reshape(query_rows, heads_local, HD)
    running_max = jnp.full((heads_local, query_rows), -1e30, jnp.float32)
    key_heads = lax.all_gather(keys_local, "band", axis=0, tiled=True).reshape(-1, heads_local, HD)
    value_heads = lax.all_gather(values_local, "band", axis=0, tiled=True).reshape(
        -1, heads_local, HD
    )
    scores = jnp.einsum(
        "qhd,khd->hqk", query_heads, key_heads, preferred_element_type=jnp.float32
    ) / math.sqrt(HD)
    new_max = jnp.maximum(running_max, jnp.max(scores, axis=2))
    weights = jnp.exp(scores - new_max[:, :, None])
    new_sum = jnp.sum(weights, axis=2)
    update = jnp.einsum(
        "hqk,khd->hqd",
        weights.astype(jnp.bfloat16),
        value_heads,
        preferred_element_type=jnp.float32,
    )
    context = (update / new_sum[:, :, None]).astype(jnp.bfloat16)
    context = jnp.transpose(context, (1, 0, 2)).reshape(query_rows, heads_local * HD)
    slab_rows = lat_dev * lon_dev
    attended = lax.psum_scatter(
        jnp.dot(context, wo, preferred_element_type=jnp.float32).astype(jnp.bfloat16),
        "var",
        scatter_dimension=0,
        tiled=True,
    ).astype(jnp.float32)
    hidden = (normed_slab.reshape(slab_rows, D).astype(jnp.float32) + attended).astype(jnp.bfloat16)
    upsampled = jnp.dot(hidden, w_up, preferred_element_type=jnp.float32).astype(jnp.bfloat16)
    height = lat_dev * R
    width = lon_dev * R
    upsampled = jnp.transpose(
        upsampled.reshape(lat_dev, lon_dev, R, R, C), (0, 2, 4, 1, 3)
    ).reshape(height, C, width)
    bias_cols = bias1[None, :, None]
    fine_pad = with_halo(upsampled, (("band", 0), ("var", 2)), 1)
    pre = conv_padded(fine_pad, conv1, height, width) + bias_cols
    active = jax.nn.gelu(pre).astype(jnp.bfloat16)
    active_pad = with_halo(active, (("band", 0), ("var", 2)), 1)
    field_out = (
        conv_padded(active_pad, conv2, height, width) + upsampled.astype(jnp.float32)
    ).astype(jnp.bfloat16)
    cotangent_pad = gradient_rim(cotangent)
    d_active = conv_padded(cotangent_pad, flipped(conv2), height, width)
    d_pre = jax.vjp(jax.nn.gelu, pre)[1](d_active)[0].astype(jnp.bfloat16)
    d_pre_pad = gradient_rim(d_pre)
    grad_fine = (
        cotangent.astype(jnp.float32) + conv_padded(d_pre_pad, flipped(conv1), height, width)
    ).astype(jnp.bfloat16)
    factor = 1.0 / math.sqrt(height * band_count * width * var_count)
    first_terms = weight_grad(fine_pad, d_pre) * factor
    second_terms = weight_grad(active_pad, cotangent) * factor
    bias_terms = jnp.sum(d_pre.astype(jnp.float32), axis=(0, 2)) * factor
    grad_conv1, grad_conv2, grad_bias = lax.psum(
        (first_terms, second_terms, bias_terms), ("band", "var")
    )
    return (field_out, grad_fine, grad_conv1, grad_conv2, grad_bias)


def solution(mesh):
    in_specs = (
        P("var", "band", None, None),
        P("var", None, None),
        P("var", None),
        P(),
        P(None, "var"),
        P(None, "var"),
        P(None, "var"),
        P("var", None),
        P(),
        P(),
        P(),
        P(),
        P("band", None, "var"),
    )
    out_specs = (P("band", None, "var"), P("band", None, "var"), P(), P(), P())
    return jax.shard_map(
        on_device, mesh=mesh, in_specs=in_specs, out_specs=out_specs, check_vma=False
    )
```

profile of v0, /device:TPU:1, one launch (start us, length us, event | category | flops | bytes accessed | tf_op | source)
XLA Modules:
  0.0 733.0 jit_solution(12546269796696864949)
XLA Ops:
  8.1 2.5 fusion.10
  10.7 85.5 %all-reduce.4.cloned.1.call-done = bf16[1,256,2048]{2,1,0:T(8,128)(2,1)} async-done(((bf16[1,256,2048]{2,1,0:T(8,128)(2,1)}), bf16[1,256,2048]{2,1,0:T(8,128)(2,1)}) %all-reduce.4.cloned.1.call-update) | async-done | bytes 1048592 | tf_op jit(solution)/shard_map/psum | solution.py:84
  100.4 2.3 convolution_convert_fusion.1
  102.8 1.7 convolution_convert_fusion.3
  104.6 86.7 %all-gather.3.cloned.1.call-done = bf16[8192,256]{1,0:T(8,128)(2,1)} async-done(((bf16[256,256]{1,0:T(8,128)(2,1)}), bf16[8192,256]{1,0:T(8,128)(2,1)}) %all-gather.3.cloned.1.call-update) | async-done | bytes 4194320 | tf_op jit(solution)/shard_map/all_gather | solution.py:97
  191.3 9.3 %multiply_reduce_fusion = (f32[2,256]{1,0:T(2,128)S(1)}, f32[2,256,8192]{2,1,0:T(8,128)}) fusion(bf16[256,2,128]{0,2,1:T(8,128)(2,1)S(1)} %bitcast.117, bf16[8192,256]{1,0:T(8,128)(2,1)} %all-gather.3.cloned.1.call-done), kind=kOutput, calls=%fused_computation.1 | convolution fusion | flops 1082129920 | bytes 21104640 | tf_op jit(solution)/shard_map/qhd,khd->hqk/dot_general | solution.py:101
  200.6 8.8 %fusion = f32[2,256]{1,0:T(2,128)S(1)} fusion(f32[2,256,8192]{2,1,0:T(8,128)} %get-tuple-element.32, f32[2,256]{1,0:T(2,128)S(1)} %broadcast_maximum_fusion), kind=kLoop, calls=%fused_computation.2 | loop fusion | flops 12582400 | bytes 16781312 | tf_op jit(solution)/shard_map/reduce_sum | solution.py:106
  209.4 68.6 %all-gather.5.cloned.1.call-done = bf16[8192,256]{1,0:T(8,128)(2,1)} async-done(((bf16[256,256]{1,0:T(8,128)(2,1)}), bf16[8192,256]{1,0:T(8,128)(2,1)}) %all-gather.5.cloned.1.call-update) | async-done | bytes 4194320 | tf_op jit(solution)/shard_map/all_gather | solution.py:98
  278.0 6.4 copy.52
  284.4 10.4 %fusion.27 = bf16[256,2,128]{0,2,1:T(8,128)(2,1)S(1)} fusion(bf16[8192,2,128]{0,2,1:T(8,128)(2,1)} %bitcast.110, f32[2,256,8192]{2,1,0:T(8,128)} %get-tuple-element.32, f32[2,256]{1,0:T(2,128)S(1)} %broadcast_maximum_fusion, f32[256,2]{0,1:T(2,128)S(1)} %bitcast.125), kind=kOutput, calls=%fused_computation.38 | convolution fusion | flops 1086455808 | bytes 21106688 | tf_op jit(solution)/shard_map/hqk,khd->hqd/dot_general | solution.py:107
  296.4 3.0 collective-permute-start.8
  299.4 1.9 collective-permute-start.9
  301.5 3.0 collective-permute-done.9
  304.6 2.2 collective-permute-start.10
  311.0 6.8 collective-permute-done.11
  321.3 11.4 %reduce-scatter.2.cloned.1.call-done = bf16[32,2048]{1,0:T(8,128)(2,1)} async-done(((bf16[256,2048]{1,0:T(8,128)(2,1)}), bf16[32,2048]{1,0:T(8,128)(2,1)}) %reduce-scatter.2.cloned.1.call-update) | async-done | bytes 131088 | tf_op jit(solution)/shard_map/reduce_scatter | solution.py:116
  332.7 3.1 convolution_convert_fusion.4
  336.1 8.2 %collective-permute-start = (bf16[1,64,128]{2,1,0:T(8,128)(2,1)S(1)}, bf16[1,64,128]{2,1,0:T(8,128)(2,1)S(1)}, u32[]{:S(2)}, u32[]{:S(2)}) collective-permute-start(bf16[1,64,128]{2,1,0:T(8,128)(2,1)S(1)} %copy.32), channel_id=1, source_target_pairs={{0,8},{8,16},{16,24},{24,32},{32,40},{40,48},{48,56},{56,64},{64,7... | collective-permute-start | bytes 49160 | tf_op jit(solution)/shard_map/ppermute | solution.py:22
  344.4 1.9 collective-permute-start.1
  347.1 2.4 collective-permute-done.1
  349.6 1.6 collective-permute-start.2
  353.2 3.3 collective-permute-done.3
  360.2 3.7 collective-permute-start.4
  363.8 1.9 collective-permute-start.5
  365.8 3.6 collective-permute-start.12
  369.4 1.9 collective-permute-start.13
  371.4 84.9 %psum.31 = f32[64]{0:T(128)} all-reduce(f32[64]{0:T(128)S(1)} %broadcast_multiply_fusion), channel_id=1, replica_groups=mesh['band'=32,'var'=8] {'band','var'}, use_global_device_ids=true, to_apply=%region_9.0 | all-reduce | flops 64 | bytes 512 | tf_op jit(solution)/shard_map/psum | solution.py:148
  459.1 4.0 collective-permute-start.14
  466.2 4.2 collective-permute-done.15
  472.8 250.3 %all-reduce.6.cloned.1.call-done = (f32[9,64,64]{2,1,0:T(8,128)}, f32[9,64,64]{2,1,0:T(8,128)}) async-done(((f32[9,64,64]{2,1,0:T(8,128)}, f32[9,64,64]{2,1,0:T(8,128)}), (f32[9,64,64]{2,1,0:T(8,128)}, f32[9,64,64]{2,1,0:T(8,128)})) %all-reduce.6.cloned.1.call-update) | async-done | bytes 294928 | tf_op jit(solution)/shard_map/psum | solution.py:148
  723.1 1.7 copy.104
  724.7 1.7 copy.105
  (118 shorter events, 29.6 us)
Async XLA Ops:
  7.2 287.6 %copy-start = (bf16[256,2048]{1,0:T(8,128)(2,1)S(1)}, bf16[256,2048]{1,0:T(8,128)(2,1)}, u32[]{:S(2)}) copy-start(bf16[256,2048]{1,0:T(8,128)(2,1)} %param.20) | copy-start | bytes 3145732
  7.2 92.1 %copy-start.2 = (bf16[2048,256]{1,0:T(8,128)(2,1)S(1)}, bf16[2048,256]{1,0:T(8,128)(2,1)}, u32[]{:S(2)}) copy-start(bf16[2048,256]{1,0:T(8,128)(2,1)} %param.18) | copy-start | bytes 3145732
  7.2 89.0 %all-reduce.4.cloned.1.call-start = ((), (), s32[]{:S(2)}) async-start(), calls=%async_computation.1 | async-start | bytes 2097152 | tf_op jit(solution)/shard_map/psum | solution.py:84
  10.6 180.7 %all-gather.3.cloned.1.call-start = ((), (), s32[]{:S(2)}) async-start(), calls=%async_computation.2 | async-start | bytes 4325376 | tf_op jit(solution)/shard_map/all_gather | solution.py:97
  100.4 177.6 %all-gather.5.cloned.1.call-start = ((), (), s32[]{:S(2)}) async-start(), calls=%async_computation.3 | async-start | bytes 4325376 | tf_op jit(solution)/shard_map/all_gather | solution.py:98
  102.8 229.9 %reduce-scatter.2.cloned.1.call-start = ((), (), s32[]{:S(2)}) async-start(), calls=%async_computation.4 | async-start | bytes 1179648 | tf_op jit(solution)/shard_map/reduce_scatter | solution.py:116
  284.4 12.0 %copy-start.1 = (bf16[4,64,128]{2,1,0:T(8,128)(2,1)S(1)}, bf16[4,64,128]{2,1,0:T(8,128)(2,1)}, u32[]{:S(2)}) copy-start(bf16[4,64,128]{2,1,0:T(8,128)(2,1)} %param.25) | copy-start | bytes 196612
  284.4 17.0 %copy-start.3 = (bf16[9,64,64]{2,1,0:T(8,128)(2,1)S(1)}, bf16[9,64,64]{2,1,0:T(8,128)(2,1)}, u32[]{:S(2)}) copy-start(bf16[9,64,64]{2,1,0:T(8,128)(2,1)} %param.24) | copy-start | bytes 221188
  284.4 17.0 %copy-start.4 = (bf16[9,64,64]{2,1,0:T(8,128)(2,1)S(1)}, bf16[9,64,64]{2,1,0:T(8,128)(2,1)}, u32[]{:S(2)}) copy-start(bf16[9,64,64]{2,1,0:T(8,128)(2,1)} %param.22) | copy-start | bytes 221188
  296.3 426.7 %all-reduce.6.cloned.1.call-start = ((), (), s32[]{:S(2)}) async-start(), calls=%async_computation.5 | async-start | bytes 1179648 | tf_op jit(solution)/shard_map/psum | solution.py:148
  296.4 5.0 collective-permute-start.8
  299.4 5.1 collective-permute-start.9
  301.4 3.1 copy-start.5
  304.6 4.3 collective-permute-start.10
  307.1 10.6 %collective-permute-start.11 = (bf16[6,64,1]{2,1,0:T(8,128)(2,1)S(1)}, bf16[6,64,1]{2,1,0:T(8,128)(2,1)S(1)}, u32[]{:S(2)}, u32[]{:S(2)}) collective-permute-start(bf16[6,64,1]{2,1,0:T(8,128)(2,1)S(1)} %get-tuple-element.15), channel_id=1, source_target_pairs={{1,0},{2,1},{3,2},{4,3},{5,4},{6,5},{7,6},{9,8},{10,9},{11,10},{12... | collective-permute-start | bytes 2312 | tf_op jit(solution)/shard_map/ppermute | solution.py:24
  321.3 35.8 %copy-start.6 = (f32[64]{0:T(128)S(1)}, f32[64]{0:T(128)}, u32[]{:S(2)}) copy-start(f32[64]{0:T(128)} %param.23) | copy-start | bytes 772
  336.1 11.0 %collective-permute-start = (bf16[1,64,128]{2,1,0:T(8,128)(2,1)S(1)}, bf16[1,64,128]{2,1,0:T(8,128)(2,1)S(1)}, u32[]{:S(2)}, u32[]{:S(2)}) collective-permute-start(bf16[1,64,128]{2,1,0:T(8,128)(2,1)S(1)} %copy.32), channel_id=1, source_target_pairs={{0,8},{8,16},{16,24},{24,32},{32,40},{40,48},{48,56},{56,64},{64,7... | collective-permute-start | bytes 49160 | tf_op jit(solution)/shard_map/ppermute | solution.py:22
  344.4 5.1 collective-permute-start.1
  349.6 3.6 collective-permute-start.2
  351.2 5.4 collective-permute-start.3
  360.2 96.1 %collective-permute-start.4 = (bf16[1,64,128]{2,1,0:T(8,128)(2,1)S(1)}, bf16[1,64,128]{2,1,0:T(8,128)(2,1)S(1)}, u32[]{:S(2)}, u32[]{:S(2)}) collective-permute-start(bf16[1,64,128]{2,1,0:T(8,128)(2,1)S(1)} %get-tuple-element.29), channel_id=1, source_target_pairs={{0,8},{8,16},{16,24},{24,32},{32,40},{40,48},{48,56},{56,64},{64,7... | collective-permute-start | bytes 49160 | tf_op jit(solution)/shard_map/ppermute | solution.py:22
  363.8 92.4 %collective-permute-start.5 = (bf16[1,64,128]{2,1,0:T(8,128)(2,1)S(1)}, bf16[1,64,128]{2,1,0:T(8,128)(2,1)S(1)}, u32[]{:S(2)}, u32[]{:S(2)}) collective-permute-start(bf16[1,64,128]{2,1,0:T(8,128)(2,1)S(1)} %get-tuple-element.30), channel_id=1, source_target_pairs={{8,0},{16,8},{24,16},{32,24},{40,32},{48,40},{56,48},{64,56},{72,6... | collective-permute-start | bytes 49160 | tf_op jit(solution)/shard_map/ppermute | solution.py:24
  365.8 93.2 %collective-permute-start.12 = (bf16[1,64,128]{2,1,0:T(8,128)(2,1)S(1)}, bf16[1,64,128]{2,1,0:T(8,128)(2,1)S(1)}, u32[]{:S(2)}, u32[]{:S(2)}) collective-permute-start(bf16[1,64,128]{2,1,0:T(8,128)(2,1)S(1)} %get-tuple-element.25), channel_id=1, source_target_pairs={{0,8},{8,16},{16,24},{24,32},{32,40},{40,48},{48,56},{56,64},{64,7... | collective-permute-start | bytes 49160 | tf_op jit(solution)/shard_map/ppermute | solution.py:22
  369.4 89.6 %collective-permute-start.13 = (bf16[1,64,128]{2,1,0:T(8,128)(2,1)S(1)}, bf16[1,64,128]{2,1,0:T(8,128)(2,1)S(1)}, u32[]{:S(2)}, u32[]{:S(2)}) collective-permute-start(bf16[1,64,128]{2,1,0:T(8,128)(2,1)S(1)} %get-tuple-element.26), channel_id=1, source_target_pairs={{8,0},{16,8},{24,16},{32,24},{40,32},{48,40},{56,48},{64,56},{72,6... | collective-permute-start | bytes 49160 | tf_op jit(solution)/shard_map/ppermute | solution.py:24
  456.4 8.1 %collective-permute-start.6 = (bf16[6,64,1]{2,1,0:T(8,128)(2,1)S(1)}, bf16[6,64,1]{2,1,0:T(8,128)(2,1)S(1)}, u32[]{:S(2)}, u32[]{:S(2)}) collective-permute-start(bf16[6,64,1]{2,1,0:T(8,128)(2,1)S(1)} %get-tuple-element.20), channel_id=1, source_target_pairs={{0,1},{1,2},{2,3},{3,4},{4,5},{5,6},{6,7},{8,9},{9,10},{10,11},{11... | collective-permute-start | bytes 2312 | tf_op jit(solution)/shard_map/ppermute | solution.py:22
  457.7 6.8 collective-permute-start.7
  459.1 7.1 collective-permute-start.14
  463.1 7.3 collective-permute-start.15
Sparse Core Ops, SparseCore 0:
  10.8 85.3 all-reduce.3
  100.5 90.7 all-gather.2
  194.7 83.2 all-gather.4
  296.4 36.2 reduce-scatter.1
  472.0 250.9 all-reduce.5
where the time goes:
time: 734 us; the launch traced here: 733 us
  waiting for transfers between devices  523 us (71%)
  blocking collectives  84.9 us (12%)
  starting transfers between devices  40.9 us (6%)
  matrix products  36.1 us (5%)
  other arithmetic  19.6 us (3%)
  local copies, waits for them, and re-layouts  14.5 us (2%)
  between operations  14.4 us (2%)
    psum x1, waiting for transfers between devices, on_device(): lax.psum((first_terms, second_terms, bias_terms), ('band', 'var'))  250 us
    all_gather x1, waiting for transfers between devices, on_device(): lax.all_gather(keys_local, 'band', axis=0, tiled=True)  86.7 us
    psum x1, waiting for transfers between devices, on_device(): lax.psum(partial_mix.astype(jnp.bfloat16), 'var').astype(jnp.float32)  85.5 us
    psum x1, blocking collectives, on_device(): lax.psum((first_terms, second_terms, bias_terms), ('band', 'var'))  84.9 us
    all_gather x1, waiting for transfers between devices, on_device(): lax.all_gather(values_local, 'band', axis=0, tiled=True)  68.6 us
    ppermute x8, starting transfers between devices, with_halo(): lax.ppermute(tail, axis, [(i, (i + 1) % count) for i in range(ends)])  27.6 us
    ppermute x8, waiting for transfers between devices, with_halo(): lax.ppermute(head, axis, [((i + 1) % count, i) for i in range(ends)])  19.7 us
  transfers between devices with their start and end apart: 21, of which 11 were waited for; matrix products, arithmetic and copies ran while one was open for 4% of the time, Pallas kernels for 0%

commit v1 on v0

v1 whole, which is shorter than its diff:
```python
import math

import jax
import jax.numpy as jnp
import numpy as np
from jax import lax
from jax.experimental import pallas as pl
from jax.experimental.pallas import tpu as pltpu
from jax.sharding import Mesh, PartitionSpec as P

D = 2048
HD = 128
C = 64
R = 4
BAND = ("xh", "z", "core")
VAR = ("y", "xl")
PLANE = ("xh", "core", "y", "xl")
BF = jnp.bfloat16
F32 = jnp.float32
VMEM_SPEC = pl.BlockSpec(memory_space=pltpu.VMEM)
SMEM_SPEC = pl.BlockSpec(memory_space=pltpu.SMEM)
SCORE_SCALE = math.log2(math.e) / math.sqrt(HD)


def dot_nn(a, b):
    return lax.dot_general(a, b, (((1,), (0,)), ((), ())), preferred_element_type=F32)


def dot_nt(a, b):
    return lax.dot_general(a, b, (((1,), (1,)), ((), ())), preferred_element_type=F32)


def dot_tn(a, b):
    return lax.dot_general(a, b, (((0,), (0,)), ((), ())), preferred_element_type=F32)


def flash_kernel(blocks, chunks, first, last):
    def body(*refs):
        q_refs = refs[:blocks]
        kv_refs = refs[blocks : blocks + chunks]
        rest = refs[blocks + chunks :]
        if not first:
            stat_in, acc_in = rest[0], rest[1]
            rest = rest[2:]
        for block in range(blocks):
            cols = slice(block * 256, (block + 1) * 256)
            stat_rows = []
            lse_rows = []
            for h in range(2):
                head = slice(h * HD, (h + 1) * HD)
                vals = slice(256 + h * HD, 256 + (h + 1) * HD)
                q = q_refs[block][:, head]
                scores = [dot_nt(kv[:, head], q) * SCORE_SCALE for kv in kv_refs]
                top = jnp.max(scores[0], axis=0, keepdims=True)
                for s in scores[1:]:
                    top = jnp.maximum(top, jnp.max(s, axis=0, keepdims=True))
                if not first:
                    old_top = stat_in[h : h + 1, cols]
                    top = jnp.maximum(top, old_top)
                    shrink = jnp.exp2(old_top - top)
                total = None
                update = None
                for s, kv in zip(scores, kv_refs):
                    w = jnp.exp2(s - top)
                    part = jnp.sum(w, axis=0, keepdims=True)
                    prod = dot_tn(kv[:, vals], w.astype(BF))
                    total = part if total is None else total + part
                    update = prod if update is None else update + prod
                if not first:
                    total = total + stat_in[2 + h : 3 + h, cols] * shrink
                    update = update + acc_in[head, cols] * shrink
                if last:
                    rest[block][head, :] = (update / total).astype(BF)
                    lse = top + jnp.log2(total)
                    high = lse.astype(BF)
                    left = lse - high.astype(F32)
                    mid = left.astype(BF)
                    low = (left - mid.astype(F32)).astype(BF)
                    lse_rows += [high.astype(F32), mid.astype(F32), low.astype(F32)]
                else:
                    rest[1][head, cols] = update
                    stat_rows.append((top, total))
            if last:
                lse_rows.append(jnp.zeros((10, 256), F32))
                rest[block][256:272, :] = jnp.concatenate(lse_rows, axis=0).astype(BF)
            else:
                for h in range(2):
                    rest[0][h : h + 1, cols] = stat_rows[h][0]
                    rest[0][2 + h : 3 + h, cols] = stat_rows[h][1]

    return body


def flash_step(queries, chunks, carry, last):
    blocks = len(queries)
    first = carry is None
    ins = list(queries) + list(chunks) + ([] if first else list(carry))
    if last:
        outs = [jax.ShapeDtypeStruct((272, 256), BF)] * blocks
    else:
        outs = [
            jax.ShapeDtypeStruct((8, 256 * blocks), F32),
            jax.ShapeDtypeStruct((256, 256 * blocks), F32),
        ]
    return pl.pallas_call(
        flash_kernel(blocks, len(chunks), first, last),
        out_shape=outs,
        in_specs=[VMEM_SPEC] * len(ins),
        out_specs=[VMEM_SPEC] * len(outs),
        name="flash_last" if last else "flash_step",
    )(*ins)


def merge_body(b0, b1, b2, b3, mat, out):
    parts = (b0, b1, b2, b3)
    context = []
    for h in range(2):
        head = slice(h * HD, (h + 1) * HD)
        lses = []
        for b in parts:
            tail = b[256:272, :].astype(F32)
            lses.append(tail[3 * h : 3 * h + 1] + tail[3 * h + 1 : 3 * h + 2] + tail[3 * h + 2 : 3 * h + 3])
        top = jnp.maximum(jnp.maximum(lses[0], lses[1]), jnp.maximum(lses[2], lses[3]))
        ws = [jnp.exp2(v - top) for v in lses]
        total = ws[0] + ws[1] + ws[2] + ws[3]
        mixed = sum(b[head, :].astype(F32) * (w / total) for b, w in zip(parts, ws))
        context.append(mixed.astype(BF))
    up = dot_tn(jnp.concatenate(context, axis=0), mat[...])
    for j in range(8):
        for half in range(2):
            rows = []
            for k in range(4):
                lanes = slice((half * 4 + k) * 128, (half * 4 + k + 1) * 128)
                out[j, half, k * 32 : (k + 1) * 32, :] = up[32 * j : 32 * j + 32, lanes].astype(BF)
                token = 32 * j + 32 if k % 2 == 0 else 32 * j - 1
                inside = 0 <= token < 256
                rows.append(up[token : token + 1, lanes] if inside else jnp.zeros((1, 128), F32))
            rows.append(jnp.zeros((12, 128), F32))
            out[j, half, 128:144, :] = jnp.concatenate(rows, axis=0).astype(BF)


def merge(parts, mat):
    return pl.pallas_call(
        merge_body,
        out_shape=jax.ShapeDtypeStruct((8, 2, 144, 128), BF),
        in_specs=[VMEM_SPEC] * 5,
        out_specs=VMEM_SPEC,
        name="merge_heads",
    )(*parts, mat)


def spread_matrix():
    spread = np.zeros((144, 2, 2, 256), np.float32)
    for a in range(2):
        for bh in range(2):
            k = 2 * a + bh
            for bl in range(2):
                for token in range(32):
                    spread[k * 32 + token, a, bl, 4 * token + 2 * bh + bl] = 1
                spread[128 + k, a, bl, (128 + bl) if bh == 0 else (254 + bl)] = 1
    return spread.reshape(144, 1024)


def gelu_pair(x):
    root = math.sqrt(2.0 / math.pi)
    t = jnp.tanh(root * (x + 0.044715 * (x * x * x)))
    half = 0.5 * (1.0 + t)
    slope = half + 0.5 * x * (1.0 - t * t) * (root * (1.0 + 3 * 0.044715 * (x * x)))
    return x * half, slope


def shifted(row):
    return jnp.concatenate(
        [pltpu.roll(row, 1, 1), row, pltpu.roll(row, row.shape[1] - 1, 1)], axis=0
    )


def fine_body(factor):
    def body(flags, own, prev, nxt, spread, grad, rim, mats, bias, field, grad_fine, terms):
        spread_all = spread[...]
        ups = []
        for block in (prev[...], own[0], own[1], nxt[...]):
            wide = dot_tn(block, spread_all)
            for a in range(2):
                ups.append(
                    wide[0:64, 512 * a : 512 * a + 256] + wide[64:128, 512 * a + 256 : 512 * a + 512]
                )
        grads = [
            jnp.concatenate([grad[r].astype(F32), rim[r].astype(F32)], axis=1) for r in range(8)
        ]
        up_taps = [shifted(u).astype(BF) for u in ups]
        grad_taps = [shifted(g).astype(BF) for g in grads]
        pre_all = dot_nn(mats[0], jnp.concatenate(up_taps, axis=1))
        act_all = dot_nn(mats[1], jnp.concatenate(grad_taps, axis=1))

        def gather(products, i, width):
            return (
                products[0:64, i * width : (i + 1) * width]
                + products[64:128, (i + 1) * width : (i + 2) * width]
                + products[128:192, (i + 2) * width : (i + 3) * width]
            )

        lane = lax.broadcasted_iota(jnp.int32, (64, 256), 1)
        cols_ok = (lane < 128) | ((lane == 128) & (flags[3] > 0)) | ((lane == 255) & (flags[2] > 0))
        offset = bias[...]
        act_taps = []
        pre_taps = []
        d_rows = []
        for i in range(6):
            pre = gather(pre_all, i, 256) + offset
            value, slope = gelu_pair(pre)
            ok = cols_ok
            if i == 0:
                ok = ok & (flags[0] > 0)
            if i == 5:
                ok = ok & (flags[1] > 0)
            value = jnp.where(ok, value, 0.0)
            d_pre = jnp.where(ok, gather(act_all, i, 256) * slope, 0.0)
            act_taps.append(shifted(value)[:, 0:128].astype(BF))
            pre_taps.append(shifted(d_pre)[:, 0:128].astype(BF))
            if 1 <= i <= 4:
                d_rows.append(d_pre[:, 0:128].astype(BF))
        act_wide = jnp.concatenate(act_taps, axis=1)
        out_all = dot_nn(mats[2], act_wide)
        fine_all = dot_nn(mats[3], jnp.concatenate(pre_taps, axis=1))
        for j in range(4):
            field[j] = (
                gather(out_all, j, 128) + ups[j + 2][:, 0:128]
            ).astype(BF)
            grad_fine[j] = (gather(fine_all, j, 128) + grads[j + 2][:, 0:128]).astype(BF)
        d_own = jnp.concatenate(d_rows, axis=1)
        g_own = jnp.concatenate([grad[r] for r in range(2, 6)], axis=1)
        for p in range(3):
            up_cut = jnp.concatenate([up_taps[r][:, 0:128] for r in range(p + 1, p + 5)], axis=1)
            first = dot_nt(up_cut, d_own)
            second = dot_nt(act_wide[:, p * 128 : p * 128 + 512], g_own)
            terms[p * 192 : (p + 1) * 192, :] = (
                jnp.concatenate([first, second], axis=1) * factor
            ).astype(BF)
        ones = jnp.ones((16, 512), BF)
        third = dot_nt(ones, d_own) * factor
        terms[576:592, :] = jnp.concatenate([third, jnp.zeros((16, 64), F32)], axis=1).astype(BF)
        terms[592:768, :] = jnp.zeros((176, 128), BF)

    return body


def fine_stage(flags, own, prev, nxt, spread, grad, rim, mats, bias, factor):
    return pl.pallas_call(
        fine_body(factor),
        out_shape=[
            jax.ShapeDtypeStruct((4, 64, 128), BF),
            jax.ShapeDtypeStruct((4, 64, 128), BF),
            jax.ShapeDtypeStruct((768, 128), BF),
        ],
        in_specs=[SMEM_SPEC] + [VMEM_SPEC] * 8,
        out_specs=[VMEM_SPEC] * 3,
        name="fine_stage",
    )(flags, own, prev, nxt, spread, grad, rim, mats, bias)


def copies(piece, axis, count):
    return lax.all_to_all(jnp.broadcast_to(piece[None], (count,) + piece.shape), axis, 0, 0)


def flip(count, bit):
    return [(i, i ^ bit) for i in range(count)]


def turn(count, step):
    return [(i, (i + step) % count) for i in range(count)]


def tap_matrix(weight):
    return jnp.transpose(weight.reshape(3, 3, C, C), (0, 3, 1, 2)).reshape(3 * C, 3 * C)


def flipped(weight):
    return jnp.transpose(weight[::-1], (0, 2, 1))


def on_device(
    patches, w_embed, var_bias, agg_gain, wq, wk, wv, wo, w_up, conv1, bias1, conv2, cotangent
):
    flattened = jnp.transpose(patches, (1, 2, 0, 3)).reshape(256, 128)
    partial_mix = jnp.dot(flattened, w_embed.reshape(128, D), preferred_element_type=F32)
    partial_mix = (partial_mix + jnp.sum(var_bias, axis=0)).astype(BF).reshape(8, 32, D)
    mixed = jnp.sum(lax.all_to_all(partial_mix, VAR, 0, 0).astype(F32), axis=0)
    normed_slab = (
        mixed * lax.rsqrt(jnp.mean(mixed * mixed, axis=-1, keepdims=True) + 1e-05) * agg_gain
    ).astype(BF)
    normed = copies(normed_slab, VAR, 8).reshape(256, D)

    keys = jnp.dot(normed, wk, preferred_element_type=F32).astype(BF)
    values = jnp.dot(normed, wv, preferred_element_type=F32).astype(BF)
    queries = jnp.dot(normed, wq, preferred_element_type=F32).astype(BF)
    keyvals = jnp.concatenate([keys, values], axis=1)

    group = ("xh", "core")
    all_queries = [queries] + [lax.ppermute(queries, group, flip(4, k)) for k in (1, 2, 3)]
    ahead = [keyvals]
    behind = [keyvals]
    for _ in range(3):
        ahead.append(lax.ppermute(ahead[-1], "z", turn(8, 1)))
        behind.append(lax.ppermute(behind[-1], "z", turn(8, -1)))
    ahead.append(lax.ppermute(ahead[-1][:128], "z", turn(8, 1)))
    behind.append(lax.ppermute(behind[-1][128:], "z", turn(8, -1)))
    carry = flash_step(all_queries, [keyvals, ahead[1], behind[1]], None, False)
    carry = flash_step(all_queries, [ahead[2], behind[2]], carry, False)
    carry = flash_step(all_queries, [ahead[3], behind[3]], carry, False)

    var_at = lax.axis_index(VAR)
    band_at = lax.axis_index(BAND)
    up_mat = jnp.dot(wo, w_up, preferred_element_type=F32).astype(BF)
    padded = jnp.pad(normed, ((1, 1), (0, 0)))
    around = lax.dynamic_slice_in_dim(padded, var_at * 32, 34, 0)
    base = jnp.dot(around, w_up, preferred_element_type=F32)
    base_main = jnp.transpose(base[1:33].reshape(32, 2, 4, 128), (1, 2, 0, 3)).reshape(2, 128, 128)
    left = base[0].reshape(2, 4, 128)
    right = base[33].reshape(2, 4, 128)
    base_rim = jnp.where(jnp.arange(4)[None, :, None] % 2 == 0, right, left)
    base_all = jnp.concatenate([base_main, base_rim, jnp.zeros((2, 12, 128), F32)], axis=1)

    shift_down = [(i, i + 1) for i in range(31)]
    shift_up = [(i + 1, i) for i in range(31)]
    cells, up_mat = lax.optimization_barrier((cotangent, up_mat))
    grad_rows = jnp.concatenate(
        [
            lax.ppermute(cells[2:4], BAND, shift_down),
            cells,
            lax.ppermute(cells[0:2], BAND, shift_up),
        ],
        axis=0,
    )
    from_right = lax.ppermute(grad_rows[:, :, 0:2], VAR, [(i + 1, i) for i in range(7)])
    from_left = lax.ppermute(grad_rows[:, :, 126:128], VAR, [(i, i + 1) for i in range(7)])
    rim = jnp.concatenate([from_right, jnp.zeros((8, C, 124), BF), from_left], axis=2)
    mats = jnp.stack(
        [tap_matrix(conv1), tap_matrix(flipped(conv2)), tap_matrix(conv2), tap_matrix(flipped(conv1))]
    )

    blocks = flash_step(all_queries, [ahead[4], behind[4]], carry, True)
    parts = [blocks[0]] + [lax.ppermute(blocks[k], group, flip(4, k)) for k in (1, 2, 3)]
    pieces = lax.all_to_all(merge(parts, up_mat), VAR, 0, 0)
    up = (jnp.sum(pieces.astype(F32), axis=0) + base_all).astype(BF)
    prev = lax.ppermute(up[1], BAND, shift_down)
    nxt = lax.ppermute(up[0], BAND, shift_up)
    flags = jnp.stack([band_at > 0, band_at < 31, var_at > 0, var_at < 7]).astype(jnp.int32)
    factor = 1.0 / math.sqrt(128 * 1024)
    spread = jnp.asarray(spread_matrix(), BF)
    field_out, grad_fine, terms = fine_stage(
        flags, up, prev, nxt, spread, grad_rows, rim, mats, bias1.reshape(C, 1), factor
    )
    shares = lax.all_to_all(terms.reshape(32, 24, 128), PLANE, 0, 0)
    share = jnp.sum(shares.astype(F32), axis=0).astype(BF)
    share = jnp.sum(copies(share, "z", 8).astype(F32), axis=0).astype(BF)
    totals = copies(share, PLANE, 32).reshape(768, 128).astype(F32)
    grad_conv1 = totals[:576, :C].reshape(9, C, C)
    grad_conv2 = totals[:576, C:].reshape(9, C, C)
    return (field_out, grad_fine, grad_conv1, grad_conv2, totals[576, :C])


def solution(mesh):
    fine_mesh = Mesh(mesh.devices.reshape(2, 8, 2, 4, 2), BAND + VAR)
    in_specs = (
        P(VAR, BAND, None, None),
        P(VAR, None, None),
        P(VAR, None),
        P(),
        P(None, VAR),
        P(None, VAR),
        P(None, VAR),
        P(VAR, None),
        P(),
        P(),
        P(),
        P(),
        P(BAND, None, VAR),
    )
    out_specs = (P(BAND, None, VAR), P(BAND, None, VAR), P(), P(), P())
    return jax.shard_map(
        on_device, mesh=fine_mesh, in_specs=in_specs, out_specs=out_specs, check_vma=False
    )
```

time: 734 us -> 195 us (0.27)
  waiting for transfers between devices: 523 us -> 23.8 us
  Pallas kernels: 0 us -> 26.8 us
  blocking collectives: 84.9 us -> 60.4 us
  matrix products: 36.1 us -> 12.6 us
  other arithmetic: 19.6 us -> 3.76 us
  between operations: 14.4 us -> 1.09 us
  starting transfers between devices: 40.9 us -> 53.9 us
    psum x2 -> x0, waiting for transfers between devices: 336 us -> none  [the longest x1 250 us: on_device(): lax.psum((first_terms, second_terms, bias_terms), ('band', 'var'))]
    all_gather x2 -> x0, waiting for transfers between devices: 155 us -> none  [the longest x1 86.7 us: on_device(): lax.all_gather(keys_local, 'band', axis=0, tiled=True)]
    psum x1 -> x0, blocking collectives: 84.9 us -> none  [on_device(): lax.psum((first_terms, second_terms, bias_terms), ('band', 'var'))]
    all_to_all x0 -> x4, blocking collectives: none -> 60.4 us  [the longest x2 24.3 us: copies(): lax.all_to_all(jnp.broadcast_to(piece[None], (count,) + piece.shape), axi...]
    pallas_call x0 -> x6, Pallas kernels: none -> 26.8 us  [the longest x4 20.6 us: flash_step(): pl.pallas_call(flash_kernel(blocks, len(chunks), first, last), out_shape=...]
    dot_general x14 -> x6, matrix products: 36.1 us -> 12.6 us  [the longest x1 4.33 us: on_device(): up_mat = jnp.dot(wo, w_up, preferred_element_type=F32).astype(BF)]
    all_to_all x0 -> x2, waiting for transfers between devices: none -> 17.1 us  [the longest x1 9.57 us: copies(): lax.all_to_all(jnp.broadcast_to(piece[None], (count,) + piece.shape), axi...]
    ppermute x16 -> x20, waiting for transfers between devices: 20 us -> 6.77 us  [the longest x3 4.17 us: on_device(): ahead.append(lax.ppermute(ahead[-1], 'z', turn(8, 1)))]
  transfers between devices with their start and end apart: 21 -> 22, of which waited for: 11 -> 5; matrix products, arithmetic and copies ran while one was open for 4% -> 9% of each run, Pallas kernels for 0% -> 10%
where the time goes in v1:
time: 195 us; the launch traced here: 194 us
  blocking collectives  60.4 us (31%)
  starting transfers between devices  53.9 us (28%)
  Pallas kernels  26.8 us (14%)
  waiting for transfers between devices  23.8 us (12%)
  matrix products  12.6 us (6%)
  local copies, waits for them, and re-layouts  11.7 us (6%)
  other arithmetic  3.76 us (2%)
    all_to_all x2, blocking collectives, copies(): lax.all_to_all(jnp.broadcast_to(piece[None], (count,) + piece.shape), axi...  24.3 us
    all_to_all x1, blocking collectives, on_device(): mixed = jnp.sum(lax.all_to_all(partial_mix, VAR, 0, 0).astype(F32), axis=0)  20.7 us
    pallas_call x4, Pallas kernels, flash_step(): pl.pallas_call(flash_kernel(blocks, len(chunks), first, last), out_shape=...  20.6 us
    all_to_all x1, blocking collectives, on_device(): shares = lax.all_to_all(terms.reshape(32, 24, 128), PLANE, 0, 0)  15.4 us
    ppermute x3, starting transfers between devices, on_device(): behind.append(lax.ppermute(behind[-1], 'z', turn(8, -1)))  12.5 us
    ppermute x3, starting transfers between devices, on_device(): lax.ppermute(queries, group, flip(4, k))  9.72 us
    all_to_all x1, waiting for transfers between devices, copies(): lax.all_to_all(jnp.broadcast_to(piece[None], (count,) + piece.shape), axi...  9.57 us
    all_to_all x1, waiting for transfers between devices, on_device(): pieces = lax.all_to_all(merge(parts, up_mat), VAR, 0, 0)  7.49 us
  transfers between devices with their start and end apart: 22, of which 5 were waited for; matrix products, arithmetic and copies ran while one was open for 9% of the time, Pallas kernels for 10%

profile of v1, /device:TPU:1, one launch (start us, length us, event | category | flops | bytes accessed | tf_op | source)
XLA Modules:
  0.0 194.2 jit_solution(4083513859823837419)
XLA Ops:
  3.0 20.7 %all_to_all.30 = bf16[8,32,2048]{2,1,0:T(8,128)(2,1)S(1)} all-to-all(bf16[8,32,2048]{2,1,0:T(8,128)(2,1)S(1)} %bitcast.59), channel_id=1, replica_groups=mesh['xh'=2,'z'=8,'core'=2,'y'=4,'xl'=2] {'y','xl'}, dimensions={0} | all-to-all | bytes 2097152 | tf_op jit(solution)/shard_map/all_to_all | solution.py:288
  25.2 3.6 %all-to-all-start.1 = ((bf16[8,32,2048]{2,1,0:T(8,128)(2,1)}), bf16[8,32,2048]{2,1,0:T(8,128)(2,1)S(1)}, u32[]{:S(2)}, u32[]{:S(2)}) async-start(bf16[8,32,2048]{2,1,0:T(8,128)(2,1)} %broadcast_in_dim.18), calls=%async_computation.1 | async-start | bytes 2097152 | tf_op jit(solution)/shard_map/all_to_all | solution.py:263
  28.8 4.3 %convolution_convert_fusion.mat = bf16[256,1024]{1,0:T(8,128)(2,1)} fusion(bf16[256,2048]{1,0:T(8,128)(2,1)S(1)} %copy-done, bf16[2048,1024]{1,0:T(8,128)(2,1)} %param.22), kind=kOutput, calls=%fused_computation.3 | convolution fusion | flops 1074003968 | bytes 5767168 | tf_op jit(solution)/shard_map/dot_general | solution.py:314
  33.1 9.6 %all-to-all-done.1 = bf16[8,32,2048]{2,1,0:T(8,128)(2,1)S(1)} async-done(((bf16[8,32,2048]{2,1,0:T(8,128)(2,1)}), bf16[8,32,2048]{2,1,0:T(8,128)(2,1)S(1)}, u32[]{:S(2)}, u32[]{:S(2)}) %all-to-all-start.1) | async-done | bytes 1048608 | tf_op jit(solution)/shard_map/all_to_all | solution.py:263
  43.2 1.7 convolution_convert_fusion.2
  44.9 1.7 collective-permute-start.3
  46.6 4.0 %collective-permute-start.7 = (bf16[256,512]{1,0:T(8,128)(2,1)S(1)}, bf16[256,512]{1,0:T(8,128)(2,1)}, u32[]{:S(2)}, u32[]{:S(2)}) collective-permute-start(bf16[256,512]{1,0:T(8,128)(2,1)S(1)} %pad_maximum_fusion.1.refs_4_), channel_id=1, source_target_pairs={{0,112},{16,0},{32,16},{48,32},{64,48},{80,64},{96,80},{112,96},{1... | collective-permute-start | bytes 786440 | tf_op jit(solution)/shard_map/ppermute | solution.py:305
  51.2 2.4 %collective-permute-start.16 = (bf16[2,64,128]{2,1,0:T(8,128)(2,1)S(1)}, bf16[2,64,128]{2,1,0:T(8,128)(2,1)S(1)}, u32[]{:S(2)}, u32[]{:S(2)}) collective-permute-start(bf16[2,64,128]{2,1,0:T(8,128)(2,1)S(1)} %get-tuple-element.44), channel_id=1, source_target_pairs={{0,8},{8,16},{16,24},{24,32},{32,40},{40,48},{48,56},{56,64},{64,7... | collective-permute-start | bytes 98312 | tf_op jit(solution)/shard_map/ppermute | solution.py:329
  53.7 3.7 %collective-permute-start.17 = (bf16[2,64,128]{2,1,0:T(8,128)(2,1)}, bf16[2,64,128]{2,1,0:T(8,128)(2,1)}, u32[]{:S(2)}, u32[]{:S(2)}) collective-permute-start(bf16[2,64,128]{2,1,0:T(8,128)(2,1)} %get-tuple-element.43), channel_id=1, source_target_pairs={{8,0},{16,8},{24,16},{32,24},{40,32},{48,40},{56,48},{64,56},{72,6... | collective-permute-start | bytes 98312 | tf_op jit(solution)/shard_map/ppermute | solution.py:331
  59.6 5.4 %collective-permute-start.8 = (bf16[256,512]{1,0:T(8,128)(2,1)}, bf16[256,512]{1,0:T(8,128)(2,1)}, u32[]{:S(2)}, u32[]{:S(2)}) collective-permute-start(bf16[256,512]{1,0:T(8,128)(2,1)} %collective-permute-done.7.refs_6_), channel_id=1, source_target_pairs={{0,112},{16,0},{32,16},{48,32},{64,48},{80,64},{96,80},{112,96},{1... | collective-permute-start | bytes 786440 | tf_op jit(solution)/shard_map/ppermute | solution.py:305
  66.5 4.2 %collective-permute-done.4.refs_4_ = bf16[256,512]{1,0:T(8,128)(2,1)} collective-permute-done((bf16[256,512]{1,0:T(8,128)(2,1)}, bf16[256,512]{1,0:T(8,128)(2,1)}, u32[]{:S(2)}, u32[]{:S(2)}) %collective-permute-start.4) | collective-permute-done | bytes 262176 | tf_op jit(solution)/shard_map/ppermute | solution.py:304
  70.6 3.0 %collective-permute-start.9 = (bf16[256,512]{1,0:T(8,128)(2,1)}, bf16[256,512]{1,0:T(8,128)(2,1)S(1)}, u32[]{:S(2)}, u32[]{:S(2)}) collective-permute-start(bf16[256,512]{1,0:T(8,128)(2,1)} %collective-permute-done.8.refs_5_), channel_id=1, source_target_pairs={{0,112},{16,0},{32,16},{48,32},{64,48},{80,64},{96,80},{112,96},{1... | collective-permute-start | bytes 786440 | tf_op jit(solution)/shard_map/ppermute | solution.py:305
  75.5 7.2 %collective-permute-start.1 = (bf16[256,256]{1,0:T(8,128)(2,1)S(1)}, bf16[256,256]{1,0:T(8,128)(2,1)S(1)}, u32[]{:S(2)}, u32[]{:S(2)}) collective-permute-start(bf16[256,256]{1,0:T(8,128)(2,1)S(1)} %convolution_convert_fusion.3.refs_0_), channel_id=1, source_target_pairs={{0,128},{8,136},{128,0},{136,8},{1,129},{9,137},{129,1},{137,9},{2... | collective-permute-start | bytes 393224 | tf_op jit(solution)/shard_map/ppermute | solution.py:300
  82.8 2.3 %collective-permute-start.2 = (bf16[256,256]{1,0:T(8,128)(2,1)S(1)}, bf16[256,256]{1,0:T(8,128)(2,1)S(1)}, u32[]{:S(2)}, u32[]{:S(2)}) collective-permute-start(bf16[256,256]{1,0:T(8,128)(2,1)S(1)} %convolution_convert_fusion.3.refs_0_), channel_id=1, source_target_pairs={{0,136},{8,128},{128,8},{136,0},{1,137},{9,129},{129,9},{137,1},{2... | collective-permute-start | bytes 393224 | tf_op jit(solution)/shard_map/ppermute | solution.py:300
  85.7 3.3 %collective-permute-start.10 = (bf16[128,512]{1,0:T(8,128)(2,1)}, bf16[128,512]{1,0:T(8,128)(2,1)}, u32[]{:S(2)}, u32[]{:S(2)}) collective-permute-start(bf16[128,512]{1,0:T(8,128)(2,1)} %slice.57), channel_id=1, source_target_pairs={{0,112},{16,0},{32,16},{48,32},{64,48},{80,64},{96,80},{112,96},{1... | collective-permute-start | bytes 393224 | tf_op jit(solution)/shard_map/ppermute | solution.py:307
  92.7 5.9 %flash_step.3 = (f32[8,1024]{1,0:T(8,128)}, f32[256,1024]{1,0:T(8,128)}) custom-call(bf16[256,256]{1,0:T(8,128)(2,1)} %copy-done.1, bf16[256,256]{1,0:T(8,128)(2,1)} %copy-done.2, bf16[256,256]{1,0:T(8,128)(2,1)} %copy-done.3, bf16[256,256]{1,0:T(8,128)(2,1)} %copy-done.4, bf16[256,512]{1,0:T(8,128)(2,1)} %copy-done.6, ...), custom_call_target="tpu_custom_call" | custom-call | tf_op jit(solution)/shard_map/flash_step/pallas_call | solution.py:105
  98.6 5.7 %flash_step.4 = (f32[8,1024]{1,0:T(8,128)}, f32[256,1024]{1,0:T(8,128)}) custom-call(bf16[256,256]{1,0:T(8,128)(2,1)} %copy-done.1, bf16[256,256]{1,0:T(8,128)(2,1)} %copy-done.2, bf16[256,256]{1,0:T(8,128)(2,1)} %copy-done.3, bf16[256,256]{1,0:T(8,128)(2,1)} %copy-done.4, bf16[256,512]{1,0:T(8,128)(2,1)} %collective-permute-done.4.refs_4_, ...), custom_call_target="tpu_custom_call" | custom-call | tf_op jit(solution)/shard_map/flash_step/pallas_call | solution.py:105
  104.3 5.7 %flash_step.5 = (f32[8,1024]{1,0:T(8,128)}, f32[256,1024]{1,0:T(8,128)}) custom-call(bf16[256,256]{1,0:T(8,128)(2,1)} %copy-done.1, bf16[256,256]{1,0:T(8,128)(2,1)} %copy-done.2, bf16[256,256]{1,0:T(8,128)(2,1)} %copy-done.3, bf16[256,256]{1,0:T(8,128)(2,1)} %copy-done.4, bf16[256,512]{1,0:T(8,128)(2,1)} %copy-done.11, bf16[256,512]{1,0:T(8,128)(2,1)} %copy-done.12, ...), custom_call_target="tpu_custom_call" | custom-call | tf_op jit(solution)/shard_map/flash_step/pallas_call | solution.py:105
  110.0 3.4 %flash_last.1 = (bf16[272,256]{1,0:T(8,128)(2,1)}, bf16[272,256]{1,0:T(8,128)(2,1)}, bf16[272,256]{1,0:T(8,128)(2,1)}, bf16[272,256]{1,0:T(8,128)(2,1)}) custom-call(bf16[256,256]{1,0:T(8,128)(2,1)} %copy-done.1, bf16[256,256]{1,0:T(8,128)(2,1)} %copy-done.2, bf16[256,256]{1,0:T(8,128)(2,1)} %copy-done.3, bf16[256,256]{1,0:T(8,128)(2,1)} %copy-done.4, ...), custom_call_target="tpu_custom_call" | custom-call | tf_op jit(solution)/shard_map/flash_last/pallas_call | solution.py:105
  113.9 3.2 %collective-permute-start.13 = (bf16[272,256]{1,0:T(8,128)(2,1)}, bf16[272,256]{1,0:T(8,128)(2,1)S(1)}, u32[]{:S(2)}, u32[]{:S(2)}) collective-permute-start(bf16[272,256]{1,0:T(8,128)(2,1)} %get-tuple-element.29), channel_id=1, source_target_pairs={{0,136},{8,128},{128,8},{136,0},{1,137},{9,129},{129,9},{137,1},{2... | collective-permute-start | bytes 417800 | tf_op jit(solution)/shard_map/ppermute | solution.py:343
  119.0 4.0 %collective-permute-start.19 = (bf16[8,64,2]{2,1,0:T(8,128)(2,1)S(1)}, bf16[8,64,2]{2,1,0:T(8,128)(2,1)S(1)}, u32[]{:S(2)}, u32[]{:S(2)}) collective-permute-start(bf16[8,64,2]{2,1,0:T(8,128)(2,1)S(1)} %get-tuple-element.40), channel_id=1, source_target_pairs={{0,1},{1,2},{2,3},{3,4},{4,5},{5,6},{6,7},{8,9},{9,10},{10,11},{11... | collective-permute-start | bytes 6152 | tf_op jit(solution)/shard_map/ppermute | solution.py:336
  124.2 2.6 %merge_heads.1 = bf16[8,2,144,128]{3,2,1,0:T(8,128)(2,1)} custom-call(bf16[272,256]{1,0:T(8,128)(2,1)} %get-tuple-element.26.b0, bf16[272,256]{1,0:T(8,128)(2,1)} %copy-done.14, bf16[272,256]{1,0:T(8,128)(2,1)} %copy-done.15, bf16[272,256]{1,0:T(8,128)(2,1)} %copy-done.16, bf16[256,1024]{1,0:T(8,128)(2,1)} %convolution_convert_fusion.mat), custom_call_target="tpu_custom_call" | custom-call | tf_op jit(solution)/shard_map/merge_heads/pallas_call | solution.py:143
  126.8 3.8 %all-to-all-start.2 = ((bf16[8,2,144,128]{3,2,1,0:T(8,128)(2,1)}), bf16[8,2,144,128]{3,2,1,0:T(8,128)(2,1)S(1)}, u32[]{:S(2)}, u32[]{:S(2)}) async-start(bf16[8,2,144,128]{3,2,1,0:T(8,128)(2,1)} %merge_heads.1), calls=%async_computation.2 | async-start | bytes 1179648 | tf_op jit(solution)/shard_map/all_to_all | solution.py:344
  130.6 3.0 %fusion.1 = f32[34,1024]{1,0:T(8,128)S(1)} fusion(bf16[2048,1024]{1,0:T(8,128)(2,1)} %param.22, s32[]{:T(128)S(6)} %select_n.19, bf16[256,2048]{1,0:T(8,128)(2,1)S(1)} %bitcast.58), kind=kOutput, calls=%fused_computation.16 | convolution fusion | flops 142606336 | bytes 5382148 | tf_op jit(solution)/shard_map/dot_general | solution.py:317
  133.8 7.5 %all-to-all-done.2 = bf16[8,2,144,128]{3,2,1,0:T(8,128)(2,1)S(1)} async-done(((bf16[8,2,144,128]{3,2,1,0:T(8,128)(2,1)}), bf16[8,2,144,128]{3,2,1,0:T(8,128)(2,1)S(1)}, u32[]{:S(2)}, u32[]{:S(2)}) %all-to-all-start.2) | async-done | bytes 589856 | tf_op jit(solution)/shard_map/all_to_all | solution.py:344
  141.5 1.9 collective-permute-start.14
  143.4 2.4 %collective-permute-start.15 = (bf16[144,128]{1,0:T(8,128)(2,1)S(1)}, bf16[144,128]{1,0:T(8,128)(2,1)S(1)}, u32[]{:S(2)}, u32[]{:S(2)}) collective-permute-start(bf16[144,128]{1,0:T(8,128)(2,1)S(1)} %get-tuple-element.41), channel_id=1, source_target_pairs={{8,0},{16,8},{24,16},{32,24},{40,32},{48,40},{56,48},{64,56},{72,6... | collective-permute-start | bytes 110600 | tf_op jit(solution)/shard_map/ppermute | solution.py:347
  146.6 2.1 %collective-permute-done.15.nxt = bf16[144,128]{1,0:T(8,128)(2,1)S(1)} collective-permute-done((bf16[144,128]{1,0:T(8,128)(2,1)S(1)}, bf16[144,128]{1,0:T(8,128)(2,1)S(1)}, u32[]{:S(2)}, u32[]{:S(2)}) %collective-permute-start.15) | collective-permute-done | bytes 36896 | tf_op jit(solution)/shard_map/ppermute | solution.py:347
  149.3 3.6 %fine_stage.1 = (bf16[4,64,128]{2,1,0:T(8,128)(2,1)}, bf16[4,64,128]{2,1,0:T(8,128)(2,1)}, bf16[768,128]{1,0:T(8,128)(2,1)}) custom-call(s32[4]{0:T(128)} %add_convert_fusion.flags, bf16[2,144,128]{2,1,0:T(8,128)(2,1)} %copy-done.8, bf16[144,128]{1,0:T(8,128)(2,1)} %copy-done.17, bf16[144,128]{1,0:T(8,128)(2,1)} %copy-done.18, ...), custom_call_target="tpu_custom_call" | custom-call | tf_op jit(solution)/shard_map/fine_stage/pallas_call | solution.py:249
  152.9 15.4 %all_to_all.31 = bf16[32,24,128]{2,1,0:T(8,128)(2,1)S(1)} all-to-all(bf16[32,24,128]{2,1,0:T(8,128)(2,1)} %bitcast.72), channel_id=1, replica_groups=mesh['xh'=2,'z'=8,'core'=2,'y'=4,'xl'=2] {'xh','core','y','xl'}, dimensions={0} | all-to-all | bytes 393216 | tf_op jit(solution)/shard_map/all_to_all | solution.py:354
  168.3 10.9 %all_to_all.32 = bf16[8,24,128]{2,1,0:T(8,128)(2,1)S(1)} all-to-all(bf16[8,24,128]{2,1,0:T(8,128)(2,1)S(1)} %broadcast_in_dim.22), channel_id=1, replica_groups=mesh['xh'=2,'z'=8,'core'=2,'y'=4,'xl'=2] {'z'}, dimensions={0} | all-to-all | bytes 98304 | tf_op jit(solution)/shard_map/all_to_all | solution.py:263
  179.3 13.5 %all_to_all.33 = bf16[32,24,128]{2,1,0:T(8,128)(2,1)S(1)} all-to-all(bf16[32,24,128]{2,1,0:T(8,128)(2,1)S(1)} %broadcast_in_dim.23), channel_id=1, replica_groups=mesh['xh'=2,'z'=8,'core'=2,'y'=4,'xl'=2] {'xh','core','y','xl'}, dimensions={0} | all-to-all | bytes 393216 | tf_op jit(solution)/shard_map/all_to_all | solution.py:263
  (118 shorter events, 21.5 us)
Async XLA Ops:
  0.6 28.2 %copy-start = (bf16[256,2048]{1,0:T(8,128)(2,1)S(1)}, bf16[256,2048]{1,0:T(8,128)(2,1)}, u32[]{:S(2)}) copy-start(bf16[256,2048]{1,0:T(8,128)(2,1)} %param.21) | copy-start | bytes 3145732
  0.6 23.4 %copy-start.19 = (f32[2048]{0:T(1024)S(1)}, f32[2048]{0:T(1024)}, u32[]{:S(2)}) copy-start(f32[2048]{0:T(1024)} %param.17) | copy-start | bytes 24580
  25.2 17.5 %all-to-all-start.1 = ((bf16[8,32,2048]{2,1,0:T(8,128)(2,1)}), bf16[8,32,2048]{2,1,0:T(8,128)(2,1)S(1)}, u32[]{:S(2)}, u32[]{:S(2)}) async-start(bf16[8,32,2048]{2,1,0:T(8,128)(2,1)} %broadcast_in_dim.18), calls=%async_computation.1 | async-start | bytes 2097152 | tf_op jit(solution)/shard_map/all_to_all | solution.py:263
  33.1 17.5 %copy-start.13 = (bf16[4,64,128]{2,1,0:T(8,128)(2,1)S(1)}, bf16[4,64,128]{2,1,0:T(8,128)(2,1)}, u32[]{:S(2)}) copy-start(bf16[4,64,128]{2,1,0:T(8,128)(2,1)} %param.26) | copy-start | bytes 196612
  33.1 24.2 %copy-start.10 = (bf16[9,64,64]{2,1,0:T(8,128)(2,1)S(1)}, bf16[9,64,64]{2,1,0:T(8,128)(2,1)}, u32[]{:S(2)}) copy-start(bf16[9,64,64]{2,1,0:T(8,128)(2,1)} %param.25) | copy-start | bytes 221188
  33.1 24.6 %copy-start.9 = (bf16[9,64,64]{2,1,0:T(8,128)(2,1)S(1)}, bf16[9,64,64]{2,1,0:T(8,128)(2,1)}, u32[]{:S(2)}) copy-start(bf16[9,64,64]{2,1,0:T(8,128)(2,1)} %param.23) | copy-start | bytes 221188
  42.7 22.9 %copy-start.20 = (f32[64]{0:T(128)S(1)}, f32[64]{0:T(128)}, u32[]{:S(2)}) copy-start(f32[64]{0:T(128)} %param.24) | copy-start | bytes 772
  44.9 46.5 %copy-start.6 = (bf16[256,512]{1,0:T(8,128)(2,1)}, bf16[256,512]{1,0:T(8,128)(2,1)S(1)}, u32[]{:S(2)}) copy-start(bf16[256,512]{1,0:T(8,128)(2,1)S(1)} %pad_maximum_fusion.1.refs_4_) | copy-start | bytes 786436
  44.9 14.7 %collective-permute-start.3 = (bf16[256,512]{1,0:T(8,128)(2,1)S(1)}, bf16[256,512]{1,0:T(8,128)(2,1)}, u32[]{:S(2)}, u32[]{:S(2)}) collective-permute-start(bf16[256,512]{1,0:T(8,128)(2,1)S(1)} %pad_maximum_fusion.1.refs_4_), channel_id=1, source_target_pairs={{0,16},{16,32},{32,48},{48,64},{64,80},{80,96},{96,112},{112,0},{1... | collective-permute-start | bytes 786440 | tf_op jit(solution)/shard_map/ppermute | solution.py:304
  46.6 13.0 %collective-permute-start.7 = (bf16[256,512]{1,0:T(8,128)(2,1)S(1)}, bf16[256,512]{1,0:T(8,128)(2,1)}, u32[]{:S(2)}, u32[]{:S(2)}) collective-permute-start(bf16[256,512]{1,0:T(8,128)(2,1)S(1)} %pad_maximum_fusion.1.refs_4_), channel_id=1, source_target_pairs={{0,112},{16,0},{32,16},{48,32},{64,48},{80,64},{96,80},{112,96},{1... | collective-permute-start | bytes 786440 | tf_op jit(solution)/shard_map/ppermute | solution.py:305
  51.2 15.2 %collective-permute-start.16 = (bf16[2,64,128]{2,1,0:T(8,128)(2,1)S(1)}, bf16[2,64,128]{2,1,0:T(8,128)(2,1)S(1)}, u32[]{:S(2)}, u32[]{:S(2)}) collective-permute-start(bf16[2,64,128]{2,1,0:T(8,128)(2,1)S(1)} %get-tuple-element.44), channel_id=1, source_target_pairs={{0,8},{8,16},{16,24},{24,32},{32,40},{40,48},{48,56},{56,64},{64,7... | collective-permute-start | bytes 98312 | tf_op jit(solution)/shard_map/ppermute | solution.py:329
  53.7 36.1 %collective-permute-start.17 = (bf16[2,64,128]{2,1,0:T(8,128)(2,1)}, bf16[2,64,128]{2,1,0:T(8,128)(2,1)}, u32[]{:S(2)}, u32[]{:S(2)}) collective-permute-start(bf16[2,64,128]{2,1,0:T(8,128)(2,1)} %get-tuple-element.43), channel_id=1, source_target_pairs={{8,0},{16,8},{24,16},{32,24},{40,32},{48,40},{56,48},{64,56},{72,6... | collective-permute-start | bytes 98312 | tf_op jit(solution)/shard_map/ppermute | solution.py:331
  59.6 11.1 %collective-permute-start.4 = (bf16[256,512]{1,0:T(8,128)(2,1)}, bf16[256,512]{1,0:T(8,128)(2,1)}, u32[]{:S(2)}, u32[]{:S(2)}) collective-permute-start(bf16[256,512]{1,0:T(8,128)(2,1)} %collective-permute-done.3.refs_5_), channel_id=1, source_target_pairs={{0,16},{16,32},{32,48},{48,64},{64,80},{80,96},{96,112},{112,0},{1... | collective-permute-start | bytes 786440 | tf_op jit(solution)/shard_map/ppermute | solution.py:304
  59.6 11.1 %collective-permute-start.8 = (bf16[256,512]{1,0:T(8,128)(2,1)}, bf16[256,512]{1,0:T(8,128)(2,1)}, u32[]{:S(2)}, u32[]{:S(2)}) collective-permute-start(bf16[256,512]{1,0:T(8,128)(2,1)} %collective-permute-done.7.refs_6_), channel_id=1, source_target_pairs={{0,112},{16,0},{32,16},{48,32},{64,48},{80,64},{96,80},{112,96},{1... | collective-permute-start | bytes 786440 | tf_op jit(solution)/shard_map/ppermute | solution.py:305
  70.6 15.1 %collective-permute-start.5 = (bf16[256,512]{1,0:T(8,128)(2,1)}, bf16[256,512]{1,0:T(8,128)(2,1)S(1)}, u32[]{:S(2)}, u32[]{:S(2)}) collective-permute-start(bf16[256,512]{1,0:T(8,128)(2,1)} %collective-permute-done.4.refs_4_), channel_id=1, source_target_pairs={{0,16},{16,32},{32,48},{48,64},{64,80},{80,96},{96,112},{112,0},{1... | collective-permute-start | bytes 786440 | tf_op jit(solution)/shard_map/ppermute | solution.py:304
  70.6 12.1 %collective-permute-start.9 = (bf16[256,512]{1,0:T(8,128)(2,1)}, bf16[256,512]{1,0:T(8,128)(2,1)S(1)}, u32[]{:S(2)}, u32[]{:S(2)}) collective-permute-start(bf16[256,512]{1,0:T(8,128)(2,1)} %collective-permute-done.8.refs_5_), channel_id=1, source_target_pairs={{0,112},{16,0},{32,16},{48,32},{64,48},{80,64},{96,80},{112,96},{1... | collective-permute-start | bytes 786440 | tf_op jit(solution)/shard_map/ppermute | solution.py:305
  75.4 16.0 %collective-permute-start = (bf16[256,256]{1,0:T(8,128)(2,1)S(1)}, bf16[256,256]{1,0:T(8,128)(2,1)S(1)}, u32[]{:S(2)}, u32[]{:S(2)}) collective-permute-start(bf16[256,256]{1,0:T(8,128)(2,1)S(1)} %convolution_convert_fusion.3.refs_0_), channel_id=1, source_target_pairs={{0,8},{8,0},{128,136},{136,128},{1,9},{9,1},{129,137},{137,129},{2... | collective-permute-start | bytes 393224 | tf_op jit(solution)/shard_map/ppermute | solution.py:300
  75.5 15.9 %collective-permute-start.1 = (bf16[256,256]{1,0:T(8,128)(2,1)S(1)}, bf16[256,256]{1,0:T(8,128)(2,1)S(1)}, u32[]{:S(2)}, u32[]{:S(2)}) collective-permute-start(bf16[256,256]{1,0:T(8,128)(2,1)S(1)} %convolution_convert_fusion.3.refs_0_), channel_id=1, source_target_pairs={{0,128},{8,136},{128,0},{136,8},{1,129},{9,137},{129,1},{137,9},{2... | collective-permute-start | bytes 393224 | tf_op jit(solution)/shard_map/ppermute | solution.py:300
  82.8 21.6 %copy-start.12 = (bf16[256,512]{1,0:T(8,128)(2,1)}, bf16[256,512]{1,0:T(8,128)(2,1)S(1)}, u32[]{:S(2)}) copy-start(bf16[256,512]{1,0:T(8,128)(2,1)S(1)} %collective-permute-done.9.refs_5_) | copy-start | bytes 786436
  82.8 8.6 %collective-permute-start.2 = (bf16[256,256]{1,0:T(8,128)(2,1)S(1)}, bf16[256,256]{1,0:T(8,128)(2,1)S(1)}, u32[]{:S(2)}, u32[]{:S(2)}) collective-permute-start(bf16[256,256]{1,0:T(8,128)(2,1)S(1)} %convolution_convert_fusion.3.refs_0_), channel_id=1, source_target_pairs={{0,136},{8,128},{128,8},{136,0},{1,137},{9,129},{129,9},{137,1},{2... | collective-permute-start | bytes 393224 | tf_op jit(solution)/shard_map/ppermute | solution.py:300
  85.7 18.6 %copy-start.11 = (bf16[256,512]{1,0:T(8,128)(2,1)}, bf16[256,512]{1,0:T(8,128)(2,1)S(1)}, u32[]{:S(2)}) copy-start(bf16[256,512]{1,0:T(8,128)(2,1)S(1)} %collective-permute-done.5.refs_4_) | copy-start | bytes 786436
  85.7 24.3 %collective-permute-start.10 = (bf16[128,512]{1,0:T(8,128)(2,1)}, bf16[128,512]{1,0:T(8,128)(2,1)}, u32[]{:S(2)}, u32[]{:S(2)}) collective-permute-start(bf16[128,512]{1,0:T(8,128)(2,1)} %slice.57), channel_id=1, source_target_pairs={{0,112},{16,0},{32,16},{48,32},{64,48},{80,64},{96,80},{112,96},{1... | collective-permute-start | bytes 393224 | tf_op jit(solution)/shard_map/ppermute | solution.py:307
  89.7 20.3 %collective-permute-start.6 = (bf16[128,512]{1,0:T(8,128)(2,1)}, bf16[128,512]{1,0:T(8,128)(2,1)}, u32[]{:S(2)}, u32[]{:S(2)}) collective-permute-start(bf16[128,512]{1,0:T(8,128)(2,1)} %slice.56), channel_id=1, source_target_pairs={{0,16},{16,32},{32,48},{48,64},{64,80},{80,96},{96,112},{112,0},{1... | collective-permute-start | bytes 393224 | tf_op jit(solution)/shard_map/ppermute | solution.py:306
  91.4 57.3 %copy-start.5 = (bf16[8,64,128]{2,1,0:T(8,128)(2,1)}, bf16[8,64,128]{2,1,0:T(8,128)(2,1)S(1)}, u32[]{:S(2)}) copy-start(bf16[8,64,128]{2,1,0:T(8,128)(2,1)S(1)} %constant_dynamic-update-slice_fusion.grad) | copy-start | bytes 393220
  113.4 9.6 %collective-permute-start.11 = (bf16[272,256]{1,0:T(8,128)(2,1)}, bf16[272,256]{1,0:T(8,128)(2,1)S(1)}, u32[]{:S(2)}, u32[]{:S(2)}) collective-permute-start(bf16[272,256]{1,0:T(8,128)(2,1)} %get-tuple-element.27), channel_id=1, source_target_pairs={{0,8},{8,0},{128,136},{136,128},{1,9},{9,1},{129,137},{137,129},{2... | collective-permute-start | bytes 417800 | tf_op jit(solution)/shard_map/ppermute | solution.py:343
  113.4 9.6 %collective-permute-start.12 = (bf16[272,256]{1,0:T(8,128)(2,1)}, bf16[272,256]{1,0:T(8,128)(2,1)S(1)}, u32[]{:S(2)}, u32[]{:S(2)}) collective-permute-start(bf16[272,256]{1,0:T(8,128)(2,1)} %get-tuple-element.28), channel_id=1, source_target_pairs={{0,128},{8,136},{128,0},{136,8},{1,129},{9,137},{129,1},{137,9},{2... | collective-permute-start | bytes 417800 | tf_op jit(solution)/shard_map/ppermute | solution.py:343
  113.9 9.7 %collective-permute-start.13 = (bf16[272,256]{1,0:T(8,128)(2,1)}, bf16[272,256]{1,0:T(8,128)(2,1)S(1)}, u32[]{:S(2)}, u32[]{:S(2)}) collective-permute-start(bf16[272,256]{1,0:T(8,128)(2,1)} %get-tuple-element.29), channel_id=1, source_target_pairs={{0,136},{8,128},{128,8},{136,0},{1,137},{9,129},{129,9},{137,1},{2... | collective-permute-start | bytes 417800 | tf_op jit(solution)/shard_map/ppermute | solution.py:343
  117.7 28.1 %collective-permute-start.18 = (bf16[8,64,2]{2,1,0:T(8,128)(2,1)}, bf16[8,64,2]{2,1,0:T(8,128)(2,1)S(1)}, u32[]{:S(2)}, u32[]{:S(2)}) collective-permute-start(bf16[8,64,2]{2,1,0:T(8,128)(2,1)} %get-tuple-element.39), channel_id=1, source_target_pairs={{1,0},{2,1},{3,2},{4,3},{5,4},{6,5},{7,6},{9,8},{10,9},{11,10},{12... | collective-permute-start | bytes 6152 | tf_op jit(solution)/shard_map/ppermute | solution.py:335
  119.0 26.8 %collective-permute-start.19 = (bf16[8,64,2]{2,1,0:T(8,128)(2,1)S(1)}, bf16[8,64,2]{2,1,0:T(8,128)(2,1)S(1)}, u32[]{:S(2)}, u32[]{:S(2)}) collective-permute-start(bf16[8,64,2]{2,1,0:T(8,128)(2,1)S(1)} %get-tuple-element.40), channel_id=1, source_target_pairs={{0,1},{1,2},{2,3},{3,4},{4,5},{5,6},{6,7},{8,9},{9,10},{10,11},{11... | collective-permute-start | bytes 6152 | tf_op jit(solution)/shard_map/ppermute | solution.py:336
  126.8 14.5 %all-to-all-start.2 = ((bf16[8,2,144,128]{3,2,1,0:T(8,128)(2,1)}), bf16[8,2,144,128]{3,2,1,0:T(8,128)(2,1)S(1)}, u32[]{:S(2)}, u32[]{:S(2)}) async-start(bf16[8,2,144,128]{3,2,1,0:T(8,128)(2,1)} %merge_heads.1), calls=%async_computation.2 | async-start | bytes 1179648 | tf_op jit(solution)/shard_map/all_to_all | solution.py:344
  141.5 5.1 %collective-permute-start.14 = (bf16[144,128]{1,0:T(8,128)(2,1)S(1)}, bf16[144,128]{1,0:T(8,128)(2,1)S(1)}, u32[]{:S(2)}, u32[]{:S(2)}) collective-permute-start(bf16[144,128]{1,0:T(8,128)(2,1)S(1)} %get-tuple-element.42), channel_id=1, source_target_pairs={{0,8},{8,16},{16,24},{24,32},{32,40},{40,48},{48,56},{56,64},{64,7... | collective-permute-start | bytes 110600 | tf_op jit(solution)/shard_map/ppermute | solution.py:346
  143.4 5.3 %collective-permute-start.15 = (bf16[144,128]{1,0:T(8,128)(2,1)S(1)}, bf16[144,128]{1,0:T(8,128)(2,1)S(1)}, u32[]{:S(2)}, u32[]{:S(2)}) collective-permute-start(bf16[144,128]{1,0:T(8,128)(2,1)S(1)} %get-tuple-element.41), channel_id=1, source_target_pairs={{8,0},{16,8},{24,16},{32,24},{40,32},{48,40},{56,48},{64,56},{72,6... | collective-permute-start | bytes 110600 | tf_op jit(solution)/shard_map/ppermute | solution.py:347
  (11 other events, 44.0 us)

commit v2 on v1

--- a/solution.py
+++ b/solution.py
@@ -289,28 +289,44 @@
     normed_slab = (
         mixed * lax.rsqrt(jnp.mean(mixed * mixed, axis=-1, keepdims=True) + 1e-05) * agg_gain
     ).astype(BF)
+    cells, normed_slab = lax.optimization_barrier((cotangent, normed_slab))
     normed = copies(normed_slab, VAR, 8).reshape(256, D)
-
-    keys = jnp.dot(normed, wk, preferred_element_type=F32).astype(BF)
-    values = jnp.dot(normed, wv, preferred_element_type=F32).astype(BF)
-    queries = jnp.dot(normed, wq, preferred_element_type=F32).astype(BF)
-    keyvals = jnp.concatenate([keys, values], axis=1)
-
-    group = ("xh", "core")
-    all_queries = [queries] + [lax.ppermute(queries, group, flip(4, k)) for k in (1, 2, 3)]
-    ahead = [keyvals]
-    behind = [keyvals]
-    for _ in range(3):
-        ahead.append(lax.ppermute(ahead[-1], "z", turn(8, 1)))
-        behind.append(lax.ppermute(behind[-1], "z", turn(8, -1)))
-    ahead.append(lax.ppermute(ahead[-1][:128], "z", turn(8, 1)))
-    behind.append(lax.ppermute(behind[-1][128:], "z", turn(8, -1)))
-    carry = flash_step(all_queries, [keyvals, ahead[1], behind[1]], None, False)
-    carry = flash_step(all_queries, [ahead[2], behind[2]], carry, False)
-    carry = flash_step(all_queries, [ahead[3], behind[3]], carry, False)
-
     var_at = lax.axis_index(VAR)
     band_at = lax.axis_index(BAND)
+    shift_down = [(i, i + 1) for i in range(31)]
+    shift_up = [(i + 1, i) for i in range(31)]
+    grad_rows = jnp.concatenate(
+        [
+            lax.ppermute(cells[2:4], BAND, shift_down),
+            cells,
+            lax.ppermute(cells[0:2], BAND, shift_up),
+        ],
+        axis=0,
+    )
+    from_right = lax.ppermute(grad_rows[:, :, 0:2], VAR, [(i + 1, i) for i in range(7)])
+    from_left = lax.ppermute(grad_rows[:, :, 126:128], VAR, [(i, i + 1) for i in range(7)])
+    rim = jnp.concatenate([from_right, jnp.zeros((8, C, 124), BF), from_left], axis=2)
+    normed, rim = lax.optimization_barrier((normed, rim))
+
+    group = ("xh", "core")
+    queries = jnp.dot(normed, wq, preferred_element_type=F32).astype(BF)
+    all_queries = [queries] + [lax.ppermute(queries, group, flip(4, k)) for k in (2, 3, 1)]
+    keys_in, queries = lax.optimization_barrier((normed, queries))
+    keys = jnp.dot(keys_in, wk, preferred_element_type=F32).astype(BF)
+    values = jnp.dot(keys_in, wv, preferred_element_type=F32).astype(BF)
+    keyvals = jnp.concatenate([keys, values], axis=1)
+    ahead, behind = keyvals, keyvals
+    carry = None
+    fresh = [keyvals]
+    for step in range(4):
+        if step == 3:
+            ahead, behind = ahead[:128], behind[128:]
+        ahead = lax.ppermute(ahead, "z", turn(8, 1))
+        behind = lax.ppermute(behind, "z", turn(8, -1))
+        carry = flash_step(all_queries, fresh, carry, False)
+        ahead, behind, carry = lax.optimization_barrier((ahead, behind, carry))
+        fresh = [ahead, behind]
+
     up_mat = jnp.dot(wo, w_up, preferred_element_type=F32).astype(BF)
     padded = jnp.pad(normed, ((1, 1), (0, 0)))
     around = lax.dynamic_slice_in_dim(padded, var_at * 32, 34, 0)
@@ -320,27 +336,12 @@
     right = base[33].reshape(2, 4, 128)
     base_rim = jnp.where(jnp.arange(4)[None, :, None] % 2 == 0, right, left)
     base_all = jnp.concatenate([base_main, base_rim, jnp.zeros((2, 12, 128), F32)], axis=1)
-
-    shift_down = [(i, i + 1) for i in range(31)]
-    shift_up = [(i + 1, i) for i in range(31)]
-    cells, up_mat = lax.optimization_barrier((cotangent, up_mat))
-    grad_rows = jnp.concatenate(
-        [
-            lax.ppermute(cells[2:4], BAND, shift_down),
-            cells,
-            lax.ppermute(cells[0:2], BAND, shift_up),
-        ],
-        axis=0,
-    )
-    from_right = lax.ppermute(grad_rows[:, :, 0:2], VAR, [(i + 1, i) for i in range(7)])
-    from_left = lax.ppermute(grad_rows[:, :, 126:128], VAR, [(i, i + 1) for i in range(7)])
-    rim = jnp.concatenate([from_right, jnp.zeros((8, C, 124), BF), from_left], axis=2)
     mats = jnp.stack(
         [tap_matrix(conv1), tap_matrix(flipped(conv2)), tap_matrix(conv2), tap_matrix(flipped(conv1))]
     )
 
-    blocks = flash_step(all_queries, [ahead[4], behind[4]], carry, True)
-    parts = [blocks[0]] + [lax.ppermute(blocks[k], group, flip(4, k)) for k in (1, 2, 3)]
+    blocks = flash_step(all_queries, fresh, carry, True)
+    parts = [blocks[0]] + [lax.ppermute(b, group, flip(4, k)) for b, k in zip(blocks[1:], (2, 3, 1))]
     pieces = lax.all_to_all(merge(parts, up_mat), VAR, 0, 0)
     up = (jnp.sum(pieces.astype(F32), axis=0) + base_all).astype(BF)
     prev = lax.ppermute(up[1], BAND, shift_down)

time: 195 us -> 196 us (level)
  Pallas kernels: 26.8 us -> 31.3 us
  local copies, waits for them, and re-layouts: 11.7 us -> 8.37 us
  starting transfers between devices: 53.9 us -> 51 us
  blocking collectives: 60.4 us -> 62.8 us
    all_to_all x1, waiting for transfers between devices: 9.57 us -> 0.01 us  [copies(): lax.all_to_all(jnp.broadcast_to(piece[None], (count,) + piece.shape), axi...]
    ppermute x3, starting transfers between devices: 9.72 us -> 3.36 us  [on_device(): lax.ppermute(queries, group, flip(4, k))]
    ppermute x3, waiting for transfers between devices: 0.01 us -> 5.94 us  [on_device(): lax.ppermute(queries, group, flip(4, k))]
    pallas_call x4 -> x5, Pallas kernels: 20.6 us -> 25.1 us  [flash_step(): pl.pallas_call(flash_kernel(blocks, len(chunks), first, last), out_shape=...]
    ppermute x1, waiting for transfers between devices: 0.01 us -> 3.56 us  [on_device(): lax.ppermute(cells[0:2], BAND, shift_up)]
    ppermute x1, starting transfers between devices: 2.44 us -> 5.24 us  [on_device(): lax.ppermute(cells[2:4], BAND, shift_down)]
    all_to_all x1, blocking collectives: 15.4 us -> 18 us  [on_device(): shares = lax.all_to_all(terms.reshape(32, 24, 128), PLANE, 0, 0)]
    all_to_all x1, starting transfers between devices: 3.76 us -> 6.39 us  [on_device(): pieces = lax.all_to_all(merge(parts, up_mat), VAR, 0, 0)]
  transfers between devices with their start and end apart: 22 -> 22, of which waited for: 5 -> 9; matrix products, arithmetic and copies ran while one was open for 9% -> 6% of each run, Pallas kernels for 10% -> 11%
where the time goes in v2:
time: 196 us; the launch traced here: 195 us
  blocking collectives  62.8 us (32%)
  starting transfers between devices  51 us (26%)
  Pallas kernels  31.3 us (16%)
  waiting for transfers between devices  24.9 us (13%)
  matrix products  11.4 us (6%)
  local copies, waits for them, and re-layouts  8.37 us (4%)
  other arithmetic  3.83 us (2%)
    pallas_call x5, Pallas kernels, flash_step(): pl.pallas_call(flash_kernel(blocks, len(chunks), first, last), out_shape=...  25.1 us
    all_to_all x2, blocking collectives, copies(): lax.all_to_all(jnp.broadcast_to(piece[None], (count,) + piece.shape), axi...  24 us
    all_to_all x1, blocking collectives, on_device(): mixed = jnp.sum(lax.all_to_all(partial_mix, VAR, 0, 0).astype(F32), axis=0)  20.8 us
    all_to_all x1, blocking collectives, on_device(): shares = lax.all_to_all(terms.reshape(32, 24, 128), PLANE, 0, 0)  18 us
    ppermute x4, starting transfers between devices, on_device(): behind = lax.ppermute(behind, 'z', turn(8, -1))  12 us
    all_to_all x1, waiting for transfers between devices, on_device(): pieces = lax.all_to_all(merge(parts, up_mat), VAR, 0, 0)  6.55 us
    all_to_all x1, starting transfers between devices, on_device(): pieces = lax.all_to_all(merge(parts, up_mat), VAR, 0, 0)  6.39 us
    ppermute x3, starting transfers between devices, on_device(): lax.ppermute(b, group, flip(4, k))  5.95 us
  transfers between devices with their start and end apart: 22, of which 9 were waited for; matrix products, arithmetic and copies ran while one was open for 6% of the time, Pallas kernels for 11%

profile of v2, /device:TPU:1, one launch (start us, length us, event | category | flops | bytes accessed | tf_op | source)
XLA Modules:
  0.0 194.8 jit_solution(15383868843449510533)
XLA Ops:
  3.1 20.8 %all_to_all.30 = bf16[8,32,2048]{2,1,0:T(8,128)(2,1)S(1)} all-to-all(bf16[8,32,2048]{2,1,0:T(8,128)(2,1)S(1)} %bitcast.59), channel_id=1, replica_groups=mesh['xh'=2,'z'=8,'core'=2,'y'=4,'xl'=2] {'y','xl'}, dimensions={0} | all-to-all | bytes 2097152 | tf_op jit(solution)/shard_map/all_to_all | solution.py:288
  25.4 3.6 %all-to-all-start.1 = ((bf16[8,32,2048]{2,1,0:T(8,128)(2,1)}), bf16[8,32,2048]{2,1,0:T(8,128)(2,1)S(1)}, u32[]{:S(2)}, u32[]{:S(2)}) async-start(bf16[8,32,2048]{2,1,0:T(8,128)(2,1)} %broadcast_in_dim.18), calls=%async_computation.1 | async-start | bytes 2097152 | tf_op jit(solution)/shard_map/all_to_all | solution.py:263
  29.0 5.2 %collective-permute-start = (bf16[2,64,128]{2,1,0:T(8,128)(2,1)S(1)}, bf16[2,64,128]{2,1,0:T(8,128)(2,1)S(1)}, u32[]{:S(2)}, u32[]{:S(2)}) collective-permute-start(bf16[2,64,128]{2,1,0:T(8,128)(2,1)S(1)} %get-tuple-element.86), channel_id=1, source_target_pairs={{0,8},{8,16},{16,24},{24,32},{32,40},{40,48},{48,56},{56,64},{64,7... | collective-permute-start | bytes 98312 | tf_op jit(solution)/shard_map/ppermute | solution.py:300
  34.3 1.9 collective-permute-start.1
  36.2 3.6 %collective-permute-done.1 = bf16[2,64,128]{2,1,0:T(8,128)(2,1)S(1)} collective-permute-done((bf16[2,64,128]{2,1,0:T(8,128)(2,1)S(1)}, bf16[2,64,128]{2,1,0:T(8,128)(2,1)S(1)}, u32[]{:S(2)}, u32[]{:S(2)}) %collective-permute-start.1) | collective-permute-done | bytes 32800 | tf_op jit(solution)/shard_map/ppermute | solution.py:302
  41.2 4.2 %collective-permute-start.3 = (bf16[8,64,2]{2,1,0:T(8,128)(2,1)S(1)}, bf16[8,64,2]{2,1,0:T(8,128)(2,1)S(1)}, u32[]{:S(2)}, u32[]{:S(2)}) collective-permute-start(bf16[8,64,2]{2,1,0:T(8,128)(2,1)S(1)} %get-tuple-element.82), channel_id=1, source_target_pairs={{0,1},{1,2},{2,3},{3,4},{4,5},{5,6},{6,7},{8,9},{9,10},{10,11},{11... | collective-permute-start | bytes 6152 | tf_op jit(solution)/shard_map/ppermute | solution.py:307
  52.6 4.8 %collective-permute-start.8 = (bf16[256,512]{1,0:T(8,128)(2,1)S(1)}, bf16[256,512]{1,0:T(8,128)(2,1)}, u32[]{:S(2)}, u32[]{:S(2)}) collective-permute-start(bf16[256,512]{1,0:T(8,128)(2,1)S(1)} %pad_maximum_fusion.1.refs_4_), channel_id=1, source_target_pairs={{0,112},{16,0},{32,16},{48,32},{64,48},{80,64},{96,80},{112,96},{1... | collective-permute-start | bytes 786440 | tf_op jit(solution)/shard_map/ppermute | solution.py:325
  57.4 2.4 %collective-permute-start.5 = (bf16[256,256]{1,0:T(8,128)(2,1)S(1)}, bf16[256,256]{1,0:T(8,128)(2,1)S(1)}, u32[]{:S(2)}, u32[]{:S(2)}) collective-permute-start(bf16[256,256]{1,0:T(8,128)(2,1)S(1)} %convolution_convert_fusion.3.refs_0_), channel_id=1, source_target_pairs={{0,136},{8,128},{128,8},{136,0},{1,137},{9,129},{129,9},{137,1},{2... | collective-permute-start | bytes 393224 | tf_op jit(solution)/shard_map/ppermute | solution.py:313
  60.8 3.4 %collective-permute-done.4.refs_1_ = bf16[256,256]{1,0:T(8,128)(2,1)S(1)} collective-permute-done((bf16[256,256]{1,0:T(8,128)(2,1)S(1)}, bf16[256,256]{1,0:T(8,128)(2,1)S(1)}, u32[]{:S(2)}, u32[]{:S(2)}) %collective-permute-start.4) | collective-permute-done | bytes 131104 | tf_op jit(solution)/shard_map/ppermute | solution.py:313
  64.1 2.6 %collective-permute-done.5.refs_2_ = bf16[256,256]{1,0:T(8,128)(2,1)S(1)} collective-permute-done((bf16[256,256]{1,0:T(8,128)(2,1)S(1)}, bf16[256,256]{1,0:T(8,128)(2,1)S(1)}, u32[]{:S(2)}, u32[]{:S(2)}) %collective-permute-start.5) | collective-permute-done | bytes 131104 | tf_op jit(solution)/shard_map/ppermute | solution.py:313
  68.0 4.7 %flash_step.4 = (f32[8,1024]{1,0:T(8,128)}, f32[256,1024]{1,0:T(8,128)}) custom-call(bf16[256,256]{1,0:T(8,128)(2,1)} %copy-done.1, bf16[256,256]{1,0:T(8,128)(2,1)} %copy-done.2, bf16[256,256]{1,0:T(8,128)(2,1)} %copy-done.3, bf16[256,256]{1,0:T(8,128)(2,1)} %copy-done.4, bf16[256,512]{1,0:T(8,128)(2,1)} %copy-done.6), custom_call_target="tpu_custom_call" | custom-call | tf_op jit(solution)/shard_map/flash_step/pallas_call | solution.py:105
  74.5 5.7 %flash_step.5 = (f32[8,1024]{1,0:T(8,128)}, f32[256,1024]{1,0:T(8,128)}) custom-call(bf16[256,256]{1,0:T(8,128)(2,1)} %copy-done.1, bf16[256,256]{1,0:T(8,128)(2,1)} %copy-done.2, bf16[256,256]{1,0:T(8,128)(2,1)} %copy-done.3, bf16[256,256]{1,0:T(8,128)(2,1)} %copy-done.4, bf16[256,512]{1,0:T(8,128)(2,1)} %copy-done.15, ...), custom_call_target="tpu_custom_call" | custom-call | tf_op jit(solution)/shard_map/flash_step/pallas_call | solution.py:105
  80.2 2.5 %collective-permute-done.9.refs_4_ = bf16[256,512]{1,0:T(8,128)(2,1)S(1)} collective-permute-done((bf16[256,512]{1,0:T(8,128)(2,1)S(1)}, bf16[256,512]{1,0:T(8,128)(2,1)S(1)}, u32[]{:S(2)}, u32[]{:S(2)}) %collective-permute-start.9) | collective-permute-done | bytes 262176 | tf_op jit(solution)/shard_map/ppermute | solution.py:324
  82.8 2.7 %collective-permute-start.12 = (bf16[256,512]{1,0:T(8,128)(2,1)S(1)}, bf16[256,512]{1,0:T(8,128)(2,1)S(1)}, u32[]{:S(2)}, u32[]{:S(2)}) collective-permute-start(bf16[256,512]{1,0:T(8,128)(2,1)S(1)} %collective-permute-done.10.refs_5_), channel_id=1, source_target_pairs={{0,112},{16,0},{32,16},{48,32},{64,48},{80,64},{96,80},{112,96},{1... | collective-permute-start | bytes 786440 | tf_op jit(solution)/shard_map/ppermute | solution.py:325
  85.4 5.7 %flash_step.6 = (f32[8,1024]{1,0:T(8,128)}, f32[256,1024]{1,0:T(8,128)}) custom-call(bf16[256,256]{1,0:T(8,128)(2,1)} %copy-done.1, bf16[256,256]{1,0:T(8,128)(2,1)} %copy-done.2, bf16[256,256]{1,0:T(8,128)(2,1)} %copy-done.3, bf16[256,256]{1,0:T(8,128)(2,1)} %copy-done.4, bf16[256,512]{1,0:T(8,128)(2,1)} %copy-done.17, bf16[256,512]{1,0:T(8,128)(2,1)} %copy-done.16, ...), custom_call_target="tpu_custom_call" | custom-call | tf_op jit(solution)/shard_map/flash_step/pallas_call | solution.py:105
  91.3 2.7 %collective-permute-start.14 = (bf16[128,512]{1,0:T(8,128)(2,1)S(1)}, bf16[128,512]{1,0:T(8,128)(2,1)S(1)}, u32[]{:S(2)}, u32[]{:S(2)}) collective-permute-start(bf16[128,512]{1,0:T(8,128)(2,1)S(1)} %slice.47), channel_id=1, source_target_pairs={{0,112},{16,0},{32,16},{48,32},{64,48},{80,64},{96,80},{112,96},{1... | collective-permute-start | bytes 393224 | tf_op jit(solution)/shard_map/ppermute | solution.py:325
  94.0 4.2 %convolution_convert_fusion.mat = bf16[256,1024]{1,0:T(8,128)(2,1)} fusion(bf16[256,2048]{1,0:T(8,128)(2,1)S(1)} %copy-done, bf16[2048,1024]{1,0:T(8,128)(2,1)} %param.22), kind=kOutput, calls=%fused_computation.3 | convolution fusion | flops 1074003968 | bytes 5767168 | tf_op jit(solution)/shard_map/dot_general | solution.py:330
  98.3 5.7 %flash_step.7 = (f32[8,1024]{1,0:T(8,128)}, f32[256,1024]{1,0:T(8,128)}) custom-call(bf16[256,256]{1,0:T(8,128)(2,1)} %copy-done.1, bf16[256,256]{1,0:T(8,128)(2,1)} %copy-done.2, bf16[256,256]{1,0:T(8,128)(2,1)} %copy-done.3, bf16[256,256]{1,0:T(8,128)(2,1)} %copy-done.4, bf16[256,512]{1,0:T(8,128)(2,1)} %copy-done.12, bf16[256,512]{1,0:T(8,128)(2,1)} %copy-done.13, ...), custom_call_target="tpu_custom_call" | custom-call | tf_op jit(solution)/shard_map/flash_step/pallas_call | solution.py:105
  104.7 3.4 %flash_last.1 = (bf16[272,256]{1,0:T(8,128)(2,1)}, bf16[272,256]{1,0:T(8,128)(2,1)}, bf16[272,256]{1,0:T(8,128)(2,1)}, bf16[272,256]{1,0:T(8,128)(2,1)}) custom-call(bf16[256,256]{1,0:T(8,128)(2,1)} %copy-done.1, bf16[256,256]{1,0:T(8,128)(2,1)} %copy-done.2, bf16[256,256]{1,0:T(8,128)(2,1)} %copy-done.3, bf16[256,256]{1,0:T(8,128)(2,1)} %copy-done.4, ...), custom_call_target="tpu_custom_call" | custom-call | tf_op jit(solution)/shard_map/flash_last/pallas_call | solution.py:105
  108.1 2.6 %collective-permute-start.15 = (bf16[272,256]{1,0:T(8,128)(2,1)}, bf16[272,256]{1,0:T(8,128)(2,1)S(1)}, u32[]{:S(2)}, u32[]{:S(2)}) collective-permute-start(bf16[272,256]{1,0:T(8,128)(2,1)} %get-tuple-element.70), channel_id=1, source_target_pairs={{0,128},{8,136},{128,0},{136,8},{1,129},{9,137},{129,1},{137,9},{2... | collective-permute-start | bytes 417800 | tf_op jit(solution)/shard_map/ppermute | solution.py:344
  110.7 3.4 %collective-permute-start.16 = (bf16[272,256]{1,0:T(8,128)(2,1)}, bf16[272,256]{1,0:T(8,128)(2,1)S(1)}, u32[]{:S(2)}, u32[]{:S(2)}) collective-permute-start(bf16[272,256]{1,0:T(8,128)(2,1)} %get-tuple-element.71), channel_id=1, source_target_pairs={{0,136},{8,128},{128,8},{136,0},{1,137},{9,129},{129,9},{137,1},{2... | collective-permute-start | bytes 417800 | tf_op jit(solution)/shard_map/ppermute | solution.py:344
  116.4 3.8 %collective-permute-done.16.b2 = bf16[272,256]{1,0:T(8,128)(2,1)S(1)} collective-permute-done((bf16[272,256]{1,0:T(8,128)(2,1)}, bf16[272,256]{1,0:T(8,128)(2,1)S(1)}, u32[]{:S(2)}, u32[]{:S(2)}) %collective-permute-start.16) | collective-permute-done | bytes 139296 | tf_op jit(solution)/shard_map/ppermute | solution.py:344
  120.9 2.6 %merge_heads.1 = bf16[8,2,144,128]{3,2,1,0:T(8,128)(2,1)} custom-call(bf16[272,256]{1,0:T(8,128)(2,1)} %get-tuple-element.69.b0, bf16[272,256]{1,0:T(8,128)(2,1)} %copy-done.18, bf16[272,256]{1,0:T(8,128)(2,1)} %copy-done.19, bf16[272,256]{1,0:T(8,128)(2,1)} %copy-done.20, bf16[256,1024]{1,0:T(8,128)(2,1)} %convolution_convert_fusion.mat), custom_call_target="tpu_custom_call" | custom-call | tf_op jit(solution)/shard_map/merge_heads/pallas_call | solution.py:143
  123.4 6.4 %all-to-all-start.2 = ((bf16[8,2,144,128]{3,2,1,0:T(8,128)(2,1)}), bf16[8,2,144,128]{3,2,1,0:T(8,128)(2,1)S(1)}, u32[]{:S(2)}, u32[]{:S(2)}) async-start(bf16[8,2,144,128]{3,2,1,0:T(8,128)(2,1)} %merge_heads.1), calls=%async_computation.2 | async-start | bytes 1179648 | tf_op jit(solution)/shard_map/all_to_all | solution.py:345
  129.8 3.0 %fusion.1 = f32[34,1024]{1,0:T(8,128)S(1)} fusion(bf16[2048,1024]{1,0:T(8,128)(2,1)} %param.22, s32[]{:T(128)S(6)} %select_n.19, bf16[256,2048]{1,0:T(8,128)(2,1)S(1)} %bitcast.58), kind=kOutput, calls=%fused_computation.16 | convolution fusion | flops 142606336 | bytes 5382148 | tf_op jit(solution)/shard_map/dot_general | solution.py:333
  133.0 6.6 %all-to-all-done.2 = bf16[8,2,144,128]{3,2,1,0:T(8,128)(2,1)S(1)} async-done(((bf16[8,2,144,128]{3,2,1,0:T(8,128)(2,1)}), bf16[8,2,144,128]{3,2,1,0:T(8,128)(2,1)S(1)}, u32[]{:S(2)}, u32[]{:S(2)}) %all-to-all-start.2) | async-done | bytes 589856 | tf_op jit(solution)/shard_map/all_to_all | solution.py:345
  139.8 2.0 %collective-permute-start.18 = (bf16[144,128]{1,0:T(8,128)(2,1)S(1)}, bf16[144,128]{1,0:T(8,128)(2,1)S(1)}, u32[]{:S(2)}, u32[]{:S(2)}) collective-permute-start(bf16[144,128]{1,0:T(8,128)(2,1)S(1)} %get-tuple-element.84), channel_id=1, source_target_pairs={{0,8},{8,16},{16,24},{24,32},{32,40},{40,48},{48,56},{56,64},{64,7... | collective-permute-start | bytes 110600 | tf_op jit(solution)/shard_map/ppermute | solution.py:347
  141.8 3.2 %collective-permute-start.19 = (bf16[144,128]{1,0:T(8,128)(2,1)S(1)}, bf16[144,128]{1,0:T(8,128)(2,1)S(1)}, u32[]{:S(2)}, u32[]{:S(2)}) collective-permute-start(bf16[144,128]{1,0:T(8,128)(2,1)S(1)} %get-tuple-element.83), channel_id=1, source_target_pairs={{8,0},{16,8},{24,16},{32,24},{40,32},{48,40},{56,48},{64,56},{72,6... | collective-permute-start | bytes 110600 | tf_op jit(solution)/shard_map/ppermute | solution.py:348
  147.6 3.6 %fine_stage.1 = (bf16[4,64,128]{2,1,0:T(8,128)(2,1)}, bf16[4,64,128]{2,1,0:T(8,128)(2,1)}, bf16[768,128]{1,0:T(8,128)(2,1)}) custom-call(s32[4]{0:T(128)} %add_convert_fusion.flags, bf16[2,144,128]{2,1,0:T(8,128)(2,1)} %copy-done.9, bf16[144,128]{1,0:T(8,128)(2,1)} %copy-done.23, bf16[144,128]{1,0:T(8,128)(2,1)} %copy-done.24, ...), custom_call_target="tpu_custom_call" | custom-call | tf_op jit(solution)/shard_map/fine_stage/pallas_call | solution.py:249
  151.3 18.0 %all_to_all.31 = bf16[32,24,128]{2,1,0:T(8,128)(2,1)S(1)} all-to-all(bf16[32,24,128]{2,1,0:T(8,128)(2,1)} %bitcast.72), channel_id=1, replica_groups=mesh['xh'=2,'z'=8,'core'=2,'y'=4,'xl'=2] {'xh','core','y','xl'}, dimensions={0} | all-to-all | bytes 393216 | tf_op jit(solution)/shard_map/all_to_all | solution.py:355
  169.3 10.5 %all_to_all.32 = bf16[8,24,128]{2,1,0:T(8,128)(2,1)S(1)} all-to-all(bf16[8,24,128]{2,1,0:T(8,128)(2,1)S(1)} %broadcast_in_dim.22), channel_id=1, replica_groups=mesh['xh'=2,'z'=8,'core'=2,'y'=4,'xl'=2] {'z'}, dimensions={0} | all-to-all | bytes 98304 | tf_op jit(solution)/shard_map/all_to_all | solution.py:263
  179.9 13.5 %all_to_all.33 = bf16[32,24,128]{2,1,0:T(8,128)(2,1)S(1)} all-to-all(bf16[32,24,128]{2,1,0:T(8,128)(2,1)S(1)} %broadcast_in_dim.23), channel_id=1, replica_groups=mesh['xh'=2,'z'=8,'core'=2,'y'=4,'xl'=2] {'xh','core','y','xl'}, dimensions={0} | all-to-all | bytes 393216 | tf_op jit(solution)/shard_map/all_to_all | solution.py:263
  (131 shorter events, 24.9 us)
Async XLA Ops:
  0.6 93.4 %copy-start = (bf16[256,2048]{1,0:T(8,128)(2,1)S(1)}, bf16[256,2048]{1,0:T(8,128)(2,1)}, u32[]{:S(2)}) copy-start(bf16[256,2048]{1,0:T(8,128)(2,1)} %param.21) | copy-start | bytes 3145732
  0.6 23.6 %copy-start.25 = (f32[2048]{0:T(1024)S(1)}, f32[2048]{0:T(1024)}, u32[]{:S(2)}) copy-start(f32[2048]{0:T(1024)} %param.17) | copy-start | bytes 24580
  1.5 27.5 %copy-start.14 = (bf16[4,64,128]{2,1,0:T(8,128)(2,1)S(1)}, bf16[4,64,128]{2,1,0:T(8,128)(2,1)}, u32[]{:S(2)}) copy-start(bf16[4,64,128]{2,1,0:T(8,128)(2,1)} %param.26) | copy-start | bytes 196612
  3.1 45.0 %copy-start.7 = (bf16[2048,256]{1,0:T(8,128)(2,1)S(1)}, bf16[2048,256]{1,0:T(8,128)(2,1)}, u32[]{:S(2)}) copy-start(bf16[2048,256]{1,0:T(8,128)(2,1)} %param.18) | copy-start | bytes 3145732
  25.4 22.7 %all-to-all-start.1 = ((bf16[8,32,2048]{2,1,0:T(8,128)(2,1)}), bf16[8,32,2048]{2,1,0:T(8,128)(2,1)S(1)}, u32[]{:S(2)}, u32[]{:S(2)}) async-start(bf16[8,32,2048]{2,1,0:T(8,128)(2,1)} %broadcast_in_dim.18), calls=%async_computation.1 | async-start | bytes 2097152 | tf_op jit(solution)/shard_map/all_to_all | solution.py:263
  29.0 7.2 %collective-permute-start = (bf16[2,64,128]{2,1,0:T(8,128)(2,1)S(1)}, bf16[2,64,128]{2,1,0:T(8,128)(2,1)S(1)}, u32[]{:S(2)}, u32[]{:S(2)}) collective-permute-start(bf16[2,64,128]{2,1,0:T(8,128)(2,1)S(1)} %get-tuple-element.86), channel_id=1, source_target_pairs={{0,8},{8,16},{16,24},{24,32},{32,40},{40,48},{48,56},{56,64},{64,7... | collective-permute-start | bytes 98312 | tf_op jit(solution)/shard_map/ppermute | solution.py:300
  34.3 5.5 %collective-permute-start.1 = (bf16[2,64,128]{2,1,0:T(8,128)(2,1)S(1)}, bf16[2,64,128]{2,1,0:T(8,128)(2,1)S(1)}, u32[]{:S(2)}, u32[]{:S(2)}) collective-permute-start(bf16[2,64,128]{2,1,0:T(8,128)(2,1)S(1)} %get-tuple-element.85), channel_id=1, source_target_pairs={{8,0},{16,8},{24,16},{32,24},{40,32},{48,40},{56,48},{64,56},{72,6... | collective-permute-start | bytes 98312 | tf_op jit(solution)/shard_map/ppermute | solution.py:302
  39.8 32.9 %copy-start.5 = (bf16[8,64,128]{2,1,0:T(8,128)(2,1)}, bf16[8,64,128]{2,1,0:T(8,128)(2,1)S(1)}, u32[]{:S(2)}) copy-start(bf16[8,64,128]{2,1,0:T(8,128)(2,1)S(1)} %constant_dynamic-update-slice_fusion.grad) | copy-start | bytes 393220
  39.9 6.3 %collective-permute-start.2 = (bf16[8,64,2]{2,1,0:T(8,128)(2,1)S(1)}, bf16[8,64,2]{2,1,0:T(8,128)(2,1)S(1)}, u32[]{:S(2)}, u32[]{:S(2)}) collective-permute-start(bf16[8,64,2]{2,1,0:T(8,128)(2,1)S(1)} %get-tuple-element.81), channel_id=1, source_target_pairs={{1,0},{2,1},{3,2},{4,3},{5,4},{6,5},{7,6},{9,8},{10,9},{11,10},{12... | collective-permute-start | bytes 6152 | tf_op jit(solution)/shard_map/ppermute | solution.py:306
  41.2 6.1 %collective-permute-start.3 = (bf16[8,64,2]{2,1,0:T(8,128)(2,1)S(1)}, bf16[8,64,2]{2,1,0:T(8,128)(2,1)S(1)}, u32[]{:S(2)}, u32[]{:S(2)}) collective-permute-start(bf16[8,64,2]{2,1,0:T(8,128)(2,1)S(1)} %get-tuple-element.82), channel_id=1, source_target_pairs={{0,1},{1,2},{2,3},{3,4},{4,5},{5,6},{6,7},{8,9},{9,10},{10,11},{11... | collective-permute-start | bytes 6152 | tf_op jit(solution)/shard_map/ppermute | solution.py:307
  48.5 18.2 %copy-start.1 = (bf16[256,256]{1,0:T(8,128)(2,1)}, bf16[256,256]{1,0:T(8,128)(2,1)S(1)}, u32[]{:S(2)}) copy-start(bf16[256,256]{1,0:T(8,128)(2,1)S(1)} %convolution_convert_fusion.3.refs_0_) | copy-start | bytes 393220
  50.7 16.0 %copy-start.6 = (bf16[256,512]{1,0:T(8,128)(2,1)}, bf16[256,512]{1,0:T(8,128)(2,1)S(1)}, u32[]{:S(2)}) copy-start(bf16[256,512]{1,0:T(8,128)(2,1)S(1)} %pad_maximum_fusion.1.refs_4_) | copy-start | bytes 786436
  50.8 21.9 %collective-permute-start.7 = (bf16[256,512]{1,0:T(8,128)(2,1)S(1)}, bf16[256,512]{1,0:T(8,128)(2,1)S(1)}, u32[]{:S(2)}, u32[]{:S(2)}) collective-permute-start(bf16[256,512]{1,0:T(8,128)(2,1)S(1)} %pad_maximum_fusion.1.refs_4_), channel_id=1, source_target_pairs={{0,16},{16,32},{32,48},{48,64},{64,80},{80,96},{96,112},{112,0},{1... | collective-permute-start | bytes 786440 | tf_op jit(solution)/shard_map/ppermute | solution.py:324
  52.6 20.1 %collective-permute-start.8 = (bf16[256,512]{1,0:T(8,128)(2,1)S(1)}, bf16[256,512]{1,0:T(8,128)(2,1)}, u32[]{:S(2)}, u32[]{:S(2)}) collective-permute-start(bf16[256,512]{1,0:T(8,128)(2,1)S(1)} %pad_maximum_fusion.1.refs_4_), channel_id=1, source_target_pairs={{0,112},{16,0},{32,16},{48,32},{64,48},{80,64},{96,80},{112,96},{1... | collective-permute-start | bytes 786440 | tf_op jit(solution)/shard_map/ppermute | solution.py:325
  57.4 6.7 %collective-permute-start.4 = (bf16[256,256]{1,0:T(8,128)(2,1)S(1)}, bf16[256,256]{1,0:T(8,128)(2,1)S(1)}, u32[]{:S(2)}, u32[]{:S(2)}) collective-permute-start(bf16[256,256]{1,0:T(8,128)(2,1)S(1)} %convolution_convert_fusion.3.refs_0_), channel_id=1, source_target_pairs={{0,128},{8,136},{128,0},{136,8},{1,129},{9,137},{129,1},{137,9},{2... | collective-permute-start | bytes 393224 | tf_op jit(solution)/shard_map/ppermute | solution.py:313
  57.4 9.3 %collective-permute-start.5 = (bf16[256,256]{1,0:T(8,128)(2,1)S(1)}, bf16[256,256]{1,0:T(8,128)(2,1)S(1)}, u32[]{:S(2)}, u32[]{:S(2)}) collective-permute-start(bf16[256,256]{1,0:T(8,128)(2,1)S(1)} %convolution_convert_fusion.3.refs_0_), channel_id=1, source_target_pairs={{0,136},{8,128},{128,8},{136,0},{1,137},{9,129},{129,9},{137,1},{2... | collective-permute-start | bytes 393224 | tf_op jit(solution)/shard_map/ppermute | solution.py:313
  59.8 6.9 %collective-permute-start.6 = (bf16[256,256]{1,0:T(8,128)(2,1)S(1)}, bf16[256,256]{1,0:T(8,128)(2,1)S(1)}, u32[]{:S(2)}, u32[]{:S(2)}) collective-permute-start(bf16[256,256]{1,0:T(8,128)(2,1)S(1)} %convolution_convert_fusion.3.refs_0_), channel_id=1, source_target_pairs={{0,8},{8,0},{128,136},{136,128},{1,9},{9,1},{129,137},{137,129},{2... | collective-permute-start | bytes 393224 | tf_op jit(solution)/shard_map/ppermute | solution.py:313
  72.7 7.5 %collective-permute-start.10 = (bf16[256,512]{1,0:T(8,128)(2,1)}, bf16[256,512]{1,0:T(8,128)(2,1)S(1)}, u32[]{:S(2)}, u32[]{:S(2)}) collective-permute-start(bf16[256,512]{1,0:T(8,128)(2,1)} %collective-permute-done.8.refs_5_), channel_id=1, source_target_pairs={{0,112},{16,0},{32,16},{48,32},{64,48},{80,64},{96,80},{112,96},{1... | collective-permute-start | bytes 786440 | tf_op jit(solution)/shard_map/ppermute | solution.py:325
  74.5 8.2 %collective-permute-start.9 = (bf16[256,512]{1,0:T(8,128)(2,1)S(1)}, bf16[256,512]{1,0:T(8,128)(2,1)S(1)}, u32[]{:S(2)}, u32[]{:S(2)}) collective-permute-start(bf16[256,512]{1,0:T(8,128)(2,1)S(1)} %collective-permute-done.7.refs_4_), channel_id=1, source_target_pairs={{0,16},{16,32},{32,48},{48,64},{64,80},{80,96},{96,112},{112,0},{1... | collective-permute-start | bytes 786440 | tf_op jit(solution)/shard_map/ppermute | solution.py:324
  82.7 8.4 %collective-permute-start.11 = (bf16[256,512]{1,0:T(8,128)(2,1)S(1)}, bf16[256,512]{1,0:T(8,128)(2,1)S(1)}, u32[]{:S(2)}, u32[]{:S(2)}) collective-permute-start(bf16[256,512]{1,0:T(8,128)(2,1)S(1)} %collective-permute-done.9.refs_4_), channel_id=1, source_target_pairs={{0,16},{16,32},{32,48},{48,64},{64,80},{80,96},{96,112},{112,0},{1... | collective-permute-start | bytes 786440 | tf_op jit(solution)/shard_map/ppermute | solution.py:324
  82.8 8.4 %collective-permute-start.12 = (bf16[256,512]{1,0:T(8,128)(2,1)S(1)}, bf16[256,512]{1,0:T(8,128)(2,1)S(1)}, u32[]{:S(2)}, u32[]{:S(2)}) collective-permute-start(bf16[256,512]{1,0:T(8,128)(2,1)S(1)} %collective-permute-done.10.refs_5_), channel_id=1, source_target_pairs={{0,112},{16,0},{32,16},{48,32},{64,48},{80,64},{96,80},{112,96},{1... | collective-permute-start | bytes 786440 | tf_op jit(solution)/shard_map/ppermute | solution.py:325
  91.2 12.8 %collective-permute-start.13 = (bf16[128,512]{1,0:T(8,128)(2,1)S(1)}, bf16[128,512]{1,0:T(8,128)(2,1)S(1)}, u32[]{:S(2)}, u32[]{:S(2)}) collective-permute-start(bf16[128,512]{1,0:T(8,128)(2,1)S(1)} %slice.46), channel_id=1, source_target_pairs={{0,16},{16,32},{32,48},{48,64},{64,80},{80,96},{96,112},{112,0},{1... | collective-permute-start | bytes 393224 | tf_op jit(solution)/shard_map/ppermute | solution.py:324
  91.3 22.8 %copy-start.11 = (bf16[9,64,64]{2,1,0:T(8,128)(2,1)S(1)}, bf16[9,64,64]{2,1,0:T(8,128)(2,1)}, u32[]{:S(2)}) copy-start(bf16[9,64,64]{2,1,0:T(8,128)(2,1)} %param.25) | copy-start | bytes 221188
  91.3 12.7 %collective-permute-start.14 = (bf16[128,512]{1,0:T(8,128)(2,1)S(1)}, bf16[128,512]{1,0:T(8,128)(2,1)S(1)}, u32[]{:S(2)}, u32[]{:S(2)}) collective-permute-start(bf16[128,512]{1,0:T(8,128)(2,1)S(1)} %slice.47), channel_id=1, source_target_pairs={{0,112},{16,0},{32,16},{48,32},{64,48},{80,64},{96,80},{112,96},{1... | collective-permute-start | bytes 393224 | tf_op jit(solution)/shard_map/ppermute | solution.py:325
  98.3 16.1 %copy-start.10 = (bf16[9,64,64]{2,1,0:T(8,128)(2,1)S(1)}, bf16[9,64,64]{2,1,0:T(8,128)(2,1)}, u32[]{:S(2)}) copy-start(bf16[9,64,64]{2,1,0:T(8,128)(2,1)} %param.23) | copy-start | bytes 221188
  108.1 8.3 %collective-permute-start.15 = (bf16[272,256]{1,0:T(8,128)(2,1)}, bf16[272,256]{1,0:T(8,128)(2,1)S(1)}, u32[]{:S(2)}, u32[]{:S(2)}) collective-permute-start(bf16[272,256]{1,0:T(8,128)(2,1)} %get-tuple-element.70), channel_id=1, source_target_pairs={{0,128},{8,136},{128,0},{136,8},{1,129},{9,137},{129,1},{137,9},{2... | collective-permute-start | bytes 417800 | tf_op jit(solution)/shard_map/ppermute | solution.py:344
  110.7 9.5 %collective-permute-start.16 = (bf16[272,256]{1,0:T(8,128)(2,1)}, bf16[272,256]{1,0:T(8,128)(2,1)S(1)}, u32[]{:S(2)}, u32[]{:S(2)}) collective-permute-start(bf16[272,256]{1,0:T(8,128)(2,1)} %get-tuple-element.71), channel_id=1, source_target_pairs={{0,136},{8,128},{128,8},{136,0},{1,137},{9,129},{129,9},{137,1},{2... | collective-permute-start | bytes 417800 | tf_op jit(solution)/shard_map/ppermute | solution.py:344
  114.1 6.1 %collective-permute-start.17 = (bf16[272,256]{1,0:T(8,128)(2,1)}, bf16[272,256]{1,0:T(8,128)(2,1)S(1)}, u32[]{:S(2)}, u32[]{:S(2)}) collective-permute-start(bf16[272,256]{1,0:T(8,128)(2,1)} %get-tuple-element.72), channel_id=1, source_target_pairs={{0,8},{8,0},{128,136},{136,128},{1,9},{9,1},{129,137},{137,129},{2... | collective-permute-start | bytes 417800 | tf_op jit(solution)/shard_map/ppermute | solution.py:344
  123.4 22.2 %copy-start.26 = (f32[64]{0:T(128)S(1)}, f32[64]{0:T(128)}, u32[]{:S(2)}) copy-start(f32[64]{0:T(128)} %param.24) | copy-start | bytes 772
  123.4 16.2 %all-to-all-start.2 = ((bf16[8,2,144,128]{3,2,1,0:T(8,128)(2,1)}), bf16[8,2,144,128]{3,2,1,0:T(8,128)(2,1)S(1)}, u32[]{:S(2)}, u32[]{:S(2)}) async-start(bf16[8,2,144,128]{3,2,1,0:T(8,128)(2,1)} %merge_heads.1), calls=%async_computation.2 | async-start | bytes 1179648 | tf_op jit(solution)/shard_map/all_to_all | solution.py:345
  139.8 6.5 %collective-permute-start.18 = (bf16[144,128]{1,0:T(8,128)(2,1)S(1)}, bf16[144,128]{1,0:T(8,128)(2,1)S(1)}, u32[]{:S(2)}, u32[]{:S(2)}) collective-permute-start(bf16[144,128]{1,0:T(8,128)(2,1)S(1)} %get-tuple-element.84), channel_id=1, source_target_pairs={{0,8},{8,16},{16,24},{24,32},{32,40},{40,48},{48,56},{56,64},{64,7... | collective-permute-start | bytes 110600 | tf_op jit(solution)/shard_map/ppermute | solution.py:347
  141.8 5.3 %collective-permute-start.19 = (bf16[144,128]{1,0:T(8,128)(2,1)S(1)}, bf16[144,128]{1,0:T(8,128)(2,1)S(1)}, u32[]{:S(2)}, u32[]{:S(2)}) collective-permute-start(bf16[144,128]{1,0:T(8,128)(2,1)S(1)} %get-tuple-element.83), channel_id=1, source_target_pairs={{8,0},{16,8},{24,16},{32,24},{40,32},{48,40},{56,48},{64,56},{72,6... | collective-permute-start | bytes 110600 | tf_op jit(solution)/shard_map/ppermute | solution.py:348
  (17 other events, 45.3 us)

commit v3 on v2

--- a/solution.py
+++ b/solution.py
@@ -8,10 +8,10 @@
 from jax.experimental.pallas import tpu as pltpu
 from jax.sharding import Mesh, PartitionSpec as P
 
+
 D = 2048
 HD = 128
 C = 64
-R = 4
 BAND = ("xh", "z", "core")
 VAR = ("y", "xl")
 PLANE = ("xh", "core", "y", "xl")
@@ -43,52 +43,59 @@
             stat_in, acc_in = rest[0], rest[1]
             rest = rest[2:]
         for block in range(blocks):
-            cols = slice(block * 256, (block + 1) * 256)
-            stat_rows = []
-            lse_rows = []
-            for h in range(2):
-                head = slice(h * HD, (h + 1) * HD)
-                vals = slice(256 + h * HD, 256 + (h + 1) * HD)
-                q = q_refs[block][:, head]
-                scores = [dot_nt(kv[:, head], q) * SCORE_SCALE for kv in kv_refs]
-                top = jnp.max(scores[0], axis=0, keepdims=True)
-                for s in scores[1:]:
-                    top = jnp.maximum(top, jnp.max(s, axis=0, keepdims=True))
-                if not first:
-                    old_top = stat_in[h : h + 1, cols]
-                    top = jnp.maximum(top, old_top)
-                    shrink = jnp.exp2(old_top - top)
-                total = None
-                update = None
-                for s, kv in zip(scores, kv_refs):
-                    w = jnp.exp2(s - top)
-                    part = jnp.sum(w, axis=0, keepdims=True)
-                    prod = dot_tn(kv[:, vals], w.astype(BF))
-                    total = part if total is None else total + part
-                    update = prod if update is None else update + prod
-                if not first:
-                    total = total + stat_in[2 + h : 3 + h, cols] * shrink
-                    update = update + acc_in[head, cols] * shrink
+            for part in range(2):
+                inner = slice(part * 128, (part + 1) * 128)
+                cols = slice(block * 256 + part * 128, block * 256 + (part + 1) * 128)
+                stats = []
+                for h in range(2):
+                    head = slice(h * HD, (h + 1) * HD)
+                    vals = slice(256 + h * HD, 256 + (h + 1) * HD)
+                    q = q_refs[block][inner, head]
+                    state = None
+                    if not first:
+                        state = (
+                            stat_in[h : h + 1, cols],
+                            stat_in[2 + h : 3 + h, cols],
+                            acc_in[head, cols],
+                        )
+                    for kv in kv_refs:
+                        s = dot_nt(kv[:, head], q) * SCORE_SCALE
+                        top = jnp.max(s, axis=0, keepdims=True)
+                        if state is not None:
+                            top = jnp.maximum(top, state[0])
+                        w = jnp.exp2(s - top)
+                        total = jnp.sum(w, axis=0, keepdims=True)
+                        update = dot_tn(kv[:, vals], w.astype(BF))
+                        if state is not None:
+                            shrink = jnp.exp2(state[0] - top)
+                            total = total + state[1] * shrink
+                            update = update + state[2] * shrink
+                        state = (top, total, update)
+                    top, total, update = state
+                    if last:
+                        rest[block][head, inner] = (update / total).astype(BF)
+                        lse = top + jnp.log2(total)
+                        high = lse.astype(BF)
+                        left = lse - high.astype(F32)
+                        mid = left.astype(BF)
+                        low = (left - mid.astype(F32)).astype(BF)
+                        stats += [high.astype(F32), mid.astype(F32), low.astype(F32)]
+                    else:
+                        rest[1][head, cols] = update
+                        stats += [top, total]
                 if last:
-                    rest[block][head, :] = (update / total).astype(BF)
-                    lse = top + jnp.log2(total)
-                    high = lse.astype(BF)
-                    left = lse - high.astype(F32)
-                    mid = left.astype(BF)
-                    low = (left - mid.astype(F32)).astype(BF)
-                    lse_rows += [high.astype(F32), mid.astype(F32), low.astype(F32)]
+                    stats.append(jnp.zeros((10, 128), F32))
+                    rest[block][256:272, inner] = jnp.concatenate(stats, axis=0).astype(BF)
                 else:
-                    rest[1][head, cols] = update
-                    stat_rows.append((top, total))
-            if last:
-                lse_rows.append(jnp.zeros((10, 256), F32))
-                rest[block][256:272, :] = jnp.concatenate(lse_rows, axis=0).astype(BF)
-            else:
-                for h in range(2):
-                    rest[0][h : h + 1, cols] = stat_rows[h][0]
-                    rest[0][2 + h : 3 + h, cols] = stat_rows[h][1]
+                    for h in range(2):
+                        rest[0][h : h + 1, cols] = stats[2 * h]
+                        rest[0][2 + h : 3 + h, cols] = stats[2 * h + 1]
 
     return body
+
+
+def near(x):
+    return pltpu.with_memory_space_constraint(x, pltpu.VMEM)
 
 
 def flash_step(queries, chunks, carry, last):
@@ -96,19 +103,20 @@
     first = carry is None
     ins = list(queries) + list(chunks) + ([] if first else list(carry))
     if last:
-        outs = [jax.ShapeDtypeStruct((272, 256), BF)] * blocks
+        outs = [pltpu.VMEM((272, 256), BF)] * blocks
     else:
         outs = [
-            jax.ShapeDtypeStruct((8, 256 * blocks), F32),
-            jax.ShapeDtypeStruct((256, 256 * blocks), F32),
+            pltpu.VMEM((8, 256 * blocks), F32),
+            pltpu.VMEM((256, 256 * blocks), F32),
         ]
     return pl.pallas_call(
         flash_kernel(blocks, len(chunks), first, last),
         out_shape=outs,
         in_specs=[VMEM_SPEC] * len(ins),
         out_specs=[VMEM_SPEC] * len(outs),
+        compiler_params=pltpu.CompilerParams(vmem_limit_bytes=12 * 2**20),
         name="flash_last" if last else "flash_step",
-    )(*ins)
+    )(*[near(x) for x in ins])
 
 
 def merge_body(b0, b1, b2, b3, mat, out):
@@ -142,11 +150,12 @@
 def merge(parts, mat):
     return pl.pallas_call(
         merge_body,
-        out_shape=jax.ShapeDtypeStruct((8, 2, 144, 128), BF),
+        out_shape=pltpu.VMEM((8, 2, 144, 128), BF),
         in_specs=[VMEM_SPEC] * 5,
         out_specs=VMEM_SPEC,
+        compiler_params=pltpu.CompilerParams(vmem_limit_bytes=12 * 2**20),
         name="merge_heads",
-    )(*parts, mat)
+    )(*[near(x) for x in parts], near(mat))
 
 
 def spread_matrix():
@@ -251,12 +260,13 @@
         out_shape=[
             jax.ShapeDtypeStruct((4, 64, 128), BF),
             jax.ShapeDtypeStruct((4, 64, 128), BF),
-            jax.ShapeDtypeStruct((768, 128), BF),
+            pltpu.VMEM((768, 128), BF),
         ],
         in_specs=[SMEM_SPEC] + [VMEM_SPEC] * 8,
         out_specs=[VMEM_SPEC] * 3,
+        compiler_params=pltpu.CompilerParams(vmem_limit_bytes=20 * 2**20),
         name="fine_stage",
-    )(flags, own, prev, nxt, spread, grad, rim, mats, bias)
+    )(flags, *[near(x) for x in (own, prev, nxt, spread, grad, rim, mats, bias)])
 
 
 def copies(piece, axis, count):
@@ -279,22 +289,22 @@
     return jnp.transpose(weight[::-1], (0, 2, 1))
 
 
-def on_device(
+def device_step(
     patches, w_embed, var_bias, agg_gain, wq, wk, wv, wo, w_up, conv1, bias1, conv2, cotangent
 ):
-    flattened = jnp.transpose(patches, (1, 2, 0, 3)).reshape(256, 128)
-    partial_mix = jnp.dot(flattened, w_embed.reshape(128, D), preferred_element_type=F32)
-    partial_mix = (partial_mix + jnp.sum(var_bias, axis=0)).astype(BF).reshape(8, 32, D)
-    mixed = jnp.sum(lax.all_to_all(partial_mix, VAR, 0, 0).astype(F32), axis=0)
-    normed_slab = (
-        mixed * lax.rsqrt(jnp.mean(mixed * mixed, axis=-1, keepdims=True) + 1e-05) * agg_gain
-    ).astype(BF)
-    cells, normed_slab = lax.optimization_barrier((cotangent, normed_slab))
-    normed = copies(normed_slab, VAR, 8).reshape(256, D)
     var_at = lax.axis_index(VAR)
     band_at = lax.axis_index(BAND)
     shift_down = [(i, i + 1) for i in range(31)]
     shift_up = [(i + 1, i) for i in range(31)]
+    group = ("xh", "core")
+
+    flattened = jnp.transpose(patches, (1, 2, 0, 3)).reshape(256, 128)
+    partial_mix = jnp.dot(flattened, w_embed.reshape(128, D), preferred_element_type=F32)
+    partial_mix = (partial_mix + jnp.sum(var_bias, axis=0)).astype(BF).reshape(8, 32, D)
+    partial_mix, cells, wo, wk, wv = lax.optimization_barrier((partial_mix, cotangent, wo, wk, wv))
+    pieces = lax.all_to_all(partial_mix, VAR, 0, 0)
+    up_mat = jnp.dot(wo, w_up, preferred_element_type=F32).astype(BF)
+    wkv = jnp.concatenate([wk, wv], axis=1)
     grad_rows = jnp.concatenate(
         [
             lax.ppermute(cells[2:4], BAND, shift_down),
@@ -303,18 +313,29 @@
         ],
         axis=0,
     )
+    pieces, up_mat, wkv, grad_rows = lax.optimization_barrier((pieces, up_mat, wkv, grad_rows))
+    mixed = jnp.sum(pieces.astype(F32), axis=0)
+    normed_slab = (
+        mixed * lax.rsqrt(jnp.mean(mixed * mixed, axis=-1, keepdims=True) + 1e-05) * agg_gain
+    ).astype(BF)
+    normed_slab, grad_rows, conv1, conv2, bias1 = lax.optimization_barrier(
+        (normed_slab, grad_rows, conv1, conv2, bias1)
+    )
+    normed = copies(normed_slab, VAR, 8).reshape(256, D)
     from_right = lax.ppermute(grad_rows[:, :, 0:2], VAR, [(i + 1, i) for i in range(7)])
     from_left = lax.ppermute(grad_rows[:, :, 126:128], VAR, [(i, i + 1) for i in range(7)])
     rim = jnp.concatenate([from_right, jnp.zeros((8, C, 124), BF), from_left], axis=2)
-    normed, rim = lax.optimization_barrier((normed, rim))
-
-    group = ("xh", "core")
+    mats = jnp.stack(
+        [tap_matrix(conv1), tap_matrix(flipped(conv2)), tap_matrix(conv2), tap_matrix(flipped(conv1))]
+    )
+    bias = bias1.reshape(C, 1)
+    flags = jnp.stack([band_at > 0, band_at < 31, var_at > 0, var_at < 7]).astype(jnp.int32)
+    normed, rim, mats, bias, flags = lax.optimization_barrier((normed, rim, mats, bias, flags))
+
     queries = jnp.dot(normed, wq, preferred_element_type=F32).astype(BF)
     all_queries = [queries] + [lax.ppermute(queries, group, flip(4, k)) for k in (2, 3, 1)]
     keys_in, queries = lax.optimization_barrier((normed, queries))
-    keys = jnp.dot(keys_in, wk, preferred_element_type=F32).astype(BF)
-    values = jnp.dot(keys_in, wv, preferred_element_type=F32).astype(BF)
-    keyvals = jnp.concatenate([keys, values], axis=1)
+    keyvals = jnp.dot(keys_in, wkv, preferred_element_type=F32).astype(BF)
     ahead, behind = keyvals, keyvals
     carry = None
     fresh = [keyvals]
@@ -327,7 +348,6 @@
         ahead, behind, carry = lax.optimization_barrier((ahead, behind, carry))
         fresh = [ahead, behind]
 
-    up_mat = jnp.dot(wo, w_up, preferred_element_type=F32).astype(BF)
     padded = jnp.pad(normed, ((1, 1), (0, 0)))
     around = lax.dynamic_slice_in_dim(padded, var_at * 32, 34, 0)
     base = jnp.dot(around, w_up, preferred_element_type=F32)
@@ -336,9 +356,6 @@
     right = base[33].reshape(2, 4, 128)
     base_rim = jnp.where(jnp.arange(4)[None, :, None] % 2 == 0, right, left)
     base_all = jnp.concatenate([base_main, base_rim, jnp.zeros((2, 12, 128), F32)], axis=1)
-    mats = jnp.stack(
-        [tap_matrix(conv1), tap_matrix(flipped(conv2)), tap_matrix(conv2), tap_matrix(flipped(conv1))]
-    )
 
     blocks = flash_step(all_queries, fresh, carry, True)
     parts = [blocks[0]] + [lax.ppermute(b, group, flip(4, k)) for b, k in zip(blocks[1:], (2, 3, 1))]
@@ -346,11 +363,10 @@
     up = (jnp.sum(pieces.astype(F32), axis=0) + base_all).astype(BF)
     prev = lax.ppermute(up[1], BAND, shift_down)
     nxt = lax.ppermute(up[0], BAND, shift_up)
-    flags = jnp.stack([band_at > 0, band_at < 31, var_at > 0, var_at < 7]).astype(jnp.int32)
     factor = 1.0 / math.sqrt(128 * 1024)
     spread = jnp.asarray(spread_matrix(), BF)
     field_out, grad_fine, terms = fine_stage(
-        flags, up, prev, nxt, spread, grad_rows, rim, mats, bias1.reshape(C, 1), factor
+        flags, up, prev, nxt, spread, grad_rows, rim, mats, bias, factor
     )
     shares = lax.all_to_all(terms.reshape(32, 24, 128), PLANE, 0, 0)
     share = jnp.sum(shares.astype(F32), axis=0).astype(BF)
@@ -380,5 +396,5 @@
     )
     out_specs = (P(BAND, None, VAR), P(BAND, None, VAR), P(), P(), P())
     return jax.shard_map(
-        on_device, mesh=fine_mesh, in_specs=in_specs, out_specs=out_specs, check_vma=False
-    )
+        device_step, mesh=fine_mesh, in_specs=in_specs, out_specs=out_specs, check_vma=False
+    )

time: 196 us -> 182 us (0.929)
  blocking collectives: 62.8 us -> 43 us
  Pallas kernels: 31.3 us -> 17.5 us
  starting transfers between devices: 51 us -> 64.7 us
  waiting for transfers between devices: 24.9 us -> 32.7 us
  local copies, waits for them, and re-layouts: 8.37 us -> 5.09 us
    all_to_all x2 -> x1, blocking collectives: 38.8 us -> 20.3 us  [device_step(): shares = lax.all_to_all(terms.reshape(32, 24, 128), PLANE, 0, 0)]
    pallas_call x5, Pallas kernels: 25.1 us -> 13.8 us  [flash_step(): pl.pallas_call(flash_kernel(blocks, len(chunks), first, last), out_shape=...]
    all_to_all x1 -> x2, starting transfers between devices: 6.39 us -> 13 us  [the longest x1 7.08 us: device_step(): pieces = lax.all_to_all(merge(parts, up_mat), VAR, 0, 0)]
    ppermute x20, starting transfers between devices: 41 us -> 47.5 us  [the longest x4 13 us: device_step(): behind = lax.ppermute(behind, 'z', turn(8, -1))]
    ppermute x20, waiting for transfers between devices: 18.4 us -> 22.8 us  [the longest x4 5.89 us: device_step(): ahead = lax.ppermute(ahead, 'z', turn(8, 1))]
    all_to_all x1 -> x2, waiting for transfers between devices: 6.55 us -> 9.86 us  [the longest x1 6.49 us: device_step(): pieces = lax.all_to_all(merge(parts, up_mat), VAR, 0, 0)]
    unnamed x56 -> x22, local copies, waits for them, and re-layouts: 3.41 us -> 0.14 us
    dot_general x6 -> x5, matrix products: 11.4 us -> 12.9 us  [the longest x1 3.44 us: device_step(): up_mat = jnp.dot(wo, w_up, preferred_element_type=F32).astype(BF)]
  transfers between devices with their start and end apart: 22 -> 23, of which waited for: 9 -> 10; matrix products, arithmetic and copies ran while one was open for 6% -> 6% of each run, Pallas kernels for 11% -> 4%
where the time goes in v3:
time: 182 us; the launch traced here: 181 us
  starting transfers between devices  64.7 us (36%)
  blocking collectives  43 us (24%)
  waiting for transfers between devices  32.7 us (18%)
  Pallas kernels  17.5 us (10%)
  matrix products  12.9 us (7%)
  local copies, waits for them, and re-layouts  5.09 us (3%)
  other arithmetic  4.28 us (2%)
    all_to_all x2, blocking collectives, copies(): lax.all_to_all(jnp.broadcast_to(piece[None], (count,) + piece.shape), axi...  22.7 us
    all_to_all x1, blocking collectives, device_step(): shares = lax.all_to_all(terms.reshape(32, 24, 128), PLANE, 0, 0)  20.3 us
    pallas_call x5, Pallas kernels, flash_step(): pl.pallas_call(flash_kernel(blocks, len(chunks), first, last), out_shape=...  13.8 us
    ppermute x4, starting transfers between devices, device_step(): behind = lax.ppermute(behind, 'z', turn(8, -1))  13 us
    ppermute x3, starting transfers between devices, device_step(): lax.ppermute(b, group, flip(4, k))  7.68 us
    ppermute x3, starting transfers between devices, device_step(): lax.ppermute(queries, group, flip(4, k))  7.36 us
    all_to_all x1, starting transfers between devices, device_step(): pieces = lax.all_to_all(merge(parts, up_mat), VAR, 0, 0)  7.08 us
    all_to_all x1, waiting for transfers between devices, device_step(): pieces = lax.all_to_all(merge(parts, up_mat), VAR, 0, 0)  6.49 us
  transfers between devices with their start and end apart: 23, of which 10 were waited for; matrix products, arithmetic and copies ran while one was open for 6% of the time, Pallas kernels for 4%

profile of v3, /device:TPU:1, one launch (start us, length us, event | category | flops | bytes accessed | tf_op | source)
XLA Modules:
  0.0 181.3 jit_solution(18429940445998587616)
XLA Ops:
  1.5 2.5 %fusion = bf16[256,2048]{1,0:T(8,128)(2,1)} fusion(bf16[256,128]{0,1:T(8,128)(2,1)} %bitcast.67, bf16[128,2048]{1,0:T(8,128)(2,1)} %bitcast.63, f32[2048]{0:T(1024)S(1)} %reduce_sum.60), kind=kOutput, calls=%fused_computation.1 | convolution fusion | flops 135266304 | bytes 1646592 | tf_op jit(solution)/shard_map/dot_general | solution.py:302
  4.0 5.9 %all-to-all-start = ((bf16[8,32,2048]{2,1,0:T(8,128)(2,1)}), bf16[8,32,2048]{2,1,0:T(8,128)(2,1)S(1)}, u32[]{:S(2)}, u32[]{:S(2)}) async-start(bf16[8,32,2048]{2,1,0:T(8,128)(2,1)} %bitcast.54), calls=%async_computation | async-start | bytes 2097152 | tf_op jit(solution)/shard_map/all_to_all | solution.py:305
  10.0 4.4 %collective-permute-start = (bf16[2,64,128]{2,1,0:T(8,128)(2,1)S(1)}, bf16[2,64,128]{2,1,0:T(8,128)(2,1)S(1)}, u32[]{:S(2)}, u32[]{:S(2)}) collective-permute-start(bf16[2,64,128]{2,1,0:T(8,128)(2,1)S(1)} %get-tuple-element.115), channel_id=1, source_target_pairs={{0,8},{8,16},{16,24},{24,32},{32,40},{40,48},{48,56},{56,64},{64,7... | collective-permute-start | bytes 98312 | tf_op jit(solution)/shard_map/ppermute | solution.py:310
  14.4 2.1 %collective-permute-start.1 = (bf16[2,64,128]{2,1,0:T(8,128)(2,1)S(1)}, bf16[2,64,128]{2,1,0:T(8,128)(2,1)S(1)}, u32[]{:S(2)}, u32[]{:S(2)}) collective-permute-start(bf16[2,64,128]{2,1,0:T(8,128)(2,1)S(1)} %get-tuple-element.116), channel_id=1, source_target_pairs={{8,0},{16,8},{24,16},{32,24},{40,32},{48,40},{56,48},{64,56},{72,6... | collective-permute-start | bytes 98312 | tf_op jit(solution)/shard_map/ppermute | solution.py:312
  16.5 3.4 %convolution_convert_fusion.mat = bf16[256,1024]{1,0:T(8,128)(2,1)S(1)} fusion(bf16[256,2048]{1,0:T(8,128)(2,1)S(1)} %copy-done, bf16[2048,1024]{1,0:T(8,128)(2,1)} %param.22), kind=kOutput, calls=%fused_computation.4 | convolution fusion | flops 1074003968 | bytes 5767168 | tf_op jit(solution)/shard_map/dot_general | solution.py:306
  21.5 3.4 %all-to-all-done = bf16[8,32,2048]{2,1,0:T(8,128)(2,1)S(1)} async-done(((bf16[8,32,2048]{2,1,0:T(8,128)(2,1)}), bf16[8,32,2048]{2,1,0:T(8,128)(2,1)S(1)}, u32[]{:S(2)}, u32[]{:S(2)}) %all-to-all-start) | async-done | bytes 1048608 | tf_op jit(solution)/shard_map/all_to_all | solution.py:305
  26.4 4.2 %all-to-all-start.1 = ((bf16[8,32,2048]{2,1,0:T(8,128)(2,1)}), bf16[8,32,2048]{2,1,0:T(8,128)(2,1)}, u32[]{:S(2)}, u32[]{:S(2)}) async-start(bf16[8,32,2048]{2,1,0:T(8,128)(2,1)} %broadcast_in_dim.18), calls=%async_computation.1 | async-start | bytes 2097152 | tf_op jit(solution)/shard_map/all_to_all | solution.py:273
  34.2 4.0 %collective-permute-start.3 = (bf16[8,64,2]{2,1,0:T(8,128)(2,1)S(1)}, bf16[8,64,2]{2,1,0:T(8,128)(2,1)S(1)}, u32[]{:S(2)}, u32[]{:S(2)}) collective-permute-start(bf16[8,64,2]{2,1,0:T(8,128)(2,1)S(1)} %get-tuple-element.112), channel_id=1, source_target_pairs={{0,1},{1,2},{2,3},{3,4},{4,5},{5,6},{6,7},{8,9},{9,10},{10,11},{11... | collective-permute-start | bytes 6152 | tf_op jit(solution)/shard_map/ppermute | solution.py:326
  39.2 5.9 %collective-permute-done.2 = bf16[8,64,2]{2,1,0:T(8,128)(2,1)S(1)} collective-permute-done((bf16[8,64,2]{2,1,0:T(8,128)(2,1)S(1)}, bf16[8,64,2]{2,1,0:T(8,128)(2,1)S(1)}, u32[]{:S(2)}, u32[]{:S(2)}) %collective-permute-start.2) | collective-permute-done | bytes 2080 | tf_op jit(solution)/shard_map/ppermute | solution.py:325
  49.1 5.3 %collective-permute-start.8 = (bf16[256,512]{1,0:T(8,128)(2,1)S(1)}, bf16[256,512]{1,0:T(8,128)(2,1)S(1)}, u32[]{:S(2)}, u32[]{:S(2)}) collective-permute-start(bf16[256,512]{1,0:T(8,128)(2,1)S(1)} %convolution_convert_fusion.1.refs_4_), channel_id=1, source_target_pairs={{0,112},{16,0},{32,16},{48,32},{64,48},{80,64},{96,80},{112,96},{1... | collective-permute-start | bytes 786440 | tf_op jit(solution)/shard_map/ppermute | solution.py:346
  54.4 4.5 %collective-permute-start.6 = (bf16[256,256]{1,0:T(8,128)(2,1)S(1)}, bf16[256,256]{1,0:T(8,128)(2,1)S(1)}, u32[]{:S(2)}, u32[]{:S(2)}) collective-permute-start(bf16[256,256]{1,0:T(8,128)(2,1)S(1)} %convolution_convert_fusion.2.refs_0_), channel_id=1, source_target_pairs={{0,8},{8,0},{128,136},{136,128},{1,9},{9,1},{129,137},{137,129},{2... | collective-permute-start | bytes 393224 | tf_op jit(solution)/shard_map/ppermute | solution.py:336
  58.9 2.7 %collective-permute-start.5 = (bf16[256,256]{1,0:T(8,128)(2,1)S(1)}, bf16[256,256]{1,0:T(8,128)(2,1)S(1)}, u32[]{:S(2)}, u32[]{:S(2)}) collective-permute-start(bf16[256,256]{1,0:T(8,128)(2,1)S(1)} %convolution_convert_fusion.2.refs_0_), channel_id=1, source_target_pairs={{0,136},{8,128},{128,8},{136,0},{1,137},{9,129},{129,9},{137,1},{2... | collective-permute-start | bytes 393224 | tf_op jit(solution)/shard_map/ppermute | solution.py:336
  61.7 3.8 %collective-permute-done.5.refs_2_ = bf16[256,256]{1,0:T(8,128)(2,1)S(1)} collective-permute-done((bf16[256,256]{1,0:T(8,128)(2,1)S(1)}, bf16[256,256]{1,0:T(8,128)(2,1)S(1)}, u32[]{:S(2)}, u32[]{:S(2)}) %collective-permute-start.5) | collective-permute-done | bytes 131104 | tf_op jit(solution)/shard_map/ppermute | solution.py:336
  65.5 2.1 %collective-permute-done.4.refs_1_ = bf16[256,256]{1,0:T(8,128)(2,1)S(1)} collective-permute-done((bf16[256,256]{1,0:T(8,128)(2,1)S(1)}, bf16[256,256]{1,0:T(8,128)(2,1)S(1)}, u32[]{:S(2)}, u32[]{:S(2)}) %collective-permute-start.4) | collective-permute-done | bytes 131104 | tf_op jit(solution)/shard_map/ppermute | solution.py:336
  68.9 3.2 %collective-permute-start.10 = (bf16[256,512]{1,0:T(8,128)(2,1)S(1)}, bf16[256,512]{1,0:T(8,128)(2,1)S(1)}, u32[]{:S(2)}, u32[]{:S(2)}) collective-permute-start(bf16[256,512]{1,0:T(8,128)(2,1)S(1)} %collective-permute-done.8.refs_5_), channel_id=1, source_target_pairs={{0,112},{16,0},{32,16},{48,32},{64,48},{80,64},{96,80},{112,96},{1... | collective-permute-start | bytes 786440 | tf_op jit(solution)/shard_map/ppermute | solution.py:346
  72.1 2.0 %flash_step.5 = (f32[8,1024]{1,0:T(8,128)S(1)}, f32[256,1024]{1,0:T(8,128)S(1)}) custom-call(bf16[256,256]{1,0:T(8,128)(2,1)S(1)} %convolution_convert_fusion.2.refs_0_, bf16[256,256]{1,0:T(8,128)(2,1)S(1)} %collective-permute-done.4.refs_1_, bf16[256,256]{1,0:T(8,128)(2,1)S(1)} %collective-permute-done.5.refs_2_, ...), custom_call_target="tpu_custom_call" | custom-call | tf_op jit(solution)/shard_map/flash_step/pallas_call | solution.py:112
  74.1 3.1 %collective-permute-done.9.refs_4_ = bf16[256,512]{1,0:T(8,128)(2,1)S(1)} collective-permute-done((bf16[256,512]{1,0:T(8,128)(2,1)S(1)}, bf16[256,512]{1,0:T(8,128)(2,1)S(1)}, u32[]{:S(2)}, u32[]{:S(2)}) %collective-permute-start.9) | collective-permute-done | bytes 262176 | tf_op jit(solution)/shard_map/ppermute | solution.py:345
  77.2 2.7 %collective-permute-start.12 = (bf16[256,512]{1,0:T(8,128)(2,1)S(1)}, bf16[256,512]{1,0:T(8,128)(2,1)S(1)}, u32[]{:S(2)}, u32[]{:S(2)}) collective-permute-start(bf16[256,512]{1,0:T(8,128)(2,1)S(1)} %collective-permute-done.10.refs_5_), channel_id=1, source_target_pairs={{0,112},{16,0},{32,16},{48,32},{64,48},{80,64},{96,80},{112,96},{1... | collective-permute-start | bytes 786440 | tf_op jit(solution)/shard_map/ppermute | solution.py:346
  81.8 2.5 %collective-permute-done.11.refs_4_ = bf16[256,512]{1,0:T(8,128)(2,1)S(1)} collective-permute-done((bf16[256,512]{1,0:T(8,128)(2,1)S(1)}, bf16[256,512]{1,0:T(8,128)(2,1)S(1)}, u32[]{:S(2)}, u32[]{:S(2)}) %collective-permute-start.11) | collective-permute-done | bytes 262176 | tf_op jit(solution)/shard_map/ppermute | solution.py:345
  89.4 6.7 %flash_last.1 = (bf16[272,256]{1,0:T(8,128)(2,1)S(1)}, bf16[272,256]{1,0:T(8,128)(2,1)S(1)}, bf16[272,256]{1,0:T(8,128)(2,1)S(1)}, bf16[272,256]{1,0:T(8,128)(2,1)S(1)}) custom-call(bf16[256,256]{1,0:T(8,128)(2,1)S(1)} %convolution_convert_fusion.2.refs_0_, bf16[256,256]{1,0:T(8,128)(2,1)S(1)} %collective-permute-done.4.refs_1_, ...), custom_call_target="tpu_custom_call" | custom-call | tf_op jit(solution)/shard_map/flash_last/pallas_call | solution.py:112
  96.1 3.7 %collective-permute-start.15 = (bf16[272,256]{1,0:T(8,128)(2,1)S(1)}, bf16[272,256]{1,0:T(8,128)(2,1)S(1)}, u32[]{:S(2)}, u32[]{:S(2)}) collective-permute-start(bf16[272,256]{1,0:T(8,128)(2,1)S(1)} %get-tuple-element.97), channel_id=1, source_target_pairs={{0,128},{8,136},{128,0},{136,8},{1,129},{9,137},{129,1},{137,9},{2... | collective-permute-start | bytes 417800 | tf_op jit(solution)/shard_map/ppermute | solution.py:361
  99.8 3.6 %collective-permute-start.16 = (bf16[272,256]{1,0:T(8,128)(2,1)S(1)}, bf16[272,256]{1,0:T(8,128)(2,1)S(1)}, u32[]{:S(2)}, u32[]{:S(2)}) collective-permute-start(bf16[272,256]{1,0:T(8,128)(2,1)S(1)} %get-tuple-element.98), channel_id=1, source_target_pairs={{0,136},{8,128},{128,8},{136,0},{1,137},{9,129},{129,9},{137,1},{2... | collective-permute-start | bytes 417800 | tf_op jit(solution)/shard_map/ppermute | solution.py:361
  103.9 4.2 %collective-permute-done.16.b2 = bf16[272,256]{1,0:T(8,128)(2,1)S(1)} collective-permute-done((bf16[272,256]{1,0:T(8,128)(2,1)S(1)}, bf16[272,256]{1,0:T(8,128)(2,1)S(1)}, u32[]{:S(2)}, u32[]{:S(2)}) %collective-permute-start.16) | collective-permute-done | bytes 139296 | tf_op jit(solution)/shard_map/ppermute | solution.py:361
  109.3 7.1 %all-to-all-start.2 = ((bf16[8,2,144,128]{3,2,1,0:T(8,128)(2,1)}), bf16[8,2,144,128]{3,2,1,0:T(8,128)(2,1)S(1)}, u32[]{:S(2)}, u32[]{:S(2)}) async-start(bf16[8,2,144,128]{3,2,1,0:T(8,128)(2,1)} %merge_heads.1), calls=%async_computation.2 | async-start | bytes 1179648 | tf_op jit(solution)/shard_map/all_to_all | solution.py:362
  116.4 3.1 %fusion.1 = f32[34,1024]{1,0:T(8,128)S(1)} fusion(bf16[2048,1024]{1,0:T(8,128)(2,1)} %param.22, s32[]{:T(128)S(6)} %select_n.19, bf16[256,2048]{1,0:T(8,128)(2,1)} %bitcast.4), kind=kOutput, calls=%fused_computation.15 | convolution fusion | flops 142606336 | bytes 5382148 | tf_op jit(solution)/shard_map/dot_general | solution.py:353
  119.8 6.5 %all-to-all-done.2 = bf16[8,2,144,128]{3,2,1,0:T(8,128)(2,1)S(1)} async-done(((bf16[8,2,144,128]{3,2,1,0:T(8,128)(2,1)}), bf16[8,2,144,128]{3,2,1,0:T(8,128)(2,1)S(1)}, u32[]{:S(2)}, u32[]{:S(2)}) %all-to-all-start.2) | async-done | bytes 589856 | tf_op jit(solution)/shard_map/all_to_all | solution.py:362
  126.5 3.8 %collective-permute-start.19 = (bf16[144,128]{1,0:T(8,128)(2,1)S(1)}, bf16[144,128]{1,0:T(8,128)(2,1)S(1)}, u32[]{:S(2)}, u32[]{:S(2)}) collective-permute-start(bf16[144,128]{1,0:T(8,128)(2,1)S(1)} %get-tuple-element.113), channel_id=1, source_target_pairs={{8,0},{16,8},{24,16},{32,24},{40,32},{48,40},{56,48},{64,56},{72,6... | collective-permute-start | bytes 110600 | tf_op jit(solution)/shard_map/ppermute | solution.py:365
  130.2 2.9 %collective-permute-start.18 = (bf16[144,128]{1,0:T(8,128)(2,1)S(1)}, bf16[144,128]{1,0:T(8,128)(2,1)S(1)}, u32[]{:S(2)}, u32[]{:S(2)}) collective-permute-start(bf16[144,128]{1,0:T(8,128)(2,1)S(1)} %get-tuple-element.114), channel_id=1, source_target_pairs={{0,8},{8,16},{16,24},{24,32},{32,40},{40,48},{48,56},{56,64},{64,7... | collective-permute-start | bytes 110600 | tf_op jit(solution)/shard_map/ppermute | solution.py:364
  134.2 2.5 %fine_stage.1 = (bf16[4,64,128]{2,1,0:T(8,128)(2,1)}, bf16[4,64,128]{2,1,0:T(8,128)(2,1)}, bf16[768,128]{1,0:T(8,128)(2,1)S(1)}) custom-call(s32[4]{0:T(128)S(1)} %add_convert_fusion.flags, bf16[2,144,128]{2,1,0:T(8,128)(2,1)S(1)} %fusion.2.own, bf16[144,128]{1,0:T(8,128)(2,1)S(1)} %collective-permute-done.18.prev, ...), custom_call_target="tpu_custom_call" | custom-call | tf_op jit(solution)/shard_map/fine_stage/pallas_call | solution.py:258
  136.7 20.3 %all_to_all.30 = bf16[32,24,128]{2,1,0:T(8,128)(2,1)S(1)} all-to-all(bf16[32,24,128]{2,1,0:T(8,128)(2,1)S(1)} %bitcast.53), channel_id=1, replica_groups=mesh['xh'=2,'z'=8,'core'=2,'y'=4,'xl'=2] {'xh','core','y','xl'}, dimensions={0} | all-to-all | bytes 393216 | tf_op jit(solution)/shard_map/all_to_all | solution.py:371
  157.1 9.4 %all_to_all.31 = bf16[8,24,128]{2,1,0:T(8,128)(2,1)S(1)} all-to-all(bf16[8,24,128]{2,1,0:T(8,128)(2,1)S(1)} %broadcast_in_dim.22), channel_id=1, replica_groups=mesh['xh'=2,'z'=8,'core'=2,'y'=4,'xl'=2] {'z'}, dimensions={0} | all-to-all | bytes 98304 | tf_op jit(solution)/shard_map/all_to_all | solution.py:273
  166.6 13.3 %all_to_all.32 = bf16[32,24,128]{2,1,0:T(8,128)(2,1)S(1)} all-to-all(bf16[32,24,128]{2,1,0:T(8,128)(2,1)S(1)} %broadcast_in_dim.23), channel_id=1, replica_groups=mesh['xh'=2,'z'=8,'core'=2,'y'=4,'xl'=2] {'xh','core','y','xl'}, dimensions={0} | all-to-all | bytes 393216 | tf_op jit(solution)/shard_map/all_to_all | solution.py:273
  (97 shorter events, 25.4 us)
Async XLA Ops:
  0.6 15.8 %copy-start = (bf16[256,2048]{1,0:T(8,128)(2,1)S(1)}, bf16[256,2048]{1,0:T(8,128)(2,1)}, u32[]{:S(2)}) copy-start(bf16[256,2048]{1,0:T(8,128)(2,1)} %param.21) | copy-start | bytes 3145732
  0.6 9.3 %copy-start.8 = (bf16[4,64,128]{2,1,0:T(8,128)(2,1)S(1)}, bf16[4,64,128]{2,1,0:T(8,128)(2,1)}, u32[]{:S(2)}) copy-start(bf16[4,64,128]{2,1,0:T(8,128)(2,1)} %param.26) | copy-start | bytes 196612
  4.0 20.8 %all-to-all-start = ((bf16[8,32,2048]{2,1,0:T(8,128)(2,1)}), bf16[8,32,2048]{2,1,0:T(8,128)(2,1)S(1)}, u32[]{:S(2)}, u32[]{:S(2)}) async-start(bf16[8,32,2048]{2,1,0:T(8,128)(2,1)} %bitcast.54), calls=%async_computation | async-start | bytes 2097152 | tf_op jit(solution)/shard_map/all_to_all | solution.py:305
  10.0 11.5 %collective-permute-start = (bf16[2,64,128]{2,1,0:T(8,128)(2,1)S(1)}, bf16[2,64,128]{2,1,0:T(8,128)(2,1)S(1)}, u32[]{:S(2)}, u32[]{:S(2)}) collective-permute-start(bf16[2,64,128]{2,1,0:T(8,128)(2,1)S(1)} %get-tuple-element.115), channel_id=1, source_target_pairs={{0,8},{8,16},{16,24},{24,32},{32,40},{40,48},{48,56},{56,64},{64,7... | collective-permute-start | bytes 98312 | tf_op jit(solution)/shard_map/ppermute | solution.py:310
  14.4 5.5 %copy-start.4 = (bf16[2048,256]{1,0:T(8,128)(2,1)S(1)}, bf16[2048,256]{1,0:T(8,128)(2,1)}, u32[]{:S(2)}) copy-start(bf16[2048,256]{1,0:T(8,128)(2,1)} %param.20) | copy-start | bytes 3145732
  14.4 5.5 %copy-start.5 = (bf16[2048,256]{1,0:T(8,128)(2,1)S(1)}, bf16[2048,256]{1,0:T(8,128)(2,1)}, u32[]{:S(2)}) copy-start(bf16[2048,256]{1,0:T(8,128)(2,1)} %param.19) | copy-start | bytes 3145732
  14.4 7.1 %collective-permute-start.1 = (bf16[2,64,128]{2,1,0:T(8,128)(2,1)S(1)}, bf16[2,64,128]{2,1,0:T(8,128)(2,1)S(1)}, u32[]{:S(2)}, u32[]{:S(2)}) collective-permute-start(bf16[2,64,128]{2,1,0:T(8,128)(2,1)S(1)} %get-tuple-element.116), channel_id=1, source_target_pairs={{8,0},{16,8},{24,16},{32,24},{40,32},{48,40},{56,48},{64,56},{72,6... | collective-permute-start | bytes 98312 | tf_op jit(solution)/shard_map/ppermute | solution.py:312
  25.0 5.8 %copy-start.7 = (bf16[9,64,64]{2,1,0:T(8,128)(2,1)S(1)}, bf16[9,64,64]{2,1,0:T(8,128)(2,1)}, u32[]{:S(2)}) copy-start(bf16[9,64,64]{2,1,0:T(8,128)(2,1)} %param.23) | copy-start | bytes 221188
  25.3 5.9 %copy-start.6 = (bf16[9,64,64]{2,1,0:T(8,128)(2,1)S(1)}, bf16[9,64,64]{2,1,0:T(8,128)(2,1)}, u32[]{:S(2)}) copy-start(bf16[9,64,64]{2,1,0:T(8,128)(2,1)} %param.25) | copy-start | bytes 221188
  26.4 18.8 %all-to-all-start.1 = ((bf16[8,32,2048]{2,1,0:T(8,128)(2,1)}), bf16[8,32,2048]{2,1,0:T(8,128)(2,1)}, u32[]{:S(2)}, u32[]{:S(2)}) async-start(bf16[8,32,2048]{2,1,0:T(8,128)(2,1)} %broadcast_in_dim.18), calls=%async_computation.1 | async-start | bytes 2097152 | tf_op jit(solution)/shard_map/all_to_all | solution.py:273
  31.0 14.3 %copy-start.3 = (bf16[2048,256]{1,0:T(8,128)(2,1)S(1)}, bf16[2048,256]{1,0:T(8,128)(2,1)}, u32[]{:S(2)}) copy-start(bf16[2048,256]{1,0:T(8,128)(2,1)} %param.18) | copy-start | bytes 3145732
  32.9 12.2 %collective-permute-start.2 = (bf16[8,64,2]{2,1,0:T(8,128)(2,1)S(1)}, bf16[8,64,2]{2,1,0:T(8,128)(2,1)S(1)}, u32[]{:S(2)}, u32[]{:S(2)}) collective-permute-start(bf16[8,64,2]{2,1,0:T(8,128)(2,1)S(1)} %get-tuple-element.111), channel_id=1, source_target_pairs={{1,0},{2,1},{3,2},{4,3},{5,4},{6,5},{7,6},{9,8},{10,9},{11,10},{12... | collective-permute-start | bytes 6152 | tf_op jit(solution)/shard_map/ppermute | solution.py:325
  34.2 10.9 %collective-permute-start.3 = (bf16[8,64,2]{2,1,0:T(8,128)(2,1)S(1)}, bf16[8,64,2]{2,1,0:T(8,128)(2,1)S(1)}, u32[]{:S(2)}, u32[]{:S(2)}) collective-permute-start(bf16[8,64,2]{2,1,0:T(8,128)(2,1)S(1)} %get-tuple-element.112), channel_id=1, source_target_pairs={{0,1},{1,2},{2,3},{3,4},{4,5},{5,6},{6,7},{8,9},{9,10},{10,11},{11... | collective-permute-start | bytes 6152 | tf_op jit(solution)/shard_map/ppermute | solution.py:326
  49.1 19.7 %collective-permute-start.8 = (bf16[256,512]{1,0:T(8,128)(2,1)S(1)}, bf16[256,512]{1,0:T(8,128)(2,1)S(1)}, u32[]{:S(2)}, u32[]{:S(2)}) collective-permute-start(bf16[256,512]{1,0:T(8,128)(2,1)S(1)} %convolution_convert_fusion.1.refs_4_), channel_id=1, source_target_pairs={{0,112},{16,0},{32,16},{48,32},{64,48},{80,64},{96,80},{112,96},{1... | collective-permute-start | bytes 786440 | tf_op jit(solution)/shard_map/ppermute | solution.py:346
  54.4 14.4 %collective-permute-start.7 = (bf16[256,512]{1,0:T(8,128)(2,1)S(1)}, bf16[256,512]{1,0:T(8,128)(2,1)S(1)}, u32[]{:S(2)}, u32[]{:S(2)}) collective-permute-start(bf16[256,512]{1,0:T(8,128)(2,1)S(1)} %convolution_convert_fusion.1.refs_4_), channel_id=1, source_target_pairs={{0,16},{16,32},{32,48},{48,64},{64,80},{80,96},{96,112},{112,0},{1... | collective-permute-start | bytes 786440 | tf_op jit(solution)/shard_map/ppermute | solution.py:345
  54.4 7.4 %collective-permute-start.6 = (bf16[256,256]{1,0:T(8,128)(2,1)S(1)}, bf16[256,256]{1,0:T(8,128)(2,1)S(1)}, u32[]{:S(2)}, u32[]{:S(2)}) collective-permute-start(bf16[256,256]{1,0:T(8,128)(2,1)S(1)} %convolution_convert_fusion.2.refs_0_), channel_id=1, source_target_pairs={{0,8},{8,0},{128,136},{136,128},{1,9},{9,1},{129,137},{137,129},{2... | collective-permute-start | bytes 393224 | tf_op jit(solution)/shard_map/ppermute | solution.py:336
  58.9 6.6 %collective-permute-start.5 = (bf16[256,256]{1,0:T(8,128)(2,1)S(1)}, bf16[256,256]{1,0:T(8,128)(2,1)S(1)}, u32[]{:S(2)}, u32[]{:S(2)}) collective-permute-start(bf16[256,256]{1,0:T(8,128)(2,1)S(1)} %convolution_convert_fusion.2.refs_0_), channel_id=1, source_target_pairs={{0,136},{8,128},{128,8},{136,0},{1,137},{9,129},{129,9},{137,1},{2... | collective-permute-start | bytes 393224 | tf_op jit(solution)/shard_map/ppermute | solution.py:336
  61.6 6.1 %collective-permute-start.4 = (bf16[256,256]{1,0:T(8,128)(2,1)S(1)}, bf16[256,256]{1,0:T(8,128)(2,1)S(1)}, u32[]{:S(2)}, u32[]{:S(2)}) collective-permute-start(bf16[256,256]{1,0:T(8,128)(2,1)S(1)} %convolution_convert_fusion.2.refs_0_), channel_id=1, source_target_pairs={{0,128},{8,136},{128,0},{136,8},{1,129},{9,137},{129,1},{137,9},{2... | collective-permute-start | bytes 393224 | tf_op jit(solution)/shard_map/ppermute | solution.py:336
  68.8 8.3 %collective-permute-start.9 = (bf16[256,512]{1,0:T(8,128)(2,1)S(1)}, bf16[256,512]{1,0:T(8,128)(2,1)S(1)}, u32[]{:S(2)}, u32[]{:S(2)}) collective-permute-start(bf16[256,512]{1,0:T(8,128)(2,1)S(1)} %collective-permute-done.7.refs_4_), channel_id=1, source_target_pairs={{0,16},{16,32},{32,48},{48,64},{64,80},{80,96},{96,112},{112,0},{1... | collective-permute-start | bytes 786440 | tf_op jit(solution)/shard_map/ppermute | solution.py:345
  68.9 8.3 %collective-permute-start.10 = (bf16[256,512]{1,0:T(8,128)(2,1)S(1)}, bf16[256,512]{1,0:T(8,128)(2,1)S(1)}, u32[]{:S(2)}, u32[]{:S(2)}) collective-permute-start(bf16[256,512]{1,0:T(8,128)(2,1)S(1)} %collective-permute-done.8.refs_5_), channel_id=1, source_target_pairs={{0,112},{16,0},{32,16},{48,32},{64,48},{80,64},{96,80},{112,96},{1... | collective-permute-start | bytes 786440 | tf_op jit(solution)/shard_map/ppermute | solution.py:346
  77.1 7.1 %collective-permute-start.11 = (bf16[256,512]{1,0:T(8,128)(2,1)S(1)}, bf16[256,512]{1,0:T(8,128)(2,1)S(1)}, u32[]{:S(2)}, u32[]{:S(2)}) collective-permute-start(bf16[256,512]{1,0:T(8,128)(2,1)S(1)} %collective-permute-done.9.refs_4_), channel_id=1, source_target_pairs={{0,16},{16,32},{32,48},{48,64},{64,80},{80,96},{96,112},{112,0},{1... | collective-permute-start | bytes 786440 | tf_op jit(solution)/shard_map/ppermute | solution.py:345
  77.2 7.1 %collective-permute-start.12 = (bf16[256,512]{1,0:T(8,128)(2,1)S(1)}, bf16[256,512]{1,0:T(8,128)(2,1)S(1)}, u32[]{:S(2)}, u32[]{:S(2)}) collective-permute-start(bf16[256,512]{1,0:T(8,128)(2,1)S(1)} %collective-permute-done.10.refs_5_), channel_id=1, source_target_pairs={{0,112},{16,0},{32,16},{48,32},{64,48},{80,64},{96,80},{112,96},{1... | collective-permute-start | bytes 786440 | tf_op jit(solution)/shard_map/ppermute | solution.py:346
  84.3 5.1 %collective-permute-start.13 = (bf16[128,512]{1,0:T(8,128)(2,1)S(1)}, bf16[128,512]{1,0:T(8,128)(2,1)S(1)}, u32[]{:S(2)}, u32[]{:S(2)}) collective-permute-start(bf16[128,512]{1,0:T(8,128)(2,1)S(1)} %slice.46), channel_id=1, source_target_pairs={{0,16},{16,32},{32,48},{48,64},{64,80},{80,96},{96,112},{112,0},{1... | collective-permute-start | bytes 393224 | tf_op jit(solution)/shard_map/ppermute | solution.py:345
  85.3 4.1 %collective-permute-start.14 = (bf16[128,512]{1,0:T(8,128)(2,1)S(1)}, bf16[128,512]{1,0:T(8,128)(2,1)S(1)}, u32[]{:S(2)}, u32[]{:S(2)}) collective-permute-start(bf16[128,512]{1,0:T(8,128)(2,1)S(1)} %slice.47), channel_id=1, source_target_pairs={{0,112},{16,0},{32,16},{48,32},{64,48},{80,64},{96,80},{112,96},{1... | collective-permute-start | bytes 393224 | tf_op jit(solution)/shard_map/ppermute | solution.py:346
  96.1 7.8 %collective-permute-start.15 = (bf16[272,256]{1,0:T(8,128)(2,1)S(1)}, bf16[272,256]{1,0:T(8,128)(2,1)S(1)}, u32[]{:S(2)}, u32[]{:S(2)}) collective-permute-start(bf16[272,256]{1,0:T(8,128)(2,1)S(1)} %get-tuple-element.97), channel_id=1, source_target_pairs={{0,128},{8,136},{128,0},{136,8},{1,129},{9,137},{129,1},{137,9},{2... | collective-permute-start | bytes 417800 | tf_op jit(solution)/shard_map/ppermute | solution.py:361
  99.8 8.2 %collective-permute-start.16 = (bf16[272,256]{1,0:T(8,128)(2,1)S(1)}, bf16[272,256]{1,0:T(8,128)(2,1)S(1)}, u32[]{:S(2)}, u32[]{:S(2)}) collective-permute-start(bf16[272,256]{1,0:T(8,128)(2,1)S(1)} %get-tuple-element.98), channel_id=1, source_target_pairs={{0,136},{8,128},{128,8},{136,0},{1,137},{9,129},{129,9},{137,1},{2... | collective-permute-start | bytes 417800 | tf_op jit(solution)/shard_map/ppermute | solution.py:361
  103.5 4.6 %collective-permute-start.17 = (bf16[272,256]{1,0:T(8,128)(2,1)S(1)}, bf16[272,256]{1,0:T(8,128)(2,1)S(1)}, u32[]{:S(2)}, u32[]{:S(2)}) collective-permute-start(bf16[272,256]{1,0:T(8,128)(2,1)S(1)} %get-tuple-element.99), channel_id=1, source_target_pairs={{0,8},{8,0},{128,136},{136,128},{1,9},{9,1},{129,137},{137,129},{2... | collective-permute-start | bytes 417800 | tf_op jit(solution)/shard_map/ppermute | solution.py:361
  109.3 16.9 %all-to-all-start.2 = ((bf16[8,2,144,128]{3,2,1,0:T(8,128)(2,1)}), bf16[8,2,144,128]{3,2,1,0:T(8,128)(2,1)S(1)}, u32[]{:S(2)}, u32[]{:S(2)}) async-start(bf16[8,2,144,128]{3,2,1,0:T(8,128)(2,1)} %merge_heads.1), calls=%async_computation.2 | async-start | bytes 1179648 | tf_op jit(solution)/shard_map/all_to_all | solution.py:362
  116.4 16.8 %copy-start.10 = (f32[64]{0:T(128)S(1)}, f32[64]{0:T(128)}, u32[]{:S(2)}) copy-start(f32[64]{0:T(128)} %param.24) | copy-start | bytes 772
  119.5 14.7 %copy-start.1 = (bf16[144,1024]{1,0:T(8,128)(2,1)S(1)}, bf16[144,1024]{1,0:T(8,128)(2,1)}, u32[]{:S(2)}) copy-start(bf16[144,1024]{1,0:T(8,128)(2,1)} %constant.62.clone.spread) | copy-start | bytes 884740
  126.5 6.8 %collective-permute-start.19 = (bf16[144,128]{1,0:T(8,128)(2,1)S(1)}, bf16[144,128]{1,0:T(8,128)(2,1)S(1)}, u32[]{:S(2)}, u32[]{:S(2)}) collective-permute-start(bf16[144,128]{1,0:T(8,128)(2,1)S(1)} %get-tuple-element.113), channel_id=1, source_target_pairs={{8,0},{16,8},{24,16},{32,24},{40,32},{48,40},{56,48},{64,56},{72,6... | collective-permute-start | bytes 110600 | tf_op jit(solution)/shard_map/ppermute | solution.py:365
  130.2 4.0 %collective-permute-start.18 = (bf16[144,128]{1,0:T(8,128)(2,1)S(1)}, bf16[144,128]{1,0:T(8,128)(2,1)S(1)}, u32[]{:S(2)}, u32[]{:S(2)}) collective-permute-start(bf16[144,128]{1,0:T(8,128)(2,1)S(1)} %get-tuple-element.114), channel_id=1, source_target_pairs={{0,8},{8,16},{16,24},{24,32},{32,40},{40,48},{48,56},{56,64},{64,7... | collective-permute-start | bytes 110600 | tf_op jit(solution)/shard_map/ppermute | solution.py:364
  (2 other events, 7.1 us)

commit v4 on v3

--- a/solution.py
+++ b/solution.py
@@ -32,6 +32,50 @@
 
 def dot_tn(a, b):
     return lax.dot_general(a, b, (((0,), (0,)), ((), ())), preferred_element_type=F32)
+
+
+def near(x):
+    return pltpu.with_memory_space_constraint(x, pltpu.VMEM)
+
+
+def mix_body(patches, weights, offsets, out):
+    lhs = patches[...]
+    offset = offsets[0:1, :] + offsets[1:2, :]
+    for k in range(8):
+        cols = slice(k * 256, (k + 1) * 256)
+        out[:, cols] = (dot_tn(lhs, weights[:, cols]) + offset[:, cols]).astype(BF)
+
+
+def mix(patches, weights, offsets):
+    return pl.pallas_call(
+        mix_body,
+        out_shape=pltpu.VMEM((256, D), BF),
+        in_specs=[VMEM_SPEC] * 3,
+        out_specs=VMEM_SPEC,
+        compiler_params=pltpu.CompilerParams(vmem_limit_bytes=12 * 2**20),
+        name="mix_variables",
+    )(near(patches), near(weights), near(offsets))
+
+
+def norm_body(pieces, gain, out):
+    total = pieces[0].astype(F32)
+    for k in range(1, 8):
+        total = total + pieces[k].astype(F32)
+    scale = lax.rsqrt(jnp.mean(total * total, axis=1, keepdims=True) + 1e-05)
+    normed = (total * scale * gain[...]).astype(BF)
+    for k in range(8):
+        out[k] = normed
+
+
+def norm_copies(pieces, gain):
+    return pl.pallas_call(
+        norm_body,
+        out_shape=pltpu.VMEM((8, 32, D), BF),
+        in_specs=[VMEM_SPEC] * 2,
+        out_specs=VMEM_SPEC,
+        compiler_params=pltpu.CompilerParams(vmem_limit_bytes=12 * 2**20),
+        name="norm_slab",
+    )(near(pieces), near(gain))
 
 
 def flash_kernel(blocks, chunks, first, last):
@@ -73,7 +117,7 @@
                         state = (top, total, update)
                     top, total, update = state
                     if last:
-                        rest[block][head, inner] = (update / total).astype(BF)
+                        rest[block][head, inner] = (update * (1.0 / total)).astype(BF)
                         lse = top + jnp.log2(total)
                         high = lse.astype(BF)
                         left = lse - high.astype(F32)
@@ -92,10 +136,6 @@
                         rest[0][2 + h : 3 + h, cols] = stats[2 * h + 1]
 
     return body
-
-
-def near(x):
-    return pltpu.with_memory_space_constraint(x, pltpu.VMEM)
 
 
 def flash_step(queries, chunks, carry, last):
@@ -170,6 +210,15 @@
     return spread.reshape(144, 1024)
 
 
+def edge_matrix():
+    edges = np.zeros((2, 2, 8, 8, 128), np.float32)
+    for q in range(2):
+        for r in range(8):
+            edges[0, q, r, r, q] = 1
+            edges[1, q, r, r, 126 + q] = 1
+    return edges.reshape(32, 1024)
+
+
 def gelu_pair(x):
     root = math.sqrt(2.0 / math.pi)
     t = jnp.tanh(root * (x + 0.044715 * (x * x * x)))
@@ -185,17 +234,23 @@
 
 
 def fine_body(factor):
-    def body(flags, own, prev, nxt, spread, grad, rim, mats, bias, field, grad_fine, terms):
+    def body(flags, own, near_up, far_up, spread, edges, grad, rim, mats, bias, field, grad_fine, terms):
         spread_all = spread[...]
         ups = []
-        for block in (prev[...], own[0], own[1], nxt[...]):
+        second_core = flags[4] > 0
+        close, distant = near_up[...].astype(F32), far_up[...].astype(F32)
+        prev = jnp.where(second_core, close, distant).astype(BF)
+        nxt = jnp.where(second_core, distant, close).astype(BF)
+        for block in (prev, own[0], own[1], nxt):
             wide = dot_tn(block, spread_all)
             for a in range(2):
                 ups.append(
                     wide[0:64, 512 * a : 512 * a + 256] + wide[64:128, 512 * a + 256 : 512 * a + 512]
                 )
+        rims = dot_tn(rim[...], edges[...])
         grads = [
-            jnp.concatenate([grad[r].astype(F32), rim[r].astype(F32)], axis=1) for r in range(8)
+            jnp.concatenate([grad[r].astype(F32), rims[:, r * 128 : (r + 1) * 128]], axis=1)
+            for r in range(8)
         ]
         up_taps = [shifted(u).astype(BF) for u in ups]
         grad_taps = [shifted(g).astype(BF) for g in grads]
@@ -254,7 +309,7 @@
     return body
 
 
-def fine_stage(flags, own, prev, nxt, spread, grad, rim, mats, bias, factor):
+def fine_stage(flags, own, near_up, far_up, spread, edges, grad, rim, mats, bias, factor):
     return pl.pallas_call(
         fine_body(factor),
         out_shape=[
@@ -262,11 +317,11 @@
             jax.ShapeDtypeStruct((4, 64, 128), BF),
             pltpu.VMEM((768, 128), BF),
         ],
-        in_specs=[SMEM_SPEC] + [VMEM_SPEC] * 8,
+        in_specs=[SMEM_SPEC] + [VMEM_SPEC] * 9,
         out_specs=[VMEM_SPEC] * 3,
         compiler_params=pltpu.CompilerParams(vmem_limit_bytes=20 * 2**20),
         name="fine_stage",
-    )(flags, *[near(x) for x in (own, prev, nxt, spread, grad, rim, mats, bias)])
+    )(flags, *[near(x) for x in (own, near_up, far_up, spread, edges, grad, rim, mats, bias)])
 
 
 def copies(piece, axis, count):
@@ -298,9 +353,9 @@
     shift_up = [(i + 1, i) for i in range(31)]
     group = ("xh", "core")
 
-    flattened = jnp.transpose(patches, (1, 2, 0, 3)).reshape(256, 128)
-    partial_mix = jnp.dot(flattened, w_embed.reshape(128, D), preferred_element_type=F32)
-    partial_mix = (partial_mix + jnp.sum(var_bias, axis=0)).astype(BF).reshape(8, 32, D)
+    core_at = lax.axis_index("core")
+    turned = jnp.transpose(patches, (0, 1, 3, 2)).reshape(128, 256)
+    partial_mix = mix(turned, w_embed.reshape(128, D), var_bias).reshape(8, 32, D)
     partial_mix, cells, wo, wk, wv = lax.optimization_barrier((partial_mix, cotangent, wo, wk, wv))
     pieces = lax.all_to_all(partial_mix, VAR, 0, 0)
     up_mat = jnp.dot(wo, w_up, preferred_element_type=F32).astype(BF)
@@ -314,42 +369,53 @@
         axis=0,
     )
     pieces, up_mat, wkv, grad_rows = lax.optimization_barrier((pieces, up_mat, wkv, grad_rows))
-    mixed = jnp.sum(pieces.astype(F32), axis=0)
-    normed_slab = (
-        mixed * lax.rsqrt(jnp.mean(mixed * mixed, axis=-1, keepdims=True) + 1e-05) * agg_gain
-    ).astype(BF)
-    normed_slab, grad_rows, conv1, conv2, bias1 = lax.optimization_barrier(
-        (normed_slab, grad_rows, conv1, conv2, bias1)
-    )
-    normed = copies(normed_slab, VAR, 8).reshape(256, D)
-    from_right = lax.ppermute(grad_rows[:, :, 0:2], VAR, [(i + 1, i) for i in range(7)])
-    from_left = lax.ppermute(grad_rows[:, :, 126:128], VAR, [(i, i + 1) for i in range(7)])
-    rim = jnp.concatenate([from_right, jnp.zeros((8, C, 124), BF), from_left], axis=2)
+    spread_out = norm_copies(pieces, agg_gain.reshape(1, D))
+    spread_out, grad_rows, conv1, conv2, bias1 = lax.optimization_barrier(
+        (spread_out, grad_rows, conv1, conv2, bias1)
+    )
+    normed = lax.all_to_all(spread_out, VAR, 0, 0).reshape(256, D)
+    edge_right = jnp.transpose(grad_rows[:, :, 0:2], (2, 0, 1)).reshape(16, C)
+    edge_left = jnp.transpose(grad_rows[:, :, 126:128], (2, 0, 1)).reshape(16, C)
     mats = jnp.stack(
         [tap_matrix(conv1), tap_matrix(flipped(conv2)), tap_matrix(conv2), tap_matrix(flipped(conv1))]
     )
     bias = bias1.reshape(C, 1)
-    flags = jnp.stack([band_at > 0, band_at < 31, var_at > 0, var_at < 7]).astype(jnp.int32)
-    normed, rim, mats, bias, flags = lax.optimization_barrier((normed, rim, mats, bias, flags))
-
+    flags = jnp.stack(
+        [band_at > 0, band_at < 31, var_at > 0, var_at < 7, core_at > 0]
+    ).astype(jnp.int32)
+    normed, edge_right, edge_left, mats, bias, flags = lax.optimization_barrier(
+        (normed, edge_right, edge_left, mats, bias, flags)
+    )
+
+    keyvals = jnp.dot(normed, wkv, preferred_element_type=F32).astype(BF)
+    ahead = lax.ppermute(keyvals, "z", turn(8, 1))
+    behind = lax.ppermute(keyvals, "z", turn(8, -1))
     queries = jnp.dot(normed, wq, preferred_element_type=F32).astype(BF)
     all_queries = [queries] + [lax.ppermute(queries, group, flip(4, k)) for k in (2, 3, 1)]
-    keys_in, queries = lax.optimization_barrier((normed, queries))
-    keyvals = jnp.dot(keys_in, wkv, preferred_element_type=F32).astype(BF)
-    ahead, behind = keyvals, keyvals
-    carry = None
-    fresh = [keyvals]
-    for step in range(4):
+    fresh = [keyvals, ahead, behind]
+    ahead = lax.ppermute(ahead, "z", turn(8, 1))
+    behind = lax.ppermute(behind, "z", turn(8, -1))
+    padded = jnp.pad(normed, ((1, 1), (0, 0)))
+    around = lax.dynamic_slice_in_dim(padded, var_at * 32, 34, 0)
+    carry = flash_step(all_queries, fresh, None, False)
+    ahead, behind, carry, edge_right, edge_left, around = lax.optimization_barrier(
+        (ahead, behind, carry, edge_right, edge_left, around)
+    )
+    from_right = lax.ppermute(edge_right, VAR, [(i + 1, i) for i in range(7)])
+    from_left = lax.ppermute(edge_left, VAR, [(i, i + 1) for i in range(7)])
+    for step in (2, 3):
+        fresh = [ahead, behind]
         if step == 3:
             ahead, behind = ahead[:128], behind[128:]
         ahead = lax.ppermute(ahead, "z", turn(8, 1))
         behind = lax.ppermute(behind, "z", turn(8, -1))
         carry = flash_step(all_queries, fresh, carry, False)
-        ahead, behind, carry = lax.optimization_barrier((ahead, behind, carry))
-        fresh = [ahead, behind]
-
-    padded = jnp.pad(normed, ((1, 1), (0, 0)))
-    around = lax.dynamic_slice_in_dim(padded, var_at * 32, 34, 0)
+        ahead, behind, carry, from_right, from_left = lax.optimization_barrier(
+            (ahead, behind, carry, from_right, from_left)
+        )
+    fresh = [ahead, behind]
+    rim = jnp.concatenate([from_right, from_left], axis=0)
+
     base = jnp.dot(around, w_up, preferred_element_type=F32)
     base_main = jnp.transpose(base[1:33].reshape(32, 2, 4, 128), (1, 2, 0, 3)).reshape(2, 128, 128)
     left = base[0].reshape(2, 4, 128)
@@ -361,12 +427,13 @@
     parts = [blocks[0]] + [lax.ppermute(b, group, flip(4, k)) for b, k in zip(blocks[1:], (2, 3, 1))]
     pieces = lax.all_to_all(merge(parts, up_mat), VAR, 0, 0)
     up = (jnp.sum(pieces.astype(F32), axis=0) + base_all).astype(BF)
-    prev = lax.ppermute(up[1], BAND, shift_down)
-    nxt = lax.ppermute(up[0], BAND, shift_up)
+    near_up = lax.ppermute(lax.dynamic_index_in_dim(up, 1 - core_at, 0, False), "core", flip(2, 1))
+    pairs = [(i, i + 1) for i in range(1, 31, 2)] + [(i + 1, i) for i in range(1, 31, 2)]
+    far_up = lax.ppermute(lax.dynamic_index_in_dim(up, core_at, 0, False), BAND, pairs)
     factor = 1.0 / math.sqrt(128 * 1024)
     spread = jnp.asarray(spread_matrix(), BF)
     field_out, grad_fine, terms = fine_stage(
-        flags, up, prev, nxt, spread, grad_rows, rim, mats, bias, factor
+        flags, up, near_up, far_up, spread, jnp.asarray(edge_matrix(), BF), grad_rows, rim, mats, bias, factor
     )
     shares = lax.all_to_all(terms.reshape(32, 24, 128), PLANE, 0, 0)
     share = jnp.sum(shares.astype(F32), axis=0).astype(BF)

time: 182 us -> 180 us (0.989)
  starting transfers between devices: 64.7 us -> 59.6 us
  local copies, waits for them, and re-layouts: 5.09 us -> 8.17 us
  Pallas kernels: 17.5 us -> 19.9 us
  waiting for transfers between devices: 32.7 us -> 35 us
  other arithmetic: 4.28 us -> 2 us
    all_to_all x1, waiting for transfers between devices: 0.01 us -> 11.8 us  [device_step(): normed = lax.all_to_all(spread_out, VAR, 0, 0).reshape(256, D)]
    ppermute x4 -> x3, waiting for transfers between devices: 5.89 us -> 0.37 us  [device_step(): ahead = lax.ppermute(ahead, 'z', turn(8, 1))]
    ppermute x4 -> x3, starting transfers between devices: 13 us -> 8.79 us  [device_step(): behind = lax.ppermute(behind, 'z', turn(8, -1))]
    ppermute x4 -> x6, starting transfers between devices: 12 us -> 14.8 us  [the longest x1 5.29 us: device_step(): behind = lax.ppermute(keyvals, 'z', turn(8, -1))]
    pallas_call x0 -> x2, Pallas kernels: none -> 2.69 us  [the longest x1 1.43 us: mix(): pl.pallas_call(mix_body, out_shape=pltpu.VMEM((256, D), BF), in_specs=[VM...]
    unnamed x22 -> x26, local copies, waits for them, and re-layouts: 0.14 us -> 2.74 us
    ppermute x4 -> x6, waiting for transfers between devices: 6.81 us -> 4.62 us  [the longest x1 3.31 us: device_step(): behind = lax.ppermute(keyvals, 'z', turn(8, -1))]
    all_to_all x1, starting transfers between devices: 7.08 us -> 5.19 us  [device_step(): pieces = lax.all_to_all(merge(parts, up_mat), VAR, 0, 0)]
  transfers between devices with their start and end apart: 23 -> 23, of which waited for: 10 -> 9; matrix products, arithmetic and copies ran while one was open for 6% -> 8% of each run, Pallas kernels for 4% -> 4%
where the time goes in v4:
time: 180 us; the launch traced here: 179 us
  starting transfers between devices  59.6 us (33%)
  blocking collectives  42.5 us (24%)
  waiting for transfers between devices  35 us (19%)
  Pallas kernels  19.9 us (11%)
  matrix products  11.1 us (6%)
  local copies, waits for them, and re-layouts  8.17 us (5%)
  other arithmetic  2 us (1%)
    all_to_all x2, blocking collectives, copies(): lax.all_to_all(jnp.broadcast_to(piece[None], (count,) + piece.shape), axi...  22.7 us
    all_to_all x1, blocking collectives, device_step(): shares = lax.all_to_all(terms.reshape(32, 24, 128), PLANE, 0, 0)  19.8 us
    pallas_call x4, Pallas kernels, flash_step(): pl.pallas_call(flash_kernel(blocks, len(chunks), first, last), out_shape=...  13.2 us
    all_to_all x1, waiting for transfers between devices, device_step(): normed = lax.all_to_all(spread_out, VAR, 0, 0).reshape(256, D)  11.8 us
    ppermute x3, starting transfers between devices, device_step(): behind = lax.ppermute(behind, 'z', turn(8, -1))  8.79 us
    ppermute x3, starting transfers between devices, device_step(): lax.ppermute(queries, group, flip(4, k))  7.43 us
    ppermute x3, starting transfers between devices, device_step(): lax.ppermute(b, group, flip(4, k))  6.48 us
    all_to_all x1, waiting for transfers between devices, device_step(): pieces = lax.all_to_all(merge(parts, up_mat), VAR, 0, 0)  5.94 us
  transfers between devices with their start and end apart: 23, of which 9 were waited for; matrix products, arithmetic and copies ran while one was open for 8% of the time, Pallas kernels for 4%

profile of v4, /device:TPU:1, one launch (start us, length us, event | category | flops | bytes accessed | tf_op | source)
XLA Modules:
  0.0 179.4 jit_solution(16590540306072623910)
XLA Ops:
  4.8 5.9 %all-to-all-start = ((bf16[8,32,2048]{2,1,0:T(8,128)(2,1)}), bf16[8,32,2048]{2,1,0:T(8,128)(2,1)S(1)}, u32[]{:S(2)}, u32[]{:S(2)}) async-start(bf16[8,32,2048]{2,1,0:T(8,128)(2,1)} %bitcast.3), calls=%async_computation | async-start | bytes 2097152 | tf_op jit(solution)/shard_map/all_to_all | solution.py:360
  11.6 4.4 %collective-permute-start = (bf16[2,64,128]{2,1,0:T(8,128)(2,1)S(1)}, bf16[2,64,128]{2,1,0:T(8,128)(2,1)S(1)}, u32[]{:S(2)}, u32[]{:S(2)}) collective-permute-start(bf16[2,64,128]{2,1,0:T(8,128)(2,1)S(1)} %get-tuple-element.117), channel_id=1, source_target_pairs={{0,8},{8,16},{16,24},{24,32},{32,40},{40,48},{48,56},{56,64},{64,7... | collective-permute-start | bytes 98312 | tf_op jit(solution)/shard_map/ppermute | solution.py:365
  16.1 2.1 %collective-permute-start.1 = (bf16[2,64,128]{2,1,0:T(8,128)(2,1)S(1)}, bf16[2,64,128]{2,1,0:T(8,128)(2,1)S(1)}, u32[]{:S(2)}, u32[]{:S(2)}) collective-permute-start(bf16[2,64,128]{2,1,0:T(8,128)(2,1)S(1)} %get-tuple-element.118), channel_id=1, source_target_pairs={{8,0},{16,8},{24,16},{32,24},{40,32},{48,40},{56,48},{64,56},{72,6... | collective-permute-start | bytes 98312 | tf_op jit(solution)/shard_map/ppermute | solution.py:367
  18.1 3.4 %convolution_convert_fusion.mat = bf16[256,1024]{1,0:T(8,128)(2,1)S(1)} fusion(bf16[256,2048]{1,0:T(8,128)(2,1)S(1)} %copy-done, bf16[2048,1024]{1,0:T(8,128)(2,1)} %param.23), kind=kOutput, calls=%fused_computation.1 | convolution fusion | flops 1074003968 | bytes 5767168 | tf_op jit(solution)/shard_map/dot_general | solution.py:361
  23.2 2.4 %all-to-all-done.pieces = bf16[8,32,2048]{2,1,0:T(8,128)(2,1)S(1)} async-done(((bf16[8,32,2048]{2,1,0:T(8,128)(2,1)}), bf16[8,32,2048]{2,1,0:T(8,128)(2,1)S(1)}, u32[]{:S(2)}, u32[]{:S(2)}) %all-to-all-start) | async-done | bytes 1048608 | tf_op jit(solution)/shard_map/all_to_all | solution.py:360
  26.9 4.2 %all-to-all-start.1 = ((bf16[8,32,2048]{2,1,0:T(8,128)(2,1)}), bf16[8,32,2048]{2,1,0:T(8,128)(2,1)}, u32[]{:S(2)}, u32[]{:S(2)}) async-start(bf16[8,32,2048]{2,1,0:T(8,128)(2,1)} %norm_slab.1), calls=%async_computation.1 | async-start | bytes 2097152 | tf_op jit(solution)/shard_map/all_to_all | solution.py:376
  33.1 11.8 %all-to-all-done.1 = bf16[8,32,2048]{2,1,0:T(8,128)(2,1)} async-done(((bf16[8,32,2048]{2,1,0:T(8,128)(2,1)}), bf16[8,32,2048]{2,1,0:T(8,128)(2,1)}, u32[]{:S(2)}, u32[]{:S(2)}) %all-to-all-start.1) | async-done | bytes 1048608 | tf_op jit(solution)/shard_map/all_to_all | solution.py:376
  44.9 2.6 %convolution_convert_fusion.1.refs_4_ = bf16[256,512]{1,0:T(8,128)(2,1)S(1)} fusion(bf16[256,2048]{1,0:T(8,128)(2,1)} %bitcast.5, bf16[2048,512]{1,0:T(8,128)(2,1)} %pad_maximum_fusion), kind=kOutput, calls=%fused_computation.2 | convolution fusion | flops 537001984 | bytes 3407872 | tf_op jit(solution)/shard_map/dot_general | solution.py:390
  47.5 5.3 %collective-permute-start.7 = (bf16[256,512]{1,0:T(8,128)(2,1)S(1)}, bf16[256,512]{1,0:T(8,128)(2,1)S(1)}, u32[]{:S(2)}, u32[]{:S(2)}) collective-permute-start(bf16[256,512]{1,0:T(8,128)(2,1)S(1)} %convolution_convert_fusion.1.refs_4_), channel_id=1, source_target_pairs={{0,112},{16,0},{32,16},{48,32},{64,48},{80,64},{96,80},{112,96},{1... | collective-permute-start | bytes 786440 | tf_op jit(solution)/shard_map/ppermute | solution.py:392
  52.8 3.3 %collective-permute-done.7.refs_6_ = bf16[256,512]{1,0:T(8,128)(2,1)S(1)} collective-permute-done((bf16[256,512]{1,0:T(8,128)(2,1)S(1)}, bf16[256,512]{1,0:T(8,128)(2,1)S(1)}, u32[]{:S(2)}, u32[]{:S(2)}) %collective-permute-start.7) | collective-permute-done | bytes 262176 | tf_op jit(solution)/shard_map/ppermute | solution.py:392
  56.1 3.1 %collective-permute-start.8 = (bf16[256,512]{1,0:T(8,128)(2,1)S(1)}, bf16[256,512]{1,0:T(8,128)(2,1)S(1)}, u32[]{:S(2)}, u32[]{:S(2)}) collective-permute-start(bf16[256,512]{1,0:T(8,128)(2,1)S(1)} %collective-permute-done.7.refs_6_), channel_id=1, source_target_pairs={{0,112},{16,0},{32,16},{48,32},{64,48},{80,64},{96,80},{112,96},{1... | collective-permute-start | bytes 786440 | tf_op jit(solution)/shard_map/ppermute | solution.py:397
  61.3 4.5 %collective-permute-start.4 = (bf16[256,256]{1,0:T(8,128)(2,1)S(1)}, bf16[256,256]{1,0:T(8,128)(2,1)S(1)}, u32[]{:S(2)}, u32[]{:S(2)}) collective-permute-start(bf16[256,256]{1,0:T(8,128)(2,1)S(1)} %convolution_convert_fusion.2.refs_0_), channel_id=1, source_target_pairs={{0,8},{8,0},{128,136},{136,128},{1,9},{9,1},{129,137},{137,129},{2... | collective-permute-start | bytes 393224 | tf_op jit(solution)/shard_map/ppermute | solution.py:394
  65.7 2.8 %collective-permute-start.3 = (bf16[256,256]{1,0:T(8,128)(2,1)S(1)}, bf16[256,256]{1,0:T(8,128)(2,1)S(1)}, u32[]{:S(2)}, u32[]{:S(2)}) collective-permute-start(bf16[256,256]{1,0:T(8,128)(2,1)S(1)} %convolution_convert_fusion.2.refs_0_), channel_id=1, source_target_pairs={{0,136},{8,128},{128,8},{136,0},{1,137},{9,129},{129,9},{137,1},{2... | collective-permute-start | bytes 393224 | tf_op jit(solution)/shard_map/ppermute | solution.py:394
  69.7 2.8 %collective-permute-done.3.refs_2_ = bf16[256,256]{1,0:T(8,128)(2,1)S(1)} collective-permute-done((bf16[256,256]{1,0:T(8,128)(2,1)S(1)}, bf16[256,256]{1,0:T(8,128)(2,1)S(1)}, u32[]{:S(2)}, u32[]{:S(2)}) %collective-permute-start.3) | collective-permute-done | bytes 131104 | tf_op jit(solution)/shard_map/ppermute | solution.py:394
  72.5 2.2 %collective-permute-done.2.refs_1_ = bf16[256,256]{1,0:T(8,128)(2,1)S(1)} collective-permute-done((bf16[256,256]{1,0:T(8,128)(2,1)S(1)}, bf16[256,256]{1,0:T(8,128)(2,1)S(1)}, u32[]{:S(2)}, u32[]{:S(2)}) %collective-permute-start.2) | collective-permute-done | bytes 131104 | tf_op jit(solution)/shard_map/ppermute | solution.py:394
  74.7 2.6 %flash_step.3 = (f32[8,1024]{1,0:T(8,128)S(1)}, f32[256,1024]{1,0:T(8,128)S(1)}) custom-call(bf16[256,256]{1,0:T(8,128)(2,1)S(1)} %convolution_convert_fusion.2.refs_0_, bf16[256,256]{1,0:T(8,128)(2,1)S(1)} %collective-permute-done.2.refs_1_, bf16[256,256]{1,0:T(8,128)(2,1)S(1)} %collective-permute-done.3.refs_2_, ...), custom_call_target="tpu_custom_call" | custom-call | tf_op jit(solution)/shard_map/flash_step/pallas_call | solution.py:152
  77.6 3.0 %collective-permute-start.10 = (bf16[256,512]{1,0:T(8,128)(2,1)S(1)}, bf16[256,512]{1,0:T(8,128)(2,1)S(1)}, u32[]{:S(2)}, u32[]{:S(2)}) collective-permute-start(bf16[256,512]{1,0:T(8,128)(2,1)S(1)} %collective-permute-done.8.refs_5_), channel_id=1, source_target_pairs={{0,112},{16,0},{32,16},{48,32},{64,48},{80,64},{96,80},{112,96},{1... | collective-permute-start | bytes 786440 | tf_op jit(solution)/shard_map/ppermute | solution.py:411
  81.9 4.0 %collective-permute-start.12 = (bf16[16,64]{1,0:T(8,128)(2,1)S(1)}, bf16[16,64]{1,0:T(8,128)(2,1)S(1)}, u32[]{:S(2)}, u32[]{:S(2)}) collective-permute-start(bf16[16,64]{1,0:T(8,128)(2,1)S(1)} %bitcast.77), channel_id=1, source_target_pairs={{0,1},{1,2},{2,3},{3,4},{4,5},{5,6},{6,7},{8,9},{9,10},{10,11},{11... | collective-permute-start | bytes 6152 | tf_op jit(solution)/shard_map/ppermute | solution.py:405
  85.9 2.0 %flash_step.4 = (f32[8,1024]{1,0:T(8,128)S(1)}, f32[256,1024]{1,0:T(8,128)S(1)}) custom-call(bf16[256,256]{1,0:T(8,128)(2,1)S(1)} %convolution_convert_fusion.2.refs_0_, bf16[256,256]{1,0:T(8,128)(2,1)S(1)} %collective-permute-done.2.refs_1_, bf16[256,256]{1,0:T(8,128)(2,1)S(1)} %collective-permute-done.3.refs_2_, ...), custom_call_target="tpu_custom_call" | custom-call | tf_op jit(solution)/shard_map/flash_step/pallas_call | solution.py:152
  88.1 2.7 %collective-permute-start.14 = (bf16[128,512]{1,0:T(8,128)(2,1)S(1)}, bf16[128,512]{1,0:T(8,128)(2,1)S(1)}, u32[]{:S(2)}, u32[]{:S(2)}) collective-permute-start(bf16[128,512]{1,0:T(8,128)(2,1)S(1)} %slice.41), channel_id=1, source_target_pairs={{0,112},{16,0},{32,16},{48,32},{64,48},{80,64},{96,80},{112,96},{1... | collective-permute-start | bytes 393224 | tf_op jit(solution)/shard_map/ppermute | solution.py:411
  93.1 6.7 %flash_last.1 = (bf16[272,256]{1,0:T(8,128)(2,1)S(1)}, bf16[272,256]{1,0:T(8,128)(2,1)S(1)}, bf16[272,256]{1,0:T(8,128)(2,1)S(1)}, bf16[272,256]{1,0:T(8,128)(2,1)S(1)}) custom-call(bf16[256,256]{1,0:T(8,128)(2,1)S(1)} %convolution_convert_fusion.2.refs_0_, bf16[256,256]{1,0:T(8,128)(2,1)S(1)} %collective-permute-done.2.refs_1_, ...), custom_call_target="tpu_custom_call" | custom-call | tf_op jit(solution)/shard_map/flash_last/pallas_call | solution.py:152
  99.7 3.2 %collective-permute-start.15 = (bf16[272,256]{1,0:T(8,128)(2,1)S(1)}, bf16[272,256]{1,0:T(8,128)(2,1)S(1)}, u32[]{:S(2)}, u32[]{:S(2)}) collective-permute-start(bf16[272,256]{1,0:T(8,128)(2,1)S(1)} %get-tuple-element.97), channel_id=1, source_target_pairs={{0,128},{8,136},{128,0},{136,8},{1,129},{9,137},{129,1},{137,9},{2... | collective-permute-start | bytes 417800 | tf_op jit(solution)/shard_map/ppermute | solution.py:427
  102.9 3.3 %collective-permute-start.16 = (bf16[272,256]{1,0:T(8,128)(2,1)S(1)}, bf16[272,256]{1,0:T(8,128)(2,1)S(1)}, u32[]{:S(2)}, u32[]{:S(2)}) collective-permute-start(bf16[272,256]{1,0:T(8,128)(2,1)S(1)} %get-tuple-element.98), channel_id=1, source_target_pairs={{0,136},{8,128},{128,8},{136,0},{1,137},{9,129},{129,9},{137,1},{2... | collective-permute-start | bytes 417800 | tf_op jit(solution)/shard_map/ppermute | solution.py:427
  106.4 4.8 %collective-permute-done.16.b2 = bf16[272,256]{1,0:T(8,128)(2,1)S(1)} collective-permute-done((bf16[272,256]{1,0:T(8,128)(2,1)S(1)}, bf16[272,256]{1,0:T(8,128)(2,1)S(1)}, u32[]{:S(2)}, u32[]{:S(2)}) %collective-permute-start.16) | collective-permute-done | bytes 139296 | tf_op jit(solution)/shard_map/ppermute | solution.py:427
  112.5 5.2 %all-to-all-start.2 = ((bf16[8,2,144,128]{3,2,1,0:T(8,128)(2,1)}), bf16[8,2,144,128]{3,2,1,0:T(8,128)(2,1)S(1)}, u32[]{:S(2)}, u32[]{:S(2)}) async-start(bf16[8,2,144,128]{3,2,1,0:T(8,128)(2,1)} %merge_heads.1), calls=%async_computation.2 | async-start | bytes 1179648 | tf_op jit(solution)/shard_map/all_to_all | solution.py:428
  117.7 3.0 %fusion.5 = f32[34,1024]{1,0:T(8,128)S(1)} fusion(bf16[34,2048]{1,0:T(8,128)(2,1)S(1)} %pad_dynamic-slice_fusion, bf16[2048,1024]{1,0:T(8,128)(2,1)} %param.23), kind=kOutput, calls=%fused_computation.25 | convolution fusion | flops 142606336 | bytes 4472832 | tf_op jit(solution)/shard_map/dot_general | solution.py:419
  120.9 5.9 %all-to-all-done.2 = bf16[8,2,144,128]{3,2,1,0:T(8,128)(2,1)S(1)} async-done(((bf16[8,2,144,128]{3,2,1,0:T(8,128)(2,1)}), bf16[8,2,144,128]{3,2,1,0:T(8,128)(2,1)S(1)}, u32[]{:S(2)}, u32[]{:S(2)}) %all-to-all-start.2) | async-done | bytes 589856 | tf_op jit(solution)/shard_map/all_to_all | solution.py:428
  127.0 3.9 %collective-permute-start.19 = (bf16[144,128]{1,0:T(8,128)(2,1)S(1)}, bf16[144,128]{1,0:T(8,128)(2,1)S(1)}, u32[]{:S(2)}, u32[]{:S(2)}) collective-permute-start(bf16[144,128]{1,0:T(8,128)(2,1)S(1)} %get-tuple-element.115), channel_id=1, source_target_pairs={{8,16},{24,32},{40,48},{56,64},{72,80},{88,96},{104,112},{120,128}... | collective-permute-start | bytes 110600 | tf_op jit(solution)/shard_map/ppermute | solution.py:432
  132.6 2.7 %fine_stage.1 = (bf16[4,64,128]{2,1,0:T(8,128)(2,1)}, bf16[4,64,128]{2,1,0:T(8,128)(2,1)}, bf16[768,128]{1,0:T(8,128)(2,1)S(1)}) custom-call(s32[5]{0:T(128)S(1)} %convert_element_type.31.flags, bf16[2,144,128]{2,1,0:T(8,128)(2,1)S(1)} %fusion.own, bf16[144,128]{1,0:T(8,128)(2,1)S(1)} %collective-permute-done.18.near_up, ...), custom_call_target="tpu_custom_call" | custom-call | tf_op jit(solution)/shard_map/fine_stage/pallas_call | solution.py:313
  135.3 19.8 %all_to_all.30 = bf16[32,24,128]{2,1,0:T(8,128)(2,1)S(1)} all-to-all(bf16[32,24,128]{2,1,0:T(8,128)(2,1)S(1)} %bitcast.61), channel_id=1, replica_groups=mesh['xh'=2,'z'=8,'core'=2,'y'=4,'xl'=2] {'xh','core','y','xl'}, dimensions={0} | all-to-all | bytes 393216 | tf_op jit(solution)/shard_map/all_to_all | solution.py:438
  155.2 9.4 %all_to_all.31 = bf16[8,24,128]{2,1,0:T(8,128)(2,1)S(1)} all-to-all(bf16[8,24,128]{2,1,0:T(8,128)(2,1)S(1)} %broadcast_in_dim.26), channel_id=1, replica_groups=mesh['xh'=2,'z'=8,'core'=2,'y'=4,'xl'=2] {'z'}, dimensions={0} | all-to-all | bytes 98304 | tf_op jit(solution)/shard_map/all_to_all | solution.py:328
  164.7 13.3 %all_to_all.32 = bf16[32,24,128]{2,1,0:T(8,128)(2,1)S(1)} all-to-all(bf16[32,24,128]{2,1,0:T(8,128)(2,1)S(1)} %broadcast_in_dim.27), channel_id=1, replica_groups=mesh['xh'=2,'z'=8,'core'=2,'y'=4,'xl'=2] {'xh','core','y','xl'}, dimensions={0} | all-to-all | bytes 393216 | tf_op jit(solution)/shard_map/all_to_all | solution.py:328
  (97 shorter events, 21.9 us)
Async XLA Ops:
  0.6 17.5 %copy-start = (bf16[256,2048]{1,0:T(8,128)(2,1)S(1)}, bf16[256,2048]{1,0:T(8,128)(2,1)}, u32[]{:S(2)}) copy-start(bf16[256,2048]{1,0:T(8,128)(2,1)} %param.22) | copy-start | bytes 3145732
  4.8 20.8 %all-to-all-start = ((bf16[8,32,2048]{2,1,0:T(8,128)(2,1)}), bf16[8,32,2048]{2,1,0:T(8,128)(2,1)S(1)}, u32[]{:S(2)}, u32[]{:S(2)}) async-start(bf16[8,32,2048]{2,1,0:T(8,128)(2,1)} %bitcast.3), calls=%async_computation | async-start | bytes 2097152 | tf_op jit(solution)/shard_map/all_to_all | solution.py:360
  10.7 10.9 %copy-start.7 = (bf16[2048,256]{1,0:T(8,128)(2,1)S(1)}, bf16[2048,256]{1,0:T(8,128)(2,1)}, u32[]{:S(2)}) copy-start(bf16[2048,256]{1,0:T(8,128)(2,1)} %param.21) | copy-start | bytes 3145732
  10.7 10.9 %copy-start.8 = (bf16[2048,256]{1,0:T(8,128)(2,1)S(1)}, bf16[2048,256]{1,0:T(8,128)(2,1)}, u32[]{:S(2)}) copy-start(bf16[2048,256]{1,0:T(8,128)(2,1)} %param.20) | copy-start | bytes 3145732
  11.6 11.5 %collective-permute-start = (bf16[2,64,128]{2,1,0:T(8,128)(2,1)S(1)}, bf16[2,64,128]{2,1,0:T(8,128)(2,1)S(1)}, u32[]{:S(2)}, u32[]{:S(2)}) collective-permute-start(bf16[2,64,128]{2,1,0:T(8,128)(2,1)S(1)} %get-tuple-element.117), channel_id=1, source_target_pairs={{0,8},{8,16},{16,24},{24,32},{32,40},{40,48},{48,56},{56,64},{64,7... | collective-permute-start | bytes 98312 | tf_op jit(solution)/shard_map/ppermute | solution.py:365
  16.0 9.6 %copy-start.6 = (f32[2048]{0:T(1024)S(1)}, f32[2048]{0:T(1024)}, u32[]{:S(2)}) copy-start(f32[2048]{0:T(1024)} %param.18) | copy-start | bytes 24580
  16.1 7.1 %collective-permute-start.1 = (bf16[2,64,128]{2,1,0:T(8,128)(2,1)S(1)}, bf16[2,64,128]{2,1,0:T(8,128)(2,1)S(1)}, u32[]{:S(2)}, u32[]{:S(2)}) collective-permute-start(bf16[2,64,128]{2,1,0:T(8,128)(2,1)S(1)} %get-tuple-element.118), channel_id=1, source_target_pairs={{8,0},{16,8},{24,16},{32,24},{40,32},{48,40},{56,48},{64,56},{72,6... | collective-permute-start | bytes 98312 | tf_op jit(solution)/shard_map/ppermute | solution.py:367
  21.6 9.7 %copy-start.10 = (bf16[9,64,64]{2,1,0:T(8,128)(2,1)S(1)}, bf16[9,64,64]{2,1,0:T(8,128)(2,1)}, u32[]{:S(2)}) copy-start(bf16[9,64,64]{2,1,0:T(8,128)(2,1)} %param.24) | copy-start | bytes 221188
  21.6 10.0 %copy-start.9 = (bf16[9,64,64]{2,1,0:T(8,128)(2,1)S(1)}, bf16[9,64,64]{2,1,0:T(8,128)(2,1)}, u32[]{:S(2)}) copy-start(bf16[9,64,64]{2,1,0:T(8,128)(2,1)} %param.26) | copy-start | bytes 221188
  26.9 18.0 %all-to-all-start.1 = ((bf16[8,32,2048]{2,1,0:T(8,128)(2,1)}), bf16[8,32,2048]{2,1,0:T(8,128)(2,1)}, u32[]{:S(2)}, u32[]{:S(2)}) async-start(bf16[8,32,2048]{2,1,0:T(8,128)(2,1)} %norm_slab.1), calls=%async_computation.1 | async-start | bytes 2097152 | tf_op jit(solution)/shard_map/all_to_all | solution.py:376
  47.5 8.6 %collective-permute-start.7 = (bf16[256,512]{1,0:T(8,128)(2,1)S(1)}, bf16[256,512]{1,0:T(8,128)(2,1)S(1)}, u32[]{:S(2)}, u32[]{:S(2)}) collective-permute-start(bf16[256,512]{1,0:T(8,128)(2,1)S(1)} %convolution_convert_fusion.1.refs_4_), channel_id=1, source_target_pairs={{0,112},{16,0},{32,16},{48,32},{64,48},{80,64},{96,80},{112,96},{1... | collective-permute-start | bytes 786440 | tf_op jit(solution)/shard_map/ppermute | solution.py:392
  52.8 6.4 %collective-permute-start.5 = (bf16[256,512]{1,0:T(8,128)(2,1)S(1)}, bf16[256,512]{1,0:T(8,128)(2,1)S(1)}, u32[]{:S(2)}, u32[]{:S(2)}) collective-permute-start(bf16[256,512]{1,0:T(8,128)(2,1)S(1)} %convolution_convert_fusion.1.refs_4_), channel_id=1, source_target_pairs={{0,16},{16,32},{32,48},{48,64},{64,80},{80,96},{96,112},{112,0},{1... | collective-permute-start | bytes 786440 | tf_op jit(solution)/shard_map/ppermute | solution.py:391
  56.1 21.2 %collective-permute-start.8 = (bf16[256,512]{1,0:T(8,128)(2,1)S(1)}, bf16[256,512]{1,0:T(8,128)(2,1)S(1)}, u32[]{:S(2)}, u32[]{:S(2)}) collective-permute-start(bf16[256,512]{1,0:T(8,128)(2,1)S(1)} %collective-permute-done.7.refs_6_), channel_id=1, source_target_pairs={{0,112},{16,0},{32,16},{48,32},{64,48},{80,64},{96,80},{112,96},{1... | collective-permute-start | bytes 786440 | tf_op jit(solution)/shard_map/ppermute | solution.py:397
  59.3 18.1 %collective-permute-start.6 = (bf16[256,512]{1,0:T(8,128)(2,1)S(1)}, bf16[256,512]{1,0:T(8,128)(2,1)S(1)}, u32[]{:S(2)}, u32[]{:S(2)}) collective-permute-start(bf16[256,512]{1,0:T(8,128)(2,1)S(1)} %collective-permute-done.5.refs_5_), channel_id=1, source_target_pairs={{0,16},{16,32},{32,48},{48,64},{64,80},{80,96},{96,112},{112,0},{1... | collective-permute-start | bytes 786440 | tf_op jit(solution)/shard_map/ppermute | solution.py:396
  61.3 8.4 %collective-permute-start.4 = (bf16[256,256]{1,0:T(8,128)(2,1)S(1)}, bf16[256,256]{1,0:T(8,128)(2,1)S(1)}, u32[]{:S(2)}, u32[]{:S(2)}) collective-permute-start(bf16[256,256]{1,0:T(8,128)(2,1)S(1)} %convolution_convert_fusion.2.refs_0_), channel_id=1, source_target_pairs={{0,8},{8,0},{128,136},{136,128},{1,9},{9,1},{129,137},{137,129},{2... | collective-permute-start | bytes 393224 | tf_op jit(solution)/shard_map/ppermute | solution.py:394
  65.7 6.7 %collective-permute-start.3 = (bf16[256,256]{1,0:T(8,128)(2,1)S(1)}, bf16[256,256]{1,0:T(8,128)(2,1)S(1)}, u32[]{:S(2)}, u32[]{:S(2)}) collective-permute-start(bf16[256,256]{1,0:T(8,128)(2,1)S(1)} %convolution_convert_fusion.2.refs_0_), channel_id=1, source_target_pairs={{0,136},{8,128},{128,8},{136,0},{1,137},{9,129},{129,9},{137,1},{2... | collective-permute-start | bytes 393224 | tf_op jit(solution)/shard_map/ppermute | solution.py:394
  68.5 6.2 %collective-permute-start.2 = (bf16[256,256]{1,0:T(8,128)(2,1)S(1)}, bf16[256,256]{1,0:T(8,128)(2,1)S(1)}, u32[]{:S(2)}, u32[]{:S(2)}) collective-permute-start(bf16[256,256]{1,0:T(8,128)(2,1)S(1)} %convolution_convert_fusion.2.refs_0_), channel_id=1, source_target_pairs={{0,128},{8,136},{128,0},{136,8},{1,129},{9,137},{129,1},{137,9},{2... | collective-permute-start | bytes 393224 | tf_op jit(solution)/shard_map/ppermute | solution.py:394
  69.7 36.6 %copy-start.12 = (f32[64]{0:T(128)S(1)}, f32[64]{0:T(128)}, u32[]{:S(2)}) copy-start(f32[64]{0:T(128)} %param.25) | copy-start | bytes 772
  77.3 10.6 %collective-permute-start.9 = (bf16[256,512]{1,0:T(8,128)(2,1)S(1)}, bf16[256,512]{1,0:T(8,128)(2,1)S(1)}, u32[]{:S(2)}, u32[]{:S(2)}) collective-permute-start(bf16[256,512]{1,0:T(8,128)(2,1)S(1)} %collective-permute-done.6.refs_4_), channel_id=1, source_target_pairs={{0,16},{16,32},{32,48},{48,64},{64,80},{80,96},{96,112},{112,0},{1... | collective-permute-start | bytes 786440 | tf_op jit(solution)/shard_map/ppermute | solution.py:410
  77.6 10.3 %collective-permute-start.10 = (bf16[256,512]{1,0:T(8,128)(2,1)S(1)}, bf16[256,512]{1,0:T(8,128)(2,1)S(1)}, u32[]{:S(2)}, u32[]{:S(2)}) collective-permute-start(bf16[256,512]{1,0:T(8,128)(2,1)S(1)} %collective-permute-done.8.refs_5_), channel_id=1, source_target_pairs={{0,112},{16,0},{32,16},{48,32},{64,48},{80,64},{96,80},{112,96},{1... | collective-permute-start | bytes 786440 | tf_op jit(solution)/shard_map/ppermute | solution.py:411
  80.6 7.3 %collective-permute-start.11 = (bf16[16,64]{1,0:T(8,128)(2,1)S(1)}, bf16[16,64]{1,0:T(8,128)(2,1)S(1)}, u32[]{:S(2)}, u32[]{:S(2)}) collective-permute-start(bf16[16,64]{1,0:T(8,128)(2,1)S(1)} %bitcast.78), channel_id=1, source_target_pairs={{1,0},{2,1},{3,2},{4,3},{5,4},{6,5},{7,6},{9,8},{10,9},{11,10},{12... | collective-permute-start | bytes 6152 | tf_op jit(solution)/shard_map/ppermute | solution.py:404
  81.9 6.0 %collective-permute-start.12 = (bf16[16,64]{1,0:T(8,128)(2,1)S(1)}, bf16[16,64]{1,0:T(8,128)(2,1)S(1)}, u32[]{:S(2)}, u32[]{:S(2)}) collective-permute-start(bf16[16,64]{1,0:T(8,128)(2,1)S(1)} %bitcast.77), channel_id=1, source_target_pairs={{0,1},{1,2},{2,3},{3,4},{4,5},{5,6},{6,7},{8,9},{9,10},{10,11},{11... | collective-permute-start | bytes 6152 | tf_op jit(solution)/shard_map/ppermute | solution.py:405
  88.0 5.1 %collective-permute-start.13 = (bf16[128,512]{1,0:T(8,128)(2,1)S(1)}, bf16[128,512]{1,0:T(8,128)(2,1)S(1)}, u32[]{:S(2)}, u32[]{:S(2)}) collective-permute-start(bf16[128,512]{1,0:T(8,128)(2,1)S(1)} %slice.40), channel_id=1, source_target_pairs={{0,16},{16,32},{32,48},{48,64},{64,80},{80,96},{96,112},{112,0},{1... | collective-permute-start | bytes 393224 | tf_op jit(solution)/shard_map/ppermute | solution.py:410
  88.1 5.0 %collective-permute-start.14 = (bf16[128,512]{1,0:T(8,128)(2,1)S(1)}, bf16[128,512]{1,0:T(8,128)(2,1)S(1)}, u32[]{:S(2)}, u32[]{:S(2)}) collective-permute-start(bf16[128,512]{1,0:T(8,128)(2,1)S(1)} %slice.41), channel_id=1, source_target_pairs={{0,112},{16,0},{32,16},{48,32},{64,48},{80,64},{96,80},{112,96},{1... | collective-permute-start | bytes 393224 | tf_op jit(solution)/shard_map/ppermute | solution.py:411
  99.7 6.7 %collective-permute-start.15 = (bf16[272,256]{1,0:T(8,128)(2,1)S(1)}, bf16[272,256]{1,0:T(8,128)(2,1)S(1)}, u32[]{:S(2)}, u32[]{:S(2)}) collective-permute-start(bf16[272,256]{1,0:T(8,128)(2,1)S(1)} %get-tuple-element.97), channel_id=1, source_target_pairs={{0,128},{8,136},{128,0},{136,8},{1,129},{9,137},{129,1},{137,9},{2... | collective-permute-start | bytes 417800 | tf_op jit(solution)/shard_map/ppermute | solution.py:427
  102.9 8.3 %collective-permute-start.16 = (bf16[272,256]{1,0:T(8,128)(2,1)S(1)}, bf16[272,256]{1,0:T(8,128)(2,1)S(1)}, u32[]{:S(2)}, u32[]{:S(2)}) collective-permute-start(bf16[272,256]{1,0:T(8,128)(2,1)S(1)} %get-tuple-element.98), channel_id=1, source_target_pairs={{0,136},{8,128},{128,8},{136,0},{1,137},{9,129},{129,9},{137,1},{2... | collective-permute-start | bytes 417800 | tf_op jit(solution)/shard_map/ppermute | solution.py:427
  106.2 5.0 %collective-permute-start.17 = (bf16[272,256]{1,0:T(8,128)(2,1)S(1)}, bf16[272,256]{1,0:T(8,128)(2,1)S(1)}, u32[]{:S(2)}, u32[]{:S(2)}) collective-permute-start(bf16[272,256]{1,0:T(8,128)(2,1)S(1)} %get-tuple-element.99), channel_id=1, source_target_pairs={{0,8},{8,0},{128,136},{136,128},{1,9},{9,1},{129,137},{137,129},{2... | collective-permute-start | bytes 417800 | tf_op jit(solution)/shard_map/ppermute | solution.py:427
  112.5 20.1 %copy-start.2 = (bf16[144,1024]{1,0:T(8,128)(2,1)S(1)}, bf16[144,1024]{1,0:T(8,128)(2,1)}, u32[]{:S(2)}) copy-start(bf16[144,1024]{1,0:T(8,128)(2,1)} %constant.67.clone.spread) | copy-start | bytes 884740
  112.5 20.1 %copy-start.4 = (bf16[32,1024]{1,0:T(8,128)(2,1)S(1)}, bf16[32,1024]{1,0:T(8,128)(2,1)}, u32[]{:S(2)}) copy-start(bf16[32,1024]{1,0:T(8,128)(2,1)} %constant.68.clone.edges) | copy-start | bytes 196612
  112.5 14.4 %all-to-all-start.2 = ((bf16[8,2,144,128]{3,2,1,0:T(8,128)(2,1)}), bf16[8,2,144,128]{3,2,1,0:T(8,128)(2,1)S(1)}, u32[]{:S(2)}, u32[]{:S(2)}) async-start(bf16[8,2,144,128]{3,2,1,0:T(8,128)(2,1)} %merge_heads.1), calls=%async_computation.2 | async-start | bytes 1179648 | tf_op jit(solution)/shard_map/all_to_all | solution.py:428
  127.0 5.5 %collective-permute-start.19 = (bf16[144,128]{1,0:T(8,128)(2,1)S(1)}, bf16[144,128]{1,0:T(8,128)(2,1)S(1)}, u32[]{:S(2)}, u32[]{:S(2)}) collective-permute-start(bf16[144,128]{1,0:T(8,128)(2,1)S(1)} %get-tuple-element.115), channel_id=1, source_target_pairs={{8,16},{24,32},{40,48},{56,64},{72,80},{88,96},{104,112},{120,128}... | collective-permute-start | bytes 110600 | tf_op jit(solution)/shard_map/ppermute | solution.py:432
  130.9 1.6 collective-permute-start.18
  (4 other events, 9.8 us)

commit v5 on v4

--- a/solution.py
+++ b/solution.py
@@ -57,12 +57,13 @@
     )(near(patches), near(weights), near(offsets))
 
 
-def norm_body(pieces, gain, out):
+def norm_body(pieces, gain, out, slab):
     total = pieces[0].astype(F32)
     for k in range(1, 8):
         total = total + pieces[k].astype(F32)
     scale = lax.rsqrt(jnp.mean(total * total, axis=1, keepdims=True) + 1e-05)
     normed = (total * scale * gain[...]).astype(BF)
+    slab[...] = normed
     for k in range(8):
         out[k] = normed
 
@@ -70,9 +71,9 @@
 def norm_copies(pieces, gain):
     return pl.pallas_call(
         norm_body,
-        out_shape=pltpu.VMEM((8, 32, D), BF),
+        out_shape=[pltpu.VMEM((8, 32, D), BF), pltpu.VMEM((32, D), BF)],
         in_specs=[VMEM_SPEC] * 2,
-        out_specs=VMEM_SPEC,
+        out_specs=[VMEM_SPEC] * 2,
         compiler_params=pltpu.CompilerParams(vmem_limit_bytes=12 * 2**20),
         name="norm_slab",
     )(near(pieces), near(gain))
@@ -86,11 +87,15 @@
         if not first:
             stat_in, acc_in = rest[0], rest[1]
             rest = rest[2:]
+        if last:
+            stat_scr, acc_scr, whole = rest[blocks], rest[blocks + 1], rest[blocks + 2]
+            for k in range(chunks):
+                whole[k * 128 : (k + 1) * 128, :] = kv_refs[k][...]
+            kv_refs = [whole]
         for block in range(blocks):
             for part in range(2):
                 inner = slice(part * 128, (part + 1) * 128)
                 cols = slice(block * 256 + part * 128, block * 256 + (part + 1) * 128)
-                stats = []
                 for h in range(2):
                     head = slice(h * HD, (h + 1) * HD)
                     vals = slice(256 + h * HD, 256 + (h + 1) * HD)
@@ -117,23 +122,26 @@
                         state = (top, total, update)
                     top, total, update = state
                     if last:
-                        rest[block][head, inner] = (update * (1.0 / total)).astype(BF)
-                        lse = top + jnp.log2(total)
-                        high = lse.astype(BF)
-                        left = lse - high.astype(F32)
-                        mid = left.astype(BF)
-                        low = (left - mid.astype(F32)).astype(BF)
-                        stats += [high.astype(F32), mid.astype(F32), low.astype(F32)]
+                        acc_scr[head, cols] = update
+                        stat_scr[h : h + 1, cols] = top
+                        stat_scr[2 + h : 3 + h, cols] = total
                     else:
                         rest[1][head, cols] = update
-                        stats += [top, total]
-                if last:
-                    stats.append(jnp.zeros((10, 128), F32))
-                    rest[block][256:272, inner] = jnp.concatenate(stats, axis=0).astype(BF)
-                else:
-                    for h in range(2):
-                        rest[0][h : h + 1, cols] = stats[2 * h]
-                        rest[0][2 + h : 3 + h, cols] = stats[2 * h + 1]
+                        rest[0][h : h + 1, cols] = top
+                        rest[0][2 + h : 3 + h, cols] = total
+        if last:
+            rows = []
+            for r in (0, 2, 1, 3):
+                value = stat_scr[r : r + 1, :]
+                high = value.astype(BF).astype(F32)
+                mid = (value - high).astype(BF).astype(F32)
+                rows += [high, mid, value - high - mid]
+            rows.append(jnp.zeros((4, 256 * blocks), F32))
+            tail = jnp.concatenate(rows, axis=0).astype(BF)
+            for block in range(blocks):
+                cols = slice(block * 256, (block + 1) * 256)
+                rest[block][0:256, :] = acc_scr[:, cols].astype(BF)
+                rest[block][256:272, :] = tail[:, cols]
 
     return body
 
@@ -154,48 +162,64 @@
         out_shape=outs,
         in_specs=[VMEM_SPEC] * len(ins),
         out_specs=[VMEM_SPEC] * len(outs),
+        scratch_shapes=[
+            pltpu.VMEM((8, 256 * blocks), F32),
+            pltpu.VMEM((256, 256 * blocks), F32),
+            pltpu.VMEM((256, 512), BF),
+        ]
+        if last
+        else [],
         compiler_params=pltpu.CompilerParams(vmem_limit_bytes=12 * 2**20),
         name="flash_last" if last else "flash_step",
     )(*[near(x) for x in ins])
 
 
-def merge_body(b0, b1, b2, b3, mat, out):
+def merge_body(place, base, b0, b1, b2, b3, mat, out):
     parts = (b0, b1, b2, b3)
+    tails = [b[256:272, :].astype(F32) for b in parts]
     context = []
     for h in range(2):
         head = slice(h * HD, (h + 1) * HD)
-        lses = []
-        for b in parts:
-            tail = b[256:272, :].astype(F32)
-            lses.append(tail[3 * h : 3 * h + 1] + tail[3 * h + 1 : 3 * h + 2] + tail[3 * h + 2 : 3 * h + 3])
-        top = jnp.maximum(jnp.maximum(lses[0], lses[1]), jnp.maximum(lses[2], lses[3]))
-        ws = [jnp.exp2(v - top) for v in lses]
-        total = ws[0] + ws[1] + ws[2] + ws[3]
-        mixed = sum(b[head, :].astype(F32) * (w / total) for b, w in zip(parts, ws))
+
+        def whole(tail, row):
+            return tail[row : row + 1] + tail[row + 1 : row + 2] + tail[row + 2 : row + 3]
+
+        tops = [whole(tail, 6 * h) for tail in tails]
+        top = jnp.maximum(jnp.maximum(tops[0], tops[1]), jnp.maximum(tops[2], tops[3]))
+        ws = [jnp.exp2(v - top) for v in tops]
+        total = sum(whole(tail, 6 * h + 3) * w for tail, w in zip(tails, ws))
+        share = 1.0 / total
+        mixed = sum(b[head, :].astype(F32) * (w * share) for b, w in zip(parts, ws))
         context.append(mixed.astype(BF))
     up = dot_tn(jnp.concatenate(context, axis=0), mat[...])
+    own = place[0]
     for j in range(8):
+        lower = jnp.where(own == j - 1, base[31:32, :], 0.0)
+        upper = jnp.where(own == j + 1, base[0:1, :], 0.0)
         for half in range(2):
             rows = []
             for k in range(4):
                 lanes = slice((half * 4 + k) * 128, (half * 4 + k + 1) * 128)
                 out[j, half, k * 32 : (k + 1) * 32, :] = up[32 * j : 32 * j + 32, lanes].astype(BF)
                 token = 32 * j + 32 if k % 2 == 0 else 32 * j - 1
-                inside = 0 <= token < 256
-                rows.append(up[token : token + 1, lanes] if inside else jnp.zeros((1, 128), F32))
+                edge = upper if k % 2 == 0 else lower
+                if 0 <= token < 256:
+                    rows.append(up[token : token + 1, lanes] + edge[:, lanes])
+                else:
+                    rows.append(jnp.zeros((1, 128), F32))
             rows.append(jnp.zeros((12, 128), F32))
             out[j, half, 128:144, :] = jnp.concatenate(rows, axis=0).astype(BF)
 
 
-def merge(parts, mat):
+def merge(place, base, parts, mat):
     return pl.pallas_call(
         merge_body,
         out_shape=pltpu.VMEM((8, 2, 144, 128), BF),
-        in_specs=[VMEM_SPEC] * 5,
+        in_specs=[SMEM_SPEC] + [VMEM_SPEC] * 6,
         out_specs=VMEM_SPEC,
         compiler_params=pltpu.CompilerParams(vmem_limit_bytes=12 * 2**20),
         name="merge_heads",
-    )(*[near(x) for x in parts], near(mat))
+    )(place, near(base), *[near(x) for x in parts], near(mat))
 
 
 def spread_matrix():
@@ -369,13 +393,17 @@
         axis=0,
     )
     pieces, up_mat, wkv, grad_rows = lax.optimization_barrier((pieces, up_mat, wkv, grad_rows))
-    spread_out = norm_copies(pieces, agg_gain.reshape(1, D))
-    spread_out, grad_rows, conv1, conv2, bias1 = lax.optimization_barrier(
-        (spread_out, grad_rows, conv1, conv2, bias1)
+    spread_out, slab = norm_copies(pieces, agg_gain.reshape(1, D))
+    spread_out, slab, grad_rows, conv1, conv2, bias1 = lax.optimization_barrier(
+        (spread_out, slab, grad_rows, conv1, conv2, bias1)
     )
     normed = lax.all_to_all(spread_out, VAR, 0, 0).reshape(256, D)
     edge_right = jnp.transpose(grad_rows[:, :, 0:2], (2, 0, 1)).reshape(16, C)
     edge_left = jnp.transpose(grad_rows[:, :, 126:128], (2, 0, 1)).reshape(16, C)
+    from_right = lax.ppermute(edge_right, VAR, [(i + 1, i) for i in range(7)])
+    from_left = lax.ppermute(edge_left, VAR, [(i, i + 1) for i in range(7)])
+    rim = jnp.concatenate([from_right, from_left], axis=0)
+    base = jnp.dot(slab, w_up, preferred_element_type=F32)
     mats = jnp.stack(
         [tap_matrix(conv1), tap_matrix(flipped(conv2)), tap_matrix(conv2), tap_matrix(flipped(conv1))]
     )
@@ -383,8 +411,8 @@
     flags = jnp.stack(
         [band_at > 0, band_at < 31, var_at > 0, var_at < 7, core_at > 0]
     ).astype(jnp.int32)
-    normed, edge_right, edge_left, mats, bias, flags = lax.optimization_barrier(
-        (normed, edge_right, edge_left, mats, bias, flags)
+    normed, rim, base, mats, bias, flags = lax.optimization_barrier(
+        (normed, rim, base, mats, bias, flags)
     )
 
     keyvals = jnp.dot(normed, wkv, preferred_element_type=F32).astype(BF)
@@ -395,14 +423,8 @@
     fresh = [keyvals, ahead, behind]
     ahead = lax.ppermute(ahead, "z", turn(8, 1))
     behind = lax.ppermute(behind, "z", turn(8, -1))
-    padded = jnp.pad(normed, ((1, 1), (0, 0)))
-    around = lax.dynamic_slice_in_dim(padded, var_at * 32, 34, 0)
     carry = flash_step(all_queries, fresh, None, False)
-    ahead, behind, carry, edge_right, edge_left, around = lax.optimization_barrier(
-        (ahead, behind, carry, edge_right, edge_left, around)
-    )
-    from_right = lax.ppermute(edge_right, VAR, [(i + 1, i) for i in range(7)])
-    from_left = lax.ppermute(edge_left, VAR, [(i, i + 1) for i in range(7)])
+    ahead, behind, carry = lax.optimization_barrier((ahead, behind, carry))
     for step in (2, 3):
         fresh = [ahead, behind]
         if step == 3:
@@ -410,22 +432,15 @@
         ahead = lax.ppermute(ahead, "z", turn(8, 1))
         behind = lax.ppermute(behind, "z", turn(8, -1))
         carry = flash_step(all_queries, fresh, carry, False)
-        ahead, behind, carry, from_right, from_left = lax.optimization_barrier(
-            (ahead, behind, carry, from_right, from_left)
-        )
+        ahead, behind, carry = lax.optimization_barrier((ahead, behind, carry))
     fresh = [ahead, behind]
-    rim = jnp.concatenate([from_right, from_left], axis=0)
-
-    base = jnp.dot(around, w_up, preferred_element_type=F32)
-    base_main = jnp.transpose(base[1:33].reshape(32, 2, 4, 128), (1, 2, 0, 3)).reshape(2, 128, 128)
-    left = base[0].reshape(2, 4, 128)
-    right = base[33].reshape(2, 4, 128)
-    base_rim = jnp.where(jnp.arange(4)[None, :, None] % 2 == 0, right, left)
-    base_all = jnp.concatenate([base_main, base_rim, jnp.zeros((2, 12, 128), F32)], axis=1)
 
     blocks = flash_step(all_queries, fresh, carry, True)
     parts = [blocks[0]] + [lax.ppermute(b, group, flip(4, k)) for b, k in zip(blocks[1:], (2, 3, 1))]
-    pieces = lax.all_to_all(merge(parts, up_mat), VAR, 0, 0)
+    place = var_at.reshape(1).astype(jnp.int32)
+    pieces = lax.all_to_all(merge(place, base, parts, up_mat), VAR, 0, 0)
+    base_main = jnp.transpose(base.reshape(32, 2, 4, 128), (1, 2, 0, 3)).reshape(2, 128, 128)
+    base_all = jnp.pad(base_main, ((0, 0), (0, 16), (0, 0)))
     up = (jnp.sum(pieces.astype(F32), axis=0) + base_all).astype(BF)
     near_up = lax.ppermute(lax.dynamic_index_in_dim(up, 1 - core_at, 0, False), "core", flip(2, 1))
     pairs = [(i, i + 1) for i in range(1, 31, 2)] + [(i + 1, i) for i in range(1, 31, 2)]

time: 180 us -> 174 us (0.967)
  Pallas kernels: 19.9 us -> 14.5 us
  local copies, waits for them, and re-layouts: 8.17 us -> 12.8 us
  waiting for transfers between devices: 35 us -> 31.2 us
    all_to_all x1, waiting for transfers between devices: 11.8 us -> 0.01 us  [device_step(): normed = lax.all_to_all(spread_out, VAR, 0, 0).reshape(256, D)]
    pallas_call x4, Pallas kernels: 13.2 us -> 7.83 us  [flash_step(): pl.pallas_call(flash_kernel(blocks, len(chunks), first, last), out_shape=...]
    all_to_all x1, waiting for transfers between devices: 5.94 us -> 9.49 us  [device_step(): pieces = lax.all_to_all(merge(place, base, parts, up_mat), VAR, 0, 0)]
    ppermute x3, waiting for transfers between devices: 0.37 us -> 3.7 us  [device_step(): ahead = lax.ppermute(ahead, 'z', turn(8, 1))]
    another operation x4, local copies, waits for them, and re-layouts: 0.66 us -> 3.22 us  [device_step(): jnp.stack([tap_matrix(conv1), tap_matrix(flipped(conv2)), tap_matrix(conv...]
    reshape x4, local copies, waits for them, and re-layouts: 0.59 us -> 2.4 us  [tap_matrix(): weight.reshape(3, 3, C, C)]
  transfers between devices with their start and end apart: 23 -> 23, of which waited for: 9 -> 10; matrix products, arithmetic and copies ran while one was open for 8% -> 11% of each run, Pallas kernels for 4% -> 4%
where the time goes in v5:
time: 174 us
  starting transfers between devices  60.9 us (35%)
  blocking collectives  40.8 us (23%)
  waiting for transfers between devices  31.2 us (18%)
  Pallas kernels  14.5 us (8%)
  local copies, waits for them, and re-layouts  12.8 us (7%)
  matrix products  10.4 us (6%)
  other arithmetic  1.84 us (1%)
    all_to_all x2, blocking collectives, copies(): lax.all_to_all(jnp.broadcast_to(piece[None], (count,) + piece.shape), axi...  22.7 us
    all_to_all x1, blocking collectives, device_step(): shares = lax.all_to_all(terms.reshape(32, 24, 128), PLANE, 0, 0)  18.1 us
    all_to_all x1, waiting for transfers between devices, device_step(): pieces = lax.all_to_all(merge(place, base, parts, up_mat), VAR, 0, 0)  9.49 us
    ppermute x3, starting transfers between devices, device_step(): behind = lax.ppermute(behind, 'z', turn(8, -1))  8.81 us
    pallas_call x4, Pallas kernels, flash_step(): pl.pallas_call(flash_kernel(blocks, len(chunks), first, last), out_shape=...  7.83 us
    ppermute x3, starting transfers between devices, device_step(): lax.ppermute(queries, group, flip(4, k))  7.61 us
    ppermute x3, starting transfers between devices, device_step(): lax.ppermute(b, group, flip(4, k))  6.45 us
    all_to_all x1, starting transfers between devices, device_step(): pieces = lax.all_to_all(merge(place, base, parts, up_mat), VAR, 0, 0)  6.18 us
  transfers between devices with their start and end apart: 23, of which 10 were waited for; matrix products, arithmetic and copies ran while one was open for 11% of the time, Pallas kernels for 4%

profile of v5, /device:TPU:1, one launch (start us, length us, event | category | flops | bytes accessed | tf_op | source)
XLA Modules:
  0.0 173.5 jit_solution(3927624491144928132)
XLA Ops:
  4.8 5.9 %all-to-all-start = ((bf16[8,32,2048]{2,1,0:T(8,128)(2,1)}), bf16[8,32,2048]{2,1,0:T(8,128)(2,1)S(1)}, u32[]{:S(2)}, u32[]{:S(2)}) async-start(bf16[8,32,2048]{2,1,0:T(8,128)(2,1)} %bitcast.3), calls=%async_computation | async-start | bytes 2097152 | tf_op jit(solution)/shard_map/all_to_all | solution.py:384
  11.7 4.4 %collective-permute-start = (bf16[2,64,128]{2,1,0:T(8,128)(2,1)S(1)}, bf16[2,64,128]{2,1,0:T(8,128)(2,1)S(1)}, u32[]{:S(2)}, u32[]{:S(2)}) collective-permute-start(bf16[2,64,128]{2,1,0:T(8,128)(2,1)S(1)} %get-tuple-element.107), channel_id=1, source_target_pairs={{0,8},{8,16},{16,24},{24,32},{32,40},{40,48},{48,56},{56,64},{64,7... | collective-permute-start | bytes 98312 | tf_op jit(solution)/shard_map/ppermute | solution.py:389
  16.1 2.1 %collective-permute-start.1 = (bf16[2,64,128]{2,1,0:T(8,128)(2,1)S(1)}, bf16[2,64,128]{2,1,0:T(8,128)(2,1)S(1)}, u32[]{:S(2)}, u32[]{:S(2)}) collective-permute-start(bf16[2,64,128]{2,1,0:T(8,128)(2,1)S(1)} %get-tuple-element.108), channel_id=1, source_target_pairs={{8,0},{16,8},{24,16},{32,24},{40,32},{48,40},{56,48},{64,56},{72,6... | collective-permute-start | bytes 98312 | tf_op jit(solution)/shard_map/ppermute | solution.py:391
  18.1 3.4 %convolution_convert_fusion.mat = bf16[256,1024]{1,0:T(8,128)(2,1)S(1)} fusion(bf16[256,2048]{1,0:T(8,128)(2,1)S(1)} %copy-done, bf16[2048,1024]{1,0:T(8,128)(2,1)} %param.23), kind=kOutput, calls=%fused_computation.1 | convolution fusion | flops 1074003968 | bytes 5767168 | tf_op jit(solution)/shard_map/dot_general | solution.py:385
  23.2 2.4 %all-to-all-done.pieces = bf16[8,32,2048]{2,1,0:T(8,128)(2,1)S(1)} async-done(((bf16[8,32,2048]{2,1,0:T(8,128)(2,1)}), bf16[8,32,2048]{2,1,0:T(8,128)(2,1)S(1)}, u32[]{:S(2)}, u32[]{:S(2)}) %all-to-all-start) | async-done | bytes 1048608 | tf_op jit(solution)/shard_map/all_to_all | solution.py:384
  26.9 3.7 %all-to-all-start.1 = ((bf16[8,32,2048]{2,1,0:T(8,128)(2,1)}), bf16[8,32,2048]{2,1,0:T(8,128)(2,1)S(1)}, u32[]{:S(2)}, u32[]{:S(2)}) async-start(bf16[8,32,2048]{2,1,0:T(8,128)(2,1)} %get-tuple-element.62), calls=%async_computation.1 | async-start | bytes 2097152 | tf_op jit(solution)/shard_map/all_to_all | solution.py:400
  38.1 3.5 %collective-permute-start.3 = (bf16[16,64]{1,0:T(8,128)(2,1)S(1)}, bf16[16,64]{1,0:T(8,128)(2,1)S(1)}, u32[]{:S(2)}, u32[]{:S(2)}) collective-permute-start(bf16[16,64]{1,0:T(8,128)(2,1)S(1)} %bitcast.77), channel_id=1, source_target_pairs={{0,1},{1,2},{2,3},{3,4},{4,5},{5,6},{6,7},{8,9},{9,10},{10,11},{11... | collective-permute-start | bytes 6152 | tf_op jit(solution)/shard_map/ppermute | solution.py:404
  42.9 3.0 %fusion.2.base = f32[32,1024]{1,0:T(8,128)S(1)} fusion(bf16[32,2048]{1,0:T(8,128)(2,1)S(1)} %get-tuple-element.64, bf16[2048,1024]{1,0:T(8,128)(2,1)} %param.23), kind=kOutput, calls=%fused_computation.19 | convolution fusion | flops 134217728 | bytes 4456448 | tf_op jit(solution)/shard_map/dot_general | solution.py:406
  46.2 2.3 %convolution_convert_fusion.1.refs_4_ = bf16[256,512]{1,0:T(8,128)(2,1)S(1)} fusion(bf16[256,2048]{1,0:T(8,128)(2,1)S(1)} %bitcast.63, bf16[2048,512]{1,0:T(8,128)(2,1)} %pad_maximum_fusion), kind=kOutput, calls=%fused_computation.2 | convolution fusion | flops 537001984 | bytes 3407872 | tf_op jit(solution)/shard_map/dot_general | solution.py:418
  48.6 5.7 %collective-permute-start.9 = (bf16[256,512]{1,0:T(8,128)(2,1)S(1)}, bf16[256,512]{1,0:T(8,128)(2,1)S(1)}, u32[]{:S(2)}, u32[]{:S(2)}) collective-permute-start(bf16[256,512]{1,0:T(8,128)(2,1)S(1)} %convolution_convert_fusion.1.refs_4_), channel_id=1, source_target_pairs={{0,112},{16,0},{32,16},{48,32},{64,48},{80,64},{96,80},{112,96},{1... | collective-permute-start | bytes 786440 | tf_op jit(solution)/shard_map/ppermute | solution.py:420
  54.2 3.3 %collective-permute-done.9.refs_6_ = bf16[256,512]{1,0:T(8,128)(2,1)S(1)} collective-permute-done((bf16[256,512]{1,0:T(8,128)(2,1)S(1)}, bf16[256,512]{1,0:T(8,128)(2,1)S(1)}, u32[]{:S(2)}, u32[]{:S(2)}) %collective-permute-start.9) | collective-permute-done | bytes 262176 | tf_op jit(solution)/shard_map/ppermute | solution.py:420
  57.5 3.1 %collective-permute-start.10 = (bf16[256,512]{1,0:T(8,128)(2,1)S(1)}, bf16[256,512]{1,0:T(8,128)(2,1)S(1)}, u32[]{:S(2)}, u32[]{:S(2)}) collective-permute-start(bf16[256,512]{1,0:T(8,128)(2,1)S(1)} %collective-permute-done.9.refs_6_), channel_id=1, source_target_pairs={{0,112},{16,0},{32,16},{48,32},{64,48},{80,64},{96,80},{112,96},{1... | collective-permute-start | bytes 786440 | tf_op jit(solution)/shard_map/ppermute | solution.py:425
  62.3 4.4 %collective-permute-start.6 = (bf16[256,256]{1,0:T(8,128)(2,1)S(1)}, bf16[256,256]{1,0:T(8,128)(2,1)S(1)}, u32[]{:S(2)}, u32[]{:S(2)}) collective-permute-start(bf16[256,256]{1,0:T(8,128)(2,1)S(1)} %convolution_convert_fusion.2.refs_0_), channel_id=1, source_target_pairs={{0,8},{8,0},{128,136},{136,128},{1,9},{9,1},{129,137},{137,129},{2... | collective-permute-start | bytes 393224 | tf_op jit(solution)/shard_map/ppermute | solution.py:422
  66.8 3.1 %collective-permute-start.5 = (bf16[256,256]{1,0:T(8,128)(2,1)S(1)}, bf16[256,256]{1,0:T(8,128)(2,1)S(1)}, u32[]{:S(2)}, u32[]{:S(2)}) collective-permute-start(bf16[256,256]{1,0:T(8,128)(2,1)S(1)} %convolution_convert_fusion.2.refs_0_), channel_id=1, source_target_pairs={{0,136},{8,128},{128,8},{136,0},{1,137},{9,129},{129,9},{137,1},{2... | collective-permute-start | bytes 393224 | tf_op jit(solution)/shard_map/ppermute | solution.py:422
  69.9 3.8 %collective-permute-done.5.refs_2_ = bf16[256,256]{1,0:T(8,128)(2,1)S(1)} collective-permute-done((bf16[256,256]{1,0:T(8,128)(2,1)S(1)}, bf16[256,256]{1,0:T(8,128)(2,1)S(1)}, u32[]{:S(2)}, u32[]{:S(2)}) %collective-permute-start.5) | collective-permute-done | bytes 131104 | tf_op jit(solution)/shard_map/ppermute | solution.py:422
  73.7 2.4 %collective-permute-done.4.refs_1_ = bf16[256,256]{1,0:T(8,128)(2,1)S(1)} collective-permute-done((bf16[256,256]{1,0:T(8,128)(2,1)S(1)}, bf16[256,256]{1,0:T(8,128)(2,1)S(1)}, u32[]{:S(2)}, u32[]{:S(2)}) %collective-permute-start.4) | collective-permute-done | bytes 131104 | tf_op jit(solution)/shard_map/ppermute | solution.py:422
  76.1 2.6 %flash_step.3 = (f32[8,1024]{1,0:T(8,128)S(1)}, f32[256,1024]{1,0:T(8,128)S(1)}) custom-call(bf16[256,256]{1,0:T(8,128)(2,1)S(1)} %convolution_convert_fusion.2.refs_0_, bf16[256,256]{1,0:T(8,128)(2,1)S(1)} %collective-permute-done.4.refs_1_, bf16[256,256]{1,0:T(8,128)(2,1)S(1)} %collective-permute-done.5.refs_2_, ...), custom_call_target="tpu_custom_call" | custom-call | tf_op jit(solution)/shard_map/flash_step/pallas_call | solution.py:160
  78.8 3.0 %collective-permute-start.12 = (bf16[256,512]{1,0:T(8,128)(2,1)S(1)}, bf16[256,512]{1,0:T(8,128)(2,1)S(1)}, u32[]{:S(2)}, u32[]{:S(2)}) collective-permute-start(bf16[256,512]{1,0:T(8,128)(2,1)S(1)} %collective-permute-done.10.refs_5_), channel_id=1, source_target_pairs={{0,112},{16,0},{32,16},{48,32},{64,48},{80,64},{96,80},{112,96},{1... | collective-permute-start | bytes 786440 | tf_op jit(solution)/shard_map/ppermute | solution.py:433
  81.8 2.0 %flash_step.4 = (f32[8,1024]{1,0:T(8,128)S(1)}, f32[256,1024]{1,0:T(8,128)S(1)}) custom-call(bf16[256,256]{1,0:T(8,128)(2,1)S(1)} %convolution_convert_fusion.2.refs_0_, bf16[256,256]{1,0:T(8,128)(2,1)S(1)} %collective-permute-done.4.refs_1_, bf16[256,256]{1,0:T(8,128)(2,1)S(1)} %collective-permute-done.5.refs_2_, ...), custom_call_target="tpu_custom_call" | custom-call | tf_op jit(solution)/shard_map/flash_step/pallas_call | solution.py:160
  83.8 3.3 %collective-permute-done.11.refs_4_ = bf16[256,512]{1,0:T(8,128)(2,1)S(1)} collective-permute-done((bf16[256,512]{1,0:T(8,128)(2,1)S(1)}, bf16[256,512]{1,0:T(8,128)(2,1)S(1)}, u32[]{:S(2)}, u32[]{:S(2)}) %collective-permute-start.11) | collective-permute-done | bytes 262176 | tf_op jit(solution)/shard_map/ppermute | solution.py:432
  87.3 2.7 %collective-permute-start.14 = (bf16[128,512]{1,0:T(8,128)(2,1)S(1)}, bf16[128,512]{1,0:T(8,128)(2,1)S(1)}, u32[]{:S(2)}, u32[]{:S(2)}) collective-permute-start(bf16[128,512]{1,0:T(8,128)(2,1)S(1)} %slice.32), channel_id=1, source_target_pairs={{0,112},{16,0},{32,16},{48,32},{64,48},{80,64},{96,80},{112,96},{1... | collective-permute-start | bytes 393224 | tf_op jit(solution)/shard_map/ppermute | solution.py:433
  90.0 2.0 %flash_step.5 = (f32[8,1024]{1,0:T(8,128)S(1)}, f32[256,1024]{1,0:T(8,128)S(1)}) custom-call(bf16[256,256]{1,0:T(8,128)(2,1)S(1)} %convolution_convert_fusion.2.refs_0_, bf16[256,256]{1,0:T(8,128)(2,1)S(1)} %collective-permute-done.4.refs_1_, bf16[256,256]{1,0:T(8,128)(2,1)S(1)} %collective-permute-done.5.refs_2_, ...), custom_call_target="tpu_custom_call" | custom-call | tf_op jit(solution)/shard_map/flash_step/pallas_call | solution.py:160
  93.6 3.5 %collective-permute-start.15 = (bf16[272,256]{1,0:T(8,128)(2,1)S(1)}, bf16[272,256]{1,0:T(8,128)(2,1)S(1)}, u32[]{:S(2)}, u32[]{:S(2)}) collective-permute-start(bf16[272,256]{1,0:T(8,128)(2,1)S(1)} %get-tuple-element.91), channel_id=1, source_target_pairs={{0,128},{8,136},{128,0},{136,8},{1,129},{9,137},{129,1},{137,9},{2... | collective-permute-start | bytes 417800 | tf_op jit(solution)/shard_map/ppermute | solution.py:439
  97.1 2.8 %collective-permute-start.16 = (bf16[272,256]{1,0:T(8,128)(2,1)S(1)}, bf16[272,256]{1,0:T(8,128)(2,1)S(1)}, u32[]{:S(2)}, u32[]{:S(2)}) collective-permute-start(bf16[272,256]{1,0:T(8,128)(2,1)S(1)} %get-tuple-element.92), channel_id=1, source_target_pairs={{0,136},{8,128},{128,8},{136,0},{1,137},{9,129},{129,9},{137,1},{2... | collective-permute-start | bytes 417800 | tf_op jit(solution)/shard_map/ppermute | solution.py:439
  100.1 4.5 %collective-permute-done.16.b2 = bf16[272,256]{1,0:T(8,128)(2,1)S(1)} collective-permute-done((bf16[272,256]{1,0:T(8,128)(2,1)S(1)}, bf16[272,256]{1,0:T(8,128)(2,1)S(1)}, u32[]{:S(2)}, u32[]{:S(2)}) %collective-permute-start.16) | collective-permute-done | bytes 139296 | tf_op jit(solution)/shard_map/ppermute | solution.py:439
  105.8 6.2 %all-to-all-start.2 = ((bf16[8,2,144,128]{3,2,1,0:T(8,128)(2,1)}), bf16[8,2,144,128]{3,2,1,0:T(8,128)(2,1)S(1)}, u32[]{:S(2)}, u32[]{:S(2)}) async-start(bf16[8,2,144,128]{3,2,1,0:T(8,128)(2,1)} %merge_heads.1), calls=%async_computation.2 | async-start | bytes 1179648 | tf_op jit(solution)/shard_map/all_to_all | solution.py:441
  112.1 9.5 %all-to-all-done.2 = bf16[8,2,144,128]{3,2,1,0:T(8,128)(2,1)S(1)} async-done(((bf16[8,2,144,128]{3,2,1,0:T(8,128)(2,1)}), bf16[8,2,144,128]{3,2,1,0:T(8,128)(2,1)S(1)}, u32[]{:S(2)}, u32[]{:S(2)}) %all-to-all-start.2) | async-done | bytes 589856 | tf_op jit(solution)/shard_map/all_to_all | solution.py:441
  121.7 5.1 %collective-permute-start.19 = (bf16[144,128]{1,0:T(8,128)(2,1)S(1)}, bf16[144,128]{1,0:T(8,128)(2,1)S(1)}, u32[]{:S(2)}, u32[]{:S(2)}) collective-permute-start(bf16[144,128]{1,0:T(8,128)(2,1)S(1)} %get-tuple-element.105), channel_id=1, source_target_pairs={{8,16},{24,32},{40,48},{56,64},{72,80},{88,96},{104,112},{120,128}... | collective-permute-start | bytes 110600 | tf_op jit(solution)/shard_map/ppermute | solution.py:447
  128.4 2.7 %fine_stage.1 = (bf16[4,64,128]{2,1,0:T(8,128)(2,1)}, bf16[4,64,128]{2,1,0:T(8,128)(2,1)}, bf16[768,128]{1,0:T(8,128)(2,1)S(1)}) custom-call(s32[5]{0:T(128)S(1)} %convert_element_type.31.flags, bf16[2,144,128]{2,1,0:T(8,128)(2,1)S(1)} %add_convert_fusion.own, bf16[144,128]{1,0:T(8,128)(2,1)S(1)} %collective-permute-done.18.near_up, ...), custom_call_target="tpu_custom_call" | custom-call | tf_op jit(solution)/shard_map/fine_stage/pallas_call | solution.py:337
  131.2 18.1 %all_to_all.30 = bf16[32,24,128]{2,1,0:T(8,128)(2,1)S(1)} all-to-all(bf16[32,24,128]{2,1,0:T(8,128)(2,1)S(1)} %bitcast.60), channel_id=1, replica_groups=mesh['xh'=2,'z'=8,'core'=2,'y'=4,'xl'=2] {'xh','core','y','xl'}, dimensions={0} | all-to-all | bytes 393216 | tf_op jit(solution)/shard_map/all_to_all | solution.py:453
  149.3 9.4 %all_to_all.31 = bf16[8,24,128]{2,1,0:T(8,128)(2,1)S(1)} all-to-all(bf16[8,24,128]{2,1,0:T(8,128)(2,1)S(1)} %broadcast_in_dim.4), channel_id=1, replica_groups=mesh['xh'=2,'z'=8,'core'=2,'y'=4,'xl'=2] {'z'}, dimensions={0} | all-to-all | bytes 98304 | tf_op jit(solution)/shard_map/all_to_all | solution.py:352
  158.8 13.3 %all_to_all.32 = bf16[32,24,128]{2,1,0:T(8,128)(2,1)S(1)} all-to-all(bf16[32,24,128]{2,1,0:T(8,128)(2,1)S(1)} %broadcast_in_dim.5), channel_id=1, replica_groups=mesh['xh'=2,'z'=8,'core'=2,'y'=4,'xl'=2] {'xh','core','y','xl'}, dimensions={0} | all-to-all | bytes 393216 | tf_op jit(solution)/shard_map/all_to_all | solution.py:352
  (98 shorter events, 25.4 us)
Async XLA Ops:
  0.6 17.5 %copy-start = (bf16[256,2048]{1,0:T(8,128)(2,1)S(1)}, bf16[256,2048]{1,0:T(8,128)(2,1)}, u32[]{:S(2)}) copy-start(bf16[256,2048]{1,0:T(8,128)(2,1)} %param.22) | copy-start | bytes 3145732
  4.8 20.8 %all-to-all-start = ((bf16[8,32,2048]{2,1,0:T(8,128)(2,1)}), bf16[8,32,2048]{2,1,0:T(8,128)(2,1)S(1)}, u32[]{:S(2)}, u32[]{:S(2)}) async-start(bf16[8,32,2048]{2,1,0:T(8,128)(2,1)} %bitcast.3), calls=%async_computation | async-start | bytes 2097152 | tf_op jit(solution)/shard_map/all_to_all | solution.py:384
  10.7 10.9 %copy-start.7 = (bf16[2048,256]{1,0:T(8,128)(2,1)S(1)}, bf16[2048,256]{1,0:T(8,128)(2,1)}, u32[]{:S(2)}) copy-start(bf16[2048,256]{1,0:T(8,128)(2,1)} %param.21) | copy-start | bytes 3145732
  10.7 10.9 %copy-start.8 = (bf16[2048,256]{1,0:T(8,128)(2,1)S(1)}, bf16[2048,256]{1,0:T(8,128)(2,1)}, u32[]{:S(2)}) copy-start(bf16[2048,256]{1,0:T(8,128)(2,1)} %param.20) | copy-start | bytes 3145732
  11.7 11.5 %collective-permute-start = (bf16[2,64,128]{2,1,0:T(8,128)(2,1)S(1)}, bf16[2,64,128]{2,1,0:T(8,128)(2,1)S(1)}, u32[]{:S(2)}, u32[]{:S(2)}) collective-permute-start(bf16[2,64,128]{2,1,0:T(8,128)(2,1)S(1)} %get-tuple-element.107), channel_id=1, source_target_pairs={{0,8},{8,16},{16,24},{24,32},{32,40},{40,48},{48,56},{56,64},{64,7... | collective-permute-start | bytes 98312 | tf_op jit(solution)/shard_map/ppermute | solution.py:389
  16.1 9.6 %copy-start.6 = (f32[2048]{0:T(1024)S(1)}, f32[2048]{0:T(1024)}, u32[]{:S(2)}) copy-start(f32[2048]{0:T(1024)} %param.18) | copy-start | bytes 24580
  16.1 7.1 %collective-permute-start.1 = (bf16[2,64,128]{2,1,0:T(8,128)(2,1)S(1)}, bf16[2,64,128]{2,1,0:T(8,128)(2,1)S(1)}, u32[]{:S(2)}, u32[]{:S(2)}) collective-permute-start(bf16[2,64,128]{2,1,0:T(8,128)(2,1)S(1)} %get-tuple-element.108), channel_id=1, source_target_pairs={{8,0},{16,8},{24,16},{32,24},{40,32},{48,40},{56,48},{64,56},{72,6... | collective-permute-start | bytes 98312 | tf_op jit(solution)/shard_map/ppermute | solution.py:391
  21.6 11.6 %copy-start.9 = (bf16[9,64,64]{2,1,0:T(8,128)(2,1)S(1)}, bf16[9,64,64]{2,1,0:T(8,128)(2,1)}, u32[]{:S(2)}) copy-start(bf16[9,64,64]{2,1,0:T(8,128)(2,1)} %param.26) | copy-start | bytes 221188
  26.9 19.4 %all-to-all-start.1 = ((bf16[8,32,2048]{2,1,0:T(8,128)(2,1)}), bf16[8,32,2048]{2,1,0:T(8,128)(2,1)S(1)}, u32[]{:S(2)}, u32[]{:S(2)}) async-start(bf16[8,32,2048]{2,1,0:T(8,128)(2,1)} %get-tuple-element.62), calls=%async_computation.1 | async-start | bytes 2097152 | tf_op jit(solution)/shard_map/all_to_all | solution.py:400
  36.7 9.2 %copy-start.12 = (bf16[1,192,192]{2,1,0:T(8,128)(2,1)S(1)}, bf16[1,192,192]{2,1,0:T(8,128)(2,1)}, u32[]{:S(2)}) copy-start(bf16[1,192,192]{2,1,0:T(8,128)(2,1)} %stack_reshape.13) | copy-start | bytes 221188
  38.1 8.0 %collective-permute-start.3 = (bf16[16,64]{1,0:T(8,128)(2,1)S(1)}, bf16[16,64]{1,0:T(8,128)(2,1)S(1)}, u32[]{:S(2)}, u32[]{:S(2)}) collective-permute-start(bf16[16,64]{1,0:T(8,128)(2,1)S(1)} %bitcast.77), channel_id=1, source_target_pairs={{0,1},{1,2},{2,3},{3,4},{4,5},{5,6},{6,7},{8,9},{9,10},{10,11},{11... | collective-permute-start | bytes 6152 | tf_op jit(solution)/shard_map/ppermute | solution.py:404
  41.6 4.6 %collective-permute-start.2 = (bf16[16,64]{1,0:T(8,128)(2,1)S(1)}, bf16[16,64]{1,0:T(8,128)(2,1)S(1)}, u32[]{:S(2)}, u32[]{:S(2)}) collective-permute-start(bf16[16,64]{1,0:T(8,128)(2,1)S(1)} %bitcast.76), channel_id=1, source_target_pairs={{1,0},{2,1},{3,2},{4,3},{5,4},{6,5},{7,6},{9,8},{10,9},{11,10},{12... | collective-permute-start | bytes 6152 | tf_op jit(solution)/shard_map/ppermute | solution.py:403
  48.6 9.0 %collective-permute-start.9 = (bf16[256,512]{1,0:T(8,128)(2,1)S(1)}, bf16[256,512]{1,0:T(8,128)(2,1)S(1)}, u32[]{:S(2)}, u32[]{:S(2)}) collective-permute-start(bf16[256,512]{1,0:T(8,128)(2,1)S(1)} %convolution_convert_fusion.1.refs_4_), channel_id=1, source_target_pairs={{0,112},{16,0},{32,16},{48,32},{64,48},{80,64},{96,80},{112,96},{1... | collective-permute-start | bytes 786440 | tf_op jit(solution)/shard_map/ppermute | solution.py:420
  54.2 6.4 %collective-permute-start.7 = (bf16[256,512]{1,0:T(8,128)(2,1)S(1)}, bf16[256,512]{1,0:T(8,128)(2,1)S(1)}, u32[]{:S(2)}, u32[]{:S(2)}) collective-permute-start(bf16[256,512]{1,0:T(8,128)(2,1)S(1)} %convolution_convert_fusion.1.refs_4_), channel_id=1, source_target_pairs={{0,16},{16,32},{32,48},{48,64},{64,80},{80,96},{96,112},{112,0},{1... | collective-permute-start | bytes 786440 | tf_op jit(solution)/shard_map/ppermute | solution.py:419
  57.5 21.1 %collective-permute-start.10 = (bf16[256,512]{1,0:T(8,128)(2,1)S(1)}, bf16[256,512]{1,0:T(8,128)(2,1)S(1)}, u32[]{:S(2)}, u32[]{:S(2)}) collective-permute-start(bf16[256,512]{1,0:T(8,128)(2,1)S(1)} %collective-permute-done.9.refs_6_), channel_id=1, source_target_pairs={{0,112},{16,0},{32,16},{48,32},{64,48},{80,64},{96,80},{112,96},{1... | collective-permute-start | bytes 786440 | tf_op jit(solution)/shard_map/ppermute | solution.py:425
  60.7 18.0 %collective-permute-start.8 = (bf16[256,512]{1,0:T(8,128)(2,1)S(1)}, bf16[256,512]{1,0:T(8,128)(2,1)S(1)}, u32[]{:S(2)}, u32[]{:S(2)}) collective-permute-start(bf16[256,512]{1,0:T(8,128)(2,1)S(1)} %collective-permute-done.7.refs_5_), channel_id=1, source_target_pairs={{0,16},{16,32},{32,48},{48,64},{64,80},{80,96},{96,112},{112,0},{1... | collective-permute-start | bytes 786440 | tf_op jit(solution)/shard_map/ppermute | solution.py:424
  62.3 7.6 %collective-permute-start.6 = (bf16[256,256]{1,0:T(8,128)(2,1)S(1)}, bf16[256,256]{1,0:T(8,128)(2,1)S(1)}, u32[]{:S(2)}, u32[]{:S(2)}) collective-permute-start(bf16[256,256]{1,0:T(8,128)(2,1)S(1)} %convolution_convert_fusion.2.refs_0_), channel_id=1, source_target_pairs={{0,8},{8,0},{128,136},{136,128},{1,9},{9,1},{129,137},{137,129},{2... | collective-permute-start | bytes 393224 | tf_op jit(solution)/shard_map/ppermute | solution.py:422
  66.8 6.9 %collective-permute-start.5 = (bf16[256,256]{1,0:T(8,128)(2,1)S(1)}, bf16[256,256]{1,0:T(8,128)(2,1)S(1)}, u32[]{:S(2)}, u32[]{:S(2)}) collective-permute-start(bf16[256,256]{1,0:T(8,128)(2,1)S(1)} %convolution_convert_fusion.2.refs_0_), channel_id=1, source_target_pairs={{0,136},{8,128},{128,8},{136,0},{1,137},{9,129},{129,9},{137,1},{2... | collective-permute-start | bytes 393224 | tf_op jit(solution)/shard_map/ppermute | solution.py:422
  69.9 6.2 %collective-permute-start.4 = (bf16[256,256]{1,0:T(8,128)(2,1)S(1)}, bf16[256,256]{1,0:T(8,128)(2,1)S(1)}, u32[]{:S(2)}, u32[]{:S(2)}) collective-permute-start(bf16[256,256]{1,0:T(8,128)(2,1)S(1)} %convolution_convert_fusion.2.refs_0_), channel_id=1, source_target_pairs={{0,128},{8,136},{128,0},{136,8},{1,129},{9,137},{129,1},{137,9},{2... | collective-permute-start | bytes 393224 | tf_op jit(solution)/shard_map/ppermute | solution.py:422
  78.7 8.4 %collective-permute-start.11 = (bf16[256,512]{1,0:T(8,128)(2,1)S(1)}, bf16[256,512]{1,0:T(8,128)(2,1)S(1)}, u32[]{:S(2)}, u32[]{:S(2)}) collective-permute-start(bf16[256,512]{1,0:T(8,128)(2,1)S(1)} %collective-permute-done.8.refs_4_), channel_id=1, source_target_pairs={{0,16},{16,32},{32,48},{48,64},{64,80},{80,96},{96,112},{112,0},{1... | collective-permute-start | bytes 786440 | tf_op jit(solution)/shard_map/ppermute | solution.py:432
  78.8 8.4 %collective-permute-start.12 = (bf16[256,512]{1,0:T(8,128)(2,1)S(1)}, bf16[256,512]{1,0:T(8,128)(2,1)S(1)}, u32[]{:S(2)}, u32[]{:S(2)}) collective-permute-start(bf16[256,512]{1,0:T(8,128)(2,1)S(1)} %collective-permute-done.10.refs_5_), channel_id=1, source_target_pairs={{0,112},{16,0},{32,16},{48,32},{64,48},{80,64},{96,80},{112,96},{1... | collective-permute-start | bytes 786440 | tf_op jit(solution)/shard_map/ppermute | solution.py:433
  87.2 39.7 %copy-start.16 = (f32[64]{0:T(128)S(1)}, f32[64]{0:T(128)}, u32[]{:S(2)}) copy-start(f32[64]{0:T(128)} %param.25) | copy-start | bytes 772
  87.2 41.3 %copy-start.2 = (bf16[144,1024]{1,0:T(8,128)(2,1)S(1)}, bf16[144,1024]{1,0:T(8,128)(2,1)}, u32[]{:S(2)}) copy-start(bf16[144,1024]{1,0:T(8,128)(2,1)} %constant.49.clone.spread) | copy-start | bytes 884740
  87.2 41.2 %copy-start.4 = (bf16[32,1024]{1,0:T(8,128)(2,1)S(1)}, bf16[32,1024]{1,0:T(8,128)(2,1)}, u32[]{:S(2)}) copy-start(bf16[32,1024]{1,0:T(8,128)(2,1)} %constant.50.clone.edges) | copy-start | bytes 196612
  87.2 5.1 %collective-permute-start.13 = (bf16[128,512]{1,0:T(8,128)(2,1)S(1)}, bf16[128,512]{1,0:T(8,128)(2,1)S(1)}, u32[]{:S(2)}, u32[]{:S(2)}) collective-permute-start(bf16[128,512]{1,0:T(8,128)(2,1)S(1)} %slice.31), channel_id=1, source_target_pairs={{0,16},{16,32},{32,48},{48,64},{64,80},{80,96},{96,112},{112,0},{1... | collective-permute-start | bytes 393224 | tf_op jit(solution)/shard_map/ppermute | solution.py:432
  87.3 5.0 %collective-permute-start.14 = (bf16[128,512]{1,0:T(8,128)(2,1)S(1)}, bf16[128,512]{1,0:T(8,128)(2,1)S(1)}, u32[]{:S(2)}, u32[]{:S(2)}) collective-permute-start(bf16[128,512]{1,0:T(8,128)(2,1)S(1)} %slice.32), channel_id=1, source_target_pairs={{0,112},{16,0},{32,16},{48,32},{64,48},{80,64},{96,80},{112,96},{1... | collective-permute-start | bytes 393224 | tf_op jit(solution)/shard_map/ppermute | solution.py:433
  93.6 6.5 %collective-permute-start.15 = (bf16[272,256]{1,0:T(8,128)(2,1)S(1)}, bf16[272,256]{1,0:T(8,128)(2,1)S(1)}, u32[]{:S(2)}, u32[]{:S(2)}) collective-permute-start(bf16[272,256]{1,0:T(8,128)(2,1)S(1)} %get-tuple-element.91), channel_id=1, source_target_pairs={{0,128},{8,136},{128,0},{136,8},{1,129},{9,137},{129,1},{137,9},{2... | collective-permute-start | bytes 417800 | tf_op jit(solution)/shard_map/ppermute | solution.py:439
  97.1 7.5 %collective-permute-start.16 = (bf16[272,256]{1,0:T(8,128)(2,1)S(1)}, bf16[272,256]{1,0:T(8,128)(2,1)S(1)}, u32[]{:S(2)}, u32[]{:S(2)}) collective-permute-start(bf16[272,256]{1,0:T(8,128)(2,1)S(1)} %get-tuple-element.92), channel_id=1, source_target_pairs={{0,136},{8,128},{128,8},{136,0},{1,137},{9,129},{129,9},{137,1},{2... | collective-permute-start | bytes 417800 | tf_op jit(solution)/shard_map/ppermute | solution.py:439
  99.8 4.7 %collective-permute-start.17 = (bf16[272,256]{1,0:T(8,128)(2,1)S(1)}, bf16[272,256]{1,0:T(8,128)(2,1)S(1)}, u32[]{:S(2)}, u32[]{:S(2)}) collective-permute-start(bf16[272,256]{1,0:T(8,128)(2,1)S(1)} %get-tuple-element.93), channel_id=1, source_target_pairs={{0,8},{8,0},{128,136},{136,128},{1,9},{9,1},{129,137},{137,129},{2... | collective-permute-start | bytes 417800 | tf_op jit(solution)/shard_map/ppermute | solution.py:439
  105.8 15.8 %all-to-all-start.2 = ((bf16[8,2,144,128]{3,2,1,0:T(8,128)(2,1)}), bf16[8,2,144,128]{3,2,1,0:T(8,128)(2,1)S(1)}, u32[]{:S(2)}, u32[]{:S(2)}) async-start(bf16[8,2,144,128]{3,2,1,0:T(8,128)(2,1)} %merge_heads.1), calls=%async_computation.2 | async-start | bytes 1179648 | tf_op jit(solution)/shard_map/all_to_all | solution.py:441
  121.7 6.7 %collective-permute-start.19 = (bf16[144,128]{1,0:T(8,128)(2,1)S(1)}, bf16[144,128]{1,0:T(8,128)(2,1)S(1)}, u32[]{:S(2)}, u32[]{:S(2)}) collective-permute-start(bf16[144,128]{1,0:T(8,128)(2,1)S(1)} %get-tuple-element.105), channel_id=1, source_target_pairs={{8,16},{24,32},{40,48},{56,64},{72,80},{88,96},{104,112},{120,128}... | collective-permute-start | bytes 110600 | tf_op jit(solution)/shard_map/ppermute | solution.py:447
  126.8 1.6 collective-permute-start.18
  (8 other events, 43.8 us)

commit v6 on v5

--- a/solution.py
+++ b/solution.py
@@ -39,22 +39,25 @@
 
 
 def mix_body(patches, weights, offsets, out):
-    lhs = patches[...]
     offset = offsets[0:1, :] + offsets[1:2, :]
-    for k in range(8):
-        cols = slice(k * 256, (k + 1) * 256)
-        out[:, cols] = (dot_tn(lhs, weights[:, cols]) + offset[:, cols]).astype(BF)
+    out[...] = (dot_tn(patches[...], weights[...]) + offset).astype(BF)
 
 
 def mix(patches, weights, offsets):
+    args = [pltpu.with_memory_space_constraint(x, pltpu.HBM) for x in (patches, weights, offsets)]
     return pl.pallas_call(
         mix_body,
-        out_shape=pltpu.VMEM((256, D), BF),
-        in_specs=[VMEM_SPEC] * 3,
-        out_specs=VMEM_SPEC,
+        grid=(4,),
+        out_shape=jax.ShapeDtypeStruct((256, D), BF),
+        in_specs=[
+            pl.BlockSpec((128, 256), lambda k: (0, 0)),
+            pl.BlockSpec((128, 512), lambda k: (0, k)),
+            pl.BlockSpec((2, 512), lambda k: (0, k)),
+        ],
+        out_specs=pl.BlockSpec((256, 512), lambda k: (0, k)),
         compiler_params=pltpu.CompilerParams(vmem_limit_bytes=12 * 2**20),
         name="mix_variables",
-    )(near(patches), near(weights), near(offsets))
+    )(*args)
 
 
 def norm_body(pieces, gain, out, slab):
@@ -394,8 +397,8 @@
     )
     pieces, up_mat, wkv, grad_rows = lax.optimization_barrier((pieces, up_mat, wkv, grad_rows))
     spread_out, slab = norm_copies(pieces, agg_gain.reshape(1, D))
-    spread_out, slab, grad_rows, conv1, conv2, bias1 = lax.optimization_barrier(
-        (spread_out, slab, grad_rows, conv1, conv2, bias1)
+    spread_out, slab, grad_rows, bias1 = lax.optimization_barrier(
+        (spread_out, slab, grad_rows, bias1)
     )
     normed = lax.all_to_all(spread_out, VAR, 0, 0).reshape(256, D)
     edge_right = jnp.transpose(grad_rows[:, :, 0:2], (2, 0, 1)).reshape(16, C)
@@ -403,17 +406,11 @@
     from_right = lax.ppermute(edge_right, VAR, [(i + 1, i) for i in range(7)])
     from_left = lax.ppermute(edge_left, VAR, [(i, i + 1) for i in range(7)])
     rim = jnp.concatenate([from_right, from_left], axis=0)
-    base = jnp.dot(slab, w_up, preferred_element_type=F32)
-    mats = jnp.stack(
-        [tap_matrix(conv1), tap_matrix(flipped(conv2)), tap_matrix(conv2), tap_matrix(flipped(conv1))]
-    )
     bias = bias1.reshape(C, 1)
     flags = jnp.stack(
         [band_at > 0, band_at < 31, var_at > 0, var_at < 7, core_at > 0]
     ).astype(jnp.int32)
-    normed, rim, base, mats, bias, flags = lax.optimization_barrier(
-        (normed, rim, base, mats, bias, flags)
-    )
+    normed, rim, bias, flags = lax.optimization_barrier((normed, rim, bias, flags))
 
     keyvals = jnp.dot(normed, wkv, preferred_element_type=F32).astype(BF)
     ahead = lax.ppermute(keyvals, "z", turn(8, 1))
@@ -435,10 +432,18 @@
         ahead, behind, carry = lax.optimization_barrier((ahead, behind, carry))
     fresh = [ahead, behind]
 
-    blocks = flash_step(all_queries, fresh, carry, True)
+    blocks = list(flash_step(all_queries, fresh, carry, True))
+    blocks[0], slab = lax.optimization_barrier((blocks[0], slab))
+    base = jnp.dot(slab, w_up, preferred_element_type=F32)
     parts = [blocks[0]] + [lax.ppermute(b, group, flip(4, k)) for b, k in zip(blocks[1:], (2, 3, 1))]
     place = var_at.reshape(1).astype(jnp.int32)
-    pieces = lax.all_to_all(merge(place, base, parts, up_mat), VAR, 0, 0)
+    merged = merge(place, base, parts, up_mat)
+    merged, conv1, conv2 = lax.optimization_barrier((merged, conv1, conv2))
+    pieces = lax.all_to_all(merged, VAR, 0, 0)
+    mats = jnp.stack(
+        [tap_matrix(conv1), tap_matrix(flipped(conv2)), tap_matrix(conv2), tap_matrix(flipped(conv1))]
+    )
+    pieces, mats = lax.optimization_barrier((pieces, mats))
     base_main = jnp.transpose(base.reshape(32, 2, 4, 128), (1, 2, 0, 3)).reshape(2, 128, 128)
     base_all = jnp.pad(base_main, ((0, 0), (0, 16), (0, 0)))
     up = (jnp.sum(pieces.astype(F32), axis=0) + base_all).astype(BF)

time: 174 us -> 172 us (0.989)
  waiting for transfers between devices: 31.2 us -> 44.8 us
  local copies, waits for them, and re-layouts: 12.8 us -> 4.4 us
  starting transfers between devices: 60.9 us -> 54.9 us
  Pallas kernels: 14.5 us -> 16.8 us
  matrix products: 10.4 us -> 8.24 us
  blocking collectives: 40.8 us -> 39 us
    ppermute x1, waiting for transfers between devices: 0.01 us -> 6 us  [device_step(): ahead = lax.ppermute(keyvals, 'z', turn(8, 1))]
    ppermute x1, waiting for transfers between devices: 0.01 us -> 5.14 us  [device_step(): from_left = lax.ppermute(edge_left, VAR, [(i, i + 1) for i in range(7)])]
    all_to_all x1, blocking collectives: 18.1 us -> 14.5 us  [device_step(): shares = lax.all_to_all(terms.reshape(32, 24, 128), PLANE, 0, 0)]
    ppermute x1, waiting for transfers between devices: 3.31 us -> 0.01 us  [device_step(): behind = lax.ppermute(keyvals, 'z', turn(8, -1))]
    ppermute x1, starting transfers between devices: 5.07 us -> 2.13 us  [device_step(): lax.ppermute(lax.dynamic_index_in_dim(up, core_at, 0, False), BAND, pairs)]
    unnamed x34 -> x22, local copies, waits for them, and re-layouts: 2.76 us -> 0.06 us
    ppermute x3, starting transfers between devices: 7.61 us -> 4.95 us  [device_step(): lax.ppermute(queries, group, flip(4, k))]
    all_to_all x1, starting transfers between devices: 6.18 us -> 3.54 us  [device_step(): pieces = lax.all_to_all(merged, VAR, 0, 0)]
  transfers between devices with their start and end apart: 23 -> 23, of which waited for: 10 -> 13; matrix products, arithmetic and copies ran while one was open for 11% -> 6% of each run, Pallas kernels for 4% -> 4%
where the time goes in v6:
time: 172 us; the launch traced here: 171 us
  starting transfers between devices  54.9 us (32%)
  waiting for transfers between devices  44.8 us (26%)
  blocking collectives  39 us (23%)
  Pallas kernels  16.8 us (10%)
  matrix products  8.24 us (5%)
  local copies, waits for them, and re-layouts  4.4 us (3%)
  other arithmetic  1.85 us (1%)
    all_to_all x2, blocking collectives, copies(): lax.all_to_all(jnp.broadcast_to(piece[None], (count,) + piece.shape), axi...  24.5 us
    all_to_all x1, blocking collectives, device_step(): shares = lax.all_to_all(terms.reshape(32, 24, 128), PLANE, 0, 0)  14.5 us
    all_to_all x1, waiting for transfers between devices, device_step(): pieces = lax.all_to_all(merged, VAR, 0, 0)  9.18 us
    ppermute x3, starting transfers between devices, device_step(): behind = lax.ppermute(behind, 'z', turn(8, -1))  8.56 us
    ppermute x1, starting transfers between devices, device_step(): behind = lax.ppermute(keyvals, 'z', turn(8, -1))  8.09 us
    pallas_call x4, Pallas kernels, flash_step(): pl.pallas_call(flash_kernel(blocks, len(chunks), first, last), out_shape=...  7.65 us
    ppermute x1, waiting for transfers between devices, device_step(): ahead = lax.ppermute(keyvals, 'z', turn(8, 1))  6 us
    all_to_all x1, starting transfers between devices, device_step(): pieces = lax.all_to_all(partial_mix, VAR, 0, 0)  5.93 us
  transfers between devices with their start and end apart: 23, of which 13 were waited for; matrix products, arithmetic and copies ran while one was open for 6% of the time, Pallas kernels for 4%

profile of v6, /device:TPU:1, one launch (start us, length us, event | category | flops | bytes accessed | tf_op | source)
XLA Modules:
  0.0 171.1 jit_solution(13752155900715990442)
XLA Ops:
  0.6 3.9 %mix_variables.1 = bf16[256,2048]{1,0:T(8,128)(2,1)} custom-call(bf16[128,256]{1,0:T(8,128)(2,1)} %bitcast.75, bf16[128,2048]{1,0:T(8,128)(2,1)} %bitcast.71, f32[2,2048]{1,0:T(2,128)} %offsets.1), custom_call_target="tpu_custom_call" | custom-call | tf_op jit(solution)/shard_map/mix_variables/pallas_call | solution.py:48
  4.6 5.9 %all-to-all-start = ((bf16[8,32,2048]{2,1,0:T(8,128)(2,1)}), bf16[8,32,2048]{2,1,0:T(8,128)(2,1)S(1)}, u32[]{:S(2)}, u32[]{:S(2)}) async-start(bf16[8,32,2048]{2,1,0:T(8,128)(2,1)} %bitcast.3), calls=%async_computation | async-start | bytes 2097152 | tf_op jit(solution)/shard_map/all_to_all | solution.py:387
  11.4 2.9 %collective-permute-start.1 = (bf16[2,64,128]{2,1,0:T(8,128)(2,1)S(1)}, bf16[2,64,128]{2,1,0:T(8,128)(2,1)S(1)}, u32[]{:S(2)}, u32[]{:S(2)}) collective-permute-start(bf16[2,64,128]{2,1,0:T(8,128)(2,1)S(1)} %get-tuple-element.114), channel_id=1, source_target_pairs={{8,0},{16,8},{24,16},{32,24},{40,32},{48,40},{56,48},{64,56},{72,6... | collective-permute-start | bytes 98312 | tf_op jit(solution)/shard_map/ppermute | solution.py:394
  14.3 3.6 %collective-permute-start = (bf16[2,64,128]{2,1,0:T(8,128)(2,1)S(1)}, bf16[2,64,128]{2,1,0:T(8,128)(2,1)S(1)}, u32[]{:S(2)}, u32[]{:S(2)}) collective-permute-start(bf16[2,64,128]{2,1,0:T(8,128)(2,1)S(1)} %get-tuple-element.113), channel_id=1, source_target_pairs={{0,8},{8,16},{16,24},{24,32},{32,40},{40,48},{48,56},{56,64},{64,7... | collective-permute-start | bytes 98312 | tf_op jit(solution)/shard_map/ppermute | solution.py:392
  17.9 3.4 %convolution_convert_fusion.mat = bf16[256,1024]{1,0:T(8,128)(2,1)S(1)} fusion(bf16[256,2048]{1,0:T(8,128)(2,1)S(1)} %copy-done, bf16[2048,1024]{1,0:T(8,128)(2,1)} %param.23), kind=kOutput, calls=%fused_computation.1 | convolution fusion | flops 1074003968 | bytes 5767168 | tf_op jit(solution)/shard_map/dot_general | solution.py:388
  23.0 2.1 %all-to-all-done.pieces = bf16[8,32,2048]{2,1,0:T(8,128)(2,1)S(1)} async-done(((bf16[8,32,2048]{2,1,0:T(8,128)(2,1)}), bf16[8,32,2048]{2,1,0:T(8,128)(2,1)S(1)}, u32[]{:S(2)}, u32[]{:S(2)}) %all-to-all-start) | async-done | bytes 1048608 | tf_op jit(solution)/shard_map/all_to_all | solution.py:387
  26.3 4.1 %all-to-all-start.1 = ((bf16[8,32,2048]{2,1,0:T(8,128)(2,1)}), bf16[8,32,2048]{2,1,0:T(8,128)(2,1)S(1)}, u32[]{:S(2)}, u32[]{:S(2)}) async-start(bf16[8,32,2048]{2,1,0:T(8,128)(2,1)} %get-tuple-element.65), calls=%async_computation.1 | async-start | bytes 2097152 | tf_op jit(solution)/shard_map/all_to_all | solution.py:403
  30.6 3.4 %collective-permute-start.3 = (bf16[16,64]{1,0:T(8,128)(2,1)S(1)}, bf16[16,64]{1,0:T(8,128)(2,1)S(1)}, u32[]{:S(2)}, u32[]{:S(2)}) collective-permute-start(bf16[16,64]{1,0:T(8,128)(2,1)S(1)} %bitcast.76), channel_id=1, source_target_pairs={{0,1},{1,2},{2,3},{3,4},{4,5},{5,6},{6,7},{8,9},{9,10},{10,11},{11... | collective-permute-start | bytes 6152 | tf_op jit(solution)/shard_map/ppermute | solution.py:407
  35.5 5.1 %collective-permute-done.3 = bf16[16,64]{1,0:T(8,128)(2,1)S(1)} collective-permute-done((bf16[16,64]{1,0:T(8,128)(2,1)S(1)}, bf16[16,64]{1,0:T(8,128)(2,1)S(1)}, u32[]{:S(2)}, u32[]{:S(2)}) %collective-permute-start.3) | collective-permute-done | bytes 2080 | tf_op jit(solution)/shard_map/ppermute | solution.py:407
  40.7 2.1 %collective-permute-done.2 = bf16[16,64]{1,0:T(8,128)(2,1)S(1)} collective-permute-done((bf16[16,64]{1,0:T(8,128)(2,1)S(1)}, bf16[16,64]{1,0:T(8,128)(2,1)S(1)}, u32[]{:S(2)}, u32[]{:S(2)}) %collective-permute-start.2) | collective-permute-done | bytes 2080 | tf_op jit(solution)/shard_map/ppermute | solution.py:406
  44.3 2.3 %convolution_convert_fusion.1.refs_4_ = bf16[256,512]{1,0:T(8,128)(2,1)S(1)} fusion(bf16[256,2048]{1,0:T(8,128)(2,1)S(1)} %bitcast.61, bf16[2048,512]{1,0:T(8,128)(2,1)} %pad_maximum_fusion), kind=kOutput, calls=%fused_computation.2 | convolution fusion | flops 537001984 | bytes 3407872 | tf_op jit(solution)/shard_map/dot_general | solution.py:415
  48.4 8.1 %collective-permute-start.9 = (bf16[256,512]{1,0:T(8,128)(2,1)S(1)}, bf16[256,512]{1,0:T(8,128)(2,1)S(1)}, u32[]{:S(2)}, u32[]{:S(2)}) collective-permute-start(bf16[256,512]{1,0:T(8,128)(2,1)S(1)} %convolution_convert_fusion.1.refs_4_), channel_id=1, source_target_pairs={{0,112},{16,0},{32,16},{48,32},{64,48},{80,64},{96,80},{112,96},{1... | collective-permute-start | bytes 786440 | tf_op jit(solution)/shard_map/ppermute | solution.py:417
  56.5 6.0 %collective-permute-done.7.refs_5_ = bf16[256,512]{1,0:T(8,128)(2,1)S(1)} collective-permute-done((bf16[256,512]{1,0:T(8,128)(2,1)S(1)}, bf16[256,512]{1,0:T(8,128)(2,1)S(1)}, u32[]{:S(2)}, u32[]{:S(2)}) %collective-permute-start.7) | collective-permute-done | bytes 262176 | tf_op jit(solution)/shard_map/ppermute | solution.py:416
  62.5 2.7 %collective-permute-start.10 = (bf16[256,512]{1,0:T(8,128)(2,1)S(1)}, bf16[256,512]{1,0:T(8,128)(2,1)S(1)}, u32[]{:S(2)}, u32[]{:S(2)}) collective-permute-start(bf16[256,512]{1,0:T(8,128)(2,1)S(1)} %collective-permute-done.9.refs_6_), channel_id=1, source_target_pairs={{0,112},{16,0},{32,16},{48,32},{64,48},{80,64},{96,80},{112,96},{1... | collective-permute-start | bytes 786440 | tf_op jit(solution)/shard_map/ppermute | solution.py:422
  66.9 4.9 %collective-permute-start.5 = (bf16[256,256]{1,0:T(8,128)(2,1)S(1)}, bf16[256,256]{1,0:T(8,128)(2,1)S(1)}, u32[]{:S(2)}, u32[]{:S(2)}) collective-permute-start(bf16[256,256]{1,0:T(8,128)(2,1)S(1)} %convolution_convert_fusion.2.refs_0_), channel_id=1, source_target_pairs={{0,136},{8,128},{128,8},{136,0},{1,137},{9,129},{129,9},{137,1},{2... | collective-permute-start | bytes 393224 | tf_op jit(solution)/shard_map/ppermute | solution.py:419
  72.2 4.5 %collective-permute-done.5.refs_2_ = bf16[256,256]{1,0:T(8,128)(2,1)S(1)} collective-permute-done((bf16[256,256]{1,0:T(8,128)(2,1)S(1)}, bf16[256,256]{1,0:T(8,128)(2,1)S(1)}, u32[]{:S(2)}, u32[]{:S(2)}) %collective-permute-start.5) | collective-permute-done | bytes 131104 | tf_op jit(solution)/shard_map/ppermute | solution.py:419
  76.8 2.5 %flash_step.3 = (f32[8,1024]{1,0:T(8,128)S(1)}, f32[256,1024]{1,0:T(8,128)S(1)}) custom-call(bf16[256,256]{1,0:T(8,128)(2,1)S(1)} %convolution_convert_fusion.2.refs_0_, bf16[256,256]{1,0:T(8,128)(2,1)S(1)} %collective-permute-done.4.refs_1_, bf16[256,256]{1,0:T(8,128)(2,1)S(1)} %collective-permute-done.5.refs_2_, ...), custom_call_target="tpu_custom_call" | custom-call | tf_op jit(solution)/shard_map/flash_step/pallas_call | solution.py:163
  79.4 2.7 %collective-permute-start.12 = (bf16[256,512]{1,0:T(8,128)(2,1)S(1)}, bf16[256,512]{1,0:T(8,128)(2,1)S(1)}, u32[]{:S(2)}, u32[]{:S(2)}) collective-permute-start(bf16[256,512]{1,0:T(8,128)(2,1)S(1)} %collective-permute-done.10.refs_5_), channel_id=1, source_target_pairs={{0,112},{16,0},{32,16},{48,32},{64,48},{80,64},{96,80},{112,96},{1... | collective-permute-start | bytes 786440 | tf_op jit(solution)/shard_map/ppermute | solution.py:430
  82.1 1.9 %flash_step.4 = (f32[8,1024]{1,0:T(8,128)S(1)}, f32[256,1024]{1,0:T(8,128)S(1)}) custom-call(bf16[256,256]{1,0:T(8,128)(2,1)S(1)} %convolution_convert_fusion.2.refs_0_, bf16[256,256]{1,0:T(8,128)(2,1)S(1)} %collective-permute-done.4.refs_1_, bf16[256,256]{1,0:T(8,128)(2,1)S(1)} %collective-permute-done.5.refs_2_, ...), custom_call_target="tpu_custom_call" | custom-call | tf_op jit(solution)/shard_map/flash_step/pallas_call | solution.py:163
  84.0 4.4 %collective-permute-done.11.refs_4_ = bf16[256,512]{1,0:T(8,128)(2,1)S(1)} collective-permute-done((bf16[256,512]{1,0:T(8,128)(2,1)S(1)}, bf16[256,512]{1,0:T(8,128)(2,1)S(1)}, u32[]{:S(2)}, u32[]{:S(2)}) %collective-permute-start.11) | collective-permute-done | bytes 262176 | tf_op jit(solution)/shard_map/ppermute | solution.py:429
  88.6 3.2 %collective-permute-start.14 = (bf16[128,512]{1,0:T(8,128)(2,1)S(1)}, bf16[128,512]{1,0:T(8,128)(2,1)S(1)}, u32[]{:S(2)}, u32[]{:S(2)}) collective-permute-start(bf16[128,512]{1,0:T(8,128)(2,1)S(1)} %slice.32), channel_id=1, source_target_pairs={{0,112},{16,0},{32,16},{48,32},{64,48},{80,64},{96,80},{112,96},{1... | collective-permute-start | bytes 393224 | tf_op jit(solution)/shard_map/ppermute | solution.py:430
  91.8 1.9 %flash_step.5 = (f32[8,1024]{1,0:T(8,128)S(1)}, f32[256,1024]{1,0:T(8,128)S(1)}) custom-call(bf16[256,256]{1,0:T(8,128)(2,1)S(1)} %convolution_convert_fusion.2.refs_0_, bf16[256,256]{1,0:T(8,128)(2,1)S(1)} %collective-permute-done.4.refs_1_, bf16[256,256]{1,0:T(8,128)(2,1)S(1)} %collective-permute-done.5.refs_2_, ...), custom_call_target="tpu_custom_call" | custom-call | tf_op jit(solution)/shard_map/flash_step/pallas_call | solution.py:163
  96.5 4.1 %collective-permute-start.16 = (bf16[272,256]{1,0:T(8,128)(2,1)S(1)}, bf16[272,256]{1,0:T(8,128)(2,1)S(1)}, u32[]{:S(2)}, u32[]{:S(2)}) collective-permute-start(bf16[272,256]{1,0:T(8,128)(2,1)S(1)} %get-tuple-element.94), channel_id=1, source_target_pairs={{0,136},{8,128},{128,8},{136,0},{1,137},{9,129},{129,9},{137,1},{2... | collective-permute-start | bytes 417800 | tf_op jit(solution)/shard_map/ppermute | solution.py:438
  102.3 4.2 %collective-permute-done.16.b2 = bf16[272,256]{1,0:T(8,128)(2,1)S(1)} collective-permute-done((bf16[272,256]{1,0:T(8,128)(2,1)S(1)}, bf16[272,256]{1,0:T(8,128)(2,1)S(1)}, u32[]{:S(2)}, u32[]{:S(2)}) %collective-permute-start.16) | collective-permute-done | bytes 139296 | tf_op jit(solution)/shard_map/ppermute | solution.py:438
  107.7 3.5 %all-to-all-start.2 = ((bf16[8,2,144,128]{3,2,1,0:T(8,128)(2,1)}), bf16[8,2,144,128]{3,2,1,0:T(8,128)(2,1)S(1)}, u32[]{:S(2)}, u32[]{:S(2)}) async-start(bf16[8,2,144,128]{3,2,1,0:T(8,128)(2,1)} %merge_heads.1), calls=%async_computation.2 | async-start | bytes 1179648 | tf_op jit(solution)/shard_map/all_to_all | solution.py:442
  112.8 9.2 %all-to-all-done.2 = bf16[8,2,144,128]{3,2,1,0:T(8,128)(2,1)S(1)} async-done(((bf16[8,2,144,128]{3,2,1,0:T(8,128)(2,1)}), bf16[8,2,144,128]{3,2,1,0:T(8,128)(2,1)S(1)}, u32[]{:S(2)}, u32[]{:S(2)}) %all-to-all-start.2) | async-done | bytes 589856 | tf_op jit(solution)/shard_map/all_to_all | solution.py:442
  122.5 2.1 %collective-permute-start.19 = (bf16[144,128]{1,0:T(8,128)(2,1)S(1)}, bf16[144,128]{1,0:T(8,128)(2,1)S(1)}, u32[]{:S(2)}, u32[]{:S(2)}) collective-permute-start(bf16[144,128]{1,0:T(8,128)(2,1)S(1)} %get-tuple-element.111), channel_id=1, source_target_pairs={{8,16},{24,32},{40,48},{56,64},{72,80},{88,96},{104,112},{120,128}... | collective-permute-start | bytes 110600 | tf_op jit(solution)/shard_map/ppermute | solution.py:452
  124.8 3.0 %collective-permute-done.19.far_up = bf16[144,128]{1,0:T(8,128)(2,1)S(1)} collective-permute-done((bf16[144,128]{1,0:T(8,128)(2,1)S(1)}, bf16[144,128]{1,0:T(8,128)(2,1)S(1)}, u32[]{:S(2)}, u32[]{:S(2)}) %collective-permute-start.19) | collective-permute-done | bytes 36896 | tf_op jit(solution)/shard_map/ppermute | solution.py:452
  127.8 2.7 %fine_stage.1 = (bf16[4,64,128]{2,1,0:T(8,128)(2,1)}, bf16[4,64,128]{2,1,0:T(8,128)(2,1)}, bf16[768,128]{1,0:T(8,128)(2,1)S(1)}) custom-call(s32[5]{0:T(128)S(1)} %convert_element_type.31.flags, bf16[2,144,128]{2,1,0:T(8,128)(2,1)S(1)} %add_convert_fusion.own, bf16[144,128]{1,0:T(8,128)(2,1)S(1)} %collective-permute-done.18.near_up, ...), custom_call_target="tpu_custom_call" | custom-call | tf_op jit(solution)/shard_map/fine_stage/pallas_call | solution.py:340
  130.5 14.5 %all_to_all.30 = bf16[32,24,128]{2,1,0:T(8,128)(2,1)S(1)} all-to-all(bf16[32,24,128]{2,1,0:T(8,128)(2,1)S(1)} %bitcast.59), channel_id=1, replica_groups=mesh['xh'=2,'z'=8,'core'=2,'y'=4,'xl'=2] {'xh','core','y','xl'}, dimensions={0} | all-to-all | bytes 393216 | tf_op jit(solution)/shard_map/all_to_all | solution.py:458
  145.1 11.0 %all_to_all.31 = bf16[8,24,128]{2,1,0:T(8,128)(2,1)S(1)} all-to-all(bf16[8,24,128]{2,1,0:T(8,128)(2,1)S(1)} %broadcast_in_dim.4), channel_id=1, replica_groups=mesh['xh'=2,'z'=8,'core'=2,'y'=4,'xl'=2] {'z'}, dimensions={0} | all-to-all | bytes 98304 | tf_op jit(solution)/shard_map/all_to_all | solution.py:355
  156.1 13.5 %all_to_all.32 = bf16[32,24,128]{2,1,0:T(8,128)(2,1)S(1)} all-to-all(bf16[32,24,128]{2,1,0:T(8,128)(2,1)S(1)} %broadcast_in_dim.5), channel_id=1, replica_groups=mesh['xh'=2,'z'=8,'core'=2,'y'=4,'xl'=2] {'xh','core','y','xl'}, dimensions={0} | all-to-all | bytes 393216 | tf_op jit(solution)/shard_map/all_to_all | solution.py:355
  (86 shorter events, 20.6 us)
Async XLA Ops:
  0.6 17.3 %copy-start = (bf16[256,2048]{1,0:T(8,128)(2,1)S(1)}, bf16[256,2048]{1,0:T(8,128)(2,1)}, u32[]{:S(2)}) copy-start(bf16[256,2048]{1,0:T(8,128)(2,1)} %param.22) | copy-start | bytes 3145732
  4.6 20.5 %all-to-all-start = ((bf16[8,32,2048]{2,1,0:T(8,128)(2,1)}), bf16[8,32,2048]{2,1,0:T(8,128)(2,1)S(1)}, u32[]{:S(2)}, u32[]{:S(2)}) async-start(bf16[8,32,2048]{2,1,0:T(8,128)(2,1)} %bitcast.3), calls=%async_computation | async-start | bytes 2097152 | tf_op jit(solution)/shard_map/all_to_all | solution.py:387
  10.5 10.9 %copy-start.5 = (bf16[2048,256]{1,0:T(8,128)(2,1)S(1)}, bf16[2048,256]{1,0:T(8,128)(2,1)}, u32[]{:S(2)}) copy-start(bf16[2048,256]{1,0:T(8,128)(2,1)} %param.21) | copy-start | bytes 3145732
  10.5 10.9 %copy-start.6 = (bf16[2048,256]{1,0:T(8,128)(2,1)S(1)}, bf16[2048,256]{1,0:T(8,128)(2,1)}, u32[]{:S(2)}) copy-start(bf16[2048,256]{1,0:T(8,128)(2,1)} %param.20) | copy-start | bytes 3145732
  11.4 11.5 %collective-permute-start.1 = (bf16[2,64,128]{2,1,0:T(8,128)(2,1)S(1)}, bf16[2,64,128]{2,1,0:T(8,128)(2,1)S(1)}, u32[]{:S(2)}, u32[]{:S(2)}) collective-permute-start(bf16[2,64,128]{2,1,0:T(8,128)(2,1)S(1)} %get-tuple-element.114), channel_id=1, source_target_pairs={{8,0},{16,8},{24,16},{32,24},{40,32},{48,40},{56,48},{64,56},{72,6... | collective-permute-start | bytes 98312 | tf_op jit(solution)/shard_map/ppermute | solution.py:394
  14.3 8.6 %collective-permute-start = (bf16[2,64,128]{2,1,0:T(8,128)(2,1)S(1)}, bf16[2,64,128]{2,1,0:T(8,128)(2,1)S(1)}, u32[]{:S(2)}, u32[]{:S(2)}) collective-permute-start(bf16[2,64,128]{2,1,0:T(8,128)(2,1)S(1)} %get-tuple-element.113), channel_id=1, source_target_pairs={{0,8},{8,16},{16,24},{24,32},{32,40},{40,48},{48,56},{56,64},{64,7... | collective-permute-start | bytes 98312 | tf_op jit(solution)/shard_map/ppermute | solution.py:392
  26.3 18.0 %all-to-all-start.1 = ((bf16[8,32,2048]{2,1,0:T(8,128)(2,1)}), bf16[8,32,2048]{2,1,0:T(8,128)(2,1)S(1)}, u32[]{:S(2)}, u32[]{:S(2)}) async-start(bf16[8,32,2048]{2,1,0:T(8,128)(2,1)} %get-tuple-element.65), calls=%async_computation.1 | async-start | bytes 2097152 | tf_op jit(solution)/shard_map/all_to_all | solution.py:403
  30.6 10.1 %collective-permute-start.3 = (bf16[16,64]{1,0:T(8,128)(2,1)S(1)}, bf16[16,64]{1,0:T(8,128)(2,1)S(1)}, u32[]{:S(2)}, u32[]{:S(2)}) collective-permute-start(bf16[16,64]{1,0:T(8,128)(2,1)S(1)} %bitcast.76), channel_id=1, source_target_pairs={{0,1},{1,2},{2,3},{3,4},{4,5},{5,6},{6,7},{8,9},{9,10},{10,11},{11... | collective-permute-start | bytes 6152 | tf_op jit(solution)/shard_map/ppermute | solution.py:407
  34.1 8.7 %collective-permute-start.2 = (bf16[16,64]{1,0:T(8,128)(2,1)S(1)}, bf16[16,64]{1,0:T(8,128)(2,1)S(1)}, u32[]{:S(2)}, u32[]{:S(2)}) collective-permute-start(bf16[16,64]{1,0:T(8,128)(2,1)S(1)} %bitcast.77), channel_id=1, source_target_pairs={{1,0},{2,1},{3,2},{4,3},{5,4},{6,5},{7,6},{9,8},{10,9},{11,10},{12... | collective-permute-start | bytes 6152 | tf_op jit(solution)/shard_map/ppermute | solution.py:406
  46.6 15.8 %collective-permute-start.7 = (bf16[256,512]{1,0:T(8,128)(2,1)S(1)}, bf16[256,512]{1,0:T(8,128)(2,1)S(1)}, u32[]{:S(2)}, u32[]{:S(2)}) collective-permute-start(bf16[256,512]{1,0:T(8,128)(2,1)S(1)} %convolution_convert_fusion.1.refs_4_), channel_id=1, source_target_pairs={{0,16},{16,32},{32,48},{48,64},{64,80},{80,96},{96,112},{112,0},{1... | collective-permute-start | bytes 786440 | tf_op jit(solution)/shard_map/ppermute | solution.py:416
  48.4 14.1 %collective-permute-start.9 = (bf16[256,512]{1,0:T(8,128)(2,1)S(1)}, bf16[256,512]{1,0:T(8,128)(2,1)S(1)}, u32[]{:S(2)}, u32[]{:S(2)}) collective-permute-start(bf16[256,512]{1,0:T(8,128)(2,1)S(1)} %convolution_convert_fusion.1.refs_4_), channel_id=1, source_target_pairs={{0,112},{16,0},{32,16},{48,32},{64,48},{80,64},{96,80},{112,96},{1... | collective-permute-start | bytes 786440 | tf_op jit(solution)/shard_map/ppermute | solution.py:417
  62.5 16.9 %collective-permute-start.8 = (bf16[256,512]{1,0:T(8,128)(2,1)S(1)}, bf16[256,512]{1,0:T(8,128)(2,1)S(1)}, u32[]{:S(2)}, u32[]{:S(2)}) collective-permute-start(bf16[256,512]{1,0:T(8,128)(2,1)S(1)} %collective-permute-done.7.refs_5_), channel_id=1, source_target_pairs={{0,16},{16,32},{32,48},{48,64},{64,80},{80,96},{96,112},{112,0},{1... | collective-permute-start | bytes 786440 | tf_op jit(solution)/shard_map/ppermute | solution.py:421
  62.5 16.9 %collective-permute-start.10 = (bf16[256,512]{1,0:T(8,128)(2,1)S(1)}, bf16[256,512]{1,0:T(8,128)(2,1)S(1)}, u32[]{:S(2)}, u32[]{:S(2)}) collective-permute-start(bf16[256,512]{1,0:T(8,128)(2,1)S(1)} %collective-permute-done.9.refs_6_), channel_id=1, source_target_pairs={{0,112},{16,0},{32,16},{48,32},{64,48},{80,64},{96,80},{112,96},{1... | collective-permute-start | bytes 786440 | tf_op jit(solution)/shard_map/ppermute | solution.py:422
  66.8 33.9 %copy-start.4 = (bf16[2048,1024]{1,0:T(8,128)(2,1)S(1)}, bf16[2048,1024]{1,0:T(8,128)(2,1)}, u32[]{:S(2)}) copy-start(bf16[2048,1024]{1,0:T(8,128)(2,1)} %param.23) | copy-start | bytes 12582916
  66.8 5.4 %collective-permute-start.4 = (bf16[256,256]{1,0:T(8,128)(2,1)S(1)}, bf16[256,256]{1,0:T(8,128)(2,1)S(1)}, u32[]{:S(2)}, u32[]{:S(2)}) collective-permute-start(bf16[256,256]{1,0:T(8,128)(2,1)S(1)} %convolution_convert_fusion.2.refs_0_), channel_id=1, source_target_pairs={{0,128},{8,136},{128,0},{136,8},{1,129},{9,137},{129,1},{137,9},{2... | collective-permute-start | bytes 393224 | tf_op jit(solution)/shard_map/ppermute | solution.py:419
  66.9 9.8 %collective-permute-start.5 = (bf16[256,256]{1,0:T(8,128)(2,1)S(1)}, bf16[256,256]{1,0:T(8,128)(2,1)S(1)}, u32[]{:S(2)}, u32[]{:S(2)}) collective-permute-start(bf16[256,256]{1,0:T(8,128)(2,1)S(1)} %convolution_convert_fusion.2.refs_0_), channel_id=1, source_target_pairs={{0,136},{8,128},{128,8},{136,0},{1,137},{9,129},{129,9},{137,1},{2... | collective-permute-start | bytes 393224 | tf_op jit(solution)/shard_map/ppermute | solution.py:419
  71.8 5.0 %collective-permute-start.6 = (bf16[256,256]{1,0:T(8,128)(2,1)S(1)}, bf16[256,256]{1,0:T(8,128)(2,1)S(1)}, u32[]{:S(2)}, u32[]{:S(2)}) collective-permute-start(bf16[256,256]{1,0:T(8,128)(2,1)S(1)} %convolution_convert_fusion.2.refs_0_), channel_id=1, source_target_pairs={{0,8},{8,0},{128,136},{136,128},{1,9},{9,1},{129,137},{137,129},{2... | collective-permute-start | bytes 393224 | tf_op jit(solution)/shard_map/ppermute | solution.py:419
  79.3 9.1 %collective-permute-start.11 = (bf16[256,512]{1,0:T(8,128)(2,1)S(1)}, bf16[256,512]{1,0:T(8,128)(2,1)S(1)}, u32[]{:S(2)}, u32[]{:S(2)}) collective-permute-start(bf16[256,512]{1,0:T(8,128)(2,1)S(1)} %collective-permute-done.8.refs_4_), channel_id=1, source_target_pairs={{0,16},{16,32},{32,48},{48,64},{64,80},{80,96},{96,112},{112,0},{1... | collective-permute-start | bytes 786440 | tf_op jit(solution)/shard_map/ppermute | solution.py:429
  79.4 9.0 %collective-permute-start.12 = (bf16[256,512]{1,0:T(8,128)(2,1)S(1)}, bf16[256,512]{1,0:T(8,128)(2,1)S(1)}, u32[]{:S(2)}, u32[]{:S(2)}) collective-permute-start(bf16[256,512]{1,0:T(8,128)(2,1)S(1)} %collective-permute-done.10.refs_5_), channel_id=1, source_target_pairs={{0,112},{16,0},{32,16},{48,32},{64,48},{80,64},{96,80},{112,96},{1... | collective-permute-start | bytes 786440 | tf_op jit(solution)/shard_map/ppermute | solution.py:430
  88.5 6.7 %collective-permute-start.13 = (bf16[128,512]{1,0:T(8,128)(2,1)S(1)}, bf16[128,512]{1,0:T(8,128)(2,1)S(1)}, u32[]{:S(2)}, u32[]{:S(2)}) collective-permute-start(bf16[128,512]{1,0:T(8,128)(2,1)S(1)} %slice.31), channel_id=1, source_target_pairs={{0,16},{16,32},{32,48},{48,64},{64,80},{80,96},{96,112},{112,0},{1... | collective-permute-start | bytes 393224 | tf_op jit(solution)/shard_map/ppermute | solution.py:429
  88.6 6.6 %collective-permute-start.14 = (bf16[128,512]{1,0:T(8,128)(2,1)S(1)}, bf16[128,512]{1,0:T(8,128)(2,1)S(1)}, u32[]{:S(2)}, u32[]{:S(2)}) collective-permute-start(bf16[128,512]{1,0:T(8,128)(2,1)S(1)} %slice.32), channel_id=1, source_target_pairs={{0,112},{16,0},{32,16},{48,32},{64,48},{80,64},{96,80},{112,96},{1... | collective-permute-start | bytes 393224 | tf_op jit(solution)/shard_map/ppermute | solution.py:430
  96.4 14.9 %copy-start.8 = (bf16[9,64,64]{2,1,0:T(8,128)(2,1)S(1)}, bf16[9,64,64]{2,1,0:T(8,128)(2,1)}, u32[]{:S(2)}) copy-start(bf16[9,64,64]{2,1,0:T(8,128)(2,1)} %param.24) | copy-start | bytes 221188
  96.4 5.8 %collective-permute-start.15 = (bf16[272,256]{1,0:T(8,128)(2,1)S(1)}, bf16[272,256]{1,0:T(8,128)(2,1)S(1)}, u32[]{:S(2)}, u32[]{:S(2)}) collective-permute-start(bf16[272,256]{1,0:T(8,128)(2,1)S(1)} %get-tuple-element.93), channel_id=1, source_target_pairs={{0,128},{8,136},{128,0},{136,8},{1,129},{9,137},{129,1},{137,9},{2... | collective-permute-start | bytes 417800 | tf_op jit(solution)/shard_map/ppermute | solution.py:438
  96.5 9.9 %collective-permute-start.16 = (bf16[272,256]{1,0:T(8,128)(2,1)S(1)}, bf16[272,256]{1,0:T(8,128)(2,1)S(1)}, u32[]{:S(2)}, u32[]{:S(2)}) collective-permute-start(bf16[272,256]{1,0:T(8,128)(2,1)S(1)} %get-tuple-element.94), channel_id=1, source_target_pairs={{0,136},{8,128},{128,8},{136,0},{1,137},{9,129},{129,9},{137,1},{2... | collective-permute-start | bytes 417800 | tf_op jit(solution)/shard_map/ppermute | solution.py:438
  100.7 11.0 %copy-start.7 = (bf16[9,64,64]{2,1,0:T(8,128)(2,1)S(1)}, bf16[9,64,64]{2,1,0:T(8,128)(2,1)}, u32[]{:S(2)}) copy-start(bf16[9,64,64]{2,1,0:T(8,128)(2,1)} %param.26) | copy-start | bytes 221188
  100.7 5.8 %collective-permute-start.17 = (bf16[272,256]{1,0:T(8,128)(2,1)S(1)}, bf16[272,256]{1,0:T(8,128)(2,1)S(1)}, u32[]{:S(2)}, u32[]{:S(2)}) collective-permute-start(bf16[272,256]{1,0:T(8,128)(2,1)S(1)} %get-tuple-element.95), channel_id=1, source_target_pairs={{0,8},{8,0},{128,136},{136,128},{1,9},{9,1},{129,137},{137,129},{2... | collective-permute-start | bytes 417800 | tf_op jit(solution)/shard_map/ppermute | solution.py:438
  106.4 18.3 %copy-start.10 = (f32[64]{0:T(128)S(1)}, f32[64]{0:T(128)}, u32[]{:S(2)}) copy-start(f32[64]{0:T(128)} %param.25) | copy-start | bytes 772
  106.4 21.4 %copy-start.1 = (bf16[144,1024]{1,0:T(8,128)(2,1)S(1)}, bf16[144,1024]{1,0:T(8,128)(2,1)}, u32[]{:S(2)}) copy-start(bf16[144,1024]{1,0:T(8,128)(2,1)} %constant.49.clone.spread) | copy-start | bytes 884740
  106.4 21.4 %copy-start.2 = (bf16[32,1024]{1,0:T(8,128)(2,1)S(1)}, bf16[32,1024]{1,0:T(8,128)(2,1)}, u32[]{:S(2)}) copy-start(bf16[32,1024]{1,0:T(8,128)(2,1)} %constant.50.clone.edges) | copy-start | bytes 196612
  107.7 14.3 %all-to-all-start.2 = ((bf16[8,2,144,128]{3,2,1,0:T(8,128)(2,1)}), bf16[8,2,144,128]{3,2,1,0:T(8,128)(2,1)S(1)}, u32[]{:S(2)}, u32[]{:S(2)}) async-start(bf16[8,2,144,128]{3,2,1,0:T(8,128)(2,1)} %merge_heads.1), calls=%async_computation.2 | async-start | bytes 1179648 | tf_op jit(solution)/shard_map/all_to_all | solution.py:442
  122.1 2.7 %collective-permute-start.18 = (bf16[144,128]{1,0:T(8,128)(2,1)S(1)}, bf16[144,128]{1,0:T(8,128)(2,1)S(1)}, u32[]{:S(2)}, u32[]{:S(2)}) collective-permute-start(bf16[144,128]{1,0:T(8,128)(2,1)S(1)} %get-tuple-element.112), channel_id=1, source_target_pairs={{0,8},{8,0},{1,9},{9,1},{2,10},{10,2},{3,11},{11,3},{4,12},{12,4},... | collective-permute-start | bytes 110600 | tf_op jit(solution)/shard_map/ppermute | solution.py:450
  122.5 5.3 %collective-permute-start.19 = (bf16[144,128]{1,0:T(8,128)(2,1)S(1)}, bf16[144,128]{1,0:T(8,128)(2,1)S(1)}, u32[]{:S(2)}, u32[]{:S(2)}) collective-permute-start(bf16[144,128]{1,0:T(8,128)(2,1)S(1)} %get-tuple-element.111), channel_id=1, source_target_pairs={{8,16},{24,32},{40,48},{56,64},{72,80},{88,96},{104,112},{120,128}... | collective-permute-start | bytes 110600 | tf_op jit(solution)/shard_map/ppermute | solution.py:452
  (2 other events, 19.4 us)

commit v7 on v6

--- a/solution.py
+++ b/solution.py
@@ -58,6 +58,33 @@
         compiler_params=pltpu.CompilerParams(vmem_limit_bytes=12 * 2**20),
         name="mix_variables",
     )(*args)
+
+
+def project(rows, weights):
+    count = 2 * len(weights)
+
+    def body(*refs):
+        x, out = refs[0], refs[-1]
+        step = pl.program_id(0)
+        for k, w in enumerate(refs[1:-1]):
+
+            @pl.when((step >= 2 * k) & (step < 2 * k + 2))
+            def _():
+                out[...] = dot_nn(x[...], w[...]).astype(BF)
+
+    def columns(k):
+        return lambda step: (0, jnp.clip(step - 2 * k, 0, 1))
+
+    return pl.pallas_call(
+        body,
+        grid=(count,),
+        out_shape=jax.ShapeDtypeStruct((256, 128 * count), BF),
+        in_specs=[VMEM_SPEC]
+        + [pl.BlockSpec((D, 128), columns(k)) for k in range(len(weights))],
+        out_specs=pl.BlockSpec((256, 128), lambda step: (0, step)),
+        compiler_params=pltpu.CompilerParams(vmem_limit_bytes=12 * 2**20),
+        name="project_rows",
+    )(near(rows), *[pltpu.with_memory_space_constraint(w, pltpu.HBM) for w in weights])
 
 
 def norm_body(pieces, gain, out, slab):
@@ -177,7 +204,7 @@
     )(*[near(x) for x in ins])
 
 
-def merge_body(place, base, b0, b1, b2, b3, mat, out):
+def merge_body(place, base, edges, b0, b1, b2, b3, mat, out):
     parts = (b0, b1, b2, b3)
     tails = [b[256:272, :].astype(F32) for b in parts]
     context = []
@@ -196,6 +223,7 @@
         context.append(mixed.astype(BF))
     up = dot_tn(jnp.concatenate(context, axis=0), mat[...])
     own = place[0]
+    sides = edges[...].astype(F32)
     for j in range(8):
         lower = jnp.where(own == j - 1, base[31:32, :], 0.0)
         upper = jnp.where(own == j + 1, base[0:1, :], 0.0)
@@ -210,19 +238,51 @@
                     rows.append(up[token : token + 1, lanes] + edge[:, lanes])
                 else:
                     rows.append(jnp.zeros((1, 128), F32))
-            rows.append(jnp.zeros((12, 128), F32))
+            source = j - 1 if half == 0 else j + 1
+            rows.append(jnp.where(own == source, sides[4 * half : 4 * half + 4], 0.0))
+            rows.append(jnp.zeros((8, 128), F32))
             out[j, half, 128:144, :] = jnp.concatenate(rows, axis=0).astype(BF)
 
 
-def merge(place, base, parts, mat):
+def merge(place, base, edges, parts, mat):
     return pl.pallas_call(
         merge_body,
         out_shape=pltpu.VMEM((8, 2, 144, 128), BF),
-        in_specs=[SMEM_SPEC] + [VMEM_SPEC] * 6,
+        in_specs=[SMEM_SPEC] + [VMEM_SPEC] * 7,
         out_specs=VMEM_SPEC,
         compiler_params=pltpu.CompilerParams(vmem_limit_bytes=12 * 2**20),
         name="merge_heads",
-    )(place, near(base), *[near(x) for x in parts], near(mat))
+    )(place, near(base), near(edges), *[near(x) for x in parts], near(mat))
+
+
+def collect_body(flags, pieces, base, grad, own, near_out, far_out):
+    for half in range(2):
+        total = pieces[0, half].astype(F32)
+        for k in range(1, 8):
+            total = total + pieces[k, half].astype(F32)
+        own[half, 0:128, :] = (total[0:128] + base[half]).astype(BF)
+        own[half, 128:144, :] = total[128:144].astype(BF)
+    core = flags[4]
+    for side, out in ((1 - core, near_out), (core, far_out)):
+        out[0:144, :] = own[side]
+        out[144:160, :] = own[1 - side, 128:144, :]
+        for k in range(2):
+            out[160 + 64 * k : 224 + 64 * k, :] = grad[2 * side + k]
+
+
+def collect(flags, pieces, base, grad):
+    return pl.pallas_call(
+        collect_body,
+        out_shape=[
+            pltpu.VMEM((2, 144, 128), BF),
+            pltpu.VMEM((288, 128), BF),
+            pltpu.VMEM((288, 128), BF),
+        ],
+        in_specs=[SMEM_SPEC] + [VMEM_SPEC] * 3,
+        out_specs=[VMEM_SPEC] * 3,
+        compiler_params=pltpu.CompilerParams(vmem_limit_bytes=12 * 2**20),
+        name="collect_slab",
+    )(flags, near(pieces), near(base), near(grad))
 
 
 def spread_matrix():
@@ -238,11 +298,12 @@
 
 
 def edge_matrix():
-    edges = np.zeros((2, 2, 8, 8, 128), np.float32)
+    edges = np.zeros((2, 16, 2, 4, 128), np.float32)
     for q in range(2):
-        for r in range(8):
-            edges[0, q, r, r, q] = 1
-            edges[1, q, r, r, 126 + q] = 1
+        for r in range(4):
+            k, m = divmod(4 * q + r, 2)
+            edges[0, 4 + k, m, r, 126 + q] = 1
+            edges[1, 4 + k, m, r, q] = 1
     return edges.reshape(32, 1024)
 
 
@@ -261,24 +322,34 @@
 
 
 def fine_body(factor):
-    def body(flags, own, near_up, far_up, spread, edges, grad, rim, mats, bias, field, grad_fine, terms):
+    def body(flags, own, near_up, far_up, spread, edges, grad, mats, bias, field, grad_fine, terms):
         spread_all = spread[...]
         ups = []
         second_core = flags[4] > 0
         close, distant = near_up[...].astype(F32), far_up[...].astype(F32)
         prev = jnp.where(second_core, close, distant).astype(BF)
         nxt = jnp.where(second_core, distant, close).astype(BF)
-        for block in (prev, own[0], own[1], nxt):
+        for block in (prev[0:144], own[0], own[1], nxt[0:144]):
             wide = dot_tn(block, spread_all)
             for a in range(2):
                 ups.append(
                     wide[0:64, 512 * a : 512 * a + 256] + wide[64:128, 512 * a + 256 : 512 * a + 512]
                 )
-        rims = dot_tn(rim[...], edges[...])
-        grads = [
-            jnp.concatenate([grad[r].astype(F32), rims[:, r * 128 : (r + 1) * 128]], axis=1)
-            for r in range(8)
+        edge_all = edges[...]
+        rows_of = [
+            [prev[160:224], prev[224:288]],
+            [grad[r] for r in range(4)],
+            [nxt[160:224], nxt[224:288]],
         ]
+        lefts = [prev[144:160], own[0, 128:144, :], nxt[128:144]]
+        rights = [prev[128:144], own[1, 128:144, :], nxt[144:160]]
+        grads = []
+        for k in range(3):
+            wide = dot_tn(jnp.concatenate([lefts[k], rights[k]], axis=0), edge_all)
+            for r, row in enumerate(rows_of[k]):
+                at = (r + 2 if k == 0 else r) * 128
+                rim = wide[0:64, at : at + 128] + wide[64:128, 512 + at : 640 + at]
+                grads.append(jnp.concatenate([row.astype(F32), rim], axis=1))
         up_taps = [shifted(u).astype(BF) for u in ups]
         grad_taps = [shifted(g).astype(BF) for g in grads]
         pre_all = dot_nn(mats[0], jnp.concatenate(up_taps, axis=1))
@@ -320,7 +391,7 @@
             ).astype(BF)
             grad_fine[j] = (gather(fine_all, j, 128) + grads[j + 2][:, 0:128]).astype(BF)
         d_own = jnp.concatenate(d_rows, axis=1)
-        g_own = jnp.concatenate([grad[r] for r in range(2, 6)], axis=1)
+        g_own = jnp.concatenate([grad[r] for r in range(4)], axis=1)
         for p in range(3):
             up_cut = jnp.concatenate([up_taps[r][:, 0:128] for r in range(p + 1, p + 5)], axis=1)
             first = dot_nt(up_cut, d_own)
@@ -336,7 +407,7 @@
     return body
 
 
-def fine_stage(flags, own, near_up, far_up, spread, edges, grad, rim, mats, bias, factor):
+def fine_stage(flags, own, near_up, far_up, spread, edges, grad, mats, bias, factor):
     return pl.pallas_call(
         fine_body(factor),
         out_shape=[
@@ -344,11 +415,11 @@
             jax.ShapeDtypeStruct((4, 64, 128), BF),
             pltpu.VMEM((768, 128), BF),
         ],
-        in_specs=[SMEM_SPEC] + [VMEM_SPEC] * 9,
+        in_specs=[SMEM_SPEC] + [VMEM_SPEC] * 8,
         out_specs=[VMEM_SPEC] * 3,
         compiler_params=pltpu.CompilerParams(vmem_limit_bytes=20 * 2**20),
         name="fine_stage",
-    )(flags, *[near(x) for x in (own, near_up, far_up, spread, edges, grad, rim, mats, bias)])
+    )(flags, *[near(x) for x in (own, near_up, far_up, spread, edges, grad, mats, bias)])
 
 
 def copies(piece, axis, count):
@@ -376,46 +447,19 @@
 ):
     var_at = lax.axis_index(VAR)
     band_at = lax.axis_index(BAND)
-    shift_down = [(i, i + 1) for i in range(31)]
-    shift_up = [(i + 1, i) for i in range(31)]
     group = ("xh", "core")
 
     core_at = lax.axis_index("core")
     turned = jnp.transpose(patches, (0, 1, 3, 2)).reshape(128, 256)
     partial_mix = mix(turned, w_embed.reshape(128, D), var_bias).reshape(8, 32, D)
-    partial_mix, cells, wo, wk, wv = lax.optimization_barrier((partial_mix, cotangent, wo, wk, wv))
     pieces = lax.all_to_all(partial_mix, VAR, 0, 0)
-    up_mat = jnp.dot(wo, w_up, preferred_element_type=F32).astype(BF)
-    wkv = jnp.concatenate([wk, wv], axis=1)
-    grad_rows = jnp.concatenate(
-        [
-            lax.ppermute(cells[2:4], BAND, shift_down),
-            cells,
-            lax.ppermute(cells[0:2], BAND, shift_up),
-        ],
-        axis=0,
-    )
-    pieces, up_mat, wkv, grad_rows = lax.optimization_barrier((pieces, up_mat, wkv, grad_rows))
     spread_out, slab = norm_copies(pieces, agg_gain.reshape(1, D))
-    spread_out, slab, grad_rows, bias1 = lax.optimization_barrier(
-        (spread_out, slab, grad_rows, bias1)
-    )
     normed = lax.all_to_all(spread_out, VAR, 0, 0).reshape(256, D)
-    edge_right = jnp.transpose(grad_rows[:, :, 0:2], (2, 0, 1)).reshape(16, C)
-    edge_left = jnp.transpose(grad_rows[:, :, 126:128], (2, 0, 1)).reshape(16, C)
-    from_right = lax.ppermute(edge_right, VAR, [(i + 1, i) for i in range(7)])
-    from_left = lax.ppermute(edge_left, VAR, [(i, i + 1) for i in range(7)])
-    rim = jnp.concatenate([from_right, from_left], axis=0)
-    bias = bias1.reshape(C, 1)
-    flags = jnp.stack(
-        [band_at > 0, band_at < 31, var_at > 0, var_at < 7, core_at > 0]
-    ).astype(jnp.int32)
-    normed, rim, bias, flags = lax.optimization_barrier((normed, rim, bias, flags))
-
-    keyvals = jnp.dot(normed, wkv, preferred_element_type=F32).astype(BF)
+
+    keyvals = project(normed, [wk, wv])
     ahead = lax.ppermute(keyvals, "z", turn(8, 1))
     behind = lax.ppermute(keyvals, "z", turn(8, -1))
-    queries = jnp.dot(normed, wq, preferred_element_type=F32).astype(BF)
+    queries = project(normed, [wq])
     all_queries = [queries] + [lax.ppermute(queries, group, flip(4, k)) for k in (2, 3, 1)]
     fresh = [keyvals, ahead, behind]
     ahead = lax.ppermute(ahead, "z", turn(8, 1))
@@ -429,15 +473,30 @@
         ahead = lax.ppermute(ahead, "z", turn(8, 1))
         behind = lax.ppermute(behind, "z", turn(8, -1))
         carry = flash_step(all_queries, fresh, carry, False)
-        ahead, behind, carry = lax.optimization_barrier((ahead, behind, carry))
+        if step == 2:
+            carry, wo = lax.optimization_barrier((carry, wo))
+            up_mat = jnp.dot(wo, w_up, preferred_element_type=F32).astype(BF)
+            ahead, behind, carry, up_mat = lax.optimization_barrier((ahead, behind, carry, up_mat))
+        else:
+            ahead, behind, carry = lax.optimization_barrier((ahead, behind, carry))
     fresh = [ahead, behind]
 
     blocks = list(flash_step(all_queries, fresh, carry, True))
-    blocks[0], slab = lax.optimization_barrier((blocks[0], slab))
+    blocks[0], slab, cells, bias1 = lax.optimization_barrier((blocks[0], slab, cotangent, bias1))
     base = jnp.dot(slab, w_up, preferred_element_type=F32)
+    edges = jnp.concatenate(
+        [
+            jnp.transpose(cells[:, :, at : at + 2], (2, 0, 1)).reshape(4, 128) for at in (126, 0)
+        ],
+        axis=0,
+    )
+    bias = bias1.reshape(C, 1)
+    flags = jnp.stack(
+        [band_at > 0, band_at < 31, var_at > 0, var_at < 7, core_at > 0]
+    ).astype(jnp.int32)
     parts = [blocks[0]] + [lax.ppermute(b, group, flip(4, k)) for b, k in zip(blocks[1:], (2, 3, 1))]
     place = var_at.reshape(1).astype(jnp.int32)
-    merged = merge(place, base, parts, up_mat)
+    merged = merge(place, base, edges, parts, up_mat)
     merged, conv1, conv2 = lax.optimization_barrier((merged, conv1, conv2))
     pieces = lax.all_to_all(merged, VAR, 0, 0)
     mats = jnp.stack(
@@ -445,15 +504,14 @@
     )
     pieces, mats = lax.optimization_barrier((pieces, mats))
     base_main = jnp.transpose(base.reshape(32, 2, 4, 128), (1, 2, 0, 3)).reshape(2, 128, 128)
-    base_all = jnp.pad(base_main, ((0, 0), (0, 16), (0, 0)))
-    up = (jnp.sum(pieces.astype(F32), axis=0) + base_all).astype(BF)
-    near_up = lax.ppermute(lax.dynamic_index_in_dim(up, 1 - core_at, 0, False), "core", flip(2, 1))
+    up, near_rows, far_rows = collect(flags, pieces, base_main, cells)
+    near_up = lax.ppermute(near_rows, "core", flip(2, 1))
     pairs = [(i, i + 1) for i in range(1, 31, 2)] + [(i + 1, i) for i in range(1, 31, 2)]
-    far_up = lax.ppermute(lax.dynamic_index_in_dim(up, core_at, 0, False), BAND, pairs)
+    far_up = lax.ppermute(far_rows, BAND, pairs)
     factor = 1.0 / math.sqrt(128 * 1024)
     spread = jnp.asarray(spread_matrix(), BF)
     field_out, grad_fine, terms = fine_stage(
-        flags, up, near_up, far_up, spread, jnp.asarray(edge_matrix(), BF), grad_rows, rim, mats, bias, factor
+        flags, up, near_up, far_up, spread, jnp.asarray(edge_matrix(), BF), cells, mats, bias, factor
     )
     shares = lax.all_to_all(terms.reshape(32, 24, 128), PLANE, 0, 0)
     share = jnp.sum(shares.astype(F32), axis=0).astype(BF)

time: 172 us -> 175 us (1.017)
  blocking collectives: 39 us -> 77.8 us
  starting transfers between devices: 54.9 us -> 35.4 us
  waiting for transfers between devices: 44.8 us -> 26.6 us
  Pallas kernels: 16.8 us -> 21.6 us
  matrix products: 8.24 us -> 5.23 us
  local copies, waits for them, and re-layouts: 4.4 us -> 6.2 us
    all_to_all x0 -> x2, blocking collectives: none -> 37.4 us  [the longest x1 20.7 us: device_step(): pieces = lax.all_to_all(partial_mix, VAR, 0, 0)]
    all_to_all x2 -> x0, starting transfers between devices: 10 us -> none  [the longest x1 5.93 us: device_step(): pieces = lax.all_to_all(partial_mix, VAR, 0, 0)]
    ppermute x6 -> x2, starting transfers between devices: 13.7 us -> 4.14 us  [the longest x1 2.13 us: device_step(): far_up = lax.ppermute(far_rows, BAND, pairs)]
    ppermute x6 -> x2, waiting for transfers between devices: 10.2 us -> 3.42 us  [the longest x1 3.41 us: device_step(): far_up = lax.ppermute(far_rows, BAND, pairs)]
    pallas_call x0 -> x3, Pallas kernels: none -> 6.38 us  [the longest x2 5.75 us: project(): pl.pallas_call(body, grid=(count,), out_shape=jax.ShapeDtypeStruct((256,...]
    ppermute x1, starting transfers between devices: 8.09 us -> 4.04 us  [device_step(): behind = lax.ppermute(keyvals, 'z', turn(8, -1))]
    dot_general x2 -> x0, matrix products: 3.98 us -> none  [the longest x1 2.31 us: device_step(): keyvals = jnp.dot(normed, wkv, preferred_element_type=F32).astype(BF)]
    all_to_all x2 -> x0, waiting for transfers between devices: 3.63 us -> none  [the longest x1 2.08 us: device_step(): pieces = lax.all_to_all(partial_mix, VAR, 0, 0)]
  transfers between devices with their start and end apart: 23 -> 17, of which waited for: 13 -> 7; matrix products, arithmetic and copies ran while one was open for 6% -> 5% of each run, Pallas kernels for 4% -> 5%
where the time goes in v7:
time: 175 us; the launch traced here: 174 us
  blocking collectives  77.8 us (44%)
  starting transfers between devices  35.4 us (20%)
  waiting for transfers between devices  26.6 us (15%)
  Pallas kernels  21.6 us (12%)
  local copies, waits for them, and re-layouts  6.2 us (4%)
  matrix products  5.23 us (3%)
    all_to_all x2, blocking collectives, copies(): lax.all_to_all(jnp.broadcast_to(piece[None], (count,) + piece.shape), axi...  23.5 us
    all_to_all x1, blocking collectives, device_step(): pieces = lax.all_to_all(partial_mix, VAR, 0, 0)  20.7 us
    all_to_all x1, blocking collectives, device_step(): shares = lax.all_to_all(terms.reshape(32, 24, 128), PLANE, 0, 0)  17 us
    all_to_all x1, blocking collectives, device_step(): normed = lax.all_to_all(spread_out, VAR, 0, 0).reshape(256, D)  16.7 us
    all_to_all x1, waiting for transfers between devices, device_step(): pieces = lax.all_to_all(merged, VAR, 0, 0)  8.18 us
    pallas_call x4, Pallas kernels, flash_step(): pl.pallas_call(flash_kernel(blocks, len(chunks), first, last), out_shape=...  8.1 us
    ppermute x3, starting transfers between devices, device_step(): behind = lax.ppermute(behind, 'z', turn(8, -1))  7.73 us
    ppermute x3, starting transfers between devices, device_step(): lax.ppermute(queries, group, flip(4, k))  7 us
  transfers between devices with their start and end apart: 17, of which 7 were waited for; matrix products, arithmetic and copies ran while one was open for 5% of the time, Pallas kernels for 5%

profile of v7, /device:TPU:1, one launch (start us, length us, event | category | flops | bytes accessed | tf_op | source)
XLA Modules:
  0.0 174.0 jit_solution(5542588892319773906)
XLA Ops:
  0.6 2.8 %mix_variables.1 = bf16[256,2048]{1,0:T(8,128)(2,1)S(1)} custom-call(bf16[128,256]{1,0:T(8,128)(2,1)} %bitcast.66, bf16[128,2048]{1,0:T(8,128)(2,1)} %bitcast.63, f32[2,2048]{1,0:T(2,128)} %offsets.1), custom_call_target="tpu_custom_call" | custom-call | tf_op jit(solution)/shard_map/mix_variables/pallas_call | solution.py:48
  3.4 20.7 %all_to_all.30.pieces = bf16[8,32,2048]{2,1,0:T(8,128)(2,1)S(1)} all-to-all(bf16[8,32,2048]{2,1,0:T(8,128)(2,1)S(1)} %bitcast.51), channel_id=1, replica_groups=mesh['xh'=2,'z'=8,'core'=2,'y'=4,'xl'=2] {'y','xl'}, dimensions={0} | all-to-all | bytes 2097152 | tf_op jit(solution)/shard_map/all_to_all | solution.py:455
  25.8 16.7 %all_to_all.31 = bf16[8,32,2048]{2,1,0:T(8,128)(2,1)S(1)} all-to-all(bf16[8,32,2048]{2,1,0:T(8,128)(2,1)S(1)} %get-tuple-element.48), channel_id=1, replica_groups=mesh['xh'=2,'z'=8,'core'=2,'y'=4,'xl'=2] {'y','xl'}, dimensions={0} | all-to-all | bytes 2097152 | tf_op jit(solution)/shard_map/all_to_all | solution.py:457
  42.5 3.8 %project_rows.3.refs_4_ = bf16[256,512]{1,0:T(8,128)(2,1)S(1)} custom-call(bf16[256,2048]{1,0:T(8,128)(2,1)S(1)} %bitcast.49, bf16[2048,256]{1,0:T(8,128)(2,1)} %refs_1_.3, bf16[2048,256]{1,0:T(8,128)(2,1)} %refs_2_.1), custom_call_target="tpu_custom_call" | custom-call | tf_op jit(solution)/shard_map/project_rows/pallas_call | solution.py:78
  46.3 1.7 collective-permute-start.3
  48.0 4.0 %collective-permute-start.5 = (bf16[256,512]{1,0:T(8,128)(2,1)S(1)}, bf16[256,512]{1,0:T(8,128)(2,1)S(1)}, u32[]{:S(2)}, u32[]{:S(2)}) collective-permute-start(bf16[256,512]{1,0:T(8,128)(2,1)S(1)} %project_rows.3.refs_4_), channel_id=1, source_target_pairs={{0,112},{16,0},{32,16},{48,32},{64,48},{80,64},{96,80},{112,96},{1... | collective-permute-start | bytes 786440 | tf_op jit(solution)/shard_map/ppermute | solution.py:461
  52.0 4.0 %collective-permute-done.3.refs_5_ = bf16[256,512]{1,0:T(8,128)(2,1)S(1)} collective-permute-done((bf16[256,512]{1,0:T(8,128)(2,1)S(1)}, bf16[256,512]{1,0:T(8,128)(2,1)S(1)}, u32[]{:S(2)}, u32[]{:S(2)}) %collective-permute-start.3) | collective-permute-done | bytes 262176 | tf_op jit(solution)/shard_map/ppermute | solution.py:460
  56.0 2.7 %collective-permute-start.6 = (bf16[256,512]{1,0:T(8,128)(2,1)S(1)}, bf16[256,512]{1,0:T(8,128)(2,1)S(1)}, u32[]{:S(2)}, u32[]{:S(2)}) collective-permute-start(bf16[256,512]{1,0:T(8,128)(2,1)S(1)} %collective-permute-done.5.refs_6_), channel_id=1, source_target_pairs={{0,112},{16,0},{32,16},{48,32},{64,48},{80,64},{96,80},{112,96},{1... | collective-permute-start | bytes 786440 | tf_op jit(solution)/shard_map/ppermute | solution.py:466
  58.7 2.0 %project_rows.2.refs_0_ = bf16[256,256]{1,0:T(8,128)(2,1)S(1)} custom-call(bf16[256,2048]{1,0:T(8,128)(2,1)S(1)} %bitcast.50, bf16[2048,256]{1,0:T(8,128)(2,1)} %refs_1_.2), custom_call_target="tpu_custom_call" | custom-call | tf_op jit(solution)/shard_map/project_rows/pallas_call | solution.py:78
  60.7 2.5 %collective-permute-start = (bf16[256,256]{1,0:T(8,128)(2,1)S(1)}, bf16[256,256]{1,0:T(8,128)(2,1)S(1)}, u32[]{:S(2)}, u32[]{:S(2)}) collective-permute-start(bf16[256,256]{1,0:T(8,128)(2,1)S(1)} %project_rows.2.refs_0_), channel_id=1, source_target_pairs={{0,128},{8,136},{128,0},{136,8},{1,129},{9,137},{129,1},{137,9},{2... | collective-permute-start | bytes 393224 | tf_op jit(solution)/shard_map/ppermute | solution.py:463
  63.2 4.5 %collective-permute-start.1 = (bf16[256,256]{1,0:T(8,128)(2,1)S(1)}, bf16[256,256]{1,0:T(8,128)(2,1)S(1)}, u32[]{:S(2)}, u32[]{:S(2)}) collective-permute-start(bf16[256,256]{1,0:T(8,128)(2,1)S(1)} %project_rows.2.refs_0_), channel_id=1, source_target_pairs={{0,136},{8,128},{128,8},{136,0},{1,137},{9,129},{129,9},{137,1},{2... | collective-permute-start | bytes 393224 | tf_op jit(solution)/shard_map/ppermute | solution.py:463
  67.7 5.0 %collective-permute-done.1.refs_2_ = bf16[256,256]{1,0:T(8,128)(2,1)S(1)} collective-permute-done((bf16[256,256]{1,0:T(8,128)(2,1)S(1)}, bf16[256,256]{1,0:T(8,128)(2,1)S(1)}, u32[]{:S(2)}, u32[]{:S(2)}) %collective-permute-start.1) | collective-permute-done | bytes 131104 | tf_op jit(solution)/shard_map/ppermute | solution.py:463
  72.6 2.4 %flash_step.3 = (f32[8,1024]{1,0:T(8,128)S(1)}, f32[256,1024]{1,0:T(8,128)S(1)}) custom-call(bf16[256,256]{1,0:T(8,128)(2,1)S(1)} %project_rows.2.refs_0_, bf16[256,256]{1,0:T(8,128)(2,1)S(1)} %collective-permute-done.refs_1_, bf16[256,256]{1,0:T(8,128)(2,1)S(1)} %collective-permute-done.1.refs_2_, bf16[256,256]{1,0:T(8,128)(2,1)S(1)} %collective-permute-done.2.refs_3_, ...), custom_call_target="tpu_custom_call" | custom-call | tf_op jit(solution)/shard_map/flash_step/pallas_call | solution.py:190
  75.2 2.7 %collective-permute-start.8 = (bf16[256,512]{1,0:T(8,128)(2,1)S(1)}, bf16[256,512]{1,0:T(8,128)(2,1)S(1)}, u32[]{:S(2)}, u32[]{:S(2)}) collective-permute-start(bf16[256,512]{1,0:T(8,128)(2,1)S(1)} %collective-permute-done.6.refs_5_), channel_id=1, source_target_pairs={{0,112},{16,0},{32,16},{48,32},{64,48},{80,64},{96,80},{112,96},{1... | collective-permute-start | bytes 786440 | tf_op jit(solution)/shard_map/ppermute | solution.py:474
  77.9 2.0 %flash_step.4 = (f32[8,1024]{1,0:T(8,128)S(1)}, f32[256,1024]{1,0:T(8,128)S(1)}) custom-call(bf16[256,256]{1,0:T(8,128)(2,1)S(1)} %project_rows.2.refs_0_, bf16[256,256]{1,0:T(8,128)(2,1)S(1)} %collective-permute-done.refs_1_, bf16[256,256]{1,0:T(8,128)(2,1)S(1)} %collective-permute-done.1.refs_2_, bf16[256,256]{1,0:T(8,128)(2,1)S(1)} %collective-permute-done.2.refs_3_, ...), custom_call_target="tpu_custom_call" | custom-call | tf_op jit(solution)/shard_map/flash_step/pallas_call | solution.py:190
  79.9 2.1 %convolution_convert_fusion.mat = bf16[256,1024]{1,0:T(8,128)(2,1)} fusion(bf16[256,2048]{1,0:T(8,128)(2,1)S(1)} %copy-done, bf16[2048,1024]{1,0:T(8,128)(2,1)S(1)} %copy-done.7), kind=kOutput, calls=%fused_computation | convolution fusion | flops 1074003968 | bytes 5767168 | tf_op jit(solution)/shard_map/dot_general | solution.py:478
  83.8 2.4 %collective-permute-start.10 = (bf16[128,512]{1,0:T(8,128)(2,1)}, bf16[128,512]{1,0:T(8,128)(2,1)S(1)}, u32[]{:S(2)}, u32[]{:S(2)}) collective-permute-start(bf16[128,512]{1,0:T(8,128)(2,1)} %slice.22), channel_id=1, source_target_pairs={{0,112},{16,0},{32,16},{48,32},{64,48},{80,64},{96,80},{112,96},{1... | collective-permute-start | bytes 393224 | tf_op jit(solution)/shard_map/ppermute | solution.py:474
  86.8 1.9 %flash_step.5 = (f32[8,1024]{1,0:T(8,128)S(1)}, f32[256,1024]{1,0:T(8,128)S(1)}) custom-call(bf16[256,256]{1,0:T(8,128)(2,1)S(1)} %project_rows.2.refs_0_, bf16[256,256]{1,0:T(8,128)(2,1)S(1)} %collective-permute-done.refs_1_, bf16[256,256]{1,0:T(8,128)(2,1)S(1)} %collective-permute-done.1.refs_2_, bf16[256,256]{1,0:T(8,128)(2,1)S(1)} %collective-permute-done.2.refs_3_, ...), custom_call_target="tpu_custom_call" | custom-call | tf_op jit(solution)/shard_map/flash_step/pallas_call | solution.py:190
  88.7 3.4 %collective-permute-done.9.refs_4_ = bf16[128,512]{1,0:T(8,128)(2,1)S(1)} collective-permute-done((bf16[128,512]{1,0:T(8,128)(2,1)}, bf16[128,512]{1,0:T(8,128)(2,1)S(1)}, u32[]{:S(2)}, u32[]{:S(2)}) %collective-permute-start.9) | collective-permute-done | bytes 131104 | tf_op jit(solution)/shard_map/ppermute | solution.py:473
  92.1 1.8 %flash_last.1 = (bf16[272,256]{1,0:T(8,128)(2,1)S(1)}, bf16[272,256]{1,0:T(8,128)(2,1)}, bf16[272,256]{1,0:T(8,128)(2,1)S(1)}, bf16[272,256]{1,0:T(8,128)(2,1)S(1)}) custom-call(bf16[256,256]{1,0:T(8,128)(2,1)S(1)} %project_rows.2.refs_0_, bf16[256,256]{1,0:T(8,128)(2,1)S(1)} %collective-permute-done.refs_1_, ...), custom_call_target="tpu_custom_call" | custom-call | tf_op jit(solution)/shard_map/flash_last/pallas_call | solution.py:190
  93.9 4.9 %collective-permute-start.11 = (bf16[272,256]{1,0:T(8,128)(2,1)}, bf16[272,256]{1,0:T(8,128)(2,1)S(1)}, u32[]{:S(2)}, u32[]{:S(2)}) collective-permute-start(bf16[272,256]{1,0:T(8,128)(2,1)} %get-tuple-element.75), channel_id=1, source_target_pairs={{0,128},{8,136},{128,0},{136,8},{1,129},{9,137},{129,1},{137,9},{2... | collective-permute-start | bytes 417800 | tf_op jit(solution)/shard_map/ppermute | solution.py:497
  98.8 2.0 %collective-permute-start.12 = (bf16[272,256]{1,0:T(8,128)(2,1)S(1)}, bf16[272,256]{1,0:T(8,128)(2,1)S(1)}, u32[]{:S(2)}, u32[]{:S(2)}) collective-permute-start(bf16[272,256]{1,0:T(8,128)(2,1)S(1)} %get-tuple-element.76), channel_id=1, source_target_pairs={{0,136},{8,128},{128,8},{136,0},{1,137},{9,129},{129,9},{137,1},{2... | collective-permute-start | bytes 417800 | tf_op jit(solution)/shard_map/ppermute | solution.py:497
  100.8 3.1 %fusion.1.base = f32[32,1024]{1,0:T(8,128)S(1)} fusion(bf16[32,2048]{1,0:T(8,128)(2,1)} %copy-done.4, bf16[2048,1024]{1,0:T(8,128)(2,1)} %param.23), kind=kOutput, calls=%fused_computation.10 | convolution fusion | flops 134217728 | bytes 4456448 | tf_op jit(solution)/shard_map/dot_general | solution.py:486
  107.3 3.8 %all-to-all-start.2 = ((bf16[8,2,144,128]{3,2,1,0:T(8,128)(2,1)}), bf16[8,2,144,128]{3,2,1,0:T(8,128)(2,1)S(1)}, u32[]{:S(2)}, u32[]{:S(2)}) async-start(bf16[8,2,144,128]{3,2,1,0:T(8,128)(2,1)} %merge_heads.1), calls=%async_computation.2 | async-start | bytes 1179648 | tf_op jit(solution)/shard_map/all_to_all | solution.py:501
  112.7 8.2 %all-to-all-done.2.pieces = bf16[8,2,144,128]{3,2,1,0:T(8,128)(2,1)S(1)} async-done(((bf16[8,2,144,128]{3,2,1,0:T(8,128)(2,1)}), bf16[8,2,144,128]{3,2,1,0:T(8,128)(2,1)S(1)}, u32[]{:S(2)}, u32[]{:S(2)}) %all-to-all-start.2) | async-done | bytes 589856 | tf_op jit(solution)/shard_map/all_to_all | solution.py:501
  121.5 2.0 %collective-permute-start.14 = (bf16[288,128]{1,0:T(8,128)(2,1)S(1)}, bf16[288,128]{1,0:T(8,128)(2,1)S(1)}, u32[]{:S(2)}, u32[]{:S(2)}) collective-permute-start(bf16[288,128]{1,0:T(8,128)(2,1)S(1)} %get-tuple-element.84), channel_id=1, source_target_pairs={{0,8},{8,0},{1,9},{9,1},{2,10},{10,2},{3,11},{11,3},{4,12},{12,4},... | collective-permute-start | bytes 221192 | tf_op jit(solution)/shard_map/ppermute | solution.py:508
  123.5 2.1 %collective-permute-start.15 = (bf16[288,128]{1,0:T(8,128)(2,1)S(1)}, bf16[288,128]{1,0:T(8,128)(2,1)S(1)}, u32[]{:S(2)}, u32[]{:S(2)}) collective-permute-start(bf16[288,128]{1,0:T(8,128)(2,1)S(1)} %get-tuple-element.85), channel_id=1, source_target_pairs={{8,16},{24,32},{40,48},{56,64},{72,80},{88,96},{104,112},{120,128}... | collective-permute-start | bytes 221192 | tf_op jit(solution)/shard_map/ppermute | solution.py:510
  125.8 3.4 %collective-permute-done.15.far_up = bf16[288,128]{1,0:T(8,128)(2,1)S(1)} collective-permute-done((bf16[288,128]{1,0:T(8,128)(2,1)S(1)}, bf16[288,128]{1,0:T(8,128)(2,1)S(1)}, u32[]{:S(2)}, u32[]{:S(2)}) %collective-permute-start.15) | collective-permute-done | bytes 73760 | tf_op jit(solution)/shard_map/ppermute | solution.py:510
  129.2 2.8 %fine_stage.1 = (bf16[4,64,128]{2,1,0:T(8,128)(2,1)}, bf16[4,64,128]{2,1,0:T(8,128)(2,1)}, bf16[768,128]{1,0:T(8,128)(2,1)S(1)}) custom-call(s32[5]{0:T(128)S(1)} %convert_element_type.16.flags, bf16[2,144,128]{2,1,0:T(8,128)(2,1)S(1)} %get-tuple-element.83.own, bf16[288,128]{1,0:T(8,128)(2,1)S(1)} %collective-permute-done.14.near_up, ...), custom_call_target="tpu_custom_call" | custom-call | tf_op jit(solution)/shard_map/fine_stage/pallas_call | solution.py:411
  132.0 17.0 %all_to_all.32 = bf16[32,24,128]{2,1,0:T(8,128)(2,1)S(1)} all-to-all(bf16[32,24,128]{2,1,0:T(8,128)(2,1)S(1)} %bitcast.53), channel_id=1, replica_groups=mesh['xh'=2,'z'=8,'core'=2,'y'=4,'xl'=2] {'xh','core','y','xl'}, dimensions={0} | all-to-all | bytes 393216 | tf_op jit(solution)/shard_map/all_to_all | solution.py:516
  149.0 10.0 %all_to_all.33 = bf16[8,24,128]{2,1,0:T(8,128)(2,1)S(1)} all-to-all(bf16[8,24,128]{2,1,0:T(8,128)(2,1)S(1)} %broadcast_in_dim.4), channel_id=1, replica_groups=mesh['xh'=2,'z'=8,'core'=2,'y'=4,'xl'=2] {'z'}, dimensions={0} | all-to-all | bytes 98304 | tf_op jit(solution)/shard_map/all_to_all | solution.py:426
  159.1 13.5 %all_to_all.34 = bf16[32,24,128]{2,1,0:T(8,128)(2,1)S(1)} all-to-all(bf16[32,24,128]{2,1,0:T(8,128)(2,1)S(1)} %broadcast_in_dim.5), channel_id=1, replica_groups=mesh['xh'=2,'z'=8,'core'=2,'y'=4,'xl'=2] {'xh','core','y','xl'}, dimensions={0} | all-to-all | bytes 393216 | tf_op jit(solution)/shard_map/all_to_all | solution.py:426
  (73 shorter events, 11.4 us)
Async XLA Ops:
  0.6 79.2 %copy-start = (bf16[256,2048]{1,0:T(8,128)(2,1)S(1)}, bf16[256,2048]{1,0:T(8,128)(2,1)}, u32[]{:S(2)}) copy-start(bf16[256,2048]{1,0:T(8,128)(2,1)} %param.22) | copy-start | bytes 3145732
  24.2 0.7 copy-start.6
  25.1 0.7 copy-start.4
  42.5 37.4 %copy-start.7 = (bf16[2048,1024]{1,0:T(8,128)(2,1)S(1)}, bf16[2048,1024]{1,0:T(8,128)(2,1)}, u32[]{:S(2)}) copy-start(bf16[2048,1024]{1,0:T(8,128)(2,1)} %param.23) | copy-start | bytes 12582916
  46.3 9.7 %collective-permute-start.3 = (bf16[256,512]{1,0:T(8,128)(2,1)S(1)}, bf16[256,512]{1,0:T(8,128)(2,1)S(1)}, u32[]{:S(2)}, u32[]{:S(2)}) collective-permute-start(bf16[256,512]{1,0:T(8,128)(2,1)S(1)} %project_rows.3.refs_4_), channel_id=1, source_target_pairs={{0,16},{16,32},{32,48},{48,64},{64,80},{80,96},{96,112},{112,0},{1... | collective-permute-start | bytes 786440 | tf_op jit(solution)/shard_map/ppermute | solution.py:460
  48.0 8.1 %collective-permute-start.5 = (bf16[256,512]{1,0:T(8,128)(2,1)S(1)}, bf16[256,512]{1,0:T(8,128)(2,1)S(1)}, u32[]{:S(2)}, u32[]{:S(2)}) collective-permute-start(bf16[256,512]{1,0:T(8,128)(2,1)S(1)} %project_rows.3.refs_4_), channel_id=1, source_target_pairs={{0,112},{16,0},{32,16},{48,32},{64,48},{80,64},{96,80},{112,96},{1... | collective-permute-start | bytes 786440 | tf_op jit(solution)/shard_map/ppermute | solution.py:461
  56.0 19.1 %collective-permute-start.4 = (bf16[256,512]{1,0:T(8,128)(2,1)S(1)}, bf16[256,512]{1,0:T(8,128)(2,1)S(1)}, u32[]{:S(2)}, u32[]{:S(2)}) collective-permute-start(bf16[256,512]{1,0:T(8,128)(2,1)S(1)} %collective-permute-done.3.refs_5_), channel_id=1, source_target_pairs={{0,16},{16,32},{32,48},{48,64},{64,80},{80,96},{96,112},{112,0},{1... | collective-permute-start | bytes 786440 | tf_op jit(solution)/shard_map/ppermute | solution.py:465
  56.0 19.1 %collective-permute-start.6 = (bf16[256,512]{1,0:T(8,128)(2,1)S(1)}, bf16[256,512]{1,0:T(8,128)(2,1)S(1)}, u32[]{:S(2)}, u32[]{:S(2)}) collective-permute-start(bf16[256,512]{1,0:T(8,128)(2,1)S(1)} %collective-permute-done.5.refs_6_), channel_id=1, source_target_pairs={{0,112},{16,0},{32,16},{48,32},{64,48},{80,64},{96,80},{112,96},{1... | collective-permute-start | bytes 786440 | tf_op jit(solution)/shard_map/ppermute | solution.py:466
  60.7 7.0 %collective-permute-start = (bf16[256,256]{1,0:T(8,128)(2,1)S(1)}, bf16[256,256]{1,0:T(8,128)(2,1)S(1)}, u32[]{:S(2)}, u32[]{:S(2)}) collective-permute-start(bf16[256,256]{1,0:T(8,128)(2,1)S(1)} %project_rows.2.refs_0_), channel_id=1, source_target_pairs={{0,128},{8,136},{128,0},{136,8},{1,129},{9,137},{129,1},{137,9},{2... | collective-permute-start | bytes 393224 | tf_op jit(solution)/shard_map/ppermute | solution.py:463
  63.2 9.4 %collective-permute-start.1 = (bf16[256,256]{1,0:T(8,128)(2,1)S(1)}, bf16[256,256]{1,0:T(8,128)(2,1)S(1)}, u32[]{:S(2)}, u32[]{:S(2)}) collective-permute-start(bf16[256,256]{1,0:T(8,128)(2,1)S(1)} %project_rows.2.refs_0_), channel_id=1, source_target_pairs={{0,136},{8,128},{128,8},{136,0},{1,137},{9,129},{129,9},{137,1},{2... | collective-permute-start | bytes 393224 | tf_op jit(solution)/shard_map/ppermute | solution.py:463
  67.6 5.0 %collective-permute-start.2 = (bf16[256,256]{1,0:T(8,128)(2,1)S(1)}, bf16[256,256]{1,0:T(8,128)(2,1)S(1)}, u32[]{:S(2)}, u32[]{:S(2)}) collective-permute-start(bf16[256,256]{1,0:T(8,128)(2,1)S(1)} %project_rows.2.refs_0_), channel_id=1, source_target_pairs={{0,8},{8,0},{128,136},{136,128},{1,9},{9,1},{129,137},{137,129},{2... | collective-permute-start | bytes 393224 | tf_op jit(solution)/shard_map/ppermute | solution.py:463
  75.1 8.0 %collective-permute-start.7 = (bf16[256,512]{1,0:T(8,128)(2,1)S(1)}, bf16[256,512]{1,0:T(8,128)(2,1)S(1)}, u32[]{:S(2)}, u32[]{:S(2)}) collective-permute-start(bf16[256,512]{1,0:T(8,128)(2,1)S(1)} %collective-permute-done.4.refs_4_), channel_id=1, source_target_pairs={{0,16},{16,32},{32,48},{48,64},{64,80},{80,96},{96,112},{112,0},{1... | collective-permute-start | bytes 786440 | tf_op jit(solution)/shard_map/ppermute | solution.py:473
  75.2 7.9 %collective-permute-start.8 = (bf16[256,512]{1,0:T(8,128)(2,1)S(1)}, bf16[256,512]{1,0:T(8,128)(2,1)S(1)}, u32[]{:S(2)}, u32[]{:S(2)}) collective-permute-start(bf16[256,512]{1,0:T(8,128)(2,1)S(1)} %collective-permute-done.6.refs_5_), channel_id=1, source_target_pairs={{0,112},{16,0},{32,16},{48,32},{64,48},{80,64},{96,80},{112,96},{1... | collective-permute-start | bytes 786440 | tf_op jit(solution)/shard_map/ppermute | solution.py:474
  83.8 4.9 %collective-permute-start.10 = (bf16[128,512]{1,0:T(8,128)(2,1)}, bf16[128,512]{1,0:T(8,128)(2,1)S(1)}, u32[]{:S(2)}, u32[]{:S(2)}) collective-permute-start(bf16[128,512]{1,0:T(8,128)(2,1)} %slice.22), channel_id=1, source_target_pairs={{0,112},{16,0},{32,16},{48,32},{64,48},{80,64},{96,80},{112,96},{1... | collective-permute-start | bytes 393224 | tf_op jit(solution)/shard_map/ppermute | solution.py:474
  86.8 5.2 %collective-permute-start.9 = (bf16[128,512]{1,0:T(8,128)(2,1)}, bf16[128,512]{1,0:T(8,128)(2,1)S(1)}, u32[]{:S(2)}, u32[]{:S(2)}) collective-permute-start(bf16[128,512]{1,0:T(8,128)(2,1)} %slice.21), channel_id=1, source_target_pairs={{0,16},{16,32},{32,48},{48,64},{64,80},{80,96},{96,112},{112,0},{1... | collective-permute-start | bytes 393224 | tf_op jit(solution)/shard_map/ppermute | solution.py:473
  86.8 17.1 %copy-start.1 = (bf16[4,64,128]{2,1,0:T(8,128)(2,1)S(1)}, bf16[4,64,128]{2,1,0:T(8,128)(2,1)}, u32[]{:S(2)}) copy-start(bf16[4,64,128]{2,1,0:T(8,128)(2,1)} %grad.1) | copy-start | bytes 196612
  88.7 17.3 %copy-start.2 = (bf16[256,1024]{1,0:T(8,128)(2,1)S(1)}, bf16[256,1024]{1,0:T(8,128)(2,1)}, u32[]{:S(2)}) copy-start(bf16[256,1024]{1,0:T(8,128)(2,1)} %convolution_convert_fusion.mat) | copy-start | bytes 1572868
  93.9 10.6 %collective-permute-start.11 = (bf16[272,256]{1,0:T(8,128)(2,1)}, bf16[272,256]{1,0:T(8,128)(2,1)S(1)}, u32[]{:S(2)}, u32[]{:S(2)}) collective-permute-start(bf16[272,256]{1,0:T(8,128)(2,1)} %get-tuple-element.75), channel_id=1, source_target_pairs={{0,128},{8,136},{128,0},{136,8},{1,129},{9,137},{129,1},{137,9},{2... | collective-permute-start | bytes 417800 | tf_op jit(solution)/shard_map/ppermute | solution.py:497
  98.8 7.3 %collective-permute-start.12 = (bf16[272,256]{1,0:T(8,128)(2,1)S(1)}, bf16[272,256]{1,0:T(8,128)(2,1)S(1)}, u32[]{:S(2)}, u32[]{:S(2)}) collective-permute-start(bf16[272,256]{1,0:T(8,128)(2,1)S(1)} %get-tuple-element.76), channel_id=1, source_target_pairs={{0,136},{8,128},{128,8},{136,0},{1,137},{9,129},{129,9},{137,1},{2... | collective-permute-start | bytes 417800 | tf_op jit(solution)/shard_map/ppermute | solution.py:497
  100.8 10.5 %copy-start.9 = (bf16[9,64,64]{2,1,0:T(8,128)(2,1)S(1)}, bf16[9,64,64]{2,1,0:T(8,128)(2,1)}, u32[]{:S(2)}) copy-start(bf16[9,64,64]{2,1,0:T(8,128)(2,1)} %param.26) | copy-start | bytes 221188
  100.8 10.9 %copy-start.8 = (bf16[9,64,64]{2,1,0:T(8,128)(2,1)S(1)}, bf16[9,64,64]{2,1,0:T(8,128)(2,1)}, u32[]{:S(2)}) copy-start(bf16[9,64,64]{2,1,0:T(8,128)(2,1)} %param.24) | copy-start | bytes 221188
  100.8 5.3 %collective-permute-start.13 = (bf16[272,256]{1,0:T(8,128)(2,1)S(1)}, bf16[272,256]{1,0:T(8,128)(2,1)S(1)}, u32[]{:S(2)}, u32[]{:S(2)}) collective-permute-start(bf16[272,256]{1,0:T(8,128)(2,1)S(1)} %get-tuple-element.77), channel_id=1, source_target_pairs={{0,8},{8,0},{128,136},{136,128},{1,9},{9,1},{129,137},{137,129},{2... | collective-permute-start | bytes 417800 | tf_op jit(solution)/shard_map/ppermute | solution.py:497
  104.2 21.5 %copy-start.10 = (f32[64]{0:T(128)S(1)}, f32[64]{0:T(128)}, u32[]{:S(2)}) copy-start(f32[64]{0:T(128)} %param.25) | copy-start | bytes 772
  104.3 24.9 %copy-start.3 = (bf16[144,1024]{1,0:T(8,128)(2,1)S(1)}, bf16[144,1024]{1,0:T(8,128)(2,1)}, u32[]{:S(2)}) copy-start(bf16[144,1024]{1,0:T(8,128)(2,1)} %constant.37.clone.spread) | copy-start | bytes 884740
  104.3 24.9 %copy-start.5 = (bf16[32,1024]{1,0:T(8,128)(2,1)S(1)}, bf16[32,1024]{1,0:T(8,128)(2,1)}, u32[]{:S(2)}) copy-start(bf16[32,1024]{1,0:T(8,128)(2,1)} %constant.38.clone.edges) | copy-start | bytes 196612
  107.3 13.6 %all-to-all-start.2 = ((bf16[8,2,144,128]{3,2,1,0:T(8,128)(2,1)}), bf16[8,2,144,128]{3,2,1,0:T(8,128)(2,1)S(1)}, u32[]{:S(2)}, u32[]{:S(2)}) async-start(bf16[8,2,144,128]{3,2,1,0:T(8,128)(2,1)} %merge_heads.1), calls=%async_computation.2 | async-start | bytes 1179648 | tf_op jit(solution)/shard_map/all_to_all | solution.py:501
  121.5 4.3 %collective-permute-start.14 = (bf16[288,128]{1,0:T(8,128)(2,1)S(1)}, bf16[288,128]{1,0:T(8,128)(2,1)S(1)}, u32[]{:S(2)}, u32[]{:S(2)}) collective-permute-start(bf16[288,128]{1,0:T(8,128)(2,1)S(1)} %get-tuple-element.84), channel_id=1, source_target_pairs={{0,8},{8,0},{1,9},{9,1},{2,10},{10,2},{3,11},{11,3},{4,12},{12,4},... | collective-permute-start | bytes 221192 | tf_op jit(solution)/shard_map/ppermute | solution.py:508
  123.5 5.7 %collective-permute-start.15 = (bf16[288,128]{1,0:T(8,128)(2,1)S(1)}, bf16[288,128]{1,0:T(8,128)(2,1)S(1)}, u32[]{:S(2)}, u32[]{:S(2)}) collective-permute-start(bf16[288,128]{1,0:T(8,128)(2,1)S(1)} %get-tuple-element.85), channel_id=1, source_target_pairs={{8,16},{24,32},{40,48},{56,64},{72,80},{88,96},{104,112},{120,128}... | collective-permute-start | bytes 221192 | tf_op jit(solution)/shard_map/ppermute | solution.py:510

commit v8 on v7

--- a/solution.py
+++ b/solution.py
@@ -58,33 +58,6 @@
         compiler_params=pltpu.CompilerParams(vmem_limit_bytes=12 * 2**20),
         name="mix_variables",
     )(*args)
-
-
-def project(rows, weights):
-    count = 2 * len(weights)
-
-    def body(*refs):
-        x, out = refs[0], refs[-1]
-        step = pl.program_id(0)
-        for k, w in enumerate(refs[1:-1]):
-
-            @pl.when((step >= 2 * k) & (step < 2 * k + 2))
-            def _():
-                out[...] = dot_nn(x[...], w[...]).astype(BF)
-
-    def columns(k):
-        return lambda step: (0, jnp.clip(step - 2 * k, 0, 1))
-
-    return pl.pallas_call(
-        body,
-        grid=(count,),
-        out_shape=jax.ShapeDtypeStruct((256, 128 * count), BF),
-        in_specs=[VMEM_SPEC]
-        + [pl.BlockSpec((D, 128), columns(k)) for k in range(len(weights))],
-        out_specs=pl.BlockSpec((256, 128), lambda step: (0, step)),
-        compiler_params=pltpu.CompilerParams(vmem_limit_bytes=12 * 2**20),
-        name="project_rows",
-    )(near(rows), *[pltpu.with_memory_space_constraint(w, pltpu.HBM) for w in weights])
 
 
 def norm_body(pieces, gain, out, slab):
@@ -422,6 +395,27 @@
     )(flags, *[near(x) for x in (own, near_up, far_up, spread, edges, grad, mats, bias)])
 
 
+def finish_body(totals, first, second, third):
+    first[...] = totals[0:576, 0:64].astype(F32)
+    second[...] = totals[0:576, 64:128].astype(F32)
+    third[...] = totals[576:584, 0:64].astype(F32)
+
+
+def finish(totals):
+    return pl.pallas_call(
+        finish_body,
+        out_shape=[
+            jax.ShapeDtypeStruct((576, 64), F32),
+            jax.ShapeDtypeStruct((576, 64), F32),
+            jax.ShapeDtypeStruct((8, 64), F32),
+        ],
+        in_specs=[VMEM_SPEC],
+        out_specs=[VMEM_SPEC] * 3,
+        compiler_params=pltpu.CompilerParams(vmem_limit_bytes=12 * 2**20),
+        name="finish_grads",
+    )(near(totals))
+
+
 def copies(piece, axis, count):
     return lax.all_to_all(jnp.broadcast_to(piece[None], (count,) + piece.shape), axis, 0, 0)
 
@@ -452,14 +446,19 @@
     core_at = lax.axis_index("core")
     turned = jnp.transpose(patches, (0, 1, 3, 2)).reshape(128, 256)
     partial_mix = mix(turned, w_embed.reshape(128, D), var_bias).reshape(8, 32, D)
+    partial_mix, wo = lax.optimization_barrier((partial_mix, wo))
     pieces = lax.all_to_all(partial_mix, VAR, 0, 0)
+    up_mat = jnp.dot(wo, w_up, preferred_element_type=F32).astype(BF)
+    pieces, up_mat = lax.optimization_barrier((pieces, up_mat))
     spread_out, slab = norm_copies(pieces, agg_gain.reshape(1, D))
     normed = lax.all_to_all(spread_out, VAR, 0, 0).reshape(256, D)
 
-    keyvals = project(normed, [wk, wv])
+    keyvals = jnp.concatenate(
+        [jnp.dot(normed, w, preferred_element_type=F32).astype(BF) for w in (wk, wv)], axis=1
+    )
     ahead = lax.ppermute(keyvals, "z", turn(8, 1))
     behind = lax.ppermute(keyvals, "z", turn(8, -1))
-    queries = project(normed, [wq])
+    queries = jnp.dot(normed, wq, preferred_element_type=F32).astype(BF)
     all_queries = [queries] + [lax.ppermute(queries, group, flip(4, k)) for k in (2, 3, 1)]
     fresh = [keyvals, ahead, behind]
     ahead = lax.ppermute(ahead, "z", turn(8, 1))
@@ -473,12 +472,7 @@
         ahead = lax.ppermute(ahead, "z", turn(8, 1))
         behind = lax.ppermute(behind, "z", turn(8, -1))
         carry = flash_step(all_queries, fresh, carry, False)
-        if step == 2:
-            carry, wo = lax.optimization_barrier((carry, wo))
-            up_mat = jnp.dot(wo, w_up, preferred_element_type=F32).astype(BF)
-            ahead, behind, carry, up_mat = lax.optimization_barrier((ahead, behind, carry, up_mat))
-        else:
-            ahead, behind, carry = lax.optimization_barrier((ahead, behind, carry))
+        ahead, behind, carry = lax.optimization_barrier((ahead, behind, carry))
     fresh = [ahead, behind]
 
     blocks = list(flash_step(all_queries, fresh, carry, True))
@@ -516,10 +510,9 @@
     shares = lax.all_to_all(terms.reshape(32, 24, 128), PLANE, 0, 0)
     share = jnp.sum(shares.astype(F32), axis=0).astype(BF)
     share = jnp.sum(copies(share, "z", 8).astype(F32), axis=0).astype(BF)
-    totals = copies(share, PLANE, 32).reshape(768, 128).astype(F32)
-    grad_conv1 = totals[:576, :C].reshape(9, C, C)
-    grad_conv2 = totals[:576, C:].reshape(9, C, C)
-    return (field_out, grad_fine, grad_conv1, grad_conv2, totals[576, :C])
+    totals = copies(share, PLANE, 32).reshape(768, 128)
+    first, second, third = finish(totals)
+    return (field_out, grad_fine, first.reshape(9, C, C), second.reshape(9, C, C), third[0])
 
 
 def solution(mesh):

time: 175 us -> 171 us (0.977)
  blocking collectives: 77.8 us -> 58.7 us
  waiting for transfers between devices: 26.6 us -> 39.6 us
  starting transfers between devices: 35.4 us -> 40.8 us
  Pallas kernels: 21.6 us -> 17.9 us
  matrix products: 5.23 us -> 8.76 us
  local copies, waits for them, and re-layouts: 6.2 us -> 3.98 us
    all_to_all x1 -> x0, blocking collectives: 20.7 us -> none  [device_step(): pieces = lax.all_to_all(partial_mix, VAR, 0, 0)]
    all_to_all x0 -> x1, waiting for transfers between devices: none -> 10.2 us  [device_step(): pieces = lax.all_to_all(partial_mix, VAR, 0, 0)]
    all_to_all x0 -> x1, starting transfers between devices: none -> 5.93 us  [device_step(): pieces = lax.all_to_all(partial_mix, VAR, 0, 0)]
    pallas_call x2 -> x1, Pallas kernels: 5.75 us -> 0.84 us  [finish(): pl.pallas_call(finish_body, out_shape=[jax.ShapeDtypeStruct((576, 64), F3...]
    dot_general x1, matrix products: 2.1 us -> 4.31 us  [device_step(): up_mat = jnp.dot(wo, w_up, preferred_element_type=F32).astype(BF)]
    all_to_all x1, blocking collectives: 16.7 us -> 18.9 us  [device_step(): normed = lax.all_to_all(spread_out, VAR, 0, 0).reshape(256, D)]
    ppermute x3, waiting for transfers between devices: 4.49 us -> 6.62 us  [device_step(): ahead = lax.ppermute(ahead, 'z', turn(8, 1))]
  transfers between devices with their start and end apart: 17 -> 18, of which waited for: 7 -> 8; matrix products, arithmetic and copies ran while one was open for 5% -> 6% of each run, Pallas kernels for 5% -> 4%
where the time goes in v8:
time: 171 us
  blocking collectives  58.7 us (34%)
  starting transfers between devices  40.8 us (24%)
  waiting for transfers between devices  39.6 us (23%)
  Pallas kernels  17.9 us (10%)
  matrix products  8.76 us (5%)
  local copies, waits for them, and re-layouts  3.98 us (2%)
    all_to_all x2, blocking collectives, copies(): lax.all_to_all(jnp.broadcast_to(piece[None], (count,) + piece.shape), axi...  23.3 us
    all_to_all x1, blocking collectives, device_step(): normed = lax.all_to_all(spread_out, VAR, 0, 0).reshape(256, D)  18.9 us
    all_to_all x1, blocking collectives, device_step(): shares = lax.all_to_all(terms.reshape(32, 24, 128), PLANE, 0, 0)  16.6 us
    all_to_all x1, waiting for transfers between devices, device_step(): pieces = lax.all_to_all(partial_mix, VAR, 0, 0)  10.2 us
    pallas_call x4, Pallas kernels, flash_step(): pl.pallas_call(flash_kernel(blocks, len(chunks), first, last), out_shape=...  8.25 us
    all_to_all x1, waiting for transfers between devices, device_step(): pieces = lax.all_to_all(merged, VAR, 0, 0)  8.17 us
    ppermute x3, starting transfers between devices, device_step(): behind = lax.ppermute(behind, 'z', turn(8, -1))  7.73 us
    ppermute x3, starting transfers between devices, device_step(): lax.ppermute(b, group, flip(4, k))  6.94 us
  transfers between devices with their start and end apart: 18, of which 8 were waited for; matrix products, arithmetic and copies ran while one was open for 6% of the time, Pallas kernels for 4%

profile of v8, /device:TPU:1, one launch (start us, length us, event | category | flops | bytes accessed | tf_op | source)
XLA Modules:
  0.0 170.9 jit_solution(4325190887978007328)
XLA Ops:
  0.6 3.9 %mix_variables.1 = bf16[256,2048]{1,0:T(8,128)(2,1)} custom-call(bf16[128,256]{1,0:T(8,128)(2,1)} %bitcast.69, bf16[128,2048]{1,0:T(8,128)(2,1)} %bitcast.68, f32[2,2048]{1,0:T(2,128)} %offsets.1), custom_call_target="tpu_custom_call" | custom-call | tf_op jit(solution)/shard_map/mix_variables/pallas_call | solution.py:48
  4.5 5.9 %all-to-all-start = ((bf16[8,32,2048]{2,1,0:T(8,128)(2,1)}), bf16[8,32,2048]{2,1,0:T(8,128)(2,1)S(1)}, u32[]{:S(2)}, u32[]{:S(2)}) async-start(bf16[8,32,2048]{2,1,0:T(8,128)(2,1)} %bitcast.9), calls=%async_computation | async-start | bytes 2097152 | tf_op jit(solution)/shard_map/all_to_all | solution.py:450
  10.5 4.3 %convolution_convert_fusion.mat = bf16[256,1024]{1,0:T(8,128)(2,1)} fusion(bf16[256,2048]{1,0:T(8,128)(2,1)S(1)} %copy-done, bf16[2048,1024]{1,0:T(8,128)(2,1)} %param.23), kind=kOutput, calls=%fused_computation | convolution fusion | flops 1074003968 | bytes 5767168 | tf_op jit(solution)/shard_map/dot_general | solution.py:451
  14.8 10.2 %all-to-all-done.pieces = bf16[8,32,2048]{2,1,0:T(8,128)(2,1)S(1)} async-done(((bf16[8,32,2048]{2,1,0:T(8,128)(2,1)}), bf16[8,32,2048]{2,1,0:T(8,128)(2,1)S(1)}, u32[]{:S(2)}, u32[]{:S(2)}) %all-to-all-start) | async-done | bytes 1048608 | tf_op jit(solution)/shard_map/all_to_all | solution.py:450
  25.3 18.9 %all_to_all.30 = bf16[8,32,2048]{2,1,0:T(8,128)(2,1)S(1)} all-to-all(bf16[8,32,2048]{2,1,0:T(8,128)(2,1)S(1)} %get-tuple-element.54), channel_id=1, replica_groups=mesh['xh'=2,'z'=8,'core'=2,'y'=4,'xl'=2] {'y','xl'}, dimensions={0} | all-to-all | bytes 2097152 | tf_op jit(solution)/shard_map/all_to_all | solution.py:454
  45.1 1.7 %collective-permute-start.3 = (bf16[256,512]{1,0:T(8,128)(2,1)S(1)}, bf16[256,512]{1,0:T(8,128)(2,1)S(1)}, u32[]{:S(2)}, u32[]{:S(2)}) collective-permute-start(bf16[256,512]{1,0:T(8,128)(2,1)S(1)} %pad_maximum_fusion.1.refs_4_), channel_id=1, source_target_pairs={{0,16},{16,32},{32,48},{48,64},{64,80},{80,96},{96,112},{112,0},{1... | collective-permute-start | bytes 786440 | tf_op jit(solution)/shard_map/ppermute | solution.py:459
  46.8 4.0 %collective-permute-start.5 = (bf16[256,512]{1,0:T(8,128)(2,1)S(1)}, bf16[256,512]{1,0:T(8,128)(2,1)S(1)}, u32[]{:S(2)}, u32[]{:S(2)}) collective-permute-start(bf16[256,512]{1,0:T(8,128)(2,1)S(1)} %pad_maximum_fusion.1.refs_4_), channel_id=1, source_target_pairs={{0,112},{16,0},{32,16},{48,32},{64,48},{80,64},{96,80},{112,96},{1... | collective-permute-start | bytes 786440 | tf_op jit(solution)/shard_map/ppermute | solution.py:460
  50.8 4.7 %collective-permute-done.3.refs_5_ = bf16[256,512]{1,0:T(8,128)(2,1)S(1)} collective-permute-done((bf16[256,512]{1,0:T(8,128)(2,1)S(1)}, bf16[256,512]{1,0:T(8,128)(2,1)S(1)}, u32[]{:S(2)}, u32[]{:S(2)}) %collective-permute-start.3) | collective-permute-done | bytes 262176 | tf_op jit(solution)/shard_map/ppermute | solution.py:459
  55.5 2.7 %collective-permute-start.6 = (bf16[256,512]{1,0:T(8,128)(2,1)S(1)}, bf16[256,512]{1,0:T(8,128)(2,1)S(1)}, u32[]{:S(2)}, u32[]{:S(2)}) collective-permute-start(bf16[256,512]{1,0:T(8,128)(2,1)S(1)} %collective-permute-done.5.refs_6_), channel_id=1, source_target_pairs={{0,112},{16,0},{32,16},{48,32},{64,48},{80,64},{96,80},{112,96},{1... | collective-permute-start | bytes 786440 | tf_op jit(solution)/shard_map/ppermute | solution.py:465
  58.6 2.5 %collective-permute-start = (bf16[256,256]{1,0:T(8,128)(2,1)S(1)}, bf16[256,256]{1,0:T(8,128)(2,1)S(1)}, u32[]{:S(2)}, u32[]{:S(2)}) collective-permute-start(bf16[256,256]{1,0:T(8,128)(2,1)S(1)} %convolution_convert_fusion.3.refs_0_), channel_id=1, source_target_pairs={{0,128},{8,136},{128,0},{136,8},{1,129},{9,137},{129,1},{137,9},{2... | collective-permute-start | bytes 393224 | tf_op jit(solution)/shard_map/ppermute | solution.py:462
  61.2 3.7 %collective-permute-start.1 = (bf16[256,256]{1,0:T(8,128)(2,1)S(1)}, bf16[256,256]{1,0:T(8,128)(2,1)S(1)}, u32[]{:S(2)}, u32[]{:S(2)}) collective-permute-start(bf16[256,256]{1,0:T(8,128)(2,1)S(1)} %convolution_convert_fusion.3.refs_0_), channel_id=1, source_target_pairs={{0,136},{8,128},{128,8},{136,0},{1,137},{9,129},{129,9},{137,1},{2... | collective-permute-start | bytes 393224 | tf_op jit(solution)/shard_map/ppermute | solution.py:462
  64.9 5.0 %collective-permute-done.1.refs_2_ = bf16[256,256]{1,0:T(8,128)(2,1)S(1)} collective-permute-done((bf16[256,256]{1,0:T(8,128)(2,1)S(1)}, bf16[256,256]{1,0:T(8,128)(2,1)S(1)}, u32[]{:S(2)}, u32[]{:S(2)}) %collective-permute-start.1) | collective-permute-done | bytes 131104 | tf_op jit(solution)/shard_map/ppermute | solution.py:462
  69.9 2.6 %flash_step.3 = (f32[8,1024]{1,0:T(8,128)S(1)}, f32[256,1024]{1,0:T(8,128)S(1)}) custom-call(bf16[256,256]{1,0:T(8,128)(2,1)S(1)} %convolution_convert_fusion.3.refs_0_, bf16[256,256]{1,0:T(8,128)(2,1)S(1)} %collective-permute-done.refs_1_, bf16[256,256]{1,0:T(8,128)(2,1)S(1)} %collective-permute-done.1.refs_2_, ...), custom_call_target="tpu_custom_call" | custom-call | tf_op jit(solution)/shard_map/flash_step/pallas_call | solution.py:163
  72.6 2.7 %collective-permute-start.8 = (bf16[256,512]{1,0:T(8,128)(2,1)S(1)}, bf16[256,512]{1,0:T(8,128)(2,1)S(1)}, u32[]{:S(2)}, u32[]{:S(2)}) collective-permute-start(bf16[256,512]{1,0:T(8,128)(2,1)S(1)} %collective-permute-done.6.refs_5_), channel_id=1, source_target_pairs={{0,112},{16,0},{32,16},{48,32},{64,48},{80,64},{96,80},{112,96},{1... | collective-permute-start | bytes 786440 | tf_op jit(solution)/shard_map/ppermute | solution.py:473
  75.3 2.0 %flash_step.4 = (f32[8,1024]{1,0:T(8,128)S(1)}, f32[256,1024]{1,0:T(8,128)S(1)}) custom-call(bf16[256,256]{1,0:T(8,128)(2,1)S(1)} %convolution_convert_fusion.3.refs_0_, bf16[256,256]{1,0:T(8,128)(2,1)S(1)} %collective-permute-done.refs_1_, bf16[256,256]{1,0:T(8,128)(2,1)S(1)} %collective-permute-done.1.refs_2_, ...), custom_call_target="tpu_custom_call" | custom-call | tf_op jit(solution)/shard_map/flash_step/pallas_call | solution.py:163
  77.3 3.3 %collective-permute-done.7.refs_4_ = bf16[256,512]{1,0:T(8,128)(2,1)S(1)} collective-permute-done((bf16[256,512]{1,0:T(8,128)(2,1)S(1)}, bf16[256,512]{1,0:T(8,128)(2,1)S(1)}, u32[]{:S(2)}, u32[]{:S(2)}) %collective-permute-start.7) | collective-permute-done | bytes 262176 | tf_op jit(solution)/shard_map/ppermute | solution.py:472
  81.2 2.4 %collective-permute-start.10 = (bf16[128,512]{1,0:T(8,128)(2,1)}, bf16[128,512]{1,0:T(8,128)(2,1)S(1)}, u32[]{:S(2)}, u32[]{:S(2)}) collective-permute-start(bf16[128,512]{1,0:T(8,128)(2,1)} %slice.16), channel_id=1, source_target_pairs={{0,112},{16,0},{32,16},{48,32},{64,48},{80,64},{96,80},{112,96},{1... | collective-permute-start | bytes 393224 | tf_op jit(solution)/shard_map/ppermute | solution.py:473
  84.3 1.9 %flash_step.5 = (f32[8,1024]{1,0:T(8,128)S(1)}, f32[256,1024]{1,0:T(8,128)S(1)}) custom-call(bf16[256,256]{1,0:T(8,128)(2,1)S(1)} %convolution_convert_fusion.3.refs_0_, bf16[256,256]{1,0:T(8,128)(2,1)S(1)} %collective-permute-done.refs_1_, bf16[256,256]{1,0:T(8,128)(2,1)S(1)} %collective-permute-done.1.refs_2_, ...), custom_call_target="tpu_custom_call" | custom-call | tf_op jit(solution)/shard_map/flash_step/pallas_call | solution.py:163
  86.1 3.4 %collective-permute-done.9.refs_4_ = bf16[128,512]{1,0:T(8,128)(2,1)S(1)} collective-permute-done((bf16[128,512]{1,0:T(8,128)(2,1)}, bf16[128,512]{1,0:T(8,128)(2,1)S(1)}, u32[]{:S(2)}, u32[]{:S(2)}) %collective-permute-start.9) | collective-permute-done | bytes 131104 | tf_op jit(solution)/shard_map/ppermute | solution.py:472
  89.5 1.8 %flash_last.1 = (bf16[272,256]{1,0:T(8,128)(2,1)S(1)}, bf16[272,256]{1,0:T(8,128)(2,1)}, bf16[272,256]{1,0:T(8,128)(2,1)S(1)}, bf16[272,256]{1,0:T(8,128)(2,1)S(1)}) custom-call(bf16[256,256]{1,0:T(8,128)(2,1)S(1)} %convolution_convert_fusion.3.refs_0_, bf16[256,256]{1,0:T(8,128)(2,1)S(1)} %collective-permute-done.refs_1_, ...), custom_call_target="tpu_custom_call" | custom-call | tf_op jit(solution)/shard_map/flash_last/pallas_call | solution.py:163
  91.3 4.9 %collective-permute-start.11 = (bf16[272,256]{1,0:T(8,128)(2,1)}, bf16[272,256]{1,0:T(8,128)(2,1)S(1)}, u32[]{:S(2)}, u32[]{:S(2)}) collective-permute-start(bf16[272,256]{1,0:T(8,128)(2,1)} %get-tuple-element.78), channel_id=1, source_target_pairs={{0,128},{8,136},{128,0},{136,8},{1,129},{9,137},{129,1},{137,9},{2... | collective-permute-start | bytes 417800 | tf_op jit(solution)/shard_map/ppermute | solution.py:491
  96.2 2.0 %collective-permute-start.12 = (bf16[272,256]{1,0:T(8,128)(2,1)S(1)}, bf16[272,256]{1,0:T(8,128)(2,1)S(1)}, u32[]{:S(2)}, u32[]{:S(2)}) collective-permute-start(bf16[272,256]{1,0:T(8,128)(2,1)S(1)} %get-tuple-element.79), channel_id=1, source_target_pairs={{0,136},{8,128},{128,8},{136,0},{1,137},{9,129},{129,9},{137,1},{2... | collective-permute-start | bytes 417800 | tf_op jit(solution)/shard_map/ppermute | solution.py:491
  98.3 3.1 %fusion.base = f32[32,1024]{1,0:T(8,128)S(1)} fusion(bf16[32,2048]{1,0:T(8,128)(2,1)} %copy-done.4, bf16[2048,1024]{1,0:T(8,128)(2,1)} %param.23), kind=kOutput, calls=%fused_computation.12 | convolution fusion | flops 134217728 | bytes 4456448 | tf_op jit(solution)/shard_map/dot_general | solution.py:480
  104.7 3.9 %all-to-all-start.2 = ((bf16[8,2,144,128]{3,2,1,0:T(8,128)(2,1)}), bf16[8,2,144,128]{3,2,1,0:T(8,128)(2,1)S(1)}, u32[]{:S(2)}, u32[]{:S(2)}) async-start(bf16[8,2,144,128]{3,2,1,0:T(8,128)(2,1)} %merge_heads.1), calls=%async_computation.2 | async-start | bytes 1179648 | tf_op jit(solution)/shard_map/all_to_all | solution.py:495
  110.3 8.2 %all-to-all-done.2.pieces = bf16[8,2,144,128]{3,2,1,0:T(8,128)(2,1)S(1)} async-done(((bf16[8,2,144,128]{3,2,1,0:T(8,128)(2,1)}), bf16[8,2,144,128]{3,2,1,0:T(8,128)(2,1)S(1)}, u32[]{:S(2)}, u32[]{:S(2)}) %all-to-all-start.2) | async-done | bytes 589856 | tf_op jit(solution)/shard_map/all_to_all | solution.py:495
  119.1 2.0 %collective-permute-start.14 = (bf16[288,128]{1,0:T(8,128)(2,1)S(1)}, bf16[288,128]{1,0:T(8,128)(2,1)S(1)}, u32[]{:S(2)}, u32[]{:S(2)}) collective-permute-start(bf16[288,128]{1,0:T(8,128)(2,1)S(1)} %get-tuple-element.87), channel_id=1, source_target_pairs={{0,8},{8,0},{1,9},{9,1},{2,10},{10,2},{3,11},{11,3},{4,12},{12,4},... | collective-permute-start | bytes 221192 | tf_op jit(solution)/shard_map/ppermute | solution.py:502
  121.1 2.1 %collective-permute-start.15 = (bf16[288,128]{1,0:T(8,128)(2,1)S(1)}, bf16[288,128]{1,0:T(8,128)(2,1)S(1)}, u32[]{:S(2)}, u32[]{:S(2)}) collective-permute-start(bf16[288,128]{1,0:T(8,128)(2,1)S(1)} %get-tuple-element.88), channel_id=1, source_target_pairs={{8,16},{24,32},{40,48},{56,64},{72,80},{88,96},{104,112},{120,128}... | collective-permute-start | bytes 221192 | tf_op jit(solution)/shard_map/ppermute | solution.py:504
  123.4 3.4 %collective-permute-done.15.far_up = bf16[288,128]{1,0:T(8,128)(2,1)S(1)} collective-permute-done((bf16[288,128]{1,0:T(8,128)(2,1)S(1)}, bf16[288,128]{1,0:T(8,128)(2,1)S(1)}, u32[]{:S(2)}, u32[]{:S(2)}) %collective-permute-start.15) | collective-permute-done | bytes 73760 | tf_op jit(solution)/shard_map/ppermute | solution.py:504
  126.8 2.8 %fine_stage.1 = (bf16[4,64,128]{2,1,0:T(8,128)(2,1)}, bf16[4,64,128]{2,1,0:T(8,128)(2,1)}, bf16[768,128]{1,0:T(8,128)(2,1)S(1)}) custom-call(s32[5]{0:T(128)S(1)} %convert_element_type.19.flags, bf16[2,144,128]{2,1,0:T(8,128)(2,1)S(1)} %get-tuple-element.86.own, bf16[288,128]{1,0:T(8,128)(2,1)S(1)} %collective-permute-done.14.near_up, ...), custom_call_target="tpu_custom_call" | custom-call | tf_op jit(solution)/shard_map/fine_stage/pallas_call | solution.py:384
  129.6 16.6 %all_to_all.31 = bf16[32,24,128]{2,1,0:T(8,128)(2,1)S(1)} all-to-all(bf16[32,24,128]{2,1,0:T(8,128)(2,1)S(1)} %bitcast.55), channel_id=1, replica_groups=mesh['xh'=2,'z'=8,'core'=2,'y'=4,'xl'=2] {'xh','core','y','xl'}, dimensions={0} | all-to-all | bytes 393216 | tf_op jit(solution)/shard_map/all_to_all | solution.py:510
  146.2 9.8 %all_to_all.32 = bf16[8,24,128]{2,1,0:T(8,128)(2,1)S(1)} all-to-all(bf16[8,24,128]{2,1,0:T(8,128)(2,1)S(1)} %broadcast_in_dim.4), channel_id=1, replica_groups=mesh['xh'=2,'z'=8,'core'=2,'y'=4,'xl'=2] {'z'}, dimensions={0} | all-to-all | bytes 98304 | tf_op jit(solution)/shard_map/all_to_all | solution.py:420
  156.1 13.5 %all_to_all.33 = bf16[32,24,128]{2,1,0:T(8,128)(2,1)S(1)} all-to-all(bf16[32,24,128]{2,1,0:T(8,128)(2,1)S(1)} %broadcast_in_dim.5), channel_id=1, replica_groups=mesh['xh'=2,'z'=8,'core'=2,'y'=4,'xl'=2] {'xh','core','y','xl'}, dimensions={0} | all-to-all | bytes 393216 | tf_op jit(solution)/shard_map/all_to_all | solution.py:420
  (79 shorter events, 10.2 us)
Async XLA Ops:
  0.6 9.8 %copy-start = (bf16[256,2048]{1,0:T(8,128)(2,1)S(1)}, bf16[256,2048]{1,0:T(8,128)(2,1)}, u32[]{:S(2)}) copy-start(bf16[256,2048]{1,0:T(8,128)(2,1)} %param.22) | copy-start | bytes 3145732
  4.5 20.5 %all-to-all-start = ((bf16[8,32,2048]{2,1,0:T(8,128)(2,1)}), bf16[8,32,2048]{2,1,0:T(8,128)(2,1)S(1)}, u32[]{:S(2)}, u32[]{:S(2)}) async-start(bf16[8,32,2048]{2,1,0:T(8,128)(2,1)} %bitcast.9), calls=%async_computation | async-start | bytes 2097152 | tf_op jit(solution)/shard_map/all_to_all | solution.py:450
  10.5 14.6 %copy-start.6 = (f32[2048]{0:T(1024)S(1)}, f32[2048]{0:T(1024)}, u32[]{:S(2)}) copy-start(f32[2048]{0:T(1024)} %param.18) | copy-start | bytes 24580
  10.5 33.7 %copy-start.7 = (bf16[2048,256]{1,0:T(8,128)(2,1)S(1)}, bf16[2048,256]{1,0:T(8,128)(2,1)}, u32[]{:S(2)}) copy-start(bf16[2048,256]{1,0:T(8,128)(2,1)} %param.21) | copy-start | bytes 3145732
  25.0 19.6 %copy-start.8 = (bf16[2048,256]{1,0:T(8,128)(2,1)S(1)}, bf16[2048,256]{1,0:T(8,128)(2,1)}, u32[]{:S(2)}) copy-start(bf16[2048,256]{1,0:T(8,128)(2,1)} %param.20) | copy-start | bytes 3145732
  25.0 33.2 %copy-start.9 = (bf16[2048,256]{1,0:T(8,128)(2,1)S(1)}, bf16[2048,256]{1,0:T(8,128)(2,1)}, u32[]{:S(2)}) copy-start(bf16[2048,256]{1,0:T(8,128)(2,1)} %param.19) | copy-start | bytes 3145732
  25.3 19.8 %copy-start.4 = (bf16[32,2048]{1,0:T(8,128)(2,1)}, bf16[32,2048]{1,0:T(8,128)(2,1)S(1)}, u32[]{:S(2)}) copy-start(bf16[32,2048]{1,0:T(8,128)(2,1)S(1)} %get-tuple-element.75) | copy-start | bytes 393220
  45.1 10.4 %collective-permute-start.3 = (bf16[256,512]{1,0:T(8,128)(2,1)S(1)}, bf16[256,512]{1,0:T(8,128)(2,1)S(1)}, u32[]{:S(2)}, u32[]{:S(2)}) collective-permute-start(bf16[256,512]{1,0:T(8,128)(2,1)S(1)} %pad_maximum_fusion.1.refs_4_), channel_id=1, source_target_pairs={{0,16},{16,32},{32,48},{48,64},{64,80},{80,96},{96,112},{112,0},{1... | collective-permute-start | bytes 786440 | tf_op jit(solution)/shard_map/ppermute | solution.py:459
  46.8 8.7 %collective-permute-start.5 = (bf16[256,512]{1,0:T(8,128)(2,1)S(1)}, bf16[256,512]{1,0:T(8,128)(2,1)S(1)}, u32[]{:S(2)}, u32[]{:S(2)}) collective-permute-start(bf16[256,512]{1,0:T(8,128)(2,1)S(1)} %pad_maximum_fusion.1.refs_4_), channel_id=1, source_target_pairs={{0,112},{16,0},{32,16},{48,32},{64,48},{80,64},{96,80},{112,96},{1... | collective-permute-start | bytes 786440 | tf_op jit(solution)/shard_map/ppermute | solution.py:460
  55.5 17.0 %collective-permute-start.4 = (bf16[256,512]{1,0:T(8,128)(2,1)S(1)}, bf16[256,512]{1,0:T(8,128)(2,1)S(1)}, u32[]{:S(2)}, u32[]{:S(2)}) collective-permute-start(bf16[256,512]{1,0:T(8,128)(2,1)S(1)} %collective-permute-done.3.refs_5_), channel_id=1, source_target_pairs={{0,16},{16,32},{32,48},{48,64},{64,80},{80,96},{96,112},{112,0},{1... | collective-permute-start | bytes 786440 | tf_op jit(solution)/shard_map/ppermute | solution.py:464
  55.5 17.0 %collective-permute-start.6 = (bf16[256,512]{1,0:T(8,128)(2,1)S(1)}, bf16[256,512]{1,0:T(8,128)(2,1)S(1)}, u32[]{:S(2)}, u32[]{:S(2)}) collective-permute-start(bf16[256,512]{1,0:T(8,128)(2,1)S(1)} %collective-permute-done.5.refs_6_), channel_id=1, source_target_pairs={{0,112},{16,0},{32,16},{48,32},{64,48},{80,64},{96,80},{112,96},{1... | collective-permute-start | bytes 786440 | tf_op jit(solution)/shard_map/ppermute | solution.py:465
  58.6 6.3 %collective-permute-start = (bf16[256,256]{1,0:T(8,128)(2,1)S(1)}, bf16[256,256]{1,0:T(8,128)(2,1)S(1)}, u32[]{:S(2)}, u32[]{:S(2)}) collective-permute-start(bf16[256,256]{1,0:T(8,128)(2,1)S(1)} %convolution_convert_fusion.3.refs_0_), channel_id=1, source_target_pairs={{0,128},{8,136},{128,0},{136,8},{1,129},{9,137},{129,1},{137,9},{2... | collective-permute-start | bytes 393224 | tf_op jit(solution)/shard_map/ppermute | solution.py:462
  61.2 8.7 %collective-permute-start.1 = (bf16[256,256]{1,0:T(8,128)(2,1)S(1)}, bf16[256,256]{1,0:T(8,128)(2,1)S(1)}, u32[]{:S(2)}, u32[]{:S(2)}) collective-permute-start(bf16[256,256]{1,0:T(8,128)(2,1)S(1)} %convolution_convert_fusion.3.refs_0_), channel_id=1, source_target_pairs={{0,136},{8,128},{128,8},{136,0},{1,137},{9,129},{129,9},{137,1},{2... | collective-permute-start | bytes 393224 | tf_op jit(solution)/shard_map/ppermute | solution.py:462
  64.9 5.0 %collective-permute-start.2 = (bf16[256,256]{1,0:T(8,128)(2,1)S(1)}, bf16[256,256]{1,0:T(8,128)(2,1)S(1)}, u32[]{:S(2)}, u32[]{:S(2)}) collective-permute-start(bf16[256,256]{1,0:T(8,128)(2,1)S(1)} %convolution_convert_fusion.3.refs_0_), channel_id=1, source_target_pairs={{0,8},{8,0},{128,136},{136,128},{1,9},{9,1},{129,137},{137,129},{2... | collective-permute-start | bytes 393224 | tf_op jit(solution)/shard_map/ppermute | solution.py:462
  72.5 8.0 %collective-permute-start.7 = (bf16[256,512]{1,0:T(8,128)(2,1)S(1)}, bf16[256,512]{1,0:T(8,128)(2,1)S(1)}, u32[]{:S(2)}, u32[]{:S(2)}) collective-permute-start(bf16[256,512]{1,0:T(8,128)(2,1)S(1)} %collective-permute-done.4.refs_4_), channel_id=1, source_target_pairs={{0,16},{16,32},{32,48},{48,64},{64,80},{80,96},{96,112},{112,0},{1... | collective-permute-start | bytes 786440 | tf_op jit(solution)/shard_map/ppermute | solution.py:472
  72.6 7.9 %collective-permute-start.8 = (bf16[256,512]{1,0:T(8,128)(2,1)S(1)}, bf16[256,512]{1,0:T(8,128)(2,1)S(1)}, u32[]{:S(2)}, u32[]{:S(2)}) collective-permute-start(bf16[256,512]{1,0:T(8,128)(2,1)S(1)} %collective-permute-done.6.refs_5_), channel_id=1, source_target_pairs={{0,112},{16,0},{32,16},{48,32},{64,48},{80,64},{96,80},{112,96},{1... | collective-permute-start | bytes 786440 | tf_op jit(solution)/shard_map/ppermute | solution.py:473
  81.2 4.9 %collective-permute-start.10 = (bf16[128,512]{1,0:T(8,128)(2,1)}, bf16[128,512]{1,0:T(8,128)(2,1)S(1)}, u32[]{:S(2)}, u32[]{:S(2)}) collective-permute-start(bf16[128,512]{1,0:T(8,128)(2,1)} %slice.16), channel_id=1, source_target_pairs={{0,112},{16,0},{32,16},{48,32},{64,48},{80,64},{96,80},{112,96},{1... | collective-permute-start | bytes 393224 | tf_op jit(solution)/shard_map/ppermute | solution.py:473
  84.3 5.2 %collective-permute-start.9 = (bf16[128,512]{1,0:T(8,128)(2,1)}, bf16[128,512]{1,0:T(8,128)(2,1)S(1)}, u32[]{:S(2)}, u32[]{:S(2)}) collective-permute-start(bf16[128,512]{1,0:T(8,128)(2,1)} %slice.15), channel_id=1, source_target_pairs={{0,16},{16,32},{32,48},{48,64},{64,80},{80,96},{96,112},{112,0},{1... | collective-permute-start | bytes 393224 | tf_op jit(solution)/shard_map/ppermute | solution.py:472
  84.3 17.1 %copy-start.1 = (bf16[4,64,128]{2,1,0:T(8,128)(2,1)S(1)}, bf16[4,64,128]{2,1,0:T(8,128)(2,1)}, u32[]{:S(2)}) copy-start(bf16[4,64,128]{2,1,0:T(8,128)(2,1)} %grad.1) | copy-start | bytes 196612
  86.1 17.3 %copy-start.2 = (bf16[256,1024]{1,0:T(8,128)(2,1)S(1)}, bf16[256,1024]{1,0:T(8,128)(2,1)}, u32[]{:S(2)}) copy-start(bf16[256,1024]{1,0:T(8,128)(2,1)} %convolution_convert_fusion.mat) | copy-start | bytes 1572868
  91.3 10.6 %collective-permute-start.11 = (bf16[272,256]{1,0:T(8,128)(2,1)}, bf16[272,256]{1,0:T(8,128)(2,1)S(1)}, u32[]{:S(2)}, u32[]{:S(2)}) collective-permute-start(bf16[272,256]{1,0:T(8,128)(2,1)} %get-tuple-element.78), channel_id=1, source_target_pairs={{0,128},{8,136},{128,0},{136,8},{1,129},{9,137},{129,1},{137,9},{2... | collective-permute-start | bytes 417800 | tf_op jit(solution)/shard_map/ppermute | solution.py:491
  96.2 7.3 %collective-permute-start.12 = (bf16[272,256]{1,0:T(8,128)(2,1)S(1)}, bf16[272,256]{1,0:T(8,128)(2,1)S(1)}, u32[]{:S(2)}, u32[]{:S(2)}) collective-permute-start(bf16[272,256]{1,0:T(8,128)(2,1)S(1)} %get-tuple-element.79), channel_id=1, source_target_pairs={{0,136},{8,128},{128,8},{136,0},{1,137},{9,129},{129,9},{137,1},{2... | collective-permute-start | bytes 417800 | tf_op jit(solution)/shard_map/ppermute | solution.py:491
  98.2 10.7 %copy-start.11 = (bf16[9,64,64]{2,1,0:T(8,128)(2,1)S(1)}, bf16[9,64,64]{2,1,0:T(8,128)(2,1)}, u32[]{:S(2)}) copy-start(bf16[9,64,64]{2,1,0:T(8,128)(2,1)} %param.26) | copy-start | bytes 221188
  98.2 11.0 %copy-start.10 = (bf16[9,64,64]{2,1,0:T(8,128)(2,1)S(1)}, bf16[9,64,64]{2,1,0:T(8,128)(2,1)}, u32[]{:S(2)}) copy-start(bf16[9,64,64]{2,1,0:T(8,128)(2,1)} %param.24) | copy-start | bytes 221188
  98.2 5.3 %collective-permute-start.13 = (bf16[272,256]{1,0:T(8,128)(2,1)S(1)}, bf16[272,256]{1,0:T(8,128)(2,1)S(1)}, u32[]{:S(2)}, u32[]{:S(2)}) collective-permute-start(bf16[272,256]{1,0:T(8,128)(2,1)S(1)} %get-tuple-element.80), channel_id=1, source_target_pairs={{0,8},{8,0},{128,136},{136,128},{1,9},{9,1},{129,137},{137,129},{2... | collective-permute-start | bytes 417800 | tf_op jit(solution)/shard_map/ppermute | solution.py:491
  101.6 21.7 %copy-start.12 = (f32[64]{0:T(128)S(1)}, f32[64]{0:T(128)}, u32[]{:S(2)}) copy-start(f32[64]{0:T(128)} %param.25) | copy-start | bytes 772
  101.7 25.1 %copy-start.3 = (bf16[144,1024]{1,0:T(8,128)(2,1)S(1)}, bf16[144,1024]{1,0:T(8,128)(2,1)}, u32[]{:S(2)}) copy-start(bf16[144,1024]{1,0:T(8,128)(2,1)} %constant.37.clone.spread) | copy-start | bytes 884740
  101.7 25.1 %copy-start.5 = (bf16[32,1024]{1,0:T(8,128)(2,1)S(1)}, bf16[32,1024]{1,0:T(8,128)(2,1)}, u32[]{:S(2)}) copy-start(bf16[32,1024]{1,0:T(8,128)(2,1)} %constant.38.clone.edges) | copy-start | bytes 196612
  104.7 13.7 %all-to-all-start.2 = ((bf16[8,2,144,128]{3,2,1,0:T(8,128)(2,1)}), bf16[8,2,144,128]{3,2,1,0:T(8,128)(2,1)S(1)}, u32[]{:S(2)}, u32[]{:S(2)}) async-start(bf16[8,2,144,128]{3,2,1,0:T(8,128)(2,1)} %merge_heads.1), calls=%async_computation.2 | async-start | bytes 1179648 | tf_op jit(solution)/shard_map/all_to_all | solution.py:495
  119.1 4.3 %collective-permute-start.14 = (bf16[288,128]{1,0:T(8,128)(2,1)S(1)}, bf16[288,128]{1,0:T(8,128)(2,1)S(1)}, u32[]{:S(2)}, u32[]{:S(2)}) collective-permute-start(bf16[288,128]{1,0:T(8,128)(2,1)S(1)} %get-tuple-element.87), channel_id=1, source_target_pairs={{0,8},{8,0},{1,9},{9,1},{2,10},{10,2},{3,11},{11,3},{4,12},{12,4},... | collective-permute-start | bytes 221192 | tf_op jit(solution)/shard_map/ppermute | solution.py:502
  121.1 5.7 %collective-permute-start.15 = (bf16[288,128]{1,0:T(8,128)(2,1)S(1)}, bf16[288,128]{1,0:T(8,128)(2,1)S(1)}, u32[]{:S(2)}, u32[]{:S(2)}) collective-permute-start(bf16[288,128]{1,0:T(8,128)(2,1)S(1)} %get-tuple-element.88), channel_id=1, source_target_pairs={{8,16},{24,32},{40,48},{56,64},{72,80},{88,96},{104,112},{120,128}... | collective-permute-start | bytes 221192 | tf_op jit(solution)/shard_map/ppermute | solution.py:504
